TPU v7x, 32 devices: a whole 2x2x4 slice. The times are simulated.
32 devices in a mesh: dp: 4 (over z), seq: 4 (over x, core), mp: 2 (over y).
Axes of the slice: x: 2, y: 2, z: 4, core: 2. Of those that a mesh axis runs over, the one named last changes fastest.
Arguments:
- hidden: bfloat16 [2, 4, 2048, 2048], P(None, 'dp', 'seq'), may hold values from -6 to 6
- w_query: bfloat16 [2048, 2048], P(('dp', 'seq'), 'mp'), may hold values from -0.125 to 0.125
- w_key: bfloat16 [2048, 1024], P(('dp', 'seq'), 'mp'), may hold values from -0.125 to 0.125
- w_value: bfloat16 [2048, 1024], P(('dp', 'seq'), 'mp'), may hold values from -0.125 to 0.125
- w_out: bfloat16 [2048, 2048], P('mp', ('dp', 'seq')), may hold values from -0.75 to 0.75
- w_gate: bfloat16 [2048, 6144], P(('dp', 'seq'), 'mp'), may hold values from -0.125 to 0.125
- w_up: bfloat16 [2048, 6144], P(('dp', 'seq'), 'mp'), may hold values from -0.125 to 0.125
- w_down: bfloat16 [6144, 2048], P('mp', ('dp', 'seq')), may hold values from -0.078125 to 0.078125
- norm_attn: bfloat16 [2048], P(('dp', 'seq')), may hold values from 0.25 to 1.75
- norm_ffn: bfloat16 [2048], P(('dp', 'seq')), may hold values from 0.25 to 1.75
- norm_query: bfloat16 [128], replicated, may hold values from 0.25 to 1.75
- norm_key: bfloat16 [128], replicated, may hold values from 0.25 to 1.75
- segments: int32 [2, 4, 2048], P(None, 'dp', 'seq'), may hold values from 0 to 7, as said below
- positions: int32 [2, 4, 2048], P(None, 'dp', 'seq'), may hold values from 0 to 2047, as said below
- cotangent: bfloat16 [2, 4, 2048, 2048], P(None, 'dp', 'seq'), may hold values from -6 to 6
Outputs:
- layer_out: bfloat16 [2, 4, 2048, 2048], P(None, 'dp', 'seq')
- grad_hidden: bfloat16 [2, 4, 2048, 2048], P(None, 'dp', 'seq')
- grad_query: float32 [2048, 2048], P(('dp', 'seq'), 'mp')
- grad_key: float32 [2048, 1024], P(('dp', 'seq'), 'mp')
- grad_value: float32 [2048, 1024], P(('dp', 'seq'), 'mp')
- grad_out: float32 [2048, 2048], P('mp', ('dp', 'seq'))
- grad_gate: float32 [2048, 6144], P(('dp', 'seq'), 'mp')
- grad_up: float32 [2048, 6144], P(('dp', 'seq'), 'mp')
- grad_down: float32 [6144, 2048], P('mp', ('dp', 'seq'))
- grad_norm_attn: float32 [2048], P(('dp', 'seq'))
- grad_norm_ffn: float32 [2048], P(('dp', 'seq'))
- grad_norm_query: float32 [128], replicated
- grad_norm_key: float32 [128], replicated
Inputs may be any that keep to these rules, and one draw needn't show every extreme that they name: `segments`: along each sequence the segment numbers never fall and start at 0; a document is a run of equal numbers, and document lengths are heavy-tailed. One sequence is a single document. `positions`: each token's position counts up by one from 0 at the first token of its document.
All inputs are finite; a program needn't handle non-finite values.
Results may differ from a plain program's by a relative error of at most 0.025.
Values may be sent and summed in bfloat16 or wider, within the bound.
No kernel may reach another device: no remote copies, remote signals or barrier semaphores. Data moves between devices by JAX's collectives and lax.ppermute only.
A program may use at most 384 MiB of HBM per device.

v0:
```python
import jax
import jax.numpy as jnp
from jax import lax
from jax.sharding import PartitionSpec as P

HEADS = 16
KV_HEADS = 8
HEAD = 128
MICRO = 2


EPS = 1e-06
ROPE_BASE = 1000000.0


def tdot(left, right):
    return lax.dot_general(
        left, right, (((0,), (0,)), ((), ())), preferred_element_type=jnp.float32
    )


def rdot(left, right):
    return lax.dot_general(
        left, right, (((1,), (1,)), ((), ())), preferred_element_type=jnp.float32
    )


def rotate(values, cosine, sine):
    half_size = values.shape[-1] // 2
    turned = jnp.concatenate([-values[..., half_size:], values[..., :half_size]], axis=-1)
    return values * cosine + turned * sine


def rotate_back(grads, cosine, sine):
    half_size = grads.shape[-1] // 2
    scaled = grads * sine
    back_part = jnp.concatenate([scaled[..., half_size:], -scaled[..., :half_size]], axis=-1)
    return grads * cosine + back_part


def norm_back(grads, values, inverse, gain):
    scaled = grads * gain
    return inverse * scaled - values * inverse**3 * jnp.mean(
        scaled * values, axis=-1, keepdims=True
    )


def masked_scores(
    queries, keys_all, seg_query, seg_keys, start_row, first_row, block_rows, score_scale
):
    raw_scores = (
        jnp.einsum("qkgd,tkd->kgqt", queries, keys_all, preferred_element_type=jnp.float32)
        * score_scale
    )
    row_ids = first_row + start_row + jnp.arange(block_rows, dtype=jnp.int32)
    key_ids = jnp.arange(keys_all.shape[0], dtype=jnp.int32)
    allowed = (seg_query[:, None] == seg_keys[None, :]) & (row_ids[:, None] >= key_ids[None, :])
    return (jnp.where(allowed[None, None], raw_scores, -1e30), queries)


def local(
    hidden,
    w_query,
    w_key,
    w_value,
    w_out,
    w_gate,
    w_up,
    w_down,
    norm_attn,
    norm_ffn,
    norm_query,
    norm_key,
    segments,
    positions,
    cotangent,
):
    row_count = hidden.shape[2]
    block_rows = min(512, row_count)
    block_starts = jnp.arange(row_count // block_rows, dtype=jnp.int32) * block_rows
    first_row = lax.axis_index("seq") * row_count
    key_segs = lax.all_gather(segments, "seq", axis=2, tiled=True)
    group_size = HEADS // KV_HEADS
    score_scale = HEAD ** (-0.5)
    gain_query = norm_query.astype(jnp.float32)
    gain_key = norm_key.astype(jnp.float32)
    frequency = ROPE_BASE ** (-(jnp.arange(HEAD // 2, dtype=jnp.float32) * 2.0) / HEAD)
    query_gain_sum = jnp.zeros((HEAD,), jnp.float32)
    key_gain_sum = jnp.zeros((HEAD,), jnp.float32)
    totals = None
    layer_rows = []
    input_grads = []
    for batch_step in range(MICRO):
        gathered = (
            lax.all_gather(w_query, ("dp", "seq"), axis=0, tiled=True),
            lax.all_gather(w_key, ("dp", "seq"), axis=0, tiled=True),
            lax.all_gather(w_value, ("dp", "seq"), axis=0, tiled=True),
            lax.all_gather(w_gate, ("dp", "seq"), axis=0, tiled=True),
            lax.all_gather(w_up, ("dp", "seq"), axis=0, tiled=True),
            lax.all_gather(norm_attn, ("dp", "seq"), axis=0, tiled=True),
            lax.all_gather(norm_ffn, ("dp", "seq"), axis=0, tiled=True),
            lax.all_gather(w_out, ("dp", "seq"), axis=1, tiled=True),
            lax.all_gather(w_down, ("dp", "seq"), axis=1, tiled=True),
        )
        (
            query_full,
            key_full,
            value_full,
            gate_full,
            up_full,
            gain_attn,
            gain_ffn,
            out_full,
            down_full,
        ) = gathered
        tokens_in = hidden[batch_step, 0].astype(jnp.float32)
        seg_query = segments[batch_step, 0]
        seg_keys = key_segs[batch_step, 0]
        angles = positions[batch_step, 0].astype(jnp.float32)[:, None] * frequency[None, :]
        angles = jnp.concatenate([angles, angles], axis=-1)[:, None, :]
        cosine = jnp.cos(angles)
        sine = jnp.sin(angles)
        inv_attn = lax.rsqrt(jnp.mean(tokens_in * tokens_in, axis=-1, keepdims=True) + EPS)
        normed_attn = (tokens_in * inv_attn * gain_attn.astype(jnp.float32)).astype(jnp.bfloat16)
        query_raw = jnp.dot(normed_attn, query_full, preferred_element_type=jnp.float32).reshape(
            row_count, -1, HEAD
        )
        key_raw = jnp.dot(normed_attn, key_full, preferred_element_type=jnp.float32).reshape(
            row_count, -1, HEAD
        )
        value_rows = jnp.dot(normed_attn, value_full, preferred_element_type=jnp.float32).astype(
            jnp.bfloat16
        )
        kv_heads = key_raw.shape[1]
        query_inv = lax.rsqrt(jnp.mean(query_raw * query_raw, axis=-1, keepdims=True) + EPS)
        key_inv = lax.rsqrt(jnp.mean(key_raw * key_raw, axis=-1, keepdims=True) + EPS)
        query_rot = rotate(query_raw * query_inv * gain_query, cosine, sine).astype(jnp.bfloat16)
        key_rot = rotate(key_raw * key_inv * gain_key, cosine, sine).astype(jnp.bfloat16)
        queries = query_rot.reshape(row_count, kv_heads, group_size, HEAD)
        key_flat = key_rot.reshape(row_count, -1)
        keys_wide, values_wide = (
            lax.all_gather(key_flat, "seq", axis=0, tiled=True),
            lax.all_gather(value_rows, "seq", axis=0, tiled=True),
        )
        keys_all = keys_wide.reshape(-1, kv_heads, HEAD)
        values_all = values_wide.reshape(-1, kv_heads, HEAD)

        def forward_block(start_row):
            scores, q_block = masked_scores(
                queries,
                keys_all,
                seg_query,
                seg_keys,
                start_row,
                first_row,
                block_rows,
                score_scale,
            )
            row_max = jnp.max(scores, axis=-1, keepdims=True)
            expo = jnp.exp(scores - row_max)
            row_sum = jnp.sum(expo, axis=-1, keepdims=True)
            probs = expo / row_sum
            mixed = jnp.einsum(
                "kgqt,tkd->qkgd",
                probs.astype(jnp.bfloat16),
                values_all,
                preferred_element_type=jnp.float32,
            )
            return (mixed, row_max[..., 0] + jnp.log(row_sum[..., 0]))

        mixed_blocks, log_sums = lax.map(forward_block, block_starts)
        attn_heads = mixed_blocks.reshape(row_count, -1).astype(jnp.bfloat16)
        attn_part = jnp.dot(attn_heads, out_full, preferred_element_type=jnp.float32)
        middle = tokens_in + lax.psum(attn_part, "mp")
        inv_rows = lax.rsqrt(jnp.mean(tokens_in * tokens_in, axis=-1, keepdims=True) + EPS)
        inv_ffn = lax.rsqrt(jnp.mean(middle * middle, axis=-1, keepdims=True) + EPS)
        normed_part = (middle * inv_ffn * gain_ffn.astype(jnp.float32)).astype(jnp.bfloat16)
        gate = jnp.dot(normed_part, gate_full, preferred_element_type=jnp.float32)
        upward = jnp.dot(normed_part, up_full, preferred_element_type=jnp.float32)
        sigma_gate = jax.nn.sigmoid(gate)
        silu_gate = gate * sigma_gate
        act = (silu_gate * upward).astype(jnp.bfloat16)
        down_part = jnp.dot(act, down_full, preferred_element_type=jnp.float32)
        layer_rows.append(
            (middle + lax.psum(down_part.astype(jnp.bfloat16), "mp").astype(jnp.float32)).astype(
                jnp.bfloat16
            )
        )
        regathered = (
            lax.all_gather(w_query, ("dp", "seq"), axis=0, tiled=True),
            lax.all_gather(w_key, ("dp", "seq"), axis=0, tiled=True),
            lax.all_gather(w_value, ("dp", "seq"), axis=0, tiled=True),
            lax.all_gather(w_gate, ("dp", "seq"), axis=0, tiled=True),
            lax.all_gather(w_up, ("dp", "seq"), axis=0, tiled=True),
            lax.all_gather(norm_attn, ("dp", "seq"), axis=0, tiled=True),
            lax.all_gather(norm_ffn, ("dp", "seq"), axis=0, tiled=True),
            lax.all_gather(w_out, ("dp", "seq"), axis=1, tiled=True),
            lax.all_gather(w_down, ("dp", "seq"), axis=1, tiled=True),
        )
        (
            query_back,
            key_back,
            value_back,
            gate_back,
            up_back,
            gain_attn_b,
            gain_ffn_b,
            out_back,
            down_back,
        ) = regathered
        keys_again, values_again = (
            lax.all_gather(key_flat, "seq", axis=0, tiled=True),
            lax.all_gather(value_rows, "seq", axis=0, tiled=True),
        )
        keys_back = keys_again.reshape(-1, kv_heads, HEAD)
        values_back = values_again.reshape(-1, kv_heads, HEAD)
        grad_rows = cotangent[batch_step, 0]
        grad_rows_f = grad_rows.astype(jnp.float32)
        grad_down_w = tdot(act, grad_rows)
        grad_act = rdot(grad_rows, down_back)
        grad_gate_in = (grad_act * upward * sigma_gate * (1.0 + gate * (1.0 - sigma_gate))).astype(
            jnp.bfloat16
        )
        grad_up_in = (grad_act * silu_gate).astype(jnp.bfloat16)
        grad_gate_w = tdot(normed_part, grad_gate_in)
        grad_up_w = tdot(normed_part, grad_up_in)
        ffn_back_part = rdot(grad_gate_in, gate_back) + rdot(grad_up_in, up_back)
        grad_normed_ffn = lax.psum(ffn_back_part, "mp")
        gain_ffn_grad = jnp.sum(grad_normed_ffn * middle * inv_ffn, axis=0)
        grad_middle = grad_rows_f + norm_back(
            grad_normed_ffn, middle, inv_ffn, gain_ffn_b.astype(jnp.float32)
        )
        grad_middle_part = grad_middle.astype(jnp.bfloat16)
        grad_out_w = tdot(attn_heads, grad_middle_part)
        grad_heads = (
            rdot(grad_middle_part, out_back)
            .astype(jnp.bfloat16)
            .reshape(row_count, kv_heads, group_size, HEAD)
        )

        def backward_block(carried, inputs_at):
            start_row, log_block = inputs_at
            grad_keys, grad_values = carried
            scores, q_block = masked_scores(
                queries,
                keys_back,
                seg_query,
                seg_keys,
                start_row,
                first_row,
                block_rows,
                score_scale,
            )
            probs = jnp.exp(scores - log_block[..., None])
            grad_probs = jnp.einsum(
                "qkgd,tkd->kgqt", grad_heads, values_back, preferred_element_type=jnp.float32
            )
            row_dot = jnp.sum(grad_probs * probs, axis=-1, keepdims=True)
            grad_scores = (probs * (grad_probs - row_dot)).astype(jnp.bfloat16)
            grad_q_block = (
                jnp.einsum(
                    "kgqt,tkd->qkgd", grad_scores, keys_back, preferred_element_type=jnp.float32
                )
                * score_scale
            )
            grad_keys = (
                grad_keys
                + jnp.einsum(
                    "kgqt,qkgd->tkd", grad_scores, q_block, preferred_element_type=jnp.float32
                )
                * score_scale
            )
            grad_values = grad_values + jnp.einsum(
                "kgqt,qkgd->tkd",
                probs.astype(jnp.bfloat16),
                grad_heads,
                preferred_element_type=jnp.float32,
            )
            return ((grad_keys, grad_values), grad_q_block)

        zero_keys = jnp.zeros(keys_back.shape, jnp.float32)
        (grad_keys_all, grad_values_all), grad_q_blocks = lax.scan(
            backward_block, (zero_keys, zero_keys), (block_starts, log_sums)
        )
        own_keys, own_values = (
            lax.psum_scatter(
                grad_keys_all.reshape(keys_back.shape[0], -1).astype(jnp.bfloat16),
                "seq",
                scatter_dimension=0,
                tiled=True,
            ).astype(jnp.float32),
            lax.psum_scatter(
                grad_values_all.reshape(keys_back.shape[0], -1).astype(jnp.bfloat16),
                "seq",
                scatter_dimension=0,
                tiled=True,
            ).astype(jnp.float32),
        )
        grad_query_rot = grad_q_blocks.reshape(row_count, -1, HEAD)
        grad_key_rot = own_keys.reshape(row_count, kv_heads, HEAD)
        query_turn = rotate_back(grad_query_rot, cosine, sine)
        key_turn = rotate_back(grad_key_rot, cosine, sine)
        query_gain_sum = query_gain_sum + jnp.sum(query_turn * query_raw * query_inv, axis=(0, 1))
        key_gain_sum = key_gain_sum + jnp.sum(key_turn * key_raw * key_inv, axis=(0, 1))
        grad_query_in = (
            norm_back(query_turn, query_raw, query_inv, gain_query)
            .astype(jnp.bfloat16)
            .reshape(row_count, -1)
        )
        grad_key_in = (
            norm_back(key_turn, key_raw, key_inv, gain_key)
            .astype(jnp.bfloat16)
            .reshape(row_count, -1)
        )
        grad_value_in = own_values.astype(jnp.bfloat16)
        grad_query_w = tdot(normed_attn, grad_query_in)
        grad_key_w = tdot(normed_attn, grad_key_in)
        grad_value_w = tdot(normed_attn, grad_value_in)
        attn_back_part = (
            rdot(grad_query_in, query_back)
            + rdot(grad_key_in, key_back)
            + rdot(grad_value_in, value_back)
        )
        grad_normed_attn = lax.psum(attn_back_part.astype(jnp.bfloat16), "mp").astype(jnp.float32)
        gain_attn_grad = jnp.sum(grad_normed_attn * tokens_in * inv_rows, axis=0)
        grad_tokens = grad_middle + norm_back(
            grad_normed_attn, tokens_in, inv_rows, gain_attn_b.astype(jnp.float32)
        )
        grad_tokens_b = grad_tokens.astype(jnp.bfloat16)
        input_grads.append(grad_tokens_b)
        local_grads = (
            grad_query_w,
            grad_key_w,
            grad_value_w,
            grad_gate_w,
            grad_up_w,
            gain_attn_grad,
            gain_ffn_grad,
            grad_out_w,
            grad_down_w,
        )
        totals = local_grads if totals is None else jax.tree.map(jnp.add, totals, local_grads)
    owned = (
        lax.psum_scatter(
            totals[0].astype(jnp.bfloat16), ("dp", "seq"), scatter_dimension=0, tiled=True
        ).astype(jnp.float32),
        lax.psum_scatter(
            totals[1].astype(jnp.bfloat16), ("dp", "seq"), scatter_dimension=0, tiled=True
        ).astype(jnp.float32),
        lax.psum_scatter(
            totals[2].astype(jnp.bfloat16), ("dp", "seq"), scatter_dimension=0, tiled=True
        ).astype(jnp.float32),
        lax.psum_scatter(
            totals[3].astype(jnp.bfloat16), ("dp", "seq"), scatter_dimension=0, tiled=True
        ).astype(jnp.float32),
        lax.psum_scatter(
            totals[4].astype(jnp.bfloat16), ("dp", "seq"), scatter_dimension=0, tiled=True
        ).astype(jnp.float32),
        lax.psum_scatter(
            totals[5].astype(jnp.bfloat16), ("dp", "seq"), scatter_dimension=0, tiled=True
        ).astype(jnp.float32),
        lax.psum_scatter(
            totals[6].astype(jnp.bfloat16), ("dp", "seq"), scatter_dimension=0, tiled=True
        ).astype(jnp.float32),
        lax.psum_scatter(
            totals[7].astype(jnp.bfloat16), ("dp", "seq"), scatter_dimension=1, tiled=True
        ).astype(jnp.float32),
        lax.psum_scatter(
            totals[8].astype(jnp.bfloat16), ("dp", "seq"), scatter_dimension=1, tiled=True
        ).astype(jnp.float32),
    )
    gain_attn_owned, gain_ffn_owned = (owned[5], owned[6])
    head_query, head_key = lax.psum((query_gain_sum, key_gain_sum), ("dp", "seq", "mp"))
    return (
        jnp.stack(layer_rows)[:, None],
        jnp.stack(input_grads)[:, None],
        owned[0],
        owned[1],
        owned[2],
        owned[7],
        owned[3],
        owned[4],
        owned[8],
        gain_attn_owned,
        gain_ffn_owned,
        head_query,
        head_key,
    )


def solution(mesh):
    return jax.shard_map(
        local,
        mesh=mesh,
        in_specs=(
            P(None, "dp", "seq", None),
            P(("dp", "seq"), "mp"),
            P(("dp", "seq"), "mp"),
            P(("dp", "seq"), "mp"),
            P("mp", ("dp", "seq")),
            P(("dp", "seq"), "mp"),
            P(("dp", "seq"), "mp"),
            P("mp", ("dp", "seq")),
            P(("dp", "seq")),
            P(("dp", "seq")),
            P(),
            P(),
            P(None, "dp", "seq"),
            P(None, "dp", "seq"),
            P(None, "dp", "seq", None),
        ),
        out_specs=(
            P(None, "dp", "seq", None),
            P(None, "dp", "seq", None),
            P(("dp", "seq"), "mp"),
            P(("dp", "seq"), "mp"),
            P(("dp", "seq"), "mp"),
            P("mp", ("dp", "seq")),
            P(("dp", "seq"), "mp"),
            P(("dp", "seq"), "mp"),
            P("mp", ("dp", "seq")),
            P(("dp", "seq")),
            P(("dp", "seq")),
            P(),
            P(),
        ),
        check_vma=False,
    )
```

profile of v0, /device:TPU:0, one launch (start us, length us, event | category | flops | bytes accessed | tf_op | source)
XLA Modules:
  0.0 2291.2 jit_solution(8221917278121558273)
XLA Ops:
  8.7 23.3 %all-gather = bf16[16,1,128]{2,1,0:T(2,128)(2,1)S(1)} all-gather(bf16[1,1,128]{2,1,0:T(2,128)(2,1)} %bitcast.428), channel_id=1, replica_groups=mesh['dp'=4,'seq'=4,'mp'=2] {'dp','seq'}, dimensions={0}, use_global_device_ids=true | all-gather | bytes 4352 | tf_op jit(solution)/shard_map/all_gather | solution.py:100
  35.7 18.6 all-gather.14.cloned.1.call-done
  64.4 32.3 %all-gather.18.cloned.1.call-done = bf16[2048,512]{1,0:T(8,128)(2,1)} async-done(((bf16[128,512]{1,0:T(8,128)(2,1)}), bf16[2048,512]{1,0:T(8,128)(2,1)}) %all-gather.18.cloned.1.call-update) | async-done | bytes 2097168 | tf_op jit(solution)/shard_map/all_gather | solution.py:96
  124.5 19.7 all-gather.16.cloned.1.call-done
  148.2 48.5 %all-gather.22.cloned.1.call-done = bf16[2048,1024]{1,0:T(8,128)(2,1)} async-done(((bf16[128,1024]{1,0:T(8,128)(2,1)}), bf16[2048,1024]{1,0:T(8,128)(2,1)}) %all-gather.22.cloned.1.call-update) | async-done | bytes 4194320 | tf_op jit(solution)/shard_map/all_gather | solution.py:95
  219.8 15.9 fusion.147
  235.8 13.2 fusion.7
  249.0 15.9 fusion.148
  264.9 13.3 fusion.6
  278.3 14.6 fusion.105
  293.0 14.7 fusion.108
  320.8 20.7 all-gather.1
  341.5 175.8 %all-reduce.13.cloned.1.call-done = (f32[512,2048]{1,0:T(8,128)}, f32[512,2048]{1,0:T(8,128)}) async-done(((f32[512,2048]{1,0:T(8,128)}, f32[512,2048]{1,0:T(8,128)}), (f32[512,2048]{1,0:T(8,128)}, f32[512,2048]{1,0:T(8,128)})) %all-reduce.13.cloned.1.call-update) | async-done | bytes 8388624 | tf_op jit(solution)/shard_map/psum | solution.py:174
  528.2 92.0 %all-gather.28.cloned.1.call-done = bf16[2048,3072]{1,0:T(8,128)(2,1)} async-done(((bf16[128,3072]{1,0:T(8,128)(2,1)}), bf16[2048,3072]{1,0:T(8,128)(2,1)}) %all-gather.28.cloned.1.call-update) | async-done | bytes 12582928 | tf_op jit(solution)/shard_map/all_gather | solution.py:99
  620.3 11.9 fusion.151
  632.2 89.1 %all-gather.26.cloned.1.call-done = bf16[2048,3072]{1,0:T(8,128)(2,1)} async-done(((bf16[128,3072]{1,0:T(8,128)(2,1)}), bf16[2048,3072]{1,0:T(8,128)(2,1)}) %all-gather.26.cloned.1.call-update) | async-done | bytes 12582928 | tf_op jit(solution)/shard_map/all_gather | solution.py:98
  721.3 12.1 fusion.150
  750.7 74.4 %all-gather.30.cloned.1.call-done = bf16[3072,2048]{1,0:T(8,128)(2,1)} async-done(((bf16[3072,128]{1,0:T(8,128)(2,1)}), bf16[3072,2048]{1,0:T(8,128)(2,1)}) %all-gather.30.cloned.1.call-update) | async-done | bytes 12582928 | tf_op jit(solution)/shard_map/all_gather | solution.py:103
  825.1 17.1 multiply_convert_fusion.2
  843.9 11.0 fusion.155
  854.9 16.9 multiply_convert_fusion
  871.8 12.1 fusion.158
  883.9 14.1 convolution_add_fusion.1
  898.0 11.7 convolution_add_fusion
  910.5 195.7 %all-reduce.11.cloned.1.call-done = (f32[512,2048]{1,0:T(8,128)}, f32[512,2048]{1,0:T(8,128)}) async-done(((f32[512,2048]{1,0:T(8,128)}, f32[512,2048]{1,0:T(8,128)}), (f32[512,2048]{1,0:T(8,128)}, f32[512,2048]{1,0:T(8,128)})) %all-reduce.11.cloned.1.call-update) | async-done | bytes 8388624 | tf_op jit(solution)/shard_map/psum | solution.py:228
  1133.8 14.9 bitcast_convert_fusion.1
  1148.8 16.1 bitcast_convert_fusion
  1164.9 23.0 %fusion = (f32[4,2,512]{2,1,0:T(2,128)S(1)}, f32[4,2048,512,2]{2,1,3,0:T(8,128)}) fusion(f32[4,2,512,2048]{2,3,1,0:T(8,128)} %get-tuple-element.300, f32[4,2,512]{2,1,0:T(2,128)S(1)} %bitcast.399, bf16[512,4,2,128]{0,3,2,1:T(8,128)(2,1)S(1)} %bitcast.355, bf16[2048,4,128,1]{2,1,0,3:T(4,128)(2,1)} %bitcast.359), kind=kOutput, calls=%fused_computation.2 | convolution fusion | flops 2172645376 | bytes 70287360 | tf_op jit(solution)/shard_map/while/body/eval_jaxpr/qkgd,tkd->kgqt/dot_general | solution.py:255
  1187.9 28.7 %fusion.2 = bf16[4,2,512,2048]{2,3,1,0:T(8,128)(2,1)} fusion(f32[4,2048,512,2]{2,1,3,0:T(8,128)} %get-tuple-element.306, f32[4,2,512,2048]{2,3,1,0:T(8,128)} %get-tuple-element.300, f32[4,2,512]{2,1,0:T(2,128)S(1)} %get-tuple-element.305, f32[4,2,512]{2,1,0:T(2,128)S(1)} %bitcast.400), kind=kLoop, calls=%fused_computation.4 | loop fusion | flops 33554432 | bytes 83918848 | tf_op jit(solution)/shard_map/while/body/eval_jaxpr/convert_element_type | solution.py:259
  1216.6 13.1 fusion.58
  1229.7 24.7 %fusion.3 = (f32[4,2,512]{2,1,0:T(2,128)S(1)}, f32[4,2048,512,2]{2,1,3,0:T(8,128)}) fusion(f32[4,2,512,2048]{2,3,1,0:T(8,128)} %get-tuple-element.302, f32[4,2,512]{2,1,0:T(2,128)S(1)} %bitcast.396, bf16[512,4,2,128]{0,3,2,1:T(8,128)(2,1)S(1)} %bitcast.353, bf16[2048,4,128,1]{2,1,0,3:T(4,128)(2,1)S(1)} %bitcast.357), kind=kOutput, calls=%fused_computation.7 | convolution fusion | flops 2172645376 | bytes 70287360 | tf_op jit(solution)/shard_map/while/body/eval_jaxpr/qkgd,tkd->kgqt/dot_general | solution.py:255
  1254.4 29.2 %fusion.5 = bf16[4,2,512,2048]{2,3,1,0:T(8,128)(2,1)} fusion(f32[4,2048,512,2]{2,1,3,0:T(8,128)} %get-tuple-element.304, f32[4,2,512,2048]{2,3,1,0:T(8,128)} %get-tuple-element.302, f32[4,2,512]{2,1,0:T(2,128)S(1)} %get-tuple-element.303, f32[4,2,512]{2,1,0:T(2,128)S(1)} %bitcast.397), kind=kLoop, calls=%fused_computation.9 | loop fusion | flops 33554432 | bytes 83918848 | tf_op jit(solution)/shard_map/while/body/eval_jaxpr/convert_element_type | solution.py:259
  1283.6 12.7 fusion.59
  1371.7 13.6 fusion.77
  1385.3 16.1 add_convert_fusion
  1401.3 16.7 copy.136
  1418.5 14.5 fusion.162
  1433.0 15.7 add_convert_fusion.1
  1449.0 14.2 fusion.161
  1463.1 15.5 add_convert_fusion.2
  1491.3 11.2 convolution_convert_fusion
  1517.7 40.8 %all-reduce.2 = (f32[128]{0:T(128)}, f32[128]{0:T(128)}) all-reduce(f32[128]{0:T(128)S(1)} %add.350, f32[128]{0:T(128)S(1)} %add.351), channel_id=1, replica_groups=mesh['dp'=4,'seq'=4,'mp'=2] {'dp','seq','mp'}, use_global_device_ids=true, to_apply=%region_49.50 | all-reduce | flops 256 | bytes 2048 | tf_op jit(solution)/shard_map/psum | solution.py:373
  1564.0 45.7 %reduce-scatter.26.cloned.1.call-done = bf16[128,512]{1,0:T(8,128)(2,1)} async-done(((bf16[2048,512]{1,0:T(8,128)(2,1)}), bf16[128,512]{1,0:T(8,128)(2,1)}) %reduce-scatter.26.cloned.1.call-update) | async-done | bytes 131088 | tf_op jit(solution)/shard_map/reduce_scatter | solution.py:347
  1611.3 136.3 %reduce-scatter.36.cloned.1.call-done = bf16[128,3072]{1,0:T(8,128)(2,1)} async-done(((bf16[2048,3072]{1,0:T(8,128)(2,1)}), bf16[128,3072]{1,0:T(8,128)(2,1)}) %reduce-scatter.36.cloned.1.call-update) | async-done | bytes 786448
  1750.4 135.5 %reduce-scatter.32.cloned.1.call-done = bf16[128,3072]{1,0:T(8,128)(2,1)} async-done(((bf16[2048,3072]{1,0:T(8,128)(2,1)}), bf16[128,3072]{1,0:T(8,128)(2,1)}) %reduce-scatter.32.cloned.1.call-update) | async-done | bytes 786448 | tf_op jit(solution)/shard_map/reduce_scatter | solution.py:356
  1888.3 135.7 %reduce-scatter.30.cloned.1.call-done = bf16[128,3072]{1,0:T(8,128)(2,1)} async-done(((bf16[2048,3072]{1,0:T(8,128)(2,1)}), bf16[128,3072]{1,0:T(8,128)(2,1)}) %reduce-scatter.30.cloned.1.call-update) | async-done | bytes 786448 | tf_op jit(solution)/shard_map/reduce_scatter | solution.py:353
  2026.4 197.6 %all-reduce.15.cloned.1.call-done = (bf16[512,2048]{1,0:T(8,128)(2,1)}, bf16[512,2048]{1,0:T(8,128)(2,1)}, bf16[512,2048]{1,0:T(8,128)(2,1)}, bf16[512,2048]{1,0:T(8,128)(2,1)}) async-done(((bf16[512,2048]{1,0:T(8,128)(2,1)}, bf16[512,2048]{1,0:T(8,128)(2,1)}, bf16[512,2048]{1,0:T(8,128)(2,1)}, bf16[512,2048]{1,0:T(8,128)(2,1)}), (bf16[512,2048]{1,0:T(8,128)(2,1)}, bf16[512,2048]{1,0:T(8,128)(2,1)}, ...) | async-done | bytes 8388624 | tf_op jit(solution)/shard_map/psum | solution.py:185
  2236.4 33.5 %all-reduce.5 = (bf16[2048]{0:T(1024)(128)(2,1)S(1)}, bf16[2048]{0:T(1024)(128)(2,1)S(1)}) all-reduce(bf16[2048]{0:T(1024)(128)(2,1)S(1)} %add_convert_fusion.12, bf16[2048]{0:T(1024)(128)(2,1)S(1)} %add_convert_fusion.11), channel_id=13, replica_groups=mesh['dp'=4,'seq'=4,'mp'=2] {'dp','seq'}, use_global_device_ids=true, to_apply=%region_43.44.clone | all-reduce | flops 4096 | bytes 16384
  (450 shorter events, 284.9 us)
Async XLA Ops:
  7.2 47.2 %all-gather.14.cloned.1.call-start = ((), (), s32[]{:S(2)}) async-start(), calls=%async_computation.11 | async-start | bytes 2228224 | tf_op jit(solution)/shard_map/all_gather | solution.py:97
  7.9 88.8 %all-gather.18.cloned.1.call-start = ((), (), s32[]{:S(2)}) async-start(), calls=%async_computation.13 | async-start | bytes 2228224 | tf_op jit(solution)/shard_map/all_gather | solution.py:96
  8.7 111.9 %all-gather.32.cloned.1.call-start = ((), (), s32[]{:S(2)}) async-start(), calls=%async_computation.20 | async-start | bytes 2621440 | tf_op jit(solution)/shard_map/all_gather | solution.py:143
  32.0 177.1 %copy-start.81 = (f32[16,1,128]{2,1,0:T(1,128)}, f32[16,1,128]{2,1,0:T(1,128)S(1)}, u32[]{:S(2)}) copy-start(f32[16,1,128]{2,1,0:T(1,128)S(1)} %convert_element_type.430) | copy-start | bytes 24580
  35.7 167.4 %copy-start.102 = (f32[512]{0:T(512)}, f32[512]{0:T(512)S(1)}, u32[]{:S(2)}) copy-start(f32[512]{0:T(512)S(1)} %get-tuple-element.269) | copy-start | bytes 6148
  35.7 173.3 %copy-start.105 = (f32[512]{0:T(512)}, f32[512]{0:T(512)S(1)}, u32[]{:S(2)}) copy-start(f32[512]{0:T(512)S(1)} %get-tuple-element.307) | copy-start | bytes 6148
  58.8 85.4 %all-gather.16.cloned.1.call-start = ((), (), s32[]{:S(2)}) async-start(), calls=%async_computation.12 | async-start | bytes 2621440 | tf_op jit(solution)/shard_map/all_gather | solution.py:143
  62.6 134.0 %all-gather.22.cloned.1.call-start = ((), (), s32[]{:S(2)}) async-start(), calls=%async_computation.15 | async-start | bytes 4456448 | tf_op jit(solution)/shard_map/all_gather | solution.py:95
  63.2 156.6 %all-gather.34.cloned.1.call-start = ((), (), s32[]{:S(2)}) async-start(), calls=%async_computation.21 | async-start | bytes 2621440 | tf_op jit(solution)/shard_map/all_gather | solution.py:142
  63.3 43.8 %copy-start.113 = (f32[128]{0:T(128)}, f32[128]{0:T(128)S(1)}, u32[]{:S(2)}) copy-start(f32[128]{0:T(128)S(1)} %convert_element_type.338) | copy-start | bytes 1540
  64.4 150.5 %copy-start.27 = (f32[512,128]{0,1:T(8,128)}, f32[512,128]{0,1:T(8,128)S(1)}, u32[]{:S(2)}) copy-start(f32[512,128]{0,1:T(8,128)S(1)} %get-tuple-element.246) | copy-start | bytes 786436
  64.4 150.5 %copy-start.39 = (f32[512,128]{0,1:T(8,128)}, f32[512,128]{0,1:T(8,128)S(1)}, u32[]{:S(2)}) copy-start(f32[512,128]{0,1:T(8,128)S(1)} %get-tuple-element.247) | copy-start | bytes 786436
  108.8 140.2 %all-gather.20.cloned.1.call-start = ((), (), s32[]{:S(2)}) async-start(), calls=%async_computation.14 | async-start | bytes 2621440 | tf_op jit(solution)/shard_map/all_gather | solution.py:142
  109.8 104.4 %copy-start.29 = (f32[512,128]{0,1:T(8,128)}, f32[512,128]{0,1:T(8,128)S(1)}, u32[]{:S(2)}) copy-start(f32[512,128]{0,1:T(8,128)S(1)} %get-tuple-element.244) | copy-start | bytes 786436
  109.8 104.4 %copy-start.41 = (f32[512,128]{0,1:T(8,128)}, f32[512,128]{0,1:T(8,128)S(1)}, u32[]{:S(2)}) copy-start(f32[512,128]{0,1:T(8,128)S(1)} %get-tuple-element.245) | copy-start | bytes 786436
  111.1 196.5 %all-gather.24.cloned.1.call-start = ((), (), s32[]{:S(2)}) async-start(), calls=%async_computation.16 | async-start | bytes 4456448 | tf_op jit(solution)/shard_map/all_gather | solution.py:102
  111.9 405.5 %all-reduce.13.cloned.1.call-start = ((), (), s32[]{:S(2)}) async-start(), calls=%async_computation.34 | async-start | bytes 16777216 | tf_op jit(solution)/shard_map/psum | solution.py:174
  117.5 95.4 %copy-start.115 = (f32[128]{0:T(128)}, f32[128]{0:T(128)S(1)}, u32[]{:S(2)}) copy-start(f32[128]{0:T(128)S(1)} %convert_element_type.342) | copy-start | bytes 1540
  214.9 34.1 %copy-start.51 = (bf16[512,8,128]{0,2,1:T(8,128)(2,1)}, bf16[512,8,128]{0,2,1:T(8,128)(2,1)S(1)}, u32[]{:S(2)}) copy-start(bf16[512,8,128]{0,2,1:T(8,128)(2,1)S(1)} %fusion.71) | copy-start | bytes 3145732
  215.6 20.2 copy-start.53
  235.8 42.5 %copy-start.84 = (f32[4,2,512]{2,1,0:T(2,128)}, f32[4,2,512]{2,1,0:T(2,128)S(1)}, u32[]{:S(2)}) copy-start(f32[4,2,512]{2,1,0:T(2,128)S(1)} %get-tuple-element.299) | copy-start | bytes 49156
  249.0 29.3 %copy-start.86 = (f32[4,2,512]{2,1,0:T(2,128)}, f32[4,2,512]{2,1,0:T(2,128)S(1)}, u32[]{:S(2)}) copy-start(f32[4,2,512]{2,1,0:T(2,128)S(1)} %fusion.7) | copy-start | bytes 49156
  264.9 28.0 %copy-start.88 = (f32[4,2,512]{2,1,0:T(2,128)}, f32[4,2,512]{2,1,0:T(2,128)S(1)}, u32[]{:S(2)}) copy-start(f32[4,2,512]{2,1,0:T(2,128)S(1)} %get-tuple-element.301) | copy-start | bytes 49156
  318.9 301.4 %all-gather.28.cloned.1.call-start = ((), (), s32[]{:S(2)}) async-start(), calls=%async_computation.18 | async-start | bytes 13369344 | tf_op jit(solution)/shard_map/all_gather | solution.py:99
  319.5 401.8 %all-gather.26.cloned.1.call-start = ((), (), s32[]{:S(2)}) async-start(), calls=%async_computation.17 | async-start | bytes 13369344 | tf_op jit(solution)/shard_map/all_gather | solution.py:98
  320.2 504.9 %all-gather.30.cloned.1.call-start = ((), (), s32[]{:S(2)}) async-start(), calls=%async_computation.19 | async-start | bytes 13369344 | tf_op jit(solution)/shard_map/all_gather | solution.py:103
  320.8 785.4 %all-reduce.11.cloned.1.call-start = ((), (), s32[]{:S(2)}) async-start(), calls=%async_computation.33 | async-start | bytes 16777216 | tf_op jit(solution)/shard_map/psum | solution.py:228
  341.5 182.9 %copy-start.79 = (f32[16,1,128]{2,1,0:T(1,128)}, f32[16,1,128]{2,1,0:T(1,128)S(1)}, u32[]{:S(2)}) copy-start(f32[16,1,128]{2,1,0:T(1,128)S(1)} %convert_element_type.431) | copy-start | bytes 24580
  528.2 213.8 %copy-start.60 = (bf16[512,2048]{1,0:T(8,128)(2,1)}, bf16[512,2048]{1,0:T(8,128)(2,1)S(1)}, u32[]{:S(2)}) copy-start(bf16[512,2048]{1,0:T(8,128)(2,1)S(1)} %get-tuple-element.261) | copy-start | bytes 6291460
  721.3 20.8 slice-start
  721.3 20.8 slice-start.1
  909.7 196.4 %copy-start.80 = (f32[16,1,128]{2,1,0:T(1,128)S(1)}, f32[16,1,128]{2,1,0:T(1,128)}, u32[]{:S(2)}) copy-start(f32[16,1,128]{2,1,0:T(1,128)} %copy-done.79) | copy-start | bytes 24580
  909.7 196.4 %copy-start.95 = (f32[512]{0:T(512)S(1)}, f32[512]{0:T(512)}, u32[]{:S(2)}) copy-start(f32[512]{0:T(512)} %copy-done.94) | copy-start | bytes 6148
  909.7 196.4 %copy-start.97 = (f32[512]{0:T(512)S(1)}, f32[512]{0:T(512)}, u32[]{:S(2)}) copy-start(f32[512]{0:T(512)} %copy-done.96) | copy-start | bytes 6148
  909.8 437.6 %reduce-scatter.18.cloned.1.call-start = ((), (), s32[]{:S(2)}) async-start(), calls=%async_computation.23 | async-start | bytes 2621440 | tf_op jit(solution)/shard_map/reduce_scatter | solution.py:292
  1148.7 204.0 %reduce-scatter.22.cloned.1.call-start = ((), (), s32[]{:S(2)}) async-start(), calls=%async_computation.25 | async-start | bytes 2621440 | tf_op jit(solution)/shard_map/reduce_scatter | solution.py:292
  1187.9 171.0 %reduce-scatter.20.cloned.1.call-start = ((), (), s32[]{:S(2)}) async-start(), calls=%async_computation.24 | async-start | bytes 2621440 | tf_op jit(solution)/shard_map/reduce_scatter | solution.py:286
  1254.4 107.0 %reduce-scatter.16.cloned.1.call-start = ((), (), s32[]{:S(2)}) async-start(), calls=%async_computation.22 | async-start | bytes 2621440 | tf_op jit(solution)/shard_map/reduce_scatter | solution.py:286
  1254.4 29.2 %copy-start.52 = (bf16[512,8,128]{0,2,1:T(8,128)(2,1)S(1)}, bf16[512,8,128]{0,2,1:T(8,128)(2,1)}, u32[]{:S(2)}) copy-start(bf16[512,8,128]{0,2,1:T(8,128)(2,1)} %copy-done.51) | copy-start | bytes 3145732
  1296.3 262.2 %reduce-scatter.34.cloned.1.call-start = ((), (), s32[]{:S(2)}) async-start(), calls=%async_computation.31 | async-start | bytes 4456448
  1312.0 248.5 %reduce-scatter.24.cloned.1.call-start = ((), (), s32[]{:S(2)}) async-start(), calls=%async_computation.26 | async-start | bytes 4456448 | tf_op jit(solution)/shard_map/reduce_scatter | solution.py:344
  1347.3 215.0 %reduce-scatter.28.cloned.1.call-start = ((), (), s32[]{:S(2)}) async-start(), calls=%async_computation.28 | async-start | bytes 2228224 | tf_op jit(solution)/shard_map/reduce_scatter | solution.py:350
  1358.6 251.1 %reduce-scatter.26.cloned.1.call-start = ((), (), s32[]{:S(2)}) async-start(), calls=%async_computation.27 | async-start | bytes 2228224 | tf_op jit(solution)/shard_map/reduce_scatter | solution.py:347
  1371.6 376.0 %reduce-scatter.36.cloned.1.call-start = ((), (), s32[]{:S(2)}) async-start(), calls=%async_computation.32 | async-start | bytes 13369344
  1418.1 467.8 %reduce-scatter.32.cloned.1.call-start = ((), (), s32[]{:S(2)}) async-start(), calls=%async_computation.30 | async-start | bytes 13369344 | tf_op jit(solution)/shard_map/reduce_scatter | solution.py:356
  1448.8 575.3 %reduce-scatter.30.cloned.1.call-start = ((), (), s32[]{:S(2)}) async-start(), calls=%async_computation.29 | async-start | bytes 13369344 | tf_op jit(solution)/shard_map/reduce_scatter | solution.py:353
  1478.6 745.4 %all-reduce.15.cloned.1.call-start = ((), (), s32[]{:S(2)}) async-start(), calls=%async_computation.35 | async-start | bytes 16777216 | tf_op jit(solution)/shard_map/psum | solution.py:185
  2233.3 42.7 %copy-start.112 = (f32[512]{0:T(512)S(1)}, f32[512]{0:T(512)}, u32[]{:S(2)}) copy-start(f32[512]{0:T(512)} %get-tuple-element.308) | copy-start | bytes 6148
  (113 other events, 540.6 us)
Sparse Core Ops, SparseCore 0:
  10.1 44.1 all-gather.13
  56.5 40.1 all-gather.17
  98.8 21.3 all-gather.31
  121.7 22.5 all-gather.15
  146.3 50.3 all-gather.21
  198.7 21.0 all-gather.33
  221.9 22.5 all-gather.19
  246.7 52.4 all-gather.23
  319.0 198.3 all-reduce.12
  519.5 100.7 all-gather.27
  622.6 98.6 all-gather.25
  723.3 101.7 all-gather.29
  909.9 196.2 all-reduce.10
  1148.8 31.5 reduce-scatter.17
  1188.0 31.5 reduce-scatter.21
  1254.5 31.6 reduce-scatter.19
  1296.5 31.8 reduce-scatter.15
  1332.1 72.7 reduce-scatter.33
  1408.8 71.8 reduce-scatter.23
  1484.2 61.0 reduce-scatter.27
  1549.0 60.5 reduce-scatter.25
  1613.7 133.8 reduce-scatter.35
  1751.7 134.1 reduce-scatter.31
  1889.8 134.1 reduce-scatter.29
  2026.6 197.3 all-reduce.14
where the time goes:
time: 2300 us; the launch traced here: 2290 us
  waiting for transfers between devices  1410 us (61%)
  matrix products  503 us (22%)
  other arithmetic  172 us (7%)
  blocking collectives  124 us (5%)
  local copies, waits for them, and re-layouts  68.1 us (3%)
    psum x1, waiting for transfers between devices, local(): lax.psum(down_part.astype(jnp.bfloat16), 'mp').astype(jnp.float32)  198 us
    psum x1, waiting for transfers between devices, local(): grad_normed_ffn = lax.psum(ffn_back_part, 'mp')  196 us
    psum x1, waiting for transfers between devices, local(): middle = tokens_in + lax.psum(attn_part, 'mp')  176 us
    unnamed x27, waiting for transfers between devices  141 us
    reduce_scatter x1, waiting for transfers between devices, local(): lax.psum_scatter(totals[3].astype(jnp.bfloat16), ('dp', 'seq'), scatter_d...  136 us
    reduce_scatter x1, waiting for transfers between devices, local(): lax.psum_scatter(totals[4].astype(jnp.bfloat16), ('dp', 'seq'), scatter_d...  136 us
    dot_general x14, matrix products, tdot(): lax.dot_general(left, right, (((0,), (0,)), ((), ())), preferred_element_...  121 us
    dot_general x14, matrix products, rdot(): lax.dot_general(left, right, (((1,), (1,)), ((), ())), preferred_element_...  104 us
  transfers between devices with their start and end apart: 25, of which 15 were waited for; matrix products, arithmetic and copies ran while one was open for 25% of the time, Pallas kernels for 0%

commit v1 on v0

v1 whole, which is shorter than its diff:
```python
import jax
import jax.numpy as jnp
from jax import lax
from jax.sharding import PartitionSpec as P

HEADS = 16
KV_HEADS = 8
HEAD = 128
MICRO = 2

EPS = 1e-06
ROPE_BASE = 1000000.0
F32 = jnp.float32
BF16 = jnp.bfloat16


def dot(left, right):
    return jnp.dot(left, right, preferred_element_type=F32)


def tdot(left, right):
    return lax.dot_general(left, right, (((0,), (0,)), ((), ())), preferred_element_type=F32)


def rdot(left, right):
    return lax.dot_general(left, right, (((1,), (1,)), ((), ())), preferred_element_type=F32)


def rotate(values, cosine, sine):
    half_size = values.shape[-1] // 2
    turned = jnp.concatenate([-values[..., half_size:], values[..., :half_size]], axis=-1)
    return values * cosine + turned * sine


def rotate_back(grads, cosine, sine):
    half_size = grads.shape[-1] // 2
    scaled = grads * sine
    back_part = jnp.concatenate([scaled[..., half_size:], -scaled[..., :half_size]], axis=-1)
    return grads * cosine + back_part


def norm_back(grads, values, inverse, gain):
    scaled = grads * gain
    return inverse * scaled - values * inverse**3 * jnp.mean(
        scaled * values, axis=-1, keepdims=True
    )


def inv_rms(values):
    return lax.rsqrt(jnp.mean(values * values, axis=-1, keepdims=True) + EPS)


def make_local(mp_size, seq_size, dp_size):
    data_axes = ("dp", "seq")
    pair = [(i, i ^ 1) for i in range(seq_size)]
    up_pairs = [(i, i + 2) for i in range(seq_size - 2)]
    down_pairs = [(i + 2, i) for i in range(seq_size - 2)]

    def mp_sum(part):
        part = lax.optimization_barrier(part.astype(BF16))
        if mp_size == 2:
            other = lax.ppermute(part, "mp", [(0, 1), (1, 0)])
            return part.astype(F32) + other.astype(F32)
        return lax.psum(part, "mp").astype(F32)

    def local(
        hidden,
        w_query,
        w_key,
        w_value,
        w_out,
        w_gate,
        w_up,
        w_down,
        norm_attn,
        norm_ffn,
        norm_query,
        norm_key,
        segments,
        positions,
        cotangent,
    ):
        rows = hidden.shape[2]
        width = hidden.shape[3]
        total = MICRO * rows
        q_cols = w_query.shape[1]
        k_cols = w_key.shape[1]
        kv_heads = k_cols // HEAD
        group = HEADS // KV_HEADS
        score_scale = HEAD ** (-0.5)
        rank = lax.axis_index("seq")
        own_rows = w_query.shape[0]

        gains = jnp.concatenate(
            [
                jnp.broadcast_to(norm_attn[:, None], (own_rows, 64)),
                jnp.broadcast_to(norm_ffn[:, None], (own_rows, 64)),
            ],
            axis=1,
        )
        first = jnp.concatenate([w_query, w_key, w_value, w_out.T, gains], axis=1)
        first = lax.all_gather(first, data_axes, axis=0, tiled=True)
        second = jnp.stack([w_gate, w_up, w_down.T])
        second, first = lax.optimization_barrier((second, first))
        second = lax.all_gather(second, data_axes, axis=1, tiled=True)
        qkv_cols = q_cols + 2 * k_cols
        w_qkv = first[:, :qkv_cols]
        w_out_t = first[:, qkv_cols : qkv_cols + q_cols]
        gain_attn = first[:, qkv_cols + q_cols].astype(F32)
        gain_ffn = first[:, qkv_cols + q_cols + 64].astype(F32)
        gate_full, up_full, down_t = second[0], second[1], second[2]
        gain_query = norm_query.astype(F32)
        gain_key = norm_key.astype(F32)

        tokens = hidden.reshape(total, width).astype(F32)
        cot = cotangent.reshape(total, width)

        seg_own = segments[:, 0]
        seg_pair = lax.ppermute(seg_own, "seq", pair)
        both = jnp.stack([seg_own, seg_pair])
        both_x = lax.ppermute(both, "seq", up_pairs)
        seg_all = jnp.zeros((MICRO, rows * seq_size), jnp.int32)

        def place(buffer, parts, axis):
            for flip, part in enumerate(parts):
                buffer = lax.dynamic_update_slice_in_dim(
                    buffer, part, jnp.bitwise_xor(rank, flip) * rows, axis
                )
            return buffer

        seg_all = place(seg_all, [both[0], both[1], both_x[0], both_x[1]], 1)

        frequency = ROPE_BASE ** (-(jnp.arange(HEAD // 2, dtype=F32) * 2.0) / HEAD)
        angles = positions.reshape(total).astype(F32)[:, None] * frequency[None, :]
        angles = jnp.concatenate([angles, angles], axis=-1)[:, None, :]
        cosine = jnp.cos(angles)
        sine = jnp.sin(angles)

        inv_attn = inv_rms(tokens)
        normed_attn = (tokens * inv_attn * gain_attn).astype(BF16)
        raw = dot(normed_attn, w_qkv)
        query_raw = raw[:, :q_cols].reshape(total, -1, HEAD)
        key_raw = raw[:, q_cols : q_cols + k_cols].reshape(total, -1, HEAD)
        values = raw[:, q_cols + k_cols :].astype(BF16)
        query_inv = inv_rms(query_raw)
        key_inv = inv_rms(key_raw)
        queries = rotate(query_raw * query_inv * gain_query, cosine, sine).astype(BF16)
        keys = rotate(key_raw * key_inv * gain_key, cosine, sine).astype(BF16)
        keys = keys.reshape(total, k_cols)
        key_ids = jnp.arange(rows * seq_size, dtype=jnp.int32)
        row_ids = rank * rows + jnp.arange(rows, dtype=jnp.int32)

        kept = []
        middles = []
        heads_out = []
        for step in range(MICRO):
            cut = slice(step * rows, (step + 1) * rows)
            own = jnp.concatenate([keys[cut], values[cut]], axis=1)
            near = lax.ppermute(own, "seq", pair)
            far = lax.ppermute(own, "seq", up_pairs)
            far_near = lax.ppermute(far, "seq", pair)
            wide = place(
                jnp.zeros((rows * seq_size, 2 * k_cols), BF16), [own, near, far, far_near], 0
            )
            keys_all = wide[:, :k_cols].reshape(-1, kv_heads, HEAD)
            values_all = wide[:, k_cols:].reshape(-1, kv_heads, HEAD)
            q_block = queries[cut].reshape(rows, kv_heads, group, HEAD)
            allowed = (seg_own[step][:, None] == seg_all[step][None, :]) & (
                row_ids[:, None] >= key_ids[None, :]
            )
            scores = (
                jnp.einsum("qkgd,tkd->kgqt", q_block, keys_all, preferred_element_type=F32)
                * score_scale
            )
            scores = jnp.where(allowed[None, None], scores, -1e30)
            row_max = jnp.max(scores, axis=-1, keepdims=True)
            expo = jnp.exp(scores - row_max)
            row_sum = jnp.sum(expo, axis=-1, keepdims=True)
            probs = (expo / row_sum).astype(BF16)
            mixed = jnp.einsum("kgqt,tkd->qkgd", probs, values_all, preferred_element_type=F32)
            attn_heads = mixed.reshape(rows, -1).astype(BF16)
            heads_out.append(attn_heads)
            kept.append((q_block, keys_all, values_all, allowed, row_max + jnp.log(row_sum)))
            attn_part = rdot(attn_heads, w_out_t)
            middles.append(tokens[cut] + mp_sum(attn_part))
        middle = jnp.concatenate(middles, axis=0)
        attn_heads = jnp.concatenate(heads_out, axis=0)

        inv_ffn = inv_rms(middle)
        normed_ffn = (middle * inv_ffn * gain_ffn).astype(BF16)
        gate = dot(normed_ffn, gate_full)
        upward = dot(normed_ffn, up_full)
        sigma = jax.nn.sigmoid(gate)
        silu = gate * sigma
        act = (silu * upward).astype(BF16)
        grad_act = dot(cot, down_t)
        grad_gate_in = (grad_act * upward * sigma * (1.0 + gate * (1.0 - sigma))).astype(BF16)
        grad_up_in = (grad_act * silu).astype(BF16)

        def scatter(grad):
            return lax.psum_scatter(
                grad.astype(BF16), data_axes, scatter_dimension=0, tiled=True
            )

        down_owned = scatter(tdot(cot, act))
        backs = []
        for step in range(MICRO):
            cut = slice(step * rows, (step + 1) * rows)
            backs.append(
                mp_sum(rdot(grad_gate_in[cut], gate_full) + rdot(grad_up_in[cut], up_full))
            )
        gate_owned = scatter(tdot(normed_ffn, grad_gate_in))
        up_owned = scatter(tdot(normed_ffn, grad_up_in))
        down_part = rdot(act, down_t)
        layer_out = (middle + mp_sum(down_part)).astype(BF16)
        grad_normed_ffn = jnp.concatenate(backs, axis=0)
        gain_ffn_grad = jnp.sum(grad_normed_ffn * middle * inv_ffn, axis=0)
        grad_middle = cot.astype(F32) + norm_back(grad_normed_ffn, middle, inv_ffn, gain_ffn)
        grad_middle_b = grad_middle.astype(BF16)
        grad_heads = dot(grad_middle_b, w_out_t).astype(BF16)
        out_owned = scatter(tdot(grad_middle_b, attn_heads))

        grad_queries = []
        grad_keys = []
        grad_values = []
        for step in range(MICRO):
            cut = slice(step * rows, (step + 1) * rows)
            q_block, keys_all, values_all, allowed, log_sum = kept[step]
            g_block = grad_heads[cut].reshape(rows, kv_heads, group, HEAD)
            scores = (
                jnp.einsum("qkgd,tkd->kgqt", q_block, keys_all, preferred_element_type=F32)
                * score_scale
            )
            probs = jnp.where(allowed[None, None], jnp.exp(scores - log_sum), 0.0)
            grad_probs = jnp.einsum(
                "qkgd,tkd->kgqt", g_block, values_all, preferred_element_type=F32
            )
            row_dot = jnp.sum(grad_probs * probs, axis=-1, keepdims=True)
            grad_scores = (probs * (grad_probs - row_dot)).astype(BF16)
            grad_queries.append(
                jnp.einsum("kgqt,tkd->qkgd", grad_scores, keys_all, preferred_element_type=F32)
                * score_scale
            )
            grad_k = (
                jnp.einsum("kgqt,qkgd->tkd", grad_scores, q_block, preferred_element_type=F32)
                * score_scale
            )
            grad_v = jnp.einsum(
                "kgqt,qkgd->tkd", probs.astype(BF16), g_block, preferred_element_type=F32
            )
            wide = jnp.concatenate(
                [grad_k.reshape(-1, k_cols), grad_v.reshape(-1, k_cols)], axis=1
            )

            def part(flip):
                return lax.dynamic_slice_in_dim(
                    wide, jnp.bitwise_xor(rank, flip) * rows, rows, 0
                )

            sent = jnp.stack([part(1), part(3)]).astype(BF16)
            got = lax.ppermute(sent, "seq", pair).astype(F32)
            far = lax.ppermute((part(2) + got[1]).astype(BF16), "seq", down_pairs).astype(F32)
            owned = part(0) + got[0] + far
            grad_keys.append(owned[:, :k_cols])
            grad_values.append(owned[:, k_cols:])
        grad_query_rot = jnp.concatenate(grad_queries, axis=0).reshape(total, -1, HEAD)
        grad_key_rot = jnp.concatenate(grad_keys, axis=0).reshape(total, -1, HEAD)
        grad_value_in = jnp.concatenate(grad_values, axis=0).astype(BF16)
        query_turn = rotate_back(grad_query_rot, cosine, sine)
        key_turn = rotate_back(grad_key_rot, cosine, sine)
        query_gain = jnp.sum(query_turn * query_raw * query_inv, axis=(0, 1))
        key_gain = jnp.sum(key_turn * key_raw * key_inv, axis=(0, 1))
        grad_query_in = norm_back(query_turn, query_raw, query_inv, gain_query)
        grad_key_in = norm_back(key_turn, key_raw, key_inv, gain_key)
        grad_qkv_in = jnp.concatenate(
            [
                grad_query_in.astype(BF16).reshape(total, -1),
                grad_key_in.astype(BF16).reshape(total, -1),
                grad_value_in,
            ],
            axis=1,
        )
        qkv_owned = scatter(tdot(normed_attn, grad_qkv_in))
        backs = []
        for step in range(MICRO):
            cut = slice(step * rows, (step + 1) * rows)
            backs.append(mp_sum(rdot(grad_qkv_in[cut], w_qkv)))
        grad_normed_attn = jnp.concatenate(backs, axis=0)
        gain_attn_grad = jnp.sum(grad_normed_attn * tokens * inv_attn, axis=0)
        grad_tokens = (
            grad_middle + norm_back(grad_normed_attn, tokens, inv_attn, gain_attn)
        ).astype(BF16)

        small = jnp.concatenate([gain_attn_grad, gain_ffn_grad, query_gain, key_gain])
        small = lax.all_gather(small, ("dp", "seq", "mp"), axis=0, tiled=False)
        small = small.reshape(dp_size * seq_size, mp_size, -1)
        head_sum = jnp.sum(small[:, :, 2 * width :], axis=(0, 1))
        owner = (lax.axis_index("dp") * seq_size + rank) * own_rows
        wide_sum = jnp.sum(small[:, 0, : 2 * width], axis=0).reshape(2, width)
        wide_sum = lax.dynamic_slice_in_dim(wide_sum, owner, own_rows, 1)

        qkv_owned = qkv_owned.astype(F32)
        return (
            layer_out.reshape(MICRO, 1, rows, width),
            grad_tokens.reshape(MICRO, 1, rows, width),
            qkv_owned[:, :q_cols],
            qkv_owned[:, q_cols : q_cols + k_cols],
            qkv_owned[:, q_cols + k_cols :],
            out_owned.T.astype(F32),
            gate_owned.astype(F32),
            up_owned.astype(F32),
            down_owned.T.astype(F32),
            wide_sum[0],
            wide_sum[1],
            head_sum[:HEAD],
            head_sum[HEAD:],
        )

    return local


def solution(mesh):
    return jax.shard_map(
        make_local(mesh.shape["mp"], mesh.shape["seq"], mesh.shape["dp"]),
        mesh=mesh,
        in_specs=(
            P(None, "dp", "seq", None),
            P(("dp", "seq"), "mp"),
            P(("dp", "seq"), "mp"),
            P(("dp", "seq"), "mp"),
            P("mp", ("dp", "seq")),
            P(("dp", "seq"), "mp"),
            P(("dp", "seq"), "mp"),
            P("mp", ("dp", "seq")),
            P(("dp", "seq")),
            P(("dp", "seq")),
            P(),
            P(),
            P(None, "dp", "seq"),
            P(None, "dp", "seq"),
            P(None, "dp", "seq", None),
        ),
        out_specs=(
            P(None, "dp", "seq", None),
            P(None, "dp", "seq", None),
            P(("dp", "seq"), "mp"),
            P(("dp", "seq"), "mp"),
            P(("dp", "seq"), "mp"),
            P("mp", ("dp", "seq")),
            P(("dp", "seq"), "mp"),
            P(("dp", "seq"), "mp"),
            P("mp", ("dp", "seq")),
            P(("dp", "seq")),
            P(("dp", "seq")),
            P(),
            P(),
        ),
        check_vma=False,
    )
```

time: 2300 us -> 1420 us (0.62)
  waiting for transfers between devices: 1410 us -> 436 us
  other arithmetic: 172 us -> 269 us
  local copies, waits for them, and re-layouts: 68.1 us -> 160 us
  matrix products: 503 us -> 440 us
  blocking collectives: 124 us -> 72.4 us
    psum x3 -> x0, waiting for transfers between devices: 569 us -> none  [the longest x1 198 us: local(): lax.psum(down_part.astype(jnp.bfloat16), 'mp').astype(jnp.float32)]
    ppermute x0 -> x19, waiting for transfers between devices: none -> 331 us  [the longest x7 262 us: mp_sum(): other = lax.ppermute(part, 'mp', [(0, 1), (1, 0)])]
    reduce_scatter x9 -> x4, waiting for transfers between devices: 317 us -> 0.01 us  [scatter(): lax.psum_scatter(grad.astype(BF16), data_axes, scatter_dimension=0, tiled...]
    all_gather x11 -> x2, waiting for transfers between devices: 379 us -> 105 us  [the longest x1 105 us: local(): first = lax.all_gather(first, data_axes, axis=0, tiled=True)]
    unnamed x27 -> x8, waiting for transfers between devices: 141 us -> 0.12 us
    dot_general x14 -> x5, matrix products: 121 us -> 80.1 us  [tdot(): lax.dot_general(left, right, (((0,), (0,)), ((), ())), preferred_element_...]
    psum x1 -> x0, blocking collectives: 40.8 us -> none  [local(): lax.psum((query_gain_sum, key_gain_sum), ('dp', 'seq', 'mp'))]
    convert_element_type x25 -> x21, other arithmetic: 78.9 us -> 117 us  [the longest x2 59.6 us: local(): grad_scores = (probs * (grad_probs - row_dot)).astype(BF16)]
  transfers between devices with their start and end apart: 25 -> 26, of which waited for: 15 -> 10; matrix products, arithmetic and copies ran while one was open for 25% -> 51% of each run, Pallas kernels for 0% -> 0%
where the time goes in v1:
time: 1420 us
  matrix products  440 us (31%)
  waiting for transfers between devices  436 us (31%)
  other arithmetic  269 us (19%)
  local copies, waits for them, and re-layouts  160 us (11%)
  blocking collectives  72.4 us (5%)
  starting transfers between devices  22.2 us (2%)
  between operations  16.4 us (1%)
    ppermute x7, waiting for transfers between devices, mp_sum(): other = lax.ppermute(part, 'mp', [(0, 1), (1, 0)])  262 us
    all_gather x1, waiting for transfers between devices, local(): first = lax.all_gather(first, data_axes, axis=0, tiled=True)  105 us
    dot_general x5, matrix products, dot(): return jnp.dot(left, right, preferred_element_type=F32)  89.2 us
    dot_general x9, matrix products, rdot(): lax.dot_general(left, right, (((1,), (1,)), ((), ())), preferred_element_...  88.5 us
    dot_general x5, matrix products, tdot(): lax.dot_general(left, right, (((0,), (0,)), ((), ())), preferred_element_...  80.1 us
    all_gather x1, blocking collectives, local(): small = lax.all_gather(small, ('dp', 'seq', 'mp'), axis=0, tiled=False)  72.4 us
    convert_element_type x2, other arithmetic, local(): grad_scores = (probs * (grad_probs - row_dot)).astype(BF16)  59.6 us
    ppermute x2, waiting for transfers between devices, local(): far = lax.ppermute(own, 'seq', up_pairs)  54.1 us
  transfers between devices with their start and end apart: 26, of which 10 were waited for; matrix products, arithmetic and copies ran while one was open for 51% of the time, Pallas kernels for 0%

profile of v1, /device:TPU:0, one launch (start us, length us, event | category | flops | bytes accessed | tf_op | source)
XLA Modules:
  0.0 1416.4 jit_solution(16835309510703785874)
XLA Ops:
  18.6 104.9 %all-gather.5.cloned.1.call-done = bf16[2048,3200]{0,1:T(8,128)(2,1)} async-done(((bf16[128,3200]{0,1:T(8,128)(2,1)}), bf16[2048,3200]{0,1:T(8,128)(2,1)}) %all-gather.5.cloned.1.call-update) | async-done | bytes 13107216 | tf_op jit(solution)/shard_map/all_gather | solution.py:102
  143.4 14.1 fusion.144
  211.7 20.5 %collective-permute-done.1 = bf16[512,1024]{1,0:T(8,128)(2,1)} collective-permute-done((bf16[512,1024]{1,0:T(8,128)(2,1)}, bf16[512,1024]{1,0:T(8,128)(2,1)}, u32[]{:S(2)}, u32[]{:S(2)}) %collective-permute-start.1) | collective-permute-done | bytes 1048608 | tf_op jit(solution)/shard_map/ppermute | solution.py:160
  243.4 33.6 %collective-permute-done.7 = bf16[512,1024]{1,0:T(8,128)(2,1)} collective-permute-done((bf16[512,1024]{1,0:T(8,128)(2,1)}, bf16[512,1024]{1,0:T(8,128)(2,1)}, u32[]{:S(2)}, u32[]{:S(2)}) %collective-permute-start.7) | collective-permute-done | bytes 1048608 | tf_op jit(solution)/shard_map/ppermute | solution.py:160
  294.1 13.9 fusion.10
  308.0 15.6 %fusion.12 = f32[4,2,512]{2,1,0:T(2,128)S(1)} fusion(f32[4,2048,512,2]{2,1,3,0:T(8,128)} %get-tuple-element.170, f32[4,2,512]{2,1,0:T(2,128)S(1)} %get-tuple-element.169, pred[512,2048]{0,1:T(8,128)(4,1)S(1)} %get-tuple-element.161), kind=kLoop, calls=%fused_computation.24 | loop fusion | flops 33550336 | bytes 34635776 | tf_op jit(solution)/shard_map/reduce_sum | solution.py:178
  323.6 16.2 %fusion.115 = bf16[4,128,2,512]{3,1,2,0:T(8,128)(2,1)S(1)} fusion(bf16[2048,4,128,1]{0,2,3,1:T(8,128)(2,1)S(1)} %bitcast.435, f32[4,2048,512,2]{2,1,3,0:T(8,128)} %get-tuple-element.170, f32[4,2,512]{2,1,0:T(2,128)S(1)} %fusion.12, f32[4,2,512]{2,1,0:T(2,128)S(1)} %get-tuple-element.169, pred[512,2048]{0,1:T(8,128)(4,1)S(1)} %get-tuple-element.161), kind=kOutput, calls=%fused_computation.205 | convolution fusion | flops 2189950976 | bytes 37781504 | tf_op jit(solution)/shard_map/kgqt,tkd->qkgd/dot_general | solution.py:180
  339.9 6.4 fusion.65
  353.2 14.1 fusion.11
  367.4 14.4 %fusion.13 = f32[4,2,512]{2,1,0:T(2,128)S(1)} fusion(f32[4,2048,512,2]{2,1,3,0:T(8,128)} %get-tuple-element.172, f32[4,2,512]{2,1,0:T(2,128)S(1)} %get-tuple-element.171, pred[512,2048]{0,1:T(8,128)(4,1)S(1)} %copy-done.19), kind=kLoop, calls=%fused_computation.25 | loop fusion | flops 33550336 | bytes 34635776 | tf_op jit(solution)/shard_map/reduce_sum | solution.py:178
  381.8 16.1 %fusion.114 = bf16[4,128,2,512]{3,1,2,0:T(8,128)(2,1)} fusion(bf16[2048,4,128,1]{0,2,3,1:T(8,128)(2,1)S(1)} %bitcast.437, f32[4,2048,512,2]{2,1,3,0:T(8,128)} %get-tuple-element.172, f32[4,2,512]{2,1,0:T(2,128)S(1)} %fusion.13, f32[4,2,512]{2,1,0:T(2,128)S(1)} %get-tuple-element.171, pred[512,2048]{0,1:T(8,128)(4,1)S(1)} %copy-done.19), kind=kOutput, calls=%fused_computation.204 | convolution fusion | flops 2189950976 | bytes 37781504 | tf_op jit(solution)/shard_map/kgqt,tkd->qkgd/dot_general | solution.py:180
  408.1 42.0 %collective-permute-done.9 = bf16[512,2048]{1,0:T(8,128)(2,1)} collective-permute-done((bf16[512,2048]{1,0:T(8,128)(2,1)S(1)}, bf16[512,2048]{1,0:T(8,128)(2,1)}, u32[]{:S(2)}, u32[]{:S(2)}) %collective-permute-start.9) | collective-permute-done | bytes 2097184 | tf_op jit(solution)/shard_map/ppermute | solution.py:62
  450.1 9.5 fusion.49
  467.4 19.2 %fusion.29 = f32[3072,1024]{0,1:T(8,128)} fusion(bf16[1024,2048]{1,0:T(8,128)(2,1)} %bitcast.418, bf16[3,2048,3072]{1,2,0:T(8,128)(2,1)} %all-gather.7.cloned.1.call-done), kind=kOutput, calls=%fused_computation.65 | convolution fusion | flops 12884901888 | bytes 29360128 | tf_op jit(solution)/shard_map/dot_general | solution.py:18
  486.6 18.0 %fusion.36 = f32[1024,3072]{1,0:T(8,128)} fusion(bf16[1024,2048]{1,0:T(8,128)(2,1)S(1)} %copy-done.50, bf16[3,2048,3072]{1,2,0:T(8,128)(2,1)} %all-gather.7.cloned.1.call-done), kind=kOutput, calls=%fused_computation.72 | convolution fusion | flops 12884901888 | bytes 29360128 | tf_op jit(solution)/shard_map/dot_general | solution.py:18
  504.6 29.2 %fusion.27 = (bf16[1024,3072]{1,0:T(8,128)(2,1)}, bf16[1024,3072]{1,0:T(8,128)(2,1)}, bf16[1024,3072]{1,0:T(8,128)(2,1)}) fusion(f32[3072,1024]{0,1:T(8,128)} %fusion.29, f32[1024,3072]{1,0:T(8,128)} %fusion.36, bf16[1024,2048]{1,0:T(8,128)(2,1)} %multiply_convert_fusion.1, bf16[3,2048,3072]{1,2,0:T(8,128)(2,1)} %all-gather.7.cloned.1.call-done), kind=kOutput, calls=%fused_computation.58 | convolution fusion | flops 12932087808 | bytes 60817408 | tf_op jit(solution)/shard_map/dot_general | solution.py:18
  533.7 12.0 fusion.31
  545.8 11.0 add_convert_fusion.3
  557.6 19.4 %fusion.54 = bf16[1024,2048]{1,0:T(8,128)(2,1)} fusion(bf16[1024,3072]{1,0:T(8,128)(2,1)} %get-tuple-element.107, bf16[3,2048,3072]{1,2,0:T(8,128)(2,1)} %all-gather.7.cloned.1.call-done), kind=kOutput, calls=%fused_computation.131 | convolution fusion | flops 12886999040 | bytes 23068672 | tf_op jit(solution)/shard_map/dot_general | solution.py:26
  578.2 9.7 fusion.32
  588.0 10.8 add_convert_fusion.4
  606.2 131.6 %collective-permute-done.11 = bf16[512,2048]{1,0:T(8,128)(2,1)S(1)} collective-permute-done((bf16[512,2048]{1,0:T(8,128)(2,1)S(1)}, bf16[512,2048]{1,0:T(8,128)(2,1)S(1)}, u32[]{:S(2)}, u32[]{:S(2)}) %collective-permute-start.11) | collective-permute-done | bytes 2097184 | tf_op jit(solution)/shard_map/ppermute | solution.py:62
  741.4 13.9 add_convert_fusion.1
  755.3 8.4 convolution_convert_fusion.3
  763.8 19.6 %convolution_convert_fusion.1 = bf16[2048,3072]{1,0:T(8,128)(2,1)} fusion(bf16[1024,2048]{1,0:T(8,128)(2,1)} %multiply_convert_fusion.1, bf16[1024,3072]{1,0:T(8,128)(2,1)} %get-tuple-element.106), kind=kOutput, calls=%fused_computation.64 | convolution fusion | flops 12891193344 | bytes 23068672 | tf_op jit(solution)/shard_map/dot_general | solution.py:22
  783.5 19.7 %convolution_convert_fusion = bf16[2048,3072]{1,0:T(8,128)(2,1)} fusion(bf16[1024,2048]{1,0:T(8,128)(2,1)} %multiply_convert_fusion.1, bf16[1024,3072]{1,0:T(8,128)(2,1)} %get-tuple-element.105), kind=kOutput, calls=%fused_computation.63 | convolution fusion | flops 12891193344 | bytes 23068672 | tf_op jit(solution)/shard_map/dot_general | solution.py:22
  807.1 20.0 %convert_bitcast_fusion = bf16[2048,3072]{0,1:T(8,128)(2,1)} fusion(bf16[1024,3072]{1,0:T(8,128)(2,1)} %get-tuple-element.107, bf16[1024,2048]{1,0:T(8,128)(2,1)} %bitcast.419), kind=kOutput, calls=%fused_computation.59 | convolution fusion | flops 12891193344 | bytes 23068672 | tf_op jit(solution)/shard_map/dot_general | solution.py:22
  827.1 16.6 %copy.346 = bf16[2048,3072]{1,0:T(8,128)(2,1)} copy(bf16[2048,3072]{0,1:T(8,128)(2,1)} %convert_bitcast_fusion) | data formatting | bytes 25165824
  843.8 8.7 fusion.111
  855.2 25.8 %fusion = (f32[4,2,512]{2,1,0:T(2,128)S(1)}, f32[4,2048,512,2]{2,1,3,0:T(8,128)}) fusion(f32[4,2048,512,2]{2,1,3,0:T(8,128)} %get-tuple-element.172, f32[4,2,512]{2,1,0:T(2,128)S(1)} %bitcast.465, pred[512,2048]{0,1:T(8,128)(4,1)S(1)} %copy-done.20, bf16[2048,4,128,1]{0,2,3,1:T(8,128)(2,1)S(1)} %bitcast.438, bf16[512,4,2,128]{0,3,2,1:T(8,128)(2,1)S(1)} %bitcast.442), kind=kOutput, calls=%fused_computation.2 | convolution fusion | flops 2189422592 | bytes 71335936 | tf_op jit(solution)/shard_map/qkgd,tkd->kgqt/dot_general | solution.py:235
  881.1 16.6 %fusion.16 = f32[4,128,2048,1]{2,1,3,0:T(8,128)} fusion(bf16[512,4,2,128]{0,3,2,1:T(8,128)(2,1)} %bitcast.443, f32[4,2048,512,2]{2,1,3,0:T(8,128)} %get-tuple-element.172, f32[4,2,512]{2,1,0:T(2,128)S(1)} %bitcast.466, pred[512,2048]{0,1:T(8,128)(4,1)S(1)} %copy-done.20), kind=kOutput, calls=%fused_computation.28 | convolution fusion | flops 2181038080 | bytes 39862272 | tf_op jit(solution)/shard_map/kgqt,qkgd->tkd/dot_general | solution.py:248
  897.7 15.8 %fusion.18 = f32[4,128,2048,1]{2,1,3,0:T(8,128)} fusion(bf16[512,4,2,128]{0,3,2,1:T(8,128)(2,1)S(1)} %bitcast.440, f32[4,2048,512,2]{2,1,3,0:T(8,128)} %get-tuple-element.170, f32[4,2,512]{2,1,0:T(2,128)S(1)} %bitcast.462, pred[512,2048]{0,1:T(8,128)(4,1)S(1)} %copy-done.18), kind=kOutput, calls=%fused_computation.29 | convolution fusion | flops 2181038080 | bytes 39862272 | tf_op jit(solution)/shard_map/kgqt,qkgd->tkd/dot_general | solution.py:248
  913.5 24.6 %fusion.3 = (f32[4,2,512]{2,1,0:T(2,128)S(1)}, f32[4,2048,512,2]{2,1,3,0:T(8,128)}) fusion(f32[4,2048,512,2]{2,1,3,0:T(8,128)} %get-tuple-element.170, f32[4,2,512]{2,1,0:T(2,128)S(1)} %bitcast.463, pred[512,2048]{0,1:T(8,128)(4,1)S(1)} %copy-done.18, bf16[2048,4,128,1]{0,2,3,1:T(8,128)(2,1)} %bitcast.436, bf16[512,4,2,128]{0,3,2,1:T(8,128)(2,1)S(1)} %bitcast.441), kind=kOutput, calls=%fused_computation.7 | convolution fusion | flops 2189422592 | bytes 71335936 | tf_op jit(solution)/shard_map/qkgd,tkd->kgqt/dot_general | solution.py:235
  938.2 29.5 %fusion.2 = bf16[4,2,512,2048]{2,3,1,0:T(8,128)(2,1)} fusion(f32[4,2048,512,2]{2,1,3,0:T(8,128)} %get-tuple-element.174, f32[4,2048,512,2]{2,1,3,0:T(8,128)} %get-tuple-element.172, f32[4,2,512]{2,1,0:T(2,128)S(1)} %get-tuple-element.173, f32[4,2,512]{2,1,0:T(2,128)S(1)} %bitcast.467, pred[512,2048]{0,1:T(8,128)(4,1)S(1)} %copy-done.20), kind=kLoop, calls=%fused_computation.4 | loop fusion | flops 50331648 | bytes 84967424 | tf_op jit(solution)/shard_map/convert_element_type | solution.py:239
  967.7 13.5 bitcast_multiply_fusion.10
  992.3 5.8 copy.341
  998.1 30.1 %fusion.5 = bf16[4,2,512,2048]{2,3,1,0:T(8,128)(2,1)} fusion(f32[4,2048,512,2]{2,1,3,0:T(8,128)} %get-tuple-element.176, f32[4,2048,512,2]{2,1,3,0:T(8,128)} %get-tuple-element.170, f32[4,2,512]{2,1,0:T(2,128)S(1)} %get-tuple-element.175, f32[4,2,512]{2,1,0:T(2,128)S(1)} %bitcast.464, pred[512,2048]{0,1:T(8,128)(4,1)S(1)} %copy-done.18), kind=kLoop, calls=%fused_computation.9 | loop fusion | flops 50331648 | bytes 84967424 | tf_op jit(solution)/shard_map/convert_element_type | solution.py:239
  1028.3 13.4 bitcast_multiply_fusion.11
  1054.8 9.4 multiply_bitcast_fusion
  1089.1 6.9 multiply_reduce_fusion.6
  1120.6 15.1 %fusion.47 = (f32[1024]{0:T(1024)S(1)}, bf16[1024,1024]{1,0:T(8,128)(2,1)}) fusion(f32[128,8,8,128]{3,2,1,0:T(8,128)} %bitcast.420, f32[1024,2048]{1,0:T(8,128)} %copy-done.25, f32[128,8,8,128]{3,2,1,0:T(8,128)} %bitcast.424, f32[1024,1024]{1,0:T(8,128)} %copy.337, f32[128,8,8,128]{3,2,1,0:T(8,128)} %bitcast.421, f32[128,8,8,128]{3,2,1,0:T(8,128)} %bitcast.422, ...), kind=kLoop, calls=%fused_computation.104 | loop fusion | flops 11533312 | bytes 31465472 | tf_op jit(solution)/shard_map/reduce_sum | solution.py:271
  1139.9 13.7 collective-permute-done.14
  1174.5 12.4 convolution_convert_fusion.2
  1190.3 9.5 fusion.74
  1206.7 41.9 %collective-permute-done.18 = bf16[512,2048]{1,0:T(8,128)(2,1)} collective-permute-done((bf16[512,2048]{1,0:T(8,128)(2,1)}, bf16[512,2048]{1,0:T(8,128)(2,1)}, u32[]{:S(2)}, u32[]{:S(2)}) %collective-permute-start.18) | collective-permute-done | bytes 2097184 | tf_op jit(solution)/shard_map/ppermute | solution.py:62
  1251.8 40.8 %collective-permute-done.17 = bf16[512,2048]{1,0:T(8,128)(2,1)} collective-permute-done((bf16[512,2048]{1,0:T(8,128)(2,1)S(1)}, bf16[512,2048]{1,0:T(8,128)(2,1)}, u32[]{:S(2)}, u32[]{:S(2)}) %collective-permute-start.17) | collective-permute-done | bytes 2097184 | tf_op jit(solution)/shard_map/ppermute | solution.py:62
  1306.3 72.4 %all-gather.1 = f32[32,1,4352]{2,1,0:T(1,128)S(1)} all-gather(f32[1,1,4352]{2,1,0:T(1,128)S(1)} %reshape.571), channel_id=2, replica_groups=mesh['dp'=4,'seq'=4,'mp'=2] {'dp','seq','mp'}, dimensions={0}, use_global_device_ids=true | all-gather | bytes 574464 | tf_op jit(solution)/shard_map/all_gather | solution.py:295
  1381.6 14.2 %add_convert_fusion = bf16[2,1,512,2048]{3,2,1,0:T(8,128)(2,1)} fusion(f32[2,1,512,2048]{3,2,1,0:T(8,128)} %bitcast.415, f32[2,1,512,2048]{3,2,1,0:T(8,128)} %bitcast.416, bf16[2,1,512,2048]{3,2,1,0:T(8,128)(2,1)} %param.29, bf16[2,1,512,2048]{3,2,1,0:T(8,128)(2,1)} %param.15, f32[2,512]{1,0:T(2,128)S(1)} %broadcast_multiply_fusion.6, ...), kind=kLoop, calls=%fused_computation.81 | loop fusion | flops 33554432 | bytes 37789696 | tf_op jit(solution)/shard_map/convert_element_type | solution.py:292
  (453 shorter events, 299.2 us)
Async XLA Ops:
  7.2 116.3 %all-gather.5.cloned.1.call-start = ((), (), s32[]{:S(2)}) async-start(), calls=%async_computation.5 | async-start | bytes 13926400 | tf_op jit(solution)/shard_map/all_gather | solution.py:102
  13.8 453.6 %all-gather.7.cloned.1.call-start = ((), (), s32[]{:S(2)}) async-start(), calls=%async_computation.6 | async-start | bytes 40108032 | tf_op jit(solution)/shard_map/all_gather | solution.py:105
  15.4 108.2 %copy-start.86 = (s32[2,1,512]{2,1,0:T(1,128)S(1)}, s32[2,1,512]{2,1,0:T(1,128)}, u32[]{:S(2)}) copy-start(s32[2,1,512]{2,1,0:T(1,128)} %param.27) | copy-start | bytes 12292
  15.4 108.5 %copy-start.99 = (s32[2,1,512]{2,1,0:T(1,128)S(1)}, s32[2,1,512]{2,1,0:T(1,128)}, u32[]{:S(2)}) copy-start(s32[2,1,512]{2,1,0:T(1,128)} %param.28) | copy-start | bytes 12292
  18.6 112.1 %copy-start.100 = (bf16[128]{0:T(256)(128)(2,1)S(1)}, bf16[128]{0:T(256)(128)(2,1)}, u32[]{:S(2)}) copy-start(bf16[128]{0:T(256)(128)(2,1)} %param.26) | copy-start | bytes 772
  18.6 112.1 %copy-start.101 = (bf16[128]{0:T(256)(128)(2,1)S(1)}, bf16[128]{0:T(256)(128)(2,1)}, u32[]{:S(2)}) copy-start(bf16[128]{0:T(256)(128)(2,1)} %param.25) | copy-start | bytes 772
  123.5 1272.4 %reduce-scatter.10.cloned.1.call-start = ((), (), s32[]{:S(2)}) async-start(), calls=%async_computation.8 | async-start | bytes 4456448 | tf_op jit(solution)/shard_map/reduce_scatter | solution.py:201
  123.6 7.3 collective-permute-start.3
  130.8 43.2 %copy-start.95 = (f32[128]{0:T(128)}, f32[128]{0:T(128)S(1)}, u32[]{:S(2)}) copy-start(f32[128]{0:T(128)S(1)} %convert_element_type.259) | copy-start | bytes 1540
  130.8 77.0 %copy-start.92 = (f32[128]{0:T(128)}, f32[128]{0:T(128)S(1)}, u32[]{:S(2)}) copy-start(f32[128]{0:T(128)S(1)} %convert_element_type.263) | copy-start | bytes 1540
  130.8 4.8 collective-permute-start.4
  138.7 184.9 %copy-start.17 = (pred[512,2048]{0,1:T(8,128)(4,1)}, pred[512,2048]{0,1:T(8,128)(4,1)S(1)}, u32[]{:S(2)}) copy-start(pred[512,2048]{0,1:T(8,128)(4,1)S(1)} %get-tuple-element.161) | copy-start | bytes 3145732
  181.8 96.8 %collective-permute-start = (bf16[512,1024]{1,0:T(8,128)(2,1)}, bf16[512,1024]{1,0:T(8,128)(2,1)}, u32[]{:S(2)}, u32[]{:S(2)}) collective-permute-start(bf16[512,1024]{1,0:T(8,128)(2,1)} %pad_maximum_fusion.10), channel_id=1, source_target_pairs={{0,2},{2,0},{4,6},{6,4},{1,3},{3,1},{5,7},{7,5},{8,10},{10,8},{12,... | collective-permute-start | bytes 3145736 | tf_op jit(solution)/shard_map/ppermute | solution.py:159
  181.9 50.3 %collective-permute-start.1 = (bf16[512,1024]{1,0:T(8,128)(2,1)}, bf16[512,1024]{1,0:T(8,128)(2,1)}, u32[]{:S(2)}, u32[]{:S(2)}) collective-permute-start(bf16[512,1024]{1,0:T(8,128)(2,1)} %pad_maximum_fusion.10), channel_id=1, source_target_pairs={{0,4},{2,6},{1,5},{3,7},{8,12},{10,14},{9,13},{11,15},{16,20},{18,... | collective-permute-start | bytes 3145736 | tf_op jit(solution)/shard_map/ppermute | solution.py:160
  191.4 89.4 %collective-permute-start.6 = (bf16[512,1024]{1,0:T(8,128)(2,1)}, bf16[512,1024]{1,0:T(8,128)(2,1)}, u32[]{:S(2)}, u32[]{:S(2)}) collective-permute-start(bf16[512,1024]{1,0:T(8,128)(2,1)} %pad_maximum_fusion.11), channel_id=1, source_target_pairs={{0,2},{2,0},{4,6},{6,4},{1,3},{3,1},{5,7},{7,5},{8,10},{10,8},{12,... | collective-permute-start | bytes 3145736 | tf_op jit(solution)/shard_map/ppermute | solution.py:159
  191.6 85.4 %collective-permute-start.7 = (bf16[512,1024]{1,0:T(8,128)(2,1)}, bf16[512,1024]{1,0:T(8,128)(2,1)}, u32[]{:S(2)}, u32[]{:S(2)}) collective-permute-start(bf16[512,1024]{1,0:T(8,128)(2,1)} %pad_maximum_fusion.11), channel_id=1, source_target_pairs={{0,4},{2,6},{1,5},{3,7},{8,12},{10,14},{9,13},{11,15},{16,20},{18,... | collective-permute-start | bytes 3145736 | tf_op jit(solution)/shard_map/ppermute | solution.py:160
  232.2 56.4 %collective-permute-start.2 = (bf16[512,1024]{1,0:T(8,128)(2,1)}, bf16[512,1024]{1,0:T(8,128)(2,1)}, u32[]{:S(2)}, u32[]{:S(2)}) collective-permute-start(bf16[512,1024]{1,0:T(8,128)(2,1)} %collective-permute-done.1), channel_id=1, source_target_pairs={{0,2},{2,0},{4,6},{6,4},{1,3},{3,1},{5,7},{7,5},{8,10},{10,8},{12,... | collective-permute-start | bytes 3145736 | tf_op jit(solution)/shard_map/ppermute | solution.py:161
  278.5 69.2 %collective-permute-start.8 = (bf16[512,1024]{1,0:T(8,128)(2,1)}, bf16[512,1024]{1,0:T(8,128)(2,1)}, u32[]{:S(2)}, u32[]{:S(2)}) collective-permute-start(bf16[512,1024]{1,0:T(8,128)(2,1)} %collective-permute-done.7), channel_id=1, source_target_pairs={{0,2},{2,0},{4,6},{6,4},{1,3},{3,1},{5,7},{7,5},{8,10},{10,8},{12,... | collective-permute-start | bytes 3145736 | tf_op jit(solution)/shard_map/ppermute | solution.py:161
  294.0 29.6 %copy-start.45 = (bf16[2048,512]{0,1:T(8,128)(2,1)}, bf16[2048,512]{0,1:T(8,128)(2,1)S(1)}, u32[]{:S(2)}) copy-start(bf16[2048,512]{0,1:T(8,128)(2,1)S(1)} %get-tuple-element.125) | copy-start | bytes 6291460
  346.2 61.9 %collective-permute-start.5 = (bf16[512,2048]{1,0:T(8,128)(2,1)}, bf16[512,2048]{1,0:T(8,128)(2,1)}, u32[]{:S(2)}, u32[]{:S(2)}) collective-permute-start(bf16[512,2048]{1,0:T(8,128)(2,1)} %fusion.65), channel_id=1, source_target_pairs={{0,1},{1,0},{2,3},{3,2},{4,5},{5,4},{6,7},{7,6},{8,9},{9,8},{10,11... | collective-permute-start | bytes 6291464 | tf_op jit(solution)/shard_map/ppermute | solution.py:62
  353.2 28.6 %copy-start.46 = (bf16[2048,512]{0,1:T(8,128)(2,1)}, bf16[2048,512]{0,1:T(8,128)(2,1)S(1)}, u32[]{:S(2)}) copy-start(bf16[2048,512]{0,1:T(8,128)(2,1)S(1)} %get-tuple-element.131) | copy-start | bytes 6291460
  402.9 47.1 %collective-permute-start.9 = (bf16[512,2048]{1,0:T(8,128)(2,1)S(1)}, bf16[512,2048]{1,0:T(8,128)(2,1)}, u32[]{:S(2)}, u32[]{:S(2)}) collective-permute-start(bf16[512,2048]{1,0:T(8,128)(2,1)S(1)} %fusion.68), channel_id=1, source_target_pairs={{0,1},{1,0},{2,3},{3,2},{4,5},{5,4},{6,7},{7,6},{8,9},{9,8},{10,11... | collective-permute-start | bytes 6291464 | tf_op jit(solution)/shard_map/ppermute | solution.py:62
  467.4 19.2 %copy-start.50 = (bf16[1024,2048]{1,0:T(8,128)(2,1)S(1)}, bf16[1024,2048]{1,0:T(8,128)(2,1)}, u32[]{:S(2)}) copy-start(bf16[1024,2048]{1,0:T(8,128)(2,1)} %multiply_convert_fusion.1) | copy-start | bytes 12582916
  545.8 32.5 %slice-start.8 = ((s8[6291456]{0:T(1024)(128)(4,1)}), s8[2097152]{0:T(1024)(128)(4,1)S(1)}, s32[]{:S(2)}) async-start(s8[6291456]{0:T(1024)(128)(4,1)} %bitcast.490), calls=%async_computation.20 | async-start | bytes 4194304
  556.8 48.6 %collective-permute-start.12 = (bf16[512,2048]{1,0:T(8,128)(2,1)S(1)}, bf16[512,2048]{1,0:T(8,128)(2,1)S(1)}, u32[]{:S(2)}, u32[]{:S(2)}) collective-permute-start(bf16[512,2048]{1,0:T(8,128)(2,1)S(1)} %add_convert_fusion.3), channel_id=1, source_target_pairs={{0,1},{1,0},{2,3},{3,2},{4,5},{5,4},{6,7},{7,6},{8,9},{9,8},{10,11... | collective-permute-start | bytes 6291464 | tf_op jit(solution)/shard_map/ppermute | solution.py:62
  557.6 20.7 %slice-start.9 = ((s8[6291456]{0:T(1024)(128)(4,1)}), s8[4194304]{0:T(1024)(128)(4,1)S(1)}, s32[]{:S(2)}) async-start(s8[6291456]{0:T(1024)(128)(4,1)} %bitcast.490), calls=%async_computation.21 | async-start | bytes 8388608
  576.9 164.4 %collective-permute-start.10 = (bf16[1024,2048]{1,0:T(8,128)(2,1)}, bf16[1024,2048]{1,0:T(8,128)(2,1)}, u32[]{:S(2)}, u32[]{:S(2)}) collective-permute-start(bf16[1024,2048]{1,0:T(8,128)(2,1)} %fusion.54), channel_id=1, source_target_pairs={{0,1},{1,0},{2,3},{3,2},{4,5},{5,4},{6,7},{7,6},{8,9},{9,8},{10,11... | collective-permute-start | bytes 12582920 | tf_op jit(solution)/shard_map/ppermute | solution.py:62
  598.8 139.0 %collective-permute-start.11 = (bf16[512,2048]{1,0:T(8,128)(2,1)S(1)}, bf16[512,2048]{1,0:T(8,128)(2,1)S(1)}, u32[]{:S(2)}, u32[]{:S(2)}) collective-permute-start(bf16[512,2048]{1,0:T(8,128)(2,1)S(1)} %add_convert_fusion.4), channel_id=1, source_target_pairs={{0,1},{1,0},{2,3},{3,2},{4,5},{5,4},{6,7},{7,6},{8,9},{9,8},{10,11... | collective-permute-start | bytes 6291464 | tf_op jit(solution)/shard_map/ppermute | solution.py:62
  605.3 133.2 %copy-start.67 = (f32[2048,1]{0,1:T(1,128)S(1)}, f32[2048,1]{0,1:T(1,128)}, u32[]{:S(2)}) copy-start(f32[2048,1]{0,1:T(1,128)} %get-tuple-element.111) | copy-start | bytes 24580
  605.3 133.2 %copy-start.73 = (f32[1024]{0:T(1024)S(1)}, f32[1024]{0:T(1024)}, u32[]{:S(2)}) copy-start(f32[1024]{0:T(1024)} %copy-done.72) | copy-start | bytes 12292
  606.1 132.4 %copy-start.6 = (f32[512,2048]{1,0:T(8,128)S(1)}, f32[512,2048]{1,0:T(8,128)}, u32[]{:S(2)}) copy-start(f32[512,2048]{1,0:T(8,128)} %copy-done.5) | copy-start | bytes 12582916
  606.2 132.4 %copy-start.8 = (f32[512,2048]{1,0:T(8,128)S(1)}, f32[512,2048]{1,0:T(8,128)}, u32[]{:S(2)}) copy-start(f32[512,2048]{1,0:T(8,128)} %get-tuple-element.121) | copy-start | bytes 12582916
  763.8 634.1 %reduce-scatter.12.cloned.1.call-start = ((), (), s32[]{:S(2)}) async-start(), calls=%async_computation.9 | async-start | bytes 13369344 | tf_op jit(solution)/shard_map/reduce_scatter | solution.py:201
  783.4 616.9 %reduce-scatter.14.cloned.1.call-start = ((), (), s32[]{:S(2)}) async-start(), calls=%async_computation.10 | async-start | bytes 13369344 | tf_op jit(solution)/shard_map/reduce_scatter | solution.py:201
  803.2 599.5 %reduce-scatter.16.cloned.1.call-start = ((), (), s32[]{:S(2)}) async-start(), calls=%async_computation.11 | async-start | bytes 13369344
  843.8 561.7 %reduce-scatter.8.cloned.1.call-start = ((), (), s32[]{:S(2)}) async-start(), calls=%async_computation.7 | async-start | bytes 8912896 | tf_op jit(solution)/shard_map/reduce_scatter | solution.py:201
  938.2 29.5 %copy-start.58 = (bf16[512,8,128]{2,0,1:T(8,128)(2,1)S(1)}, bf16[512,8,128]{2,0,1:T(8,128)(2,1)}, u32[]{:S(2)}) copy-start(bf16[512,8,128]{2,0,1:T(8,128)(2,1)} %copy.271) | copy-start | bytes 3145732
  998.1 30.1 %copy-start.56 = (bf16[512,8,128]{2,0,1:T(8,128)(2,1)S(1)}, bf16[512,8,128]{2,0,1:T(8,128)(2,1)}, u32[]{:S(2)}) copy-start(bf16[512,8,128]{2,0,1:T(8,128)(2,1)} %copy.264) | copy-start | bytes 3145732
  1053.3 44.9 %collective-permute-start.15 = (bf16[2,512,1024]{2,1,0:T(8,128)(2,1)}, bf16[2,512,1024]{2,1,0:T(8,128)(2,1)S(1)}, u32[]{:S(2)}, u32[]{:S(2)}) collective-permute-start(bf16[2,512,1024]{2,1,0:T(8,128)(2,1)} %pad_maximum_fusion.7), channel_id=1, source_target_pairs={{0,2},{2,0},{4,6},{6,4},{1,3},{3,1},{5,7},{7,5},{8,10},{10,8},{12,... | collective-permute-start | bytes 6291464 | tf_op jit(solution)/shard_map/ppermute | solution.py:261
  1068.3 36.2 %collective-permute-start.13 = (bf16[2,512,1024]{2,1,0:T(8,128)(2,1)}, bf16[2,512,1024]{2,1,0:T(8,128)(2,1)}, u32[]{:S(2)}, u32[]{:S(2)}) collective-permute-start(bf16[2,512,1024]{2,1,0:T(8,128)(2,1)} %pad_maximum_fusion.6), channel_id=1, source_target_pairs={{0,2},{2,0},{4,6},{6,4},{1,3},{3,1},{5,7},{7,5},{8,10},{10,8},{12,... | collective-permute-start | bytes 6291464 | tf_op jit(solution)/shard_map/ppermute | solution.py:261
  1102.9 32.8 %collective-permute-start.16 = (bf16[512,1024]{1,0:T(8,128)(2,1)S(1)}, bf16[512,1024]{1,0:T(8,128)(2,1)}, u32[]{:S(2)}, u32[]{:S(2)}) collective-permute-start(bf16[512,1024]{1,0:T(8,128)(2,1)S(1)} %fusion.83), channel_id=1, source_target_pairs={{4,0},{6,2},{5,1},{7,3},{12,8},{14,10},{13,9},{15,11},{20,16},{22,... | collective-permute-start | bytes 3145736 | tf_op jit(solution)/shard_map/ppermute | solution.py:262
  1108.8 44.7 %collective-permute-start.14 = (bf16[512,1024]{1,0:T(8,128)(2,1)S(1)}, bf16[512,1024]{1,0:T(8,128)(2,1)}, u32[]{:S(2)}, u32[]{:S(2)}) collective-permute-start(bf16[512,1024]{1,0:T(8,128)(2,1)S(1)} %fusion.93), channel_id=1, source_target_pairs={{4,0},{6,2},{5,1},{7,3},{12,8},{14,10},{13,9},{15,11},{20,16},{22,... | collective-permute-start | bytes 3145736 | tf_op jit(solution)/shard_map/ppermute | solution.py:262
  1199.8 48.8 %collective-permute-start.18 = (bf16[512,2048]{1,0:T(8,128)(2,1)}, bf16[512,2048]{1,0:T(8,128)(2,1)}, u32[]{:S(2)}, u32[]{:S(2)}) collective-permute-start(bf16[512,2048]{1,0:T(8,128)(2,1)} %fusion.74), channel_id=1, source_target_pairs={{0,1},{1,0},{2,3},{3,2},{4,5},{5,4},{6,7},{7,6},{8,9},{9,8},{10,11... | collective-permute-start | bytes 6291464 | tf_op jit(solution)/shard_map/ppermute | solution.py:62
  1205.4 46.3 %copy-start.63 = (bf16[512,2048]{1,0:T(8,128)(2,1)}, bf16[512,2048]{1,0:T(8,128)(2,1)S(1)}, u32[]{:S(2)}) copy-start(bf16[512,2048]{1,0:T(8,128)(2,1)S(1)} %fusion.71) | copy-start | bytes 6291460
  1205.5 87.0 %collective-permute-start.17 = (bf16[512,2048]{1,0:T(8,128)(2,1)S(1)}, bf16[512,2048]{1,0:T(8,128)(2,1)}, u32[]{:S(2)}, u32[]{:S(2)}) collective-permute-start(bf16[512,2048]{1,0:T(8,128)(2,1)S(1)} %fusion.71), channel_id=1, source_target_pairs={{0,1},{1,0},{2,3},{3,2},{4,5},{5,4},{6,7},{7,6},{8,9},{9,8},{10,11... | collective-permute-start | bytes 6291464 | tf_op jit(solution)/shard_map/ppermute | solution.py:62
  1251.7 48.4 %copy-start.9 = (f32[512,2048]{1,0:T(8,128)}, f32[512,2048]{1,0:T(8,128)S(1)}, u32[]{:S(2)}) copy-start(f32[512,2048]{1,0:T(8,128)S(1)} %convert_add_fusion) | copy-start | bytes 12582916
  1301.1 80.5 %copy-start.68 = (f32[2048,1]{0,1:T(1,128)S(1)}, f32[2048,1]{0,1:T(1,128)}, u32[]{:S(2)}) copy-start(f32[2048,1]{0,1:T(1,128)} %get-tuple-element.111) | copy-start | bytes 24580
  1301.1 80.5 %copy-start.91 = (f32[2,512]{1,0:T(2,128)S(1)}, f32[2,512]{1,0:T(2,128)}, u32[]{:S(2)}) copy-start(f32[2,512]{1,0:T(2,128)} %get-tuple-element.152) | copy-start | bytes 12292
  (94 other events, 597.3 us)
Sparse Core Ops, SparseCore 0:
  13.9 109.4 all-gather.4
  125.0 236.3 all-gather.6
  763.9 72.8 reduce-scatter.9
  840.7 133.9 reduce-scatter.11
  978.6 147.5 reduce-scatter.13
  1130.2 133.7 reduce-scatter.15
  1268.1 104.6 reduce-scatter.7

commit v2 on v1

--- a/solution.py
+++ b/solution.py
@@ -1,6 +1,10 @@
+import functools
+
 import jax
 import jax.numpy as jnp
 from jax import lax
+from jax.experimental import pallas as pl
+from jax.experimental.pallas import tpu as pltpu
 from jax.sharding import PartitionSpec as P
 
 HEADS = 16
@@ -12,6 +16,8 @@
 ROPE_BASE = 1000000.0
 F32 = jnp.float32
 BF16 = jnp.bfloat16
+SCALE = HEAD ** (-0.5)
+EXP2_SCALE = SCALE * 1.4426950408889634
 
 
 def dot(left, right):
@@ -50,18 +56,123 @@
     return lax.rsqrt(jnp.mean(values * values, axis=-1, keepdims=True) + EPS)
 
 
+def forward_kernel(tile, group, need, q, k0,v0,k1,v1,k2,v2,k3,v3, seg_q, seg_k, out, log_sum, acc, den):
+    rows=q.shape[0]
+    tiles=[(g,t) for g in range(group) for t in range(rows//tile)]
+    def run(flip, k, v):
+        for g,t in tiles:
+            cut=slice(t*tile,(t+1)*tile)
+            n=(t+1)*tile if flip==0 else rows
+            s=rdot(q[cut,g*HEAD:(g+1)*HEAD], k[:n,:])
+            ok=seg_q[cut,:]==seg_k[flip:flip+1,:n]
+            if flip==0:
+                ok&=(lax.broadcasted_iota(jnp.int32,(tile,n),0)+t*tile)>=lax.broadcasted_iota(jnp.int32,(tile,n),1)
+            e=jnp.where(ok,jnp.exp2(s*EXP2_SCALE),0.0)
+            mixed=dot(e.astype(BF16),v[:n,:])
+            total=jnp.sum(e,axis=1,keepdims=True)
+            at=slice(g*rows+t*tile,g*rows+(t+1)*tile)
+            if flip==0:
+                acc[at,:]=mixed; den[at,:]=total
+            else:
+                acc[at,:]+=mixed; den[at,:]+=total
+    run(0,k0,v0)
+    for flip,(k,v) in ((1,(k1,v1)),(2,(k2,v2)),(3,(k3,v3))):
+        pl.when(need[flip]>0)(functools.partial(run,flip,k,v))
+    for g in range(group):
+        at=slice(g*rows,(g+1)*rows)
+        out[:,g*HEAD:(g+1)*HEAD]=(acc[at,:]/den[at,:]).astype(out.dtype)
+    log_sum[0]=jnp.log2(den[...])
+
+def attend(need, queries, step, parts, seg_q, seg_k, k_cols, group, tile=256):
+    rows=parts[0].shape[0]; kv=k_cols//HEAD
+    kspec=pl.BlockSpec((rows,HEAD),lambda h,n:(0,h))
+    vspec=pl.BlockSpec((rows,HEAD),lambda h,n:(0,h+kv))
+    return pl.pallas_call(
+        functools.partial(forward_kernel,tile,group),
+        grid_spec=pltpu.PrefetchScalarGridSpec(
+            num_scalar_prefetch=1, grid=(kv,),
+            in_specs=[pl.BlockSpec((rows,group*HEAD),lambda h,n:(step,h))]+[kspec,vspec]*4+[
+                pl.BlockSpec((rows,1),lambda h,n:(0,0)), pl.BlockSpec((4,rows),lambda h,n:(0,0))],
+            out_specs=[pl.BlockSpec((rows,group*HEAD),lambda h,n:(0,h)), pl.BlockSpec((1,group*rows,1),lambda h,n:(h,0,0))],
+            scratch_shapes=[pltpu.VMEM((group*rows,HEAD),F32),pltpu.VMEM((group*rows,1),F32)]),
+        out_shape=[jax.ShapeDtypeStruct((rows,kv*group*HEAD),BF16),jax.ShapeDtypeStruct((kv,group*rows,1),F32)],
+        name="attend",
+    )(need,queries,*[p for part in parts for p in (part,part)],seg_q,seg_k)
+
+def backward_kernel(tile, group, need, q, g_out, k0,v0,k1,v1,k2,v2,k3,v3, seg_q, seg_k, stats, dq, d0,d1,d2,d3, acc):
+    rows=q.shape[0]
+    tiles=[(g,t) for g in range(group) for t in range(rows//tile)]
+    def run(flip,k,v,d,dk_acc,dv_acc):
+        for idx,(g,t) in enumerate(tiles):
+            cut=slice(t*tile,(t+1)*tile)
+            at=slice(g*rows+t*tile,g*rows+(t+1)*tile)
+            n=(t+1)*tile if flip==0 else rows
+            qt=q[cut,g*HEAD:(g+1)*HEAD]; dt=g_out[cut,g*HEAD:(g+1)*HEAD]
+            kn=k[:n,:]
+            s=rdot(kn,qt)
+            ok=seg_k[:n,flip:flip+1]==seg_q[:,cut]
+            if flip==0:
+                ok&=(lax.broadcasted_iota(jnp.int32,(n,tile),1)+t*tile)>=lax.broadcasted_iota(jnp.int32,(n,tile),0)
+            p=jnp.where(ok,jnp.exp2(s*EXP2_SCALE-stats[0,0:1,at]),0.0)
+            dp=rdot(v[:n,:],dt)
+            ds=(p*(dp-stats[0,1:2,at])).astype(BF16)
+            dv=dot(p.astype(BF16),dt)
+            dk=dot(ds,qt)
+            if idx==0:
+                dk_acc[...]=jnp.zeros_like(dk_acc); dv_acc[...]=jnp.zeros_like(dv_acc)
+            dk_acc[:n,:]+=dk
+            dv_acc[:n,:]+=dv
+            back=tdot(ds,kn)*SCALE
+            o=(cut,slice(g*HEAD,(g+1)*HEAD))
+            if flip==0: dq[o]=back
+            else: dq[o]+=back
+        d[0]=(dk_acc[...]*SCALE).astype(d.dtype)
+        d[1]=dv_acc[...].astype(d.dtype)
+    run(0,k0,v0,d0,acc.at[0],acc.at[1])
+    for flip,(k,v,d) in ((1,(k1,v1,d1)),(2,(k2,v2,d2)),(3,(k3,v3,d3))):
+        pl.when(need[flip]>0)(functools.partial(run,flip,k,v,d,acc.at[0],acc.at[1]))
+        def clear(d=d): d[...]=jnp.zeros_like(d)
+        pl.when(need[flip]<=0)(clear)
+
+def attend_back(need, queries, grad_heads, step, parts, seg_q, seg_k, stats, k_cols, group, tile=256):
+    rows=parts[0].shape[0]; kv=k_cols//HEAD
+    kspec=pl.BlockSpec((rows,HEAD),lambda h,n:(0,h))
+    vspec=pl.BlockSpec((rows,HEAD),lambda h,n:(0,h+kv))
+    qspec=pl.BlockSpec((rows,group*HEAD),lambda h,n:(step,h))
+    dspec=pl.BlockSpec((2,rows,HEAD),lambda h,n:(0,0,h))
+    types=(F32,BF16,F32,BF16)
+    return pl.pallas_call(
+        functools.partial(backward_kernel,tile,group),
+        grid_spec=pltpu.PrefetchScalarGridSpec(
+            num_scalar_prefetch=1, grid=(kv,),
+            in_specs=[qspec,qspec]+[kspec,vspec]*4+[
+                pl.BlockSpec((1,rows),lambda h,n:(0,0)), pl.BlockSpec((rows,4),lambda h,n:(0,0)),
+                pl.BlockSpec((1,2,group*rows),lambda h,n:(h,0,0))],
+            out_specs=[pl.BlockSpec((rows,group*HEAD),lambda h,n:(0,h))]+[dspec]*4,
+            scratch_shapes=[pltpu.VMEM((2,rows,HEAD),F32)]),
+        out_shape=[jax.ShapeDtypeStruct((rows,kv*group*HEAD),F32)]+[jax.ShapeDtypeStruct((2,rows,k_cols),t) for t in types],
+        name="attend_back",
+    )(need,queries,grad_heads,*[p for part in parts for p in (part,part)],seg_q,seg_k,stats)
+
+
 def make_local(mp_size, seq_size, dp_size):
     data_axes = ("dp", "seq")
     pair = [(i, i ^ 1) for i in range(seq_size)]
     up_pairs = [(i, i + 2) for i in range(seq_size - 2)]
     down_pairs = [(i + 2, i) for i in range(seq_size - 2)]
 
-    def mp_sum(part):
+    def scatter(grad):
+        return lax.psum_scatter(grad, data_axes, scatter_dimension=0, tiled=True)
+
+    def mp_part(part):
         part = lax.optimization_barrier(part.astype(BF16))
         if mp_size == 2:
-            other = lax.ppermute(part, "mp", [(0, 1), (1, 0)])
-            return part.astype(F32) + other.astype(F32)
-        return lax.psum(part, "mp").astype(F32)
+            return part, lax.ppermute(part, "mp", [(0, 1), (1, 0)])
+        return lax.psum(part, "mp"), jnp.zeros(part.shape, BF16)
+
+    def mp_sum(part):
+        mine, other = mp_part(part)
+        return mine.astype(F32) + other.astype(F32)
 
     def local(
         hidden,
@@ -87,7 +198,6 @@
         k_cols = w_key.shape[1]
         kv_heads = k_cols // HEAD
         group = HEADS // KV_HEADS
-        score_scale = HEAD ** (-0.5)
         rank = lax.axis_index("seq")
         own_rows = w_query.shape[0]
 
@@ -103,6 +213,14 @@
         second = jnp.stack([w_gate, w_up, w_down.T])
         second, first = lax.optimization_barrier((second, first))
         second = lax.all_gather(second, data_axes, axis=1, tiled=True)
+        tokens = hidden.reshape(total, width).astype(F32)
+        inv_attn = inv_rms(tokens)
+        frequency = ROPE_BASE ** (-(jnp.arange(HEAD // 2, dtype=F32) * 2.0) / HEAD)
+        angles = positions.reshape(total).astype(F32)[:, None] * frequency[None, :]
+        angles = jnp.concatenate([angles, angles], axis=-1)[:, None, :]
+        cosine = jnp.cos(angles)
+        sine = jnp.sin(angles)
+        first, cosine, sine, inv_attn = lax.optimization_barrier((first, cosine, sine, inv_attn))
         qkv_cols = q_cols + 2 * k_cols
         w_qkv = first[:, :qkv_cols]
         w_out_t = first[:, qkv_cols : qkv_cols + q_cols]
@@ -112,31 +230,17 @@
         gain_query = norm_query.astype(F32)
         gain_key = norm_key.astype(F32)
 
-        tokens = hidden.reshape(total, width).astype(F32)
         cot = cotangent.reshape(total, width)
 
         seg_own = segments[:, 0]
         seg_pair = lax.ppermute(seg_own, "seq", pair)
         both = jnp.stack([seg_own, seg_pair])
         both_x = lax.ppermute(both, "seq", up_pairs)
-        seg_all = jnp.zeros((MICRO, rows * seq_size), jnp.int32)
-
-        def place(buffer, parts, axis):
-            for flip, part in enumerate(parts):
-                buffer = lax.dynamic_update_slice_in_dim(
-                    buffer, part, jnp.bitwise_xor(rank, flip) * rows, axis
-                )
-            return buffer
-
-        seg_all = place(seg_all, [both[0], both[1], both_x[0], both_x[1]], 1)
-
-        frequency = ROPE_BASE ** (-(jnp.arange(HEAD // 2, dtype=F32) * 2.0) / HEAD)
-        angles = positions.reshape(total).astype(F32)[:, None] * frequency[None, :]
-        angles = jnp.concatenate([angles, angles], axis=-1)[:, None, :]
-        cosine = jnp.cos(angles)
-        sine = jnp.sin(angles)
-
-        inv_attn = inv_rms(tokens)
+        seg_keys = jnp.stack([both[0], both[1], both_x[0], both_x[1]])
+        flips = jnp.arange(4, dtype=jnp.int32)
+        near_enough = (seg_keys[:, :, -1] == seg_own[None, :, 0]) | (flips[:, None] == 0)
+        need = (near_enough & (jnp.bitwise_xor(rank, flips)[:, None] <= rank)).astype(jnp.int32)
+
         normed_attn = (tokens * inv_attn * gain_attn).astype(BF16)
         raw = dot(normed_attn, w_qkv)
         query_raw = raw[:, :q_cols].reshape(total, -1, HEAD)
@@ -145,11 +249,9 @@
         query_inv = inv_rms(query_raw)
         key_inv = inv_rms(key_raw)
         queries = rotate(query_raw * query_inv * gain_query, cosine, sine).astype(BF16)
+        queries = queries.reshape(total, q_cols)
         keys = rotate(key_raw * key_inv * gain_key, cosine, sine).astype(BF16)
         keys = keys.reshape(total, k_cols)
-        key_ids = jnp.arange(rows * seq_size, dtype=jnp.int32)
-        row_ids = rank * rows + jnp.arange(rows, dtype=jnp.int32)
-
         kept = []
         middles = []
         heads_out = []
@@ -159,28 +261,20 @@
             near = lax.ppermute(own, "seq", pair)
             far = lax.ppermute(own, "seq", up_pairs)
             far_near = lax.ppermute(far, "seq", pair)
-            wide = place(
-                jnp.zeros((rows * seq_size, 2 * k_cols), BF16), [own, near, far, far_near], 0
+            parts = (own, near, far, far_near)
+            attn_heads, log_sum = attend(
+                need[:, step],
+                queries,
+                step,
+                parts,
+                seg_own[step][:, None],
+                seg_keys[:, step],
+                k_cols,
+                group,
+                rows,
             )
-            keys_all = wide[:, :k_cols].reshape(-1, kv_heads, HEAD)
-            values_all = wide[:, k_cols:].reshape(-1, kv_heads, HEAD)
-            q_block = queries[cut].reshape(rows, kv_heads, group, HEAD)
-            allowed = (seg_own[step][:, None] == seg_all[step][None, :]) & (
-                row_ids[:, None] >= key_ids[None, :]
-            )
-            scores = (
-                jnp.einsum("qkgd,tkd->kgqt", q_block, keys_all, preferred_element_type=F32)
-                * score_scale
-            )
-            scores = jnp.where(allowed[None, None], scores, -1e30)
-            row_max = jnp.max(scores, axis=-1, keepdims=True)
-            expo = jnp.exp(scores - row_max)
-            row_sum = jnp.sum(expo, axis=-1, keepdims=True)
-            probs = (expo / row_sum).astype(BF16)
-            mixed = jnp.einsum("kgqt,tkd->qkgd", probs, values_all, preferred_element_type=F32)
-            attn_heads = mixed.reshape(rows, -1).astype(BF16)
             heads_out.append(attn_heads)
-            kept.append((q_block, keys_all, values_all, allowed, row_max + jnp.log(row_sum)))
+            kept.append((parts, log_sum))
             attn_part = rdot(attn_heads, w_out_t)
             middles.append(tokens[cut] + mp_sum(attn_part))
         middle = jnp.concatenate(middles, axis=0)
@@ -193,76 +287,62 @@
         sigma = jax.nn.sigmoid(gate)
         silu = gate * sigma
         act = (silu * upward).astype(BF16)
-        grad_act = dot(cot, down_t)
+        down_grad = tdot(cot, act).astype(BF16)
+        down_owned = scatter(down_grad)
+        cot_late, act, down_grad = lax.optimization_barrier((cot, act, down_grad))
+        grad_act = dot(cot_late, down_t)
         grad_gate_in = (grad_act * upward * sigma * (1.0 + gate * (1.0 - sigma))).astype(BF16)
         grad_up_in = (grad_act * silu).astype(BF16)
-
-        def scatter(grad):
-            return lax.psum_scatter(
-                grad.astype(BF16), data_axes, scatter_dimension=0, tiled=True
-            )
-
-        down_owned = scatter(tdot(cot, act))
         backs = []
         for step in range(MICRO):
             cut = slice(step * rows, (step + 1) * rows)
             backs.append(
-                mp_sum(rdot(grad_gate_in[cut], gate_full) + rdot(grad_up_in[cut], up_full))
+                mp_part(rdot(grad_gate_in[cut], gate_full) + rdot(grad_up_in[cut], up_full))
             )
-        gate_owned = scatter(tdot(normed_ffn, grad_gate_in))
-        up_owned = scatter(tdot(normed_ffn, grad_up_in))
-        down_part = rdot(act, down_t)
-        layer_out = (middle + mp_sum(down_part)).astype(BF16)
+        gate_grad = tdot(normed_ffn, grad_gate_in).astype(BF16)
+        gate_owned = scatter(gate_grad)
+        up_grad = tdot(normed_ffn, grad_up_in).astype(BF16)
+        up_owned = scatter(up_grad)
+        backs, act, gate_grad, up_grad = lax.optimization_barrier((backs, act, gate_grad, up_grad))
+        backs = [mine.astype(F32) + other.astype(F32) for mine, other in backs]
+        layer_out = (middle + mp_sum(rdot(act, down_t))).astype(BF16)
         grad_normed_ffn = jnp.concatenate(backs, axis=0)
         gain_ffn_grad = jnp.sum(grad_normed_ffn * middle * inv_ffn, axis=0)
         grad_middle = cot.astype(F32) + norm_back(grad_normed_ffn, middle, inv_ffn, gain_ffn)
         grad_middle_b = grad_middle.astype(BF16)
         grad_heads = dot(grad_middle_b, w_out_t).astype(BF16)
-        out_owned = scatter(tdot(grad_middle_b, attn_heads))
+        out_owned = scatter(tdot(grad_middle_b, attn_heads).astype(BF16))
 
         grad_queries = []
         grad_keys = []
         grad_values = []
         for step in range(MICRO):
             cut = slice(step * rows, (step + 1) * rows)
-            q_block, keys_all, values_all, allowed, log_sum = kept[step]
-            g_block = grad_heads[cut].reshape(rows, kv_heads, group, HEAD)
-            scores = (
-                jnp.einsum("qkgd,tkd->kgqt", q_block, keys_all, preferred_element_type=F32)
-                * score_scale
+            parts, log_sum = kept[step]
+            dots = grad_heads[cut].astype(F32) * heads_out[step].astype(F32)
+            dots = jnp.sum(dots.reshape(rows, kv_heads, group, HEAD), axis=-1)
+            dots = dots.transpose(1, 2, 0).reshape(kv_heads, 1, group * rows)
+            stats = jnp.concatenate([log_sum.reshape(kv_heads, 1, group * rows), dots], axis=1)
+            grad_q, d_own, d_near, d_far, d_far_near = attend_back(
+                need[:, step],
+                queries,
+                grad_heads,
+                step,
+                parts,
+                seg_own[step][None],
+                seg_keys[:, step].T,
+                stats,
+                k_cols,
+                group,
+                rows,
             )
-            probs = jnp.where(allowed[None, None], jnp.exp(scores - log_sum), 0.0)
-            grad_probs = jnp.einsum(
-                "qkgd,tkd->kgqt", g_block, values_all, preferred_element_type=F32
-            )
-            row_dot = jnp.sum(grad_probs * probs, axis=-1, keepdims=True)
-            grad_scores = (probs * (grad_probs - row_dot)).astype(BF16)
-            grad_queries.append(
-                jnp.einsum("kgqt,tkd->qkgd", grad_scores, keys_all, preferred_element_type=F32)
-                * score_scale
-            )
-            grad_k = (
-                jnp.einsum("kgqt,qkgd->tkd", grad_scores, q_block, preferred_element_type=F32)
-                * score_scale
-            )
-            grad_v = jnp.einsum(
-                "kgqt,qkgd->tkd", probs.astype(BF16), g_block, preferred_element_type=F32
-            )
-            wide = jnp.concatenate(
-                [grad_k.reshape(-1, k_cols), grad_v.reshape(-1, k_cols)], axis=1
-            )
-
-            def part(flip):
-                return lax.dynamic_slice_in_dim(
-                    wide, jnp.bitwise_xor(rank, flip) * rows, rows, 0
-                )
-
-            sent = jnp.stack([part(1), part(3)]).astype(BF16)
-            got = lax.ppermute(sent, "seq", pair).astype(F32)
-            far = lax.ppermute((part(2) + got[1]).astype(BF16), "seq", down_pairs).astype(F32)
-            owned = part(0) + got[0] + far
-            grad_keys.append(owned[:, :k_cols])
-            grad_values.append(owned[:, k_cols:])
+            grad_queries.append(grad_q)
+            got = lax.ppermute(jnp.stack([d_near, d_far_near]), "seq", pair).astype(F32)
+            far = lax.ppermute((d_far + got[1]).astype(BF16), "seq", down_pairs).astype(F32)
+            owned = d_own + got[0] + far
+            grad_keys.append(owned[0])
+            grad_values.append(owned[1])
+        grad_queries, down_owned = lax.optimization_barrier((grad_queries, down_owned))
         grad_query_rot = jnp.concatenate(grad_queries, axis=0).reshape(total, -1, HEAD)
         grad_key_rot = jnp.concatenate(grad_keys, axis=0).reshape(total, -1, HEAD)
         grad_value_in = jnp.concatenate(grad_values, axis=0).astype(BF16)
@@ -280,7 +360,8 @@
             ],
             axis=1,
         )
-        qkv_owned = scatter(tdot(normed_attn, grad_qkv_in))
+        grad_qkv_in, gate_owned = lax.optimization_barrier((grad_qkv_in, gate_owned))
+        qkv_owned = scatter(tdot(normed_attn, grad_qkv_in).astype(BF16))
         backs = []
         for step in range(MICRO):
             cut = slice(step * rows, (step + 1) * rows)

time: 1420 us -> 1270 us (0.89)
  matrix products: 440 us -> 269 us
  waiting for transfers between devices: 436 us -> 528 us
  other arithmetic: 269 us -> 197 us
  local copies, waits for them, and re-layouts: 160 us -> 104 us
  Pallas kernels: 0 us -> 39.7 us
    dot_general x12 -> x0, matrix products: 182 us -> none  [the longest x2 50.5 us: local(): jnp.einsum('qkgd,tkd->kgqt', g_block, values_all, preferred_element_type=...]
    ppermute x11, waiting for transfers between devices: 276 us -> 335 us  [the longest x7 274 us: mp_part(): return (part, lax.ppermute(part, 'mp', [(0, 1), (1, 0)]))]
    convert_element_type x6 -> x5, other arithmetic: 65.2 us -> 5.81 us  [the longest x2 2.99 us: local(): (d_far + got[1]).astype(BF16)]
    pallas_call x0 -> x4, Pallas kernels: none -> 39.7 us  [the longest x2 22.7 us: attend_back(): pl.pallas_call(functools.partial(backward_kernel, tile, group), grid_spec...]
    reshape x7 -> x6, local copies, waits for them, and re-layouts: 35.5 us -> 6.6 us  [the longest x2 6.48 us: local(): dots = jnp.sum(dots.reshape(rows, kv_heads, group, HEAD), axis=-1)]
    reduce_sum x2, other arithmetic: 30 us -> 6.34 us  [local(): dots = jnp.sum(dots.reshape(rows, kv_heads, group, HEAD), axis=-1)]
    ppermute x1, waiting for transfers between devices: 1.26 us -> 20.8 us  [local(): both_x = lax.ppermute(both, 'seq', up_pairs)]
    mul x1 -> x3, other arithmetic: 0.2 us -> 15.7 us  [the longest x1 9.09 us: norm_back(): scaled = grads * gain]
  transfers between devices with their start and end apart: 26 -> 26, of which waited for: 10 -> 13; matrix products, arithmetic and copies ran while one was open for 51% -> 37% of each run, Pallas kernels for 0% -> 3%
where the time goes in v2:
time: 1270 us; the launch traced here: 1260 us
  waiting for transfers between devices  528 us (42%)
  matrix products  269 us (21%)
  other arithmetic  197 us (16%)
  local copies, waits for them, and re-layouts  104 us (8%)
  blocking collectives  67.6 us (5%)
  Pallas kernels  39.7 us (3%)
  starting transfers between devices  35.8 us (3%)
  between operations  16.2 us (1%)
    ppermute x7, waiting for transfers between devices, mp_part(): return (part, lax.ppermute(part, 'mp', [(0, 1), (1, 0)]))  274 us
    all_gather x1, waiting for transfers between devices, local(): first = lax.all_gather(first, data_axes, axis=0, tiled=True)  105 us
    dot_general x9, matrix products, rdot(): lax.dot_general(left, right, (((1,), (1,)), ((), ())), preferred_element_...  96.2 us
    dot_general x5, matrix products, dot(): return jnp.dot(left, right, preferred_element_type=F32)  95.8 us
    dot_general x5, matrix products, tdot(): lax.dot_general(left, right, (((0,), (0,)), ((), ())), preferred_element_...  77.2 us
    all_gather x1, blocking collectives, local(): small = lax.all_gather(small, ('dp', 'seq', 'mp'), axis=0, tiled=False)  67.6 us
    ppermute x2, waiting for transfers between devices, local(): far = lax.ppermute(own, 'seq', up_pairs)  66.9 us
    ppermute x2, waiting for transfers between devices, local(): lax.ppermute((d_far + got[1]).astype(BF16), 'seq', down_pairs).astype(F32)  61.1 us
  transfers between devices with their start and end apart: 26, of which 13 were waited for; matrix products, arithmetic and copies ran while one was open for 37% of the time, Pallas kernels for 3%

profile of v2, /device:TPU:0, one launch (start us, length us, event | category | flops | bytes accessed | tf_op | source)
XLA Modules:
  0.0 1258.5 jit_solution(5513165221485787374)
XLA Ops:
  18.6 104.9 %all-gather.5.cloned.1.call-done = bf16[2048,3200]{0,1:T(8,128)(2,1)} async-done(((bf16[128,3200]{0,1:T(8,128)(2,1)}), bf16[2048,3200]{0,1:T(8,128)(2,1)}) %all-gather.5.cloned.1.call-update) | async-done | bytes 13107216 | tf_op jit(solution)/shard_map/all_gather | solution.py:212
  136.7 20.8 %collective-permute-done.1 = s32[2,2,512]{0,2,1:T(8,128)S(1)} collective-permute-done((s32[2,2,512]{0,2,1:T(8,128)S(1)}, s32[2,2,512]{0,2,1:T(8,128)S(1)}, u32[]{:S(2)}, u32[]{:S(2)}) %collective-permute-start.1) | collective-permute-done | bytes 8224 | tf_op jit(solution)/shard_map/ppermute | solution.py:238
  166.0 14.2 %fusion.87 = (bf16[1024,2048]{1,0:T(8,128)(2,1)}, f32[1024,2048]{1,0:T(8,128)S(1)}) fusion(bf16[1024,2048]{1,0:T(8,128)(2,1)S(1)} %fusion.10, bf16[2048,3200]{0,1:T(8,128)(2,1)} %all-gather.5.cloned.1.call-done), kind=kOutput, calls=%fused_computation.219 | convolution fusion | flops 8592031744 | bytes 25165824 | tf_op jit(solution)/shard_map/dot_general | solution.py:24
  201.3 5.4 collective-permute-start.3
  226.0 25.6 %collective-permute-done.3.k2.v2 = bf16[512,1024]{1,0:T(8,128)(2,1)} collective-permute-done((bf16[512,1024]{1,0:T(8,128)(2,1)S(1)}, bf16[512,1024]{1,0:T(8,128)(2,1)}, u32[]{:S(2)}, u32[]{:S(2)}) %collective-permute-start.3) | collective-permute-done | bytes 1048608 | tf_op jit(solution)/shard_map/ppermute | solution.py:262
  255.3 41.2 %collective-permute-done.7.k2.v2 = bf16[512,1024]{1,0:T(8,128)(2,1)} collective-permute-done((bf16[512,1024]{1,0:T(8,128)(2,1)S(1)}, bf16[512,1024]{1,0:T(8,128)(2,1)}, u32[]{:S(2)}, u32[]{:S(2)}) %collective-permute-start.7) | collective-permute-done | bytes 1048608 | tf_op jit(solution)/shard_map/ppermute | solution.py:262
  302.7 8.6 attend.2
  311.3 4.9 fusion.37
  318.1 8.3 attend.3
  326.4 5.0 fusion.40
  336.3 26.4 %collective-permute-done.5 = bf16[512,2048]{1,0:T(8,128)(2,1)} collective-permute-done((bf16[512,2048]{1,0:T(8,128)(2,1)S(1)}, bf16[512,2048]{1,0:T(8,128)(2,1)}, u32[]{:S(2)}, u32[]{:S(2)}) %collective-permute-start.5) | collective-permute-done | bytes 2097184 | tf_op jit(solution)/shard_map/ppermute | solution.py:170
  362.6 44.9 %collective-permute-done.9 = bf16[512,2048]{1,0:T(8,128)(2,1)} collective-permute-done((bf16[512,2048]{1,0:T(8,128)(2,1)S(1)}, bf16[512,2048]{1,0:T(8,128)(2,1)}, u32[]{:S(2)}, u32[]{:S(2)}) %collective-permute-start.9) | collective-permute-done | bytes 2097184 | tf_op jit(solution)/shard_map/ppermute | solution.py:170
  407.6 9.6 fusion.25
  424.6 19.4 %fusion.5 = f32[1024,3072]{1,0:T(8,128)} fusion(bf16[1024,2048]{1,0:T(8,128)(2,1)} %multiply_convert_fusion.3, bf16[3,2048,3072]{1,2,0:T(8,128)(2,1)} %all-gather.7.cloned.1.call-done), kind=kOutput, calls=%fused_computation.15 | convolution fusion | flops 12884901888 | bytes 29360128 | tf_op jit(solution)/shard_map/dot_general | solution.py:24
  443.9 23.7 %multiply_convert_fusion.2 = (bf16[1024,3072]{1,0:T(8,128)(2,1)}, f32[1024,3072]{1,0:T(8,128)}) fusion(f32[1024,3072]{1,0:T(8,128)} %fusion.5, bf16[1024,2048]{1,0:T(8,128)(2,1)} %multiply_convert_fusion.3, bf16[3,2048,3072]{1,2,0:T(8,128)(2,1)} %all-gather.7.cloned.1.call-done), kind=kOutput, calls=%fused_computation.6 | convolution fusion | flops 12903776256 | bytes 48234496 | tf_op jit(solution)/shard_map/dot_general | solution.py:24
  467.7 19.5 %convert_bitcast_fusion = bf16[2048,3072]{0,1:T(8,128)(2,1)} fusion(bf16[1024,3072]{1,0:T(8,128)(2,1)} %get-tuple-element.55, bf16[1024,2048]{1,0:T(8,128)(2,1)} %bitcast.300), kind=kOutput, calls=%fused_computation.5 | convolution fusion | flops 12891193344 | bytes 23068672 | tf_op jit(solution)/shard_map/dot_general | solution.py:28
  487.2 16.7 %copy.186 = bf16[2048,3072]{1,0:T(8,128)(2,1)} copy(bf16[2048,3072]{0,1:T(8,128)(2,1)} %convert_bitcast_fusion) | data formatting | bytes 25165824
  503.9 30.5 %multiply_convert_fusion = (bf16[1024,3072]{1,0:T(8,128)(2,1)}, bf16[1024,3072]{1,0:T(8,128)(2,1)}) fusion(f32[1024,3072]{1,0:T(8,128)} %fusion.5, f32[1024,3072]{1,0:T(8,128)} %get-tuple-element.239, bf16[1024,2048]{1,0:T(8,128)(2,1)} %bitcast.301, bf16[3,2048,3072]{1,2,0:T(8,128)(2,1)} %all-gather.7.cloned.1.call-done), kind=kOutput, calls=%fused_computation.3 | convolution fusion | flops 12925796352 | bytes 54525952 | tf_op jit(solution)/shard_map/dot_general | solution.py:24
  534.5 18.9 %convolution_convert_fusion.1 = bf16[2048,3072]{1,0:T(8,128)(2,1)} fusion(bf16[1024,2048]{1,0:T(8,128)(2,1)S(1)} %copy-done.33, bf16[1024,3072]{1,0:T(8,128)(2,1)} %get-tuple-element.181), kind=kOutput, calls=%fused_computation.10 | convolution fusion | flops 12891193344 | bytes 23068672 | tf_op jit(solution)/shard_map/dot_general | solution.py:28
  553.5 13.8 %fusion.4 = f32[512,2048]{1,0:T(8,128)} fusion(bf16[3,2048,3072]{1,2,0:T(8,128)(2,1)} %all-gather.7.cloned.1.call-done, bf16[1024,3072]{1,0:T(8,128)(2,1)} %get-tuple-element.181), kind=kOutput, calls=%fused_computation.14 | convolution fusion | flops 6442450944 | bytes 19922944 | tf_op jit(solution)/shard_map/dot_general | solution.py:32
  567.3 12.9 %add_convert_fusion.4 = bf16[512,2048]{1,0:T(8,128)(2,1)S(1)} fusion(f32[512,2048]{1,0:T(8,128)} %fusion.4, bf16[3,2048,3072]{1,2,0:T(8,128)(2,1)} %all-gather.7.cloned.1.call-done, bf16[1024,3072]{1,0:T(8,128)(2,1)} %get-tuple-element.180), kind=kOutput, calls=%fused_computation.75 | convolution fusion | flops 6444548096 | bytes 22020096 | tf_op jit(solution)/shard_map/dot_general | solution.py:32
  582.0 11.2 fusion.3
  593.2 13.5 %add_convert_fusion.3 = bf16[512,2048]{1,0:T(8,128)(2,1)} fusion(f32[512,2048]{1,0:T(8,128)} %fusion.3, bf16[3,2048,3072]{1,2,0:T(8,128)(2,1)} %all-gather.7.cloned.1.call-done, bf16[1024,3072]{1,0:T(8,128)(2,1)S(1)} %bitcast.351), kind=kOutput, calls=%fused_computation.74 | convolution fusion | flops 6444548096 | bytes 22020096 | tf_op jit(solution)/shard_map/dot_general | solution.py:32
  606.9 16.3 %convolution_convert_fusion = bf16[2048,3072]{1,0:T(8,128)(2,1)} fusion(bf16[1024,2048]{1,0:T(8,128)(2,1)S(1)} %copy-done.34, bf16[1024,3072]{1,0:T(8,128)(2,1)S(1)} %bitcast.351), kind=kOutput, calls=%fused_computation.9 | convolution fusion | flops 12891193344 | bytes 23068672 | tf_op jit(solution)/shard_map/dot_general | solution.py:28
  627.9 44.9 %collective-permute-done.11 = bf16[512,2048]{1,0:T(8,128)(2,1)} collective-permute-done((bf16[512,2048]{1,0:T(8,128)(2,1)}, bf16[512,2048]{1,0:T(8,128)(2,1)}, u32[]{:S(2)}, u32[]{:S(2)}) %collective-permute-start.11) | collective-permute-done | bytes 2097184 | tf_op jit(solution)/shard_map/ppermute | solution.py:170
  672.8 19.6 %fusion.26 = bf16[1024,2048]{1,0:T(8,128)(2,1)} fusion(bf16[1024,3072]{1,0:T(8,128)(2,1)} %get-tuple-element.55, bf16[3,2048,3072]{1,2,0:T(8,128)(2,1)} %all-gather.7.cloned.1.call-done), kind=kOutput, calls=%fused_computation.78 | convolution fusion | flops 12886999040 | bytes 23068672 | tf_op jit(solution)/shard_map/dot_general | solution.py:32
  704.2 81.7 %collective-permute-done.12 = bf16[1024,2048]{1,0:T(8,128)(2,1)} collective-permute-done((bf16[1024,2048]{1,0:T(8,128)(2,1)}, bf16[1024,2048]{1,0:T(8,128)(2,1)}, u32[]{:S(2)}, u32[]{:S(2)}) %collective-permute-start.12) | collective-permute-done | bytes 4194336 | tf_op jit(solution)/shard_map/ppermute | solution.py:170
  785.9 14.3 %add_convert_fusion.1 = (bf16[1024,2048]{1,0:T(8,128)(2,1)}, bf16[1024,2048]{1,0:T(8,128)(2,1)}, f32[1024,2048]{1,0:T(8,128)}, f32[1024,2048]{1,0:T(8,128)}) fusion(f32[1024]{0:T(1024)S(1)} %broadcast_multiply_fusion.3, f32[1024]{0:T(1024)S(1)} %copy-done.71, f32[2048]{0:T(1024)S(1)} %bitcast.331, f32[1024]{0:T(1024)S(1)} %copy-done.64, ...), kind=kLoop, calls=%fused_computation.29 | loop fusion | flops 31457280 | bytes 54546432 | tf_op jit(solution)/shard_map/convert_element_type | solution.py:312
  800.2 8.4 convolution_convert_fusion.3
  810.9 8.1 fusion.71.g_out
  829.5 11.4 attend_back.2
  844.1 5.6 collective-permute-start.13
  857.9 11.3 attend_back.3
  871.0 5.8 collective-permute-start.15
  890.0 34.0 %collective-permute-done.14 = bf16[2,512,512]{2,1,0:T(8,128)(2,1)} collective-permute-done((bf16[2,512,512]{2,1,0:T(8,128)(2,1)}, bf16[2,512,512]{2,1,0:T(8,128)(2,1)}, u32[]{:S(2)}, u32[]{:S(2)}) %collective-permute-start.14) | collective-permute-done | bytes 1048608 | tf_op jit(solution)/shard_map/ppermute | solution.py:341
  929.4 27.1 %collective-permute-done.16 = bf16[2,512,512]{2,1,0:T(8,128)(2,1)S(1)} collective-permute-done((bf16[2,512,512]{2,1,0:T(8,128)(2,1)}, bf16[2,512,512]{2,1,0:T(8,128)(2,1)S(1)}, u32[]{:S(2)}, u32[]{:S(2)}) %collective-permute-start.16) | collective-permute-done | bytes 1048608 | tf_op jit(solution)/shard_map/ppermute | solution.py:341
  993.5 4.8 fusion.81
  998.3 9.1 fusion.20
  1014.7 8.8 fusion.23
  1023.6 9.8 maximum_maximum_fusion
  1033.4 14.1 %convolution_convert_fusion.2 = bf16[2048,2048]{1,0:T(8,128)(2,1)} fusion(bf16[1024,2048]{1,0:T(8,128)(2,1)} %copy-done.36, bf16[1024,2048]{1,0:T(8,128)(2,1)} %maximum_maximum_fusion), kind=kOutput, calls=%fused_computation.35 | convolution fusion | flops 8594128896 | bytes 16777216 | tf_op jit(solution)/shard_map/dot_general | solution.py:28
  1047.5 10.3 fusion.46
  1059.4 5.0 fusion.43
  1075.2 31.4 %collective-permute-done.18 = bf16[512,2048]{1,0:T(8,128)(2,1)} collective-permute-done((bf16[512,2048]{1,0:T(8,128)(2,1)}, bf16[512,2048]{1,0:T(8,128)(2,1)}, u32[]{:S(2)}, u32[]{:S(2)}) %collective-permute-start.18) | collective-permute-done | bytes 2097184 | tf_op jit(solution)/shard_map/ppermute | solution.py:170
  1109.8 40.0 %collective-permute-done.17 = bf16[512,2048]{1,0:T(8,128)(2,1)} collective-permute-done((bf16[512,2048]{1,0:T(8,128)(2,1)S(1)}, bf16[512,2048]{1,0:T(8,128)(2,1)}, u32[]{:S(2)}, u32[]{:S(2)}) %collective-permute-start.17) | collective-permute-done | bytes 2097184 | tf_op jit(solution)/shard_map/ppermute | solution.py:170
  1157.7 5.1 multiply_reduce_fusion.1
  1162.9 67.6 %all-gather.1 = f32[32,1,4352]{2,1,0:T(1,128)S(1)} all-gather(f32[1,1,4352]{2,1,0:T(1,128)S(1)} %reshape.512), channel_id=2, replica_groups=mesh['dp'=4,'seq'=4,'mp'=2] {'dp','seq','mp'}, dimensions={0}, use_global_device_ids=true | all-gather | bytes 574464 | tf_op jit(solution)/shard_map/all_gather | solution.py:376
  1233.4 14.2 %add_convert_fusion = bf16[2,1,512,2048]{3,2,1,0:T(8,128)(2,1)} fusion(f32[2,1,512,2048]{3,2,1,0:T(8,128)} %bitcast.291, f32[2,1,512,2048]{3,2,1,0:T(8,128)} %bitcast.292, bf16[2,1,512,2048]{3,2,1,0:T(8,128)(2,1)} %param.29, bf16[2,1,512,2048]{3,2,1,0:T(8,128)(2,1)} %param.15, f32[2,512]{1,0:T(2,128)S(1)} %broadcast_multiply_fusion.4, ...), kind=kLoop, calls=%fused_computation.27 | loop fusion | flops 33554432 | bytes 37789696 | tf_op jit(solution)/shard_map/convert_element_type | solution.py:373
  (393 shorter events, 233.6 us)
Async XLA Ops:
  7.2 116.3 %all-gather.5.cloned.1.call-start = ((), (), s32[]{:S(2)}) async-start(), calls=%async_computation.5 | async-start | bytes 13926400 | tf_op jit(solution)/shard_map/all_gather | solution.py:212
  13.8 410.8 %all-gather.7.cloned.1.call-start = ((), (), s32[]{:S(2)}) async-start(), calls=%async_computation.6 | async-start | bytes 40108032 | tf_op jit(solution)/shard_map/all_gather | solution.py:215
  15.4 108.2 %copy-start.72 = (s32[2,1,512]{2,1,0:T(1,128)S(1)}, s32[2,1,512]{2,1,0:T(1,128)}, u32[]{:S(2)}) copy-start(s32[2,1,512]{2,1,0:T(1,128)} %param.27) | copy-start | bytes 12292
  15.4 108.5 %copy-start.78 = (bf16[128]{0:T(256)(128)(2,1)S(1)}, bf16[128]{0:T(256)(128)(2,1)}, u32[]{:S(2)}) copy-start(bf16[128]{0:T(256)(128)(2,1)} %param.25) | copy-start | bytes 772
  15.4 108.5 %copy-start.77 = (s32[2,1,512]{2,1,0:T(1,128)S(1)}, s32[2,1,512]{2,1,0:T(1,128)}, u32[]{:S(2)}) copy-start(s32[2,1,512]{2,1,0:T(1,128)} %param.28) | copy-start | bytes 12292
  123.5 860.6 %reduce-scatter.16.cloned.1.call-start = ((), (), s32[]{:S(2)}) async-start(), calls=%async_computation.11 | async-start | bytes 13369344
  123.6 7.0 collective-permute-start
  123.9 94.0 %copy-start.75 = (f32[128]{0:T(128)}, f32[128]{0:T(128)S(1)}, u32[]{:S(2)}) copy-start(f32[128]{0:T(128)S(1)} %convert_element_type.240) | copy-start | bytes 1540
  126.4 125.3 %copy-start.26 = (f32[1024,1,128]{2,0,1:T(8,128)}, f32[1024,1,128]{2,0,1:T(8,128)S(1)}, u32[]{:S(2)}) copy-start(f32[1024,1,128]{2,0,1:T(8,128)S(1)} %get-tuple-element.49) | copy-start | bytes 1572868
  126.4 170.1 %copy-start.20 = (f32[1024,1,128]{2,0,1:T(8,128)}, f32[1024,1,128]{2,0,1:T(8,128)S(1)}, u32[]{:S(2)}) copy-start(f32[1024,1,128]{2,0,1:T(8,128)S(1)} %get-tuple-element.48) | copy-start | bytes 1572868
  126.4 171.6 %copy-start.66 = (f32[1024]{0:T(1024)}, f32[1024]{0:T(1024)S(1)}, u32[]{:S(2)}) copy-start(f32[1024]{0:T(1024)S(1)} %broadcast_bitcast_fusion) | copy-start | bytes 12292
  130.8 26.7 %collective-permute-start.1 = (s32[2,2,512]{0,2,1:T(8,128)S(1)}, s32[2,2,512]{0,2,1:T(8,128)S(1)}, u32[]{:S(2)}, u32[]{:S(2)}) collective-permute-start(s32[2,2,512]{0,2,1:T(8,128)S(1)} %copy.154), channel_id=1, source_target_pairs={{0,4},{2,6},{1,5},{3,7},{8,12},{10,14},{9,13},{11,15},{16,20},{18,... | collective-permute-start | bytes 24584 | tf_op jit(solution)/shard_map/ppermute | solution.py:238
  134.7 31.3 %copy-start.68 = (f32[1,1,2,512]{3,1,2,0:T(1,128)}, f32[1,1,2,512]{3,1,2,0:T(1,128)S(1)}, u32[]{:S(2)}) copy-start(f32[1,1,2,512]{3,1,2,0:T(1,128)S(1)} %copy.191) | copy-start | bytes 12292
  134.7 61.8 %copy-start.73 = (f32[128]{0:T(128)}, f32[128]{0:T(128)S(1)}, u32[]{:S(2)}) copy-start(f32[128]{0:T(128)S(1)} %convert_element_type.242) | copy-start | bytes 1540
  162.7 259.2 %copy-start.57 = (f32[2048,1]{0,1:T(1,128)}, f32[2048,1]{0,1:T(1,128)S(1)}, u32[]{:S(2)}) copy-start(f32[2048,1]{0,1:T(1,128)S(1)} %get-tuple-element.185) | copy-start | bytes 24580
  201.2 101.5 %collective-permute-start.2 = (bf16[512,1024]{1,0:T(8,128)(2,1)S(1)}, bf16[512,1024]{1,0:T(8,128)(2,1)}, u32[]{:S(2)}, u32[]{:S(2)}) collective-permute-start(bf16[512,1024]{1,0:T(8,128)(2,1)S(1)} %pad_maximum_fusion.8.k0.v0), channel_id=1, source_target_pairs={{0,2},{2,0},{4,6},{6,4},{1,3},{3,1},{5,7},{7,5},{8,10},{10,8},{12,... | collective-permute-start | bytes 3145736 | tf_op jit(solution)/shard_map/ppermute | solution.py:261
  201.3 50.4 %collective-permute-start.3 = (bf16[512,1024]{1,0:T(8,128)(2,1)S(1)}, bf16[512,1024]{1,0:T(8,128)(2,1)}, u32[]{:S(2)}, u32[]{:S(2)}) collective-permute-start(bf16[512,1024]{1,0:T(8,128)(2,1)S(1)} %pad_maximum_fusion.8.k0.v0), channel_id=1, source_target_pairs={{0,4},{2,6},{1,5},{3,7},{8,12},{10,14},{9,13},{11,15},{16,20},{18,... | collective-permute-start | bytes 3145736 | tf_op jit(solution)/shard_map/ppermute | solution.py:262
  206.9 111.2 %collective-permute-start.6 = (bf16[512,1024]{1,0:T(8,128)(2,1)S(1)}, bf16[512,1024]{1,0:T(8,128)(2,1)}, u32[]{:S(2)}, u32[]{:S(2)}) collective-permute-start(bf16[512,1024]{1,0:T(8,128)(2,1)S(1)} %pad_maximum_fusion.9.k0.v0), channel_id=1, source_target_pairs={{0,2},{2,0},{4,6},{6,4},{1,3},{3,1},{5,7},{7,5},{8,10},{10,8},{12,... | collective-permute-start | bytes 3145736 | tf_op jit(solution)/shard_map/ppermute | solution.py:261
  207.2 89.3 %collective-permute-start.7 = (bf16[512,1024]{1,0:T(8,128)(2,1)S(1)}, bf16[512,1024]{1,0:T(8,128)(2,1)}, u32[]{:S(2)}, u32[]{:S(2)}) collective-permute-start(bf16[512,1024]{1,0:T(8,128)(2,1)S(1)} %pad_maximum_fusion.9.k0.v0), channel_id=1, source_target_pairs={{0,4},{2,6},{1,5},{3,7},{8,12},{10,14},{9,13},{11,15},{16,20},{18,... | collective-permute-start | bytes 3145736 | tf_op jit(solution)/shard_map/ppermute | solution.py:262
  222.7 75.3 %slice-start.2 = ((s8[8388608]{0:T(1024)(128)(4,1)}), s8[4194304]{0:T(1024)(128)(4,1)S(1)}, s32[]{:S(2)}) async-start(s8[8388608]{0:T(1024)(128)(4,1)} %bitcast.289), calls=%async_computation.14 | async-start | bytes 8388608
  251.7 51.0 %collective-permute-start.4 = (bf16[512,1024]{1,0:T(8,128)(2,1)}, bf16[512,1024]{1,0:T(8,128)(2,1)}, u32[]{:S(2)}, u32[]{:S(2)}) collective-permute-start(bf16[512,1024]{1,0:T(8,128)(2,1)} %collective-permute-done.3.k2.v2), channel_id=1, source_target_pairs={{0,2},{2,0},{4,6},{6,4},{1,3},{3,1},{5,7},{7,5},{8,10},{10,8},{12,... | collective-permute-start | bytes 3145736 | tf_op jit(solution)/shard_map/ppermute | solution.py:263
  251.7 46.3 %slice-start.3 = ((s8[8388608]{0:T(1024)(128)(4,1)}), s8[4194304]{0:T(1024)(128)(4,1)S(1)}, s32[]{:S(2)}) async-start(s8[8388608]{0:T(1024)(128)(4,1)} %bitcast.289), calls=%async_computation.15 | async-start | bytes 8388608
  255.2 41.5 %copy-start.32 = (f32[1024,8]{1,0:T(8,128)S(1)}, f32[1024,8]{1,0:T(8,128)}, u32[]{:S(2)}) copy-start(f32[1024,8]{1,0:T(8,128)} %copy.163) | copy-start | bytes 98308
  296.5 21.6 %collective-permute-start.8 = (bf16[512,1024]{1,0:T(8,128)(2,1)}, bf16[512,1024]{1,0:T(8,128)(2,1)}, u32[]{:S(2)}, u32[]{:S(2)}) collective-permute-start(bf16[512,1024]{1,0:T(8,128)(2,1)} %collective-permute-done.7.k2.v2), channel_id=1, source_target_pairs={{0,2},{2,0},{4,6},{6,4},{1,3},{3,1},{5,7},{7,5},{8,10},{10,8},{12,... | collective-permute-start | bytes 3145736 | tf_op jit(solution)/shard_map/ppermute | solution.py:263
  316.3 46.3 %collective-permute-start.5 = (bf16[512,2048]{1,0:T(8,128)(2,1)S(1)}, bf16[512,2048]{1,0:T(8,128)(2,1)}, u32[]{:S(2)}, u32[]{:S(2)}) collective-permute-start(bf16[512,2048]{1,0:T(8,128)(2,1)S(1)} %fusion.37), channel_id=1, source_target_pairs={{0,1},{1,0},{2,3},{3,2},{4,5},{5,4},{6,7},{7,6},{8,9},{9,8},{10,11... | collective-permute-start | bytes 6291464 | tf_op jit(solution)/shard_map/ppermute | solution.py:170
  331.4 76.2 %collective-permute-start.9 = (bf16[512,2048]{1,0:T(8,128)(2,1)S(1)}, bf16[512,2048]{1,0:T(8,128)(2,1)}, u32[]{:S(2)}, u32[]{:S(2)}) collective-permute-start(bf16[512,2048]{1,0:T(8,128)(2,1)S(1)} %fusion.40), channel_id=1, source_target_pairs={{0,1},{1,0},{2,3},{3,2},{4,5},{5,4},{6,7},{7,6},{8,9},{9,8},{10,11... | collective-permute-start | bytes 6291464 | tf_op jit(solution)/shard_map/ppermute | solution.py:170
  503.9 529.5 %reduce-scatter.8.cloned.1.call-start = ((), (), s32[]{:S(2)}) async-start(), calls=%async_computation.7 | async-start | bytes 13369344 | tf_op jit(solution)/shard_map/reduce_scatter | solution.py:165
  503.9 30.5 %copy-start.33 = (bf16[1024,2048]{1,0:T(8,128)(2,1)S(1)}, bf16[1024,2048]{1,0:T(8,128)(2,1)}, u32[]{:S(2)}) copy-start(bf16[1024,2048]{1,0:T(8,128)(2,1)} %multiply_convert_fusion.3) | copy-start | bytes 12582916
  553.4 513.7 %reduce-scatter.12.cloned.1.call-start = ((), (), s32[]{:S(2)}) async-start(), calls=%async_computation.9 | async-start | bytes 4456448 | tf_op jit(solution)/shard_map/reduce_scatter | solution.py:165
  553.4 28.6 %slice-start.8 = ((s8[6291456]{0:T(1024)(128)(4,1)}), s8[4194304]{0:T(1024)(128)(4,1)S(1)}, s32[]{:S(2)}) async-start(s8[6291456]{0:T(1024)(128)(4,1)} %bitcast.348), calls=%async_computation.20 | async-start | bytes 8388608
  553.4 39.7 %slice-start.10 = ((s8[6291456]{0:T(1024)(128)(4,1)}), s8[4194304]{0:T(1024)(128)(4,1)S(1)}, s32[]{:S(2)}) async-start(s8[6291456]{0:T(1024)(128)(4,1)} %bitcast.350), calls=%async_computation.22 | async-start | bytes 8388608
  580.2 47.7 %collective-permute-start.10 = (bf16[512,2048]{1,0:T(8,128)(2,1)S(1)}, bf16[512,2048]{1,0:T(8,128)(2,1)}, u32[]{:S(2)}, u32[]{:S(2)}) collective-permute-start(bf16[512,2048]{1,0:T(8,128)(2,1)S(1)} %add_convert_fusion.4), channel_id=1, source_target_pairs={{0,1},{1,0},{2,3},{3,2},{4,5},{5,4},{6,7},{7,6},{8,9},{9,8},{10,11... | collective-permute-start | bytes 6291464 | tf_op jit(solution)/shard_map/ppermute | solution.py:170
  606.7 66.1 %collective-permute-start.11 = (bf16[512,2048]{1,0:T(8,128)(2,1)}, bf16[512,2048]{1,0:T(8,128)(2,1)}, u32[]{:S(2)}, u32[]{:S(2)}) collective-permute-start(bf16[512,2048]{1,0:T(8,128)(2,1)} %add_convert_fusion.3), channel_id=1, source_target_pairs={{0,1},{1,0},{2,3},{3,2},{4,5},{5,4},{6,7},{7,6},{8,9},{9,8},{10,11... | collective-permute-start | bytes 6291464 | tf_op jit(solution)/shard_map/ppermute | solution.py:170
  692.4 93.5 %collective-permute-start.12 = (bf16[1024,2048]{1,0:T(8,128)(2,1)}, bf16[1024,2048]{1,0:T(8,128)(2,1)}, u32[]{:S(2)}, u32[]{:S(2)}) collective-permute-start(bf16[1024,2048]{1,0:T(8,128)(2,1)} %fusion.26), channel_id=1, source_target_pairs={{0,1},{1,0},{2,3},{3,2},{4,5},{5,4},{6,7},{7,6},{8,9},{9,8},{10,11... | collective-permute-start | bytes 12582920 | tf_op jit(solution)/shard_map/ppermute | solution.py:170
  701.4 84.5 %copy-start.23 = (bf16[2,1,512,2048]{3,2,1,0:T(8,128)(2,1)S(1)}, bf16[2,1,512,2048]{3,2,1,0:T(8,128)(2,1)}, u32[]{:S(2)}) copy-start(bf16[2,1,512,2048]{3,2,1,0:T(8,128)(2,1)} %param.29) | copy-start | bytes 12582916
  701.4 84.5 %copy-start.71 = (f32[1024]{0:T(1024)S(1)}, f32[1024]{0:T(1024)}, u32[]{:S(2)}) copy-start(f32[1024]{0:T(1024)} %get-tuple-element.226) | copy-start | bytes 12292
  808.7 262.9 %reduce-scatter.14.cloned.1.call-start = ((), (), s32[]{:S(2)}) async-start(), calls=%async_computation.10 | async-start | bytes 13369344 | tf_op jit(solution)/shard_map/reduce_scatter | solution.py:165
  809.2 438.4 %reduce-scatter.10.cloned.1.call-start = ((), (), s32[]{:S(2)}) async-start(), calls=%async_computation.8 | async-start | bytes 8912896 | tf_op jit(solution)/shard_map/reduce_scatter | solution.py:165
  844.1 32.6 %collective-permute-start.13 = (bf16[2,2,512,512]{3,2,1,0:T(8,128)(2,1)}, bf16[2,2,512,512]{3,2,1,0:T(8,128)(2,1)}, u32[]{:S(2)}, u32[]{:S(2)}) collective-permute-start(bf16[2,2,512,512]{3,2,1,0:T(8,128)(2,1)} %pad_maximum_fusion.5), channel_id=1, source_target_pairs={{0,2},{2,0},{4,6},{6,4},{1,3},{3,1},{5,7},{7,5},{8,10},{10,8},{12,... | collective-permute-start | bytes 6291464 | tf_op jit(solution)/shard_map/ppermute | solution.py:340
  871.0 11.2 collective-permute-start.15
  880.6 43.4 %collective-permute-start.14 = (bf16[2,512,512]{2,1,0:T(8,128)(2,1)}, bf16[2,512,512]{2,1,0:T(8,128)(2,1)}, u32[]{:S(2)}, u32[]{:S(2)}) collective-permute-start(bf16[2,512,512]{2,1,0:T(8,128)(2,1)} %fusion.61), channel_id=1, source_target_pairs={{4,0},{6,2},{5,1},{7,3},{12,8},{14,10},{13,9},{15,11},{20,16},{22,... | collective-permute-start | bytes 3145736 | tf_op jit(solution)/shard_map/ppermute | solution.py:341
  882.8 41.2 %copy-start.40 = (f32[2,512,512]{2,1,0:T(8,128)S(1)}, f32[2,512,512]{2,1,0:T(8,128)}, u32[]{:S(2)}) copy-start(f32[2,512,512]{2,1,0:T(8,128)} %get-tuple-element.66) | copy-start | bytes 6291460
  886.2 70.3 %collective-permute-start.16 = (bf16[2,512,512]{2,1,0:T(8,128)(2,1)}, bf16[2,512,512]{2,1,0:T(8,128)(2,1)S(1)}, u32[]{:S(2)}, u32[]{:S(2)}) collective-permute-start(bf16[2,512,512]{2,1,0:T(8,128)(2,1)} %fusion.57), channel_id=1, source_target_pairs={{4,0},{6,2},{5,1},{7,3},{12,8},{14,10},{13,9},{15,11},{20,16},{22,... | collective-permute-start | bytes 3145736 | tf_op jit(solution)/shard_map/ppermute | solution.py:341
  1057.8 48.8 %collective-permute-start.18 = (bf16[512,2048]{1,0:T(8,128)(2,1)}, bf16[512,2048]{1,0:T(8,128)(2,1)}, u32[]{:S(2)}, u32[]{:S(2)}) collective-permute-start(bf16[512,2048]{1,0:T(8,128)(2,1)} %fusion.46), channel_id=1, source_target_pairs={{0,1},{1,0},{2,3},{3,2},{4,5},{5,4},{6,7},{7,6},{8,9},{9,8},{10,11... | collective-permute-start | bytes 6291464 | tf_op jit(solution)/shard_map/ppermute | solution.py:170
  1064.4 85.4 %collective-permute-start.17 = (bf16[512,2048]{1,0:T(8,128)(2,1)S(1)}, bf16[512,2048]{1,0:T(8,128)(2,1)}, u32[]{:S(2)}, u32[]{:S(2)}) collective-permute-start(bf16[512,2048]{1,0:T(8,128)(2,1)S(1)} %fusion.43), channel_id=1, source_target_pairs={{0,1},{1,0},{2,3},{3,2},{4,5},{5,4},{6,7},{7,6},{8,9},{9,8},{10,11... | collective-permute-start | bytes 6291464 | tf_op jit(solution)/shard_map/ppermute | solution.py:170
  1106.7 43.2 %copy-start.51 = (bf16[512,2048]{1,0:T(8,128)(2,1)S(1)}, bf16[512,2048]{1,0:T(8,128)(2,1)}, u32[]{:S(2)}) copy-start(bf16[512,2048]{1,0:T(8,128)(2,1)} %copy-done.50) | copy-start | bytes 6291460
  1109.8 46.9 %copy-start.8 = (f32[512,2048]{1,0:T(8,128)}, f32[512,2048]{1,0:T(8,128)S(1)}, u32[]{:S(2)}) copy-start(f32[512,2048]{1,0:T(8,128)S(1)} %convert_add_fusion) | copy-start | bytes 12582916
  1157.7 75.6 %copy-start.59 = (f32[2048,1]{0,1:T(1,128)S(1)}, f32[2048,1]{0,1:T(1,128)}, u32[]{:S(2)}) copy-start(f32[2048,1]{0,1:T(1,128)} %copy-done.57) | copy-start | bytes 24580
  (70 other events, 468.8 us)
Sparse Core Ops, SparseCore 0:
  13.9 109.4 all-gather.4
  125.0 244.4 all-gather.6
  504.0 141.9 reduce-scatter.15
  649.9 134.1 reduce-scatter.7
  808.8 87.3 reduce-scatter.11
  900.1 134.1 reduce-scatter.13
  1047.6 101.6 reduce-scatter.9

commit v3 on v2

--- a/solution.py
+++ b/solution.py
@@ -4,6 +4,7 @@
 import jax.numpy as jnp
 from jax import lax
 from jax.experimental import pallas as pl
+from jax.experimental.layout import Layout, with_layout_constraint
 from jax.experimental.pallas import tpu as pltpu
 from jax.sharding import PartitionSpec as P
 
@@ -30,19 +31,6 @@
 
 def rdot(left, right):
     return lax.dot_general(left, right, (((1,), (1,)), ((), ())), preferred_element_type=F32)
-
-
-def rotate(values, cosine, sine):
-    half_size = values.shape[-1] // 2
-    turned = jnp.concatenate([-values[..., half_size:], values[..., :half_size]], axis=-1)
-    return values * cosine + turned * sine
-
-
-def rotate_back(grads, cosine, sine):
-    half_size = grads.shape[-1] // 2
-    scaled = grads * sine
-    back_part = jnp.concatenate([scaled[..., half_size:], -scaled[..., :half_size]], axis=-1)
-    return grads * cosine + back_part
 
 
 def norm_back(grads, values, inverse, gain):
@@ -81,7 +69,7 @@
     for g in range(group):
         at=slice(g*rows,(g+1)*rows)
         out[:,g*HEAD:(g+1)*HEAD]=(acc[at,:]/den[at,:]).astype(out.dtype)
-    log_sum[0]=jnp.log2(den[...])
+    log_sum[0] = jnp.transpose(jnp.broadcast_to(jnp.log2(den[...]), (group * rows, HEAD)))[0:1]
 
 def attend(need, queries, step, parts, seg_q, seg_k, k_cols, group, tile=256):
     rows=parts[0].shape[0]; kv=k_cols//HEAD
@@ -93,14 +81,19 @@
             num_scalar_prefetch=1, grid=(kv,),
             in_specs=[pl.BlockSpec((rows,group*HEAD),lambda h,n:(step,h))]+[kspec,vspec]*4+[
                 pl.BlockSpec((rows,1),lambda h,n:(0,0)), pl.BlockSpec((4,rows),lambda h,n:(0,0))],
-            out_specs=[pl.BlockSpec((rows,group*HEAD),lambda h,n:(0,h)), pl.BlockSpec((1,group*rows,1),lambda h,n:(h,0,0))],
+            out_specs=[pl.BlockSpec((rows,group*HEAD),lambda h,n:(0,h)), pl.BlockSpec((1,1,group*rows),lambda h,n:(h,0,0))],
             scratch_shapes=[pltpu.VMEM((group*rows,HEAD),F32),pltpu.VMEM((group*rows,1),F32)]),
-        out_shape=[jax.ShapeDtypeStruct((rows,kv*group*HEAD),BF16),jax.ShapeDtypeStruct((kv,group*rows,1),F32)],
+        out_shape=[jax.ShapeDtypeStruct((rows,kv*group*HEAD),BF16),jax.ShapeDtypeStruct((kv,1,group*rows),F32)],
         name="attend",
     )(need,queries,*[p for part in parts for p in (part,part)],seg_q,seg_k)
 
-def backward_kernel(tile, group, need, q, g_out, k0,v0,k1,v1,k2,v2,k3,v3, seg_q, seg_k, stats, dq, d0,d1,d2,d3, acc):
+def backward_kernel(tile, group, need, q, g_out, heads, k0,v0,k1,v1,k2,v2,k3,v3, seg_q, seg_k, log_sum, dq, d0,d1,d2,d3, acc, delta):
     rows=q.shape[0]
+    ones=jnp.ones((8,HEAD),F32)
+    for g in range(group):
+        lanes=slice(g*HEAD,(g+1)*HEAD)
+        product=g_out[:,lanes].astype(F32)*heads[:,lanes].astype(F32)
+        delta[:,g*rows:(g+1)*rows]=lax.dot_general(ones,product,(((1,),(1,)),((),())),precision=lax.Precision.HIGHEST,preferred_element_type=F32)
     tiles=[(g,t) for g in range(group) for t in range(rows//tile)]
     def run(flip,k,v,d,dk_acc,dv_acc):
         for idx,(g,t) in enumerate(tiles):
@@ -113,9 +106,9 @@
             ok=seg_k[:n,flip:flip+1]==seg_q[:,cut]
             if flip==0:
                 ok&=(lax.broadcasted_iota(jnp.int32,(n,tile),1)+t*tile)>=lax.broadcasted_iota(jnp.int32,(n,tile),0)
-            p=jnp.where(ok,jnp.exp2(s*EXP2_SCALE-stats[0,0:1,at]),0.0)
+            p=jnp.where(ok,jnp.exp2(s*EXP2_SCALE-log_sum[0,0:1,at]),0.0)
             dp=rdot(v[:n,:],dt)
-            ds=(p*(dp-stats[0,1:2,at])).astype(BF16)
+            ds=(p*(dp-delta[0:1,at])).astype(BF16)
             dv=dot(p.astype(BF16),dt)
             dk=dot(ds,qt)
             if idx==0:
@@ -134,7 +127,7 @@
         def clear(d=d): d[...]=jnp.zeros_like(d)
         pl.when(need[flip]<=0)(clear)
 
-def attend_back(need, queries, grad_heads, step, parts, seg_q, seg_k, stats, k_cols, group, tile=256):
+def attend_back(need, queries, grad_heads, heads, step, parts, seg_q, seg_k, log_sum, k_cols, group, tile=256):
     rows=parts[0].shape[0]; kv=k_cols//HEAD
     kspec=pl.BlockSpec((rows,HEAD),lambda h,n:(0,h))
     vspec=pl.BlockSpec((rows,HEAD),lambda h,n:(0,h+kv))
@@ -145,14 +138,109 @@
         functools.partial(backward_kernel,tile,group),
         grid_spec=pltpu.PrefetchScalarGridSpec(
             num_scalar_prefetch=1, grid=(kv,),
-            in_specs=[qspec,qspec]+[kspec,vspec]*4+[
+            in_specs=[qspec,qspec,pl.BlockSpec((rows,group*HEAD),lambda h,n:(0,h))]+[kspec,vspec]*4+[
                 pl.BlockSpec((1,rows),lambda h,n:(0,0)), pl.BlockSpec((rows,4),lambda h,n:(0,0)),
-                pl.BlockSpec((1,2,group*rows),lambda h,n:(h,0,0))],
+                pl.BlockSpec((1,1,group*rows),lambda h,n:(h,0,0))],
             out_specs=[pl.BlockSpec((rows,group*HEAD),lambda h,n:(0,h))]+[dspec]*4,
-            scratch_shapes=[pltpu.VMEM((2,rows,HEAD),F32)]),
+            scratch_shapes=[pltpu.VMEM((2,rows,HEAD),F32),pltpu.VMEM((8,group*rows),F32)]),
         out_shape=[jax.ShapeDtypeStruct((rows,kv*group*HEAD),F32)]+[jax.ShapeDtypeStruct((2,rows,k_cols),t) for t in types],
         name="attend_back",
-    )(need,queries,grad_heads,*[p for part in parts for p in (part,part)],seg_q,seg_k,stats)
+    )(need,queries,grad_heads,heads,*[p for part in parts for p in (part,part)],seg_q,seg_k,log_sum)
+
+
+def rope_kernel(q_heads, k_heads, raw, turn, gains, queries, pairs):
+    cosine, sine = turn[0], turn[1]
+    for head in range(q_heads + k_heads):
+        values = raw[:, head * HEAD : (head + 1) * HEAD]
+        inverse = lax.rsqrt(jnp.mean(values * values, axis=-1, keepdims=True) + EPS)
+        gain = gains[0:1] if head < q_heads else gains[1:2]
+        scaled = values * inverse * gain
+        turned = (scaled * cosine + pltpu.roll(scaled, HEAD // 2, 1) * sine).astype(BF16)
+        if head < q_heads:
+            queries[:, head * HEAD : (head + 1) * HEAD] = turned
+        else:
+            at = head - q_heads
+            pairs[:, at * HEAD : (at + 1) * HEAD] = turned
+    cols = (q_heads + k_heads) * HEAD
+    pairs[:, k_heads * HEAD :] = raw[:, cols:].astype(BF16)
+
+
+def rope(raw, turn, gains, q_cols, k_cols, block=256):
+    total = raw.shape[0]
+    return pl.pallas_call(
+        functools.partial(rope_kernel, q_cols // HEAD, k_cols // HEAD),
+        grid=(total // block,),
+        in_specs=[
+            pl.BlockSpec((block, raw.shape[1]), lambda i: (i, 0)),
+            pl.BlockSpec((2, block, HEAD), lambda i: (0, i, 0)),
+            pl.BlockSpec((2, HEAD), lambda i: (0, 0)),
+        ],
+        out_specs=[
+            pl.BlockSpec((block, q_cols), lambda i: (i, 0)),
+            pl.BlockSpec((block, 2 * k_cols), lambda i: (i, 0)),
+        ],
+        out_shape=[
+            jax.ShapeDtypeStruct((total, q_cols), BF16),
+            jax.ShapeDtypeStruct((total, 2 * k_cols), BF16),
+        ],
+        name="rope",
+    )(raw, turn, gains)
+
+
+def rope_back_kernel(q_heads, k_heads, raw, turn, gains, dq, d_own, d_near, d_far, out, sums):
+    cosine, sine = turn[0], turn[1]
+
+    @pl.when(pl.program_id(0) == 0)
+    def _():
+        sums[...] = jnp.zeros_like(sums)
+
+    for head in range(q_heads + k_heads):
+        lanes = slice(head * HEAD, (head + 1) * HEAD)
+        which = 0 if head < q_heads else 1
+        if which == 0:
+            grads = dq[:, lanes]
+        else:
+            at = slice((head - q_heads) * HEAD, (head - q_heads + 1) * HEAD)
+            grads = d_own[0, :, at] + d_near[0, :, at].astype(F32) + d_far[0, :, at].astype(F32)
+        values = raw[:, lanes]
+        inverse = lax.rsqrt(jnp.mean(values * values, axis=-1, keepdims=True) + EPS)
+        unit = values * inverse
+        turned = grads * cosine - pltpu.roll(grads, HEAD // 2, 1) * sine
+        sums[which : which + 1] += jnp.sum(turned * unit, axis=0, keepdims=True)
+        scaled = turned * gains[which : which + 1]
+        mean = jnp.mean(scaled * unit, axis=-1, keepdims=True)
+        out[:, lanes] = (inverse * (scaled - unit * mean)).astype(BF16)
+    cols = (q_heads + k_heads) * HEAD
+    out[:, cols:] = (d_own[1] + d_near[1].astype(F32) + d_far[1].astype(F32)).astype(BF16)
+
+
+def rope_back(raw, turn, gains, dq, d_own, d_near, d_far, step, q_cols, k_cols, block=256):
+    rows = dq.shape[0]
+    base = step * (rows // block)
+    cols = q_cols + 2 * k_cols
+    dspec = pl.BlockSpec((2, block, k_cols), lambda i: (0, i, 0))
+    return pl.pallas_call(
+        functools.partial(rope_back_kernel, q_cols // HEAD, k_cols // HEAD),
+        grid=(rows // block,),
+        in_specs=[
+            pl.BlockSpec((block, cols), lambda i: (base + i, 0)),
+            pl.BlockSpec((2, block, HEAD), lambda i: (0, base + i, 0)),
+            pl.BlockSpec((2, HEAD), lambda i: (0, 0)),
+            pl.BlockSpec((block, q_cols), lambda i: (i, 0)),
+            dspec,
+            dspec,
+            dspec,
+        ],
+        out_specs=[
+            pl.BlockSpec((block, cols), lambda i: (i, 0)),
+            pl.BlockSpec((2, HEAD), lambda i: (0, 0)),
+        ],
+        out_shape=[
+            jax.ShapeDtypeStruct((rows, cols), BF16),
+            jax.ShapeDtypeStruct((2, HEAD), F32),
+        ],
+        name="rope_back",
+    )(raw, turn, gains, dq, d_own, d_near, d_far)
 
 
 def make_local(mp_size, seq_size, dp_size):
@@ -164,11 +252,22 @@
     def scatter(grad):
         return lax.psum_scatter(grad, data_axes, scatter_dimension=0, tiled=True)
 
+    def mp_other(part):
+        if mp_size == 2:
+            return lax.ppermute(part, "mp", [(0, 1), (1, 0)])
+        return (lax.psum(part.astype(F32), "mp") - part.astype(F32)).astype(BF16)
+
     def mp_part(part):
         part = lax.optimization_barrier(part.astype(BF16))
-        if mp_size == 2:
-            return part, lax.ppermute(part, "mp", [(0, 1), (1, 0)])
-        return lax.psum(part, "mp"), jnp.zeros(part.shape, BF16)
+        return part, mp_other(part)
+
+    def butterfly(value, axis, size):
+        flip = 1
+        while flip < size:
+            moves = [(i, i ^ flip) for i in range(size)]
+            value = value + lax.ppermute(value, axis, moves)
+            flip *= 2
+        return value
 
     def mp_sum(part):
         mine, other = mp_part(part)
@@ -196,7 +295,6 @@
         total = MICRO * rows
         q_cols = w_query.shape[1]
         k_cols = w_key.shape[1]
-        kv_heads = k_cols // HEAD
         group = HEADS // KV_HEADS
         rank = lax.axis_index("seq")
         own_rows = w_query.shape[0]
@@ -217,21 +315,14 @@
         inv_attn = inv_rms(tokens)
         frequency = ROPE_BASE ** (-(jnp.arange(HEAD // 2, dtype=F32) * 2.0) / HEAD)
         angles = positions.reshape(total).astype(F32)[:, None] * frequency[None, :]
-        angles = jnp.concatenate([angles, angles], axis=-1)[:, None, :]
         cosine = jnp.cos(angles)
         sine = jnp.sin(angles)
-        first, cosine, sine, inv_attn = lax.optimization_barrier((first, cosine, sine, inv_attn))
-        qkv_cols = q_cols + 2 * k_cols
-        w_qkv = first[:, :qkv_cols]
-        w_out_t = first[:, qkv_cols : qkv_cols + q_cols]
-        gain_attn = first[:, qkv_cols + q_cols].astype(F32)
-        gain_ffn = first[:, qkv_cols + q_cols + 64].astype(F32)
-        gate_full, up_full, down_t = second[0], second[1], second[2]
-        gain_query = norm_query.astype(F32)
-        gain_key = norm_key.astype(F32)
-
-        cot = cotangent.reshape(total, width)
-
+        turn = jnp.stack(
+            [
+                jnp.concatenate([cosine, cosine], axis=-1),
+                jnp.concatenate([-sine, sine], axis=-1),
+            ]
+        )
         seg_own = segments[:, 0]
         seg_pair = lax.ppermute(seg_own, "seq", pair)
         both = jnp.stack([seg_own, seg_pair])
@@ -240,24 +331,29 @@
         flips = jnp.arange(4, dtype=jnp.int32)
         near_enough = (seg_keys[:, :, -1] == seg_own[None, :, 0]) | (flips[:, None] == 0)
         need = (near_enough & (jnp.bitwise_xor(rank, flips)[:, None] <= rank)).astype(jnp.int32)
+        first, turn, inv_attn, seg_keys, need = lax.optimization_barrier(
+            (first, turn, inv_attn, seg_keys, need)
+        )
+        qkv_cols = q_cols + 2 * k_cols
+        w_qkv = first[:, :qkv_cols]
+        w_out_t = first[:, qkv_cols : qkv_cols + q_cols]
+        gain_attn = first[:, qkv_cols + q_cols].astype(F32)
+        gain_ffn = first[:, qkv_cols + q_cols + 64].astype(F32)
+        gate_full, up_full, down_t = second[0], second[1], second[2]
+        gain_heads = jnp.stack([norm_query, norm_key]).astype(F32)
+
+        cot = lax.optimization_barrier(cotangent.reshape(total, width))
 
         normed_attn = (tokens * inv_attn * gain_attn).astype(BF16)
         raw = dot(normed_attn, w_qkv)
-        query_raw = raw[:, :q_cols].reshape(total, -1, HEAD)
-        key_raw = raw[:, q_cols : q_cols + k_cols].reshape(total, -1, HEAD)
-        values = raw[:, q_cols + k_cols :].astype(BF16)
-        query_inv = inv_rms(query_raw)
-        key_inv = inv_rms(key_raw)
-        queries = rotate(query_raw * query_inv * gain_query, cosine, sine).astype(BF16)
-        queries = queries.reshape(total, q_cols)
-        keys = rotate(key_raw * key_inv * gain_key, cosine, sine).astype(BF16)
-        keys = keys.reshape(total, k_cols)
+        queries, pairs = rope(raw, turn, gain_heads, q_cols, k_cols)
+
         kept = []
         middles = []
         heads_out = []
         for step in range(MICRO):
             cut = slice(step * rows, (step + 1) * rows)
-            own = jnp.concatenate([keys[cut], values[cut]], axis=1)
+            own = pairs[cut]
             near = lax.ppermute(own, "seq", pair)
             far = lax.ppermute(own, "seq", up_pairs)
             far_near = lax.ppermute(far, "seq", pair)
@@ -288,6 +384,7 @@
         silu = gate * sigma
         act = (silu * upward).astype(BF16)
         down_grad = tdot(cot, act).astype(BF16)
+        down_grad = with_layout_constraint(down_grad, Layout((0, 1)))
         down_owned = scatter(down_grad)
         cot_late, act, down_grad = lax.optimization_barrier((cot, act, down_grad))
         grad_act = dot(cot_late, down_t)
@@ -303,82 +400,81 @@
         gate_owned = scatter(gate_grad)
         up_grad = tdot(normed_ffn, grad_up_in).astype(BF16)
         up_owned = scatter(up_grad)
-        backs, act, gate_grad, up_grad = lax.optimization_barrier((backs, act, gate_grad, up_grad))
+        down_mine = lax.optimization_barrier(rdot(act, down_t).astype(BF16))
+        backs, gate_grad, up_grad, down_mine = lax.optimization_barrier(
+            (backs, gate_grad, up_grad, down_mine)
+        )
+        down_other = mp_other(down_mine)
+        gain_ffn_part = jnp.concatenate([mine for mine, _ in backs], axis=0).astype(F32)
+        gain_ffn_part = jnp.sum(gain_ffn_part * middle * inv_ffn, axis=0)
         backs = [mine.astype(F32) + other.astype(F32) for mine, other in backs]
-        layer_out = (middle + mp_sum(rdot(act, down_t))).astype(BF16)
         grad_normed_ffn = jnp.concatenate(backs, axis=0)
-        gain_ffn_grad = jnp.sum(grad_normed_ffn * middle * inv_ffn, axis=0)
         grad_middle = cot.astype(F32) + norm_back(grad_normed_ffn, middle, inv_ffn, gain_ffn)
         grad_middle_b = grad_middle.astype(BF16)
         grad_heads = dot(grad_middle_b, w_out_t).astype(BF16)
         out_owned = scatter(tdot(grad_middle_b, attn_heads).astype(BF16))
 
-        grad_queries = []
-        grad_keys = []
-        grad_values = []
+        grads_in = []
+        head_sums = []
+        sides = []
         for step in range(MICRO):
-            cut = slice(step * rows, (step + 1) * rows)
             parts, log_sum = kept[step]
-            dots = grad_heads[cut].astype(F32) * heads_out[step].astype(F32)
-            dots = jnp.sum(dots.reshape(rows, kv_heads, group, HEAD), axis=-1)
-            dots = dots.transpose(1, 2, 0).reshape(kv_heads, 1, group * rows)
-            stats = jnp.concatenate([log_sum.reshape(kv_heads, 1, group * rows), dots], axis=1)
             grad_q, d_own, d_near, d_far, d_far_near = attend_back(
                 need[:, step],
                 queries,
                 grad_heads,
+                heads_out[step],
                 step,
                 parts,
                 seg_own[step][None],
                 seg_keys[:, step].T,
-                stats,
+                log_sum,
                 k_cols,
                 group,
                 rows,
             )
-            grad_queries.append(grad_q)
-            got = lax.ppermute(jnp.stack([d_near, d_far_near]), "seq", pair).astype(F32)
-            far = lax.ppermute((d_far + got[1]).astype(BF16), "seq", down_pairs).astype(F32)
-            owned = d_own + got[0] + far
-            grad_keys.append(owned[0])
-            grad_values.append(owned[1])
-        grad_queries, down_owned = lax.optimization_barrier((grad_queries, down_owned))
-        grad_query_rot = jnp.concatenate(grad_queries, axis=0).reshape(total, -1, HEAD)
-        grad_key_rot = jnp.concatenate(grad_keys, axis=0).reshape(total, -1, HEAD)
-        grad_value_in = jnp.concatenate(grad_values, axis=0).astype(BF16)
-        query_turn = rotate_back(grad_query_rot, cosine, sine)
-        key_turn = rotate_back(grad_key_rot, cosine, sine)
-        query_gain = jnp.sum(query_turn * query_raw * query_inv, axis=(0, 1))
-        key_gain = jnp.sum(key_turn * key_raw * key_inv, axis=(0, 1))
-        grad_query_in = norm_back(query_turn, query_raw, query_inv, gain_query)
-        grad_key_in = norm_back(key_turn, key_raw, key_inv, gain_key)
-        grad_qkv_in = jnp.concatenate(
-            [
-                grad_query_in.astype(BF16).reshape(total, -1),
-                grad_key_in.astype(BF16).reshape(total, -1),
-                grad_value_in,
-            ],
-            axis=1,
-        )
-        grad_qkv_in, gate_owned = lax.optimization_barrier((grad_qkv_in, gate_owned))
+            got = lax.ppermute(d_near, "seq", pair)
+            got_far = lax.ppermute(d_far_near, "seq", pair)
+            far = lax.ppermute(
+                (d_far + got_far.astype(F32)).astype(BF16), "seq", down_pairs
+            )
+            sides.append((grad_q, d_own, got, far))
+        for step in range(MICRO):
+            if step == MICRO - 1:
+                down_other, down_owned, side = lax.optimization_barrier(
+                    (down_other, down_owned, sides[step])
+                )
+            else:
+                side = sides[step]
+            grad_in, sums = rope_back(raw, turn, gain_heads, *side, step, q_cols, k_cols)
+            grads_in.append(grad_in)
+            head_sums.append(sums)
+        layer_out = (middle + (down_mine.astype(F32) + down_other.astype(F32))).astype(BF16)
+        backs = [mp_part(rdot(grad_in, w_qkv)) for grad_in in grads_in]
+        grad_qkv_in = jnp.concatenate(grads_in, axis=0)
+        mines = [mine for mine, _ in backs]
+        grad_qkv_in, gate_owned, mines = lax.optimization_barrier(
+            (grad_qkv_in, gate_owned, mines)
+        )
         qkv_owned = scatter(tdot(normed_attn, grad_qkv_in).astype(BF16))
-        backs = []
-        for step in range(MICRO):
-            cut = slice(step * rows, (step + 1) * rows)
-            backs.append(mp_sum(rdot(grad_qkv_in[cut], w_qkv)))
-        grad_normed_attn = jnp.concatenate(backs, axis=0)
-        gain_attn_grad = jnp.sum(grad_normed_attn * tokens * inv_attn, axis=0)
+        gain_attn_part = jnp.concatenate([mine for mine, _ in backs], axis=0).astype(F32)
+        gain_attn_part = jnp.sum(gain_attn_part * tokens * inv_attn, axis=0)
+        head_sum = (head_sums[0] + head_sums[1]).reshape(-1)
+        small = jnp.concatenate([gain_attn_part, gain_ffn_part, head_sum]).reshape(-1, HEAD)
+        small = butterfly(small, "seq", seq_size)
+        small = butterfly(small, "dp", dp_size)
+        small = butterfly(small, "mp", mp_size).reshape(-1)
+        head_sum = small[2 * width :]
+        owner = (lax.axis_index("dp") * seq_size + rank) * own_rows
+        wide_sum = small[: 2 * width].reshape(2, width)
+        wide_sum = lax.dynamic_slice_in_dim(wide_sum, owner, own_rows, 1)
+
+        grad_normed_attn = jnp.concatenate(
+            [mine.astype(F32) + other.astype(F32) for mine, other in backs], axis=0
+        )
         grad_tokens = (
             grad_middle + norm_back(grad_normed_attn, tokens, inv_attn, gain_attn)
         ).astype(BF16)
-
-        small = jnp.concatenate([gain_attn_grad, gain_ffn_grad, query_gain, key_gain])
-        small = lax.all_gather(small, ("dp", "seq", "mp"), axis=0, tiled=False)
-        small = small.reshape(dp_size * seq_size, mp_size, -1)
-        head_sum = jnp.sum(small[:, :, 2 * width :], axis=(0, 1))
-        owner = (lax.axis_index("dp") * seq_size + rank) * own_rows
-        wide_sum = jnp.sum(small[:, 0, : 2 * width], axis=0).reshape(2, width)
-        wide_sum = lax.dynamic_slice_in_dim(wide_sum, owner, own_rows, 1)
 
         qkv_owned = qkv_owned.astype(F32)
         return (

time: 1270 us -> 1100 us (0.87)
  other arithmetic: 197 us -> 97.2 us
  local copies, waits for them, and re-layouts: 104 us -> 36.4 us
  blocking collectives: 67.6 us -> 0 us
  waiting for transfers between devices: 528 us -> 561 us
  Pallas kernels: 39.7 us -> 68.1 us
    reduce_scatter x4 -> x5, waiting for transfers between devices: 0.02 us -> 93 us  [scatter(): return lax.psum_scatter(grad, data_axes, scatter_dimension=0, tiled=True)]
    all_gather x1 -> x0, blocking collectives: 67.6 us -> none  [local(): small = lax.all_gather(small, ('dp', 'seq', 'mp'), axis=0, tiled=False)]
    ppermute x11 -> x18, waiting for transfers between devices: 335 us -> 278 us  [the longest x7 210 us: mp_other(): return lax.ppermute(part, 'mp', [(0, 1), (1, 0)])]
    unnamed x206 -> x117, local copies, waits for them, and re-layouts: 49.9 us -> 19.9 us
    pallas_call x0 -> x3, Pallas kernels: none -> 25 us  [the longest x2 15.6 us: rope_back(): pl.pallas_call(functools.partial(rope_back_kernel, q_cols // HEAD, k_cols...]
    mul x7 -> x0, other arithmetic: 24.6 us -> none  [the longest x1 9.09 us: norm_back(): scaled = grads * gain]
    reduce_sum x12 -> x2, other arithmetic: 34.3 us -> 10.8 us  [the longest x1 6.15 us: local(): gain_attn_part = jnp.sum(gain_attn_part * tokens * inv_attn, axis=0)]
    ppermute x1, waiting for transfers between devices: 20.8 us -> 0.83 us  [local(): both_x = lax.ppermute(both, 'seq', up_pairs)]
  transfers between devices with their start and end apart: 26 -> 33, of which waited for: 13 -> 15; matrix products, arithmetic and copies ran while one was open for 37% -> 30% of each run, Pallas kernels for 3% -> 6%
where the time goes in v3:
time: 1100 us; the launch traced here: 1090 us
  waiting for transfers between devices  561 us (51%)
  matrix products  272 us (25%)
  other arithmetic  97.2 us (9%)
  Pallas kernels  68.1 us (6%)
  starting transfers between devices  45.2 us (4%)
  local copies, waits for them, and re-layouts  36.4 us (3%)
  between operations  15.1 us (1%)
    ppermute x7, waiting for transfers between devices, mp_other(): return lax.ppermute(part, 'mp', [(0, 1), (1, 0)])  210 us
    all_gather x1, waiting for transfers between devices, local(): first = lax.all_gather(first, data_axes, axis=0, tiled=True)  105 us
    dot_general x9, matrix products, rdot(): lax.dot_general(left, right, (((1,), (1,)), ((), ())), preferred_element_...  100 us
    reduce_scatter x5, waiting for transfers between devices, scatter(): return lax.psum_scatter(grad, data_axes, scatter_dimension=0, tiled=True)  93 us
    dot_general x5, matrix products, dot(): return jnp.dot(left, right, preferred_element_type=F32)  92.1 us
    ppermute x2, waiting for transfers between devices, local(): far = lax.ppermute(own, 'seq', up_pairs)  83.7 us
    dot_general x5, matrix products, tdot(): lax.dot_general(left, right, (((0,), (0,)), ((), ())), preferred_element_...  79.4 us
    ppermute x2, waiting for transfers between devices, local(): lax.ppermute((d_far + got_far.astype(F32)).astype(BF16), 'seq', down_pairs)  64 us
  transfers between devices with their start and end apart: 33, of which 15 were waited for; matrix products, arithmetic and copies ran while one was open for 30% of the time, Pallas kernels for 6%

profile of v3, /device:TPU:0, one launch (start us, length us, event | category | flops | bytes accessed | tf_op | source)
XLA Modules:
  0.0 1094.4 jit_solution(7451240711367748426)
XLA Ops:
  18.6 104.9 %all-gather.3.cloned.1.call-done = bf16[2048,3200]{0,1:T(8,128)(2,1)} async-done(((bf16[128,3200]{0,1:T(8,128)(2,1)}), bf16[2048,3200]{0,1:T(8,128)(2,1)}) %all-gather.3.cloned.1.call-update) | async-done | bytes 13107216 | tf_op jit(solution)/shard_map/all_gather | solution.py:310
  138.1 11.1 %fusion.23.raw = f32[1024,2048]{1,0:T(8,128)} fusion(bf16[1024,2048]{1,0:T(8,128)(2,1)S(1)} %fusion.14, bf16[2048,3200]{0,1:T(8,128)(2,1)S(1)} %copy-done.46), kind=kOutput, calls=%fused_computation.48 | convolution fusion | flops 8589934592 | bytes 20971520 | tf_op jit(solution)/shard_map/dot_general | solution.py:25
  149.2 9.3 rope.1
  167.6 43.1 %collective-permute-done.7.k2.v2 = bf16[512,1024]{1,0:T(8,128)(2,1)S(1)} collective-permute-done((bf16[512,1024]{1,0:T(8,128)(2,1)S(1)}, bf16[512,1024]{1,0:T(8,128)(2,1)S(1)}, u32[]{:S(2)}, u32[]{:S(2)}) %collective-permute-start.7) | collective-permute-done | bytes 1048608 | tf_op jit(solution)/shard_map/ppermute | solution.py:358
  214.6 40.7 %collective-permute-done.3.k2.v2 = bf16[512,1024]{1,0:T(8,128)(2,1)} collective-permute-done((bf16[512,1024]{1,0:T(8,128)(2,1)S(1)}, bf16[512,1024]{1,0:T(8,128)(2,1)}, u32[]{:S(2)}, u32[]{:S(2)}) %collective-permute-start.3) | collective-permute-done | bytes 1048608 | tf_op jit(solution)/shard_map/ppermute | solution.py:358
  260.1 8.2 attend.3
  268.3 6.2 fusion.41
  274.5 8.8 attend.2
  283.3 5.1 fusion.38
  290.6 4.4 convert_element_type.205
  294.9 36.3 %collective-permute-done.5 = bf16[512,2048]{1,0:T(8,128)(2,1)S(1)} collective-permute-done((bf16[512,2048]{1,0:T(8,128)(2,1)S(1)}, bf16[512,2048]{1,0:T(8,128)(2,1)S(1)}, u32[]{:S(2)}, u32[]{:S(2)}) %collective-permute-start.5) | collective-permute-done | bytes 2097184 | tf_op jit(solution)/shard_map/ppermute | solution.py:257
  332.5 43.7 %collective-permute-done.9 = bf16[512,2048]{1,0:T(8,128)(2,1)} collective-permute-done((bf16[512,2048]{1,0:T(8,128)(2,1)S(1)}, bf16[512,2048]{1,0:T(8,128)(2,1)}, u32[]{:S(2)}, u32[]{:S(2)}) %collective-permute-start.9) | collective-permute-done | bytes 2097184 | tf_op jit(solution)/shard_map/ppermute | solution.py:257
  376.2 9.5 fusion.26
  393.1 19.1 %fusion.5 = f32[1024,3072]{1,0:T(8,128)} fusion(bf16[1024,2048]{1,0:T(8,128)(2,1)} %multiply_convert_fusion.3, bf16[3,2048,3072]{1,2,0:T(8,128)(2,1)} %all-gather.5.cloned.1.call-done), kind=kOutput, calls=%fused_computation.15 | convolution fusion | flops 12884901888 | bytes 29360128 | tf_op jit(solution)/shard_map/dot_general | solution.py:25
  412.2 24.1 %multiply_convert_fusion.2 = (bf16[1024,3072]{1,0:T(8,128)(2,1)}, f32[1024,3072]{1,0:T(8,128)}) fusion(f32[1024,3072]{1,0:T(8,128)} %fusion.5, bf16[1024,2048]{1,0:T(8,128)(2,1)} %multiply_convert_fusion.3, bf16[3,2048,3072]{1,2,0:T(8,128)(2,1)} %all-gather.5.cloned.1.call-done), kind=kOutput, calls=%fused_computation.6 | convolution fusion | flops 12903776256 | bytes 48234496 | tf_op jit(solution)/shard_map/dot_general | solution.py:25
  436.3 19.3 %convert_bitcast_fusion = bf16[2048,3072]{1,0:T(8,128)(2,1)} fusion(bf16[1024,3072]{1,0:T(8,128)(2,1)} %get-tuple-element.67, bf16[1024,2048]{1,0:T(8,128)(2,1)} %bitcast.159), kind=kOutput, calls=%fused_computation.5 | convolution fusion | flops 12891193344 | bytes 23068672 | tf_op jit(solution)/shard_map/dot_general | solution.py:29
  455.7 27.4 %multiply_convert_fusion = (bf16[1024,3072]{1,0:T(8,128)(2,1)}, bf16[1024,3072]{1,0:T(8,128)(2,1)}) fusion(f32[1024,3072]{1,0:T(8,128)} %fusion.5, f32[1024,3072]{1,0:T(8,128)} %get-tuple-element.187, bf16[1024,2048]{1,0:T(8,128)(2,1)} %bitcast.160, bf16[3,2048,3072]{1,2,0:T(8,128)(2,1)} %all-gather.5.cloned.1.call-done), kind=kOutput, calls=%fused_computation.3 | convolution fusion | flops 12925796352 | bytes 54525952 | tf_op jit(solution)/shard_map/dot_general | solution.py:25
  483.1 19.5 %convolution_convert_fusion.1 = bf16[2048,3072]{1,0:T(8,128)(2,1)} fusion(bf16[1024,2048]{1,0:T(8,128)(2,1)S(1)} %copy-done.15, bf16[1024,3072]{1,0:T(8,128)(2,1)} %get-tuple-element.154), kind=kOutput, calls=%fused_computation.10 | convolution fusion | flops 12891193344 | bytes 23068672 | tf_op jit(solution)/shard_map/dot_general | solution.py:29
  502.6 20.6 %fusion.27 = bf16[1024,2048]{1,0:T(8,128)(2,1)} fusion(bf16[1024,3072]{1,0:T(8,128)(2,1)} %get-tuple-element.67, bf16[3,2048,3072]{1,2,0:T(8,128)(2,1)} %all-gather.5.cloned.1.call-done), kind=kOutput, calls=%fused_computation.62 | convolution fusion | flops 12886999040 | bytes 23068672 | tf_op jit(solution)/shard_map/dot_general | solution.py:33
  523.3 12.0 %fusion.3 = f32[512,2048]{1,0:T(8,128)} fusion(bf16[3,2048,3072]{1,2,0:T(8,128)(2,1)} %all-gather.5.cloned.1.call-done, bf16[1024,3072]{1,0:T(8,128)(2,1)} %get-tuple-element.154), kind=kOutput, calls=%fused_computation.13 | convolution fusion | flops 6442450944 | bytes 19922944 | tf_op jit(solution)/shard_map/dot_general | solution.py:33
  535.3 12.8 %add_convert_fusion.1 = bf16[512,2048]{1,0:T(8,128)(2,1)S(1)} fusion(f32[512,2048]{1,0:T(8,128)} %fusion.3, bf16[3,2048,3072]{1,2,0:T(8,128)(2,1)} %all-gather.5.cloned.1.call-done, bf16[1024,3072]{1,0:T(8,128)(2,1)} %get-tuple-element.153), kind=kOutput, calls=%fused_computation.60 | convolution fusion | flops 6444548096 | bytes 22020096 | tf_op jit(solution)/shard_map/dot_general | solution.py:33
  549.7 11.2 %fusion.4 = f32[512,2048]{1,0:T(8,128)} fusion(bf16[3,2048,3072]{1,2,0:T(8,128)(2,1)} %all-gather.5.cloned.1.call-done, bf16[1024,3072]{1,0:T(8,128)(2,1)S(1)} %bitcast.188), kind=kOutput, calls=%fused_computation.14 | convolution fusion | flops 6442450944 | bytes 19922944 | tf_op jit(solution)/shard_map/dot_general | solution.py:33
  561.0 13.5 %add_convert_fusion.2 = bf16[512,2048]{1,0:T(8,128)(2,1)} fusion(f32[512,2048]{1,0:T(8,128)} %fusion.4, bf16[3,2048,3072]{1,2,0:T(8,128)(2,1)} %all-gather.5.cloned.1.call-done, bf16[1024,3072]{1,0:T(8,128)(2,1)S(1)} %bitcast.190), kind=kOutput, calls=%fused_computation.61 | convolution fusion | flops 6444548096 | bytes 22020096 | tf_op jit(solution)/shard_map/dot_general | solution.py:33
  575.0 16.1 %convolution_convert_fusion = bf16[2048,3072]{1,0:T(8,128)(2,1)} fusion(bf16[1024,2048]{1,0:T(8,128)(2,1)S(1)} %copy-done.16, bf16[1024,3072]{1,0:T(8,128)(2,1)S(1)} %bitcast.190), kind=kOutput, calls=%fused_computation.9 | convolution fusion | flops 12891193344 | bytes 23068672 | tf_op jit(solution)/shard_map/dot_general | solution.py:29
  591.1 44.0 %collective-permute-done.10 = bf16[512,2048]{1,0:T(8,128)(2,1)} collective-permute-done((bf16[512,2048]{1,0:T(8,128)(2,1)}, bf16[512,2048]{1,0:T(8,128)(2,1)}, u32[]{:S(2)}, u32[]{:S(2)}) %collective-permute-start.10) | collective-permute-done | bytes 2097184 | tf_op jit(solution)/shard_map/ppermute | solution.py:257
  643.2 4.7 multiply_reduce_fusion
  648.5 8.3 subtract_add_fusion
  656.8 10.3 convolution_convert_fusion.3
  669.3 10.5 fusion.59.g_out
  679.9 13.0 %attend_back.3 = (f32[512,1024]{1,0:T(8,128)}, f32[2,512,512]{2,1,0:T(8,128)}, bf16[2,512,512]{2,1,0:T(8,128)(2,1)}, f32[2,512,512]{2,1,0:T(8,128)}, bf16[2,512,512]{2,1,0:T(8,128)(2,1)}) custom-call(s32[4]{0:T(128)} %get-tuple-element.184.need, bf16[1024,1024]{1,0:T(8,128)(2,1)} %get-tuple-element.60.q, bf16[1024,1024]{1,0:T(8,128)(2,1)} %fusion.59.g_out, ...), custom_call_target="tpu_custom_call" | custom-call | tf_op jit(solution)/shard_map/attend_back/pallas_call | solution.py:137
  692.9 12.8 %collective-permute-start.17 = (bf16[2,512,512]{2,1,0:T(8,128)(2,1)}, bf16[2,512,512]{2,1,0:T(8,128)(2,1)S(1)}, u32[]{:S(2)}, u32[]{:S(2)}) collective-permute-start(bf16[2,512,512]{2,1,0:T(8,128)(2,1)} %get-tuple-element.85), channel_id=1, source_target_pairs={{0,2},{2,0},{4,6},{6,4},{1,3},{3,1},{5,7},{7,5},{8,10},{10,8},{12,... | collective-permute-start | bytes 3145736 | tf_op jit(solution)/shard_map/ppermute | solution.py:437
  705.7 13.0 %attend_back.2 = (f32[512,1024]{1,0:T(8,128)}, f32[2,512,512]{2,1,0:T(8,128)}, bf16[2,512,512]{2,1,0:T(8,128)(2,1)}, f32[2,512,512]{2,1,0:T(8,128)}, bf16[2,512,512]{2,1,0:T(8,128)(2,1)}) custom-call(s32[4]{0:T(128)} %get-tuple-element.185.need, bf16[1024,1024]{1,0:T(8,128)(2,1)} %get-tuple-element.60.q, bf16[1024,1024]{1,0:T(8,128)(2,1)} %fusion.59.g_out, ...), custom_call_target="tpu_custom_call" | custom-call | tf_op jit(solution)/shard_map/attend_back/pallas_call | solution.py:137
  718.7 6.2 collective-permute-start.14
  731.6 48.3 %collective-permute-done.18.d_far = bf16[2,512,512]{2,1,0:T(8,128)(2,1)S(1)} collective-permute-done((bf16[2,512,512]{2,1,0:T(8,128)(2,1)S(1)}, bf16[2,512,512]{2,1,0:T(8,128)(2,1)S(1)}, u32[]{:S(2)}, u32[]{:S(2)}) %collective-permute-start.18) | collective-permute-done | bytes 1048608 | tf_op jit(solution)/shard_map/ppermute | solution.py:438
  780.8 8.0 rope_back.2
  788.8 8.5 fusion.44
  797.3 15.7 %collective-permute-done.15.d_far = bf16[2,512,512]{2,1,0:T(8,128)(2,1)} collective-permute-done((bf16[2,512,512]{2,1,0:T(8,128)(2,1)}, bf16[2,512,512]{2,1,0:T(8,128)(2,1)}, u32[]{:S(2)}, u32[]{:S(2)}) %collective-permute-start.15) | collective-permute-done | bytes 1048608 | tf_op jit(solution)/shard_map/ppermute | solution.py:438
  813.1 7.7 rope_back.3
  820.7 10.2 fusion.47
  833.5 14.2 %convolution_convert_fusion.2 = bf16[2048,2048]{1,0:T(8,128)(2,1)} fusion(bf16[1024,2048]{1,0:T(8,128)(2,1)} %copy-done.17, bf16[1024,2048]{1,0:T(8,128)(2,1)} %pad_maximum_fusion.2), kind=kOutput, calls=%fused_computation.43 | convolution fusion | flops 8594128896 | bytes 16777216 | tf_op jit(solution)/shard_map/dot_general | solution.py:29
  851.1 45.4 %collective-permute-done.19 = bf16[512,2048]{1,0:T(8,128)(2,1)} collective-permute-done((bf16[512,2048]{1,0:T(8,128)(2,1)S(1)}, bf16[512,2048]{1,0:T(8,128)(2,1)}, u32[]{:S(2)}, u32[]{:S(2)}) %collective-permute-start.19) | collective-permute-done | bytes 2097184 | tf_op jit(solution)/shard_map/ppermute | solution.py:257
  898.9 40.9 %collective-permute-done.20 = bf16[512,2048]{1,0:T(8,128)(2,1)} collective-permute-done((bf16[512,2048]{1,0:T(8,128)(2,1)}, bf16[512,2048]{1,0:T(8,128)(2,1)}, u32[]{:S(2)}, u32[]{:S(2)}) %collective-permute-start.20) | collective-permute-done | bytes 2097184 | tf_op jit(solution)/shard_map/ppermute | solution.py:257
  942.2 4.5 pad_maximum_fusion.1
  948.2 6.1 fusion.10
  956.6 9.1 add_convert_fusion
  968.9 8.0 reduce-scatter.14.cloned.1.call-done
  985.6 12.1 %fusion.18 = bf16[1024,2048]{1,0:T(8,128)(2,1)} fusion(f32[1024,2048]{1,0:T(8,128)} %subtract_add_fusion, bf16[2,1,512,2048]{3,2,1,0:T(8,128)(2,1)} %param.15, f32[1024]{0:T(1024)S(1)} %bitcast.178, f32[1024]{0:T(1024)S(1)} %bitcast.177, f32[2048]{0:T(1024)S(1)} %bitcast.169, f32[1024]{0:T(1024)S(1)} %bitcast.175, f32[512,2048]{1,0:T(8,128)} %copy-done.8, ...), kind=kLoop, calls=%fused_computation.36 | loop fusion | flops 18874368 | bytes 25186304 | tf_op jit(solution)/shard_map/convert_element_type | solution.py:477
  998.8 85.0 %reduce-scatter.10.cloned.1.call-done = bf16[128,2048]{1,0:T(8,128)(2,1)} async-done(((bf16[2048,2048]{1,0:T(8,128)(2,1)}), bf16[128,2048]{1,0:T(8,128)(2,1)}) %reduce-scatter.10.cloned.1.call-update) | async-done | bytes 524304 | tf_op jit(solution)/shard_map/reduce_scatter | solution.py:253
  (240 shorter events, 105.9 us)
Async XLA Ops:
  7.2 116.3 %all-gather.3.cloned.1.call-start = ((), (), s32[]{:S(2)}) async-start(), calls=%async_computation.5 | async-start | bytes 13926400 | tf_op jit(solution)/shard_map/all_gather | solution.py:310
  10.5 113.1 %copy-start.40 = (s32[2,1,512]{2,1,0:T(1,128)S(1)}, s32[2,1,512]{2,1,0:T(1,128)}, u32[]{:S(2)}) copy-start(s32[2,1,512]{2,1,0:T(1,128)} %param.27) | copy-start | bytes 12292
  10.5 113.4 %copy-start.41 = (s32[2,1,512]{2,1,0:T(1,128)S(1)}, s32[2,1,512]{2,1,0:T(1,128)}, u32[]{:S(2)}) copy-start(s32[2,1,512]{2,1,0:T(1,128)} %param.28) | copy-start | bytes 12292
  13.8 379.3 %all-gather.5.cloned.1.call-start = ((), (), s32[]{:S(2)}) async-start(), calls=%async_computation.6 | async-start | bytes 40108032 | tf_op jit(solution)/shard_map/all_gather | solution.py:313
  18.6 113.5 %copy-start.44 = (bf16[128]{0:T(256)(128)(2,1)S(1)}, bf16[128]{0:T(256)(128)(2,1)}, u32[]{:S(2)}) copy-start(bf16[128]{0:T(256)(128)(2,1)} %param.26) | copy-start | bytes 772
  18.6 113.5 %copy-start.45 = (bf16[128]{0:T(256)(128)(2,1)S(1)}, bf16[128]{0:T(256)(128)(2,1)}, u32[]{:S(2)}) copy-start(bf16[128]{0:T(256)(128)(2,1)} %param.25) | copy-start | bytes 772
  123.5 689.5 %reduce-scatter.6.cloned.1.call-start = ((), (), s32[]{:S(2)}) async-start(), calls=%async_computation.7 | async-start | bytes 13369344 | tf_op jit(solution)/shard_map/reduce_scatter | solution.py:253
  123.6 4.7 collective-permute-start
  128.3 5.2 collective-permute-start.1
  134.6 255.9 %copy-start.33 = (f32[2048,1]{0,1:T(1,128)}, f32[2048,1]{0,1:T(1,128)S(1)}, u32[]{:S(2)}) copy-start(f32[2048,1]{0,1:T(1,128)S(1)} %get-tuple-element.156) | copy-start | bytes 24580
  160.6 99.5 %copy-start.9 = (bf16[512,1024]{1,0:T(8,128)(2,1)}, bf16[512,1024]{1,0:T(8,128)(2,1)S(1)}, u32[]{:S(2)}) copy-start(bf16[512,1024]{1,0:T(8,128)(2,1)S(1)} %get-tuple-element.160.k0.v0) | copy-start | bytes 3145732
  160.6 107.7 %copy-start.10 = (bf16[512,1024]{1,0:T(8,128)(2,1)}, bf16[512,1024]{1,0:T(8,128)(2,1)S(1)}, u32[]{:S(2)}) copy-start(bf16[512,1024]{1,0:T(8,128)(2,1)S(1)} %get-tuple-element.159.k0.v0) | copy-start | bytes 3145732
  160.6 50.1 %collective-permute-start.7 = (bf16[512,1024]{1,0:T(8,128)(2,1)S(1)}, bf16[512,1024]{1,0:T(8,128)(2,1)S(1)}, u32[]{:S(2)}, u32[]{:S(2)}) collective-permute-start(bf16[512,1024]{1,0:T(8,128)(2,1)S(1)} %get-tuple-element.160.k0.v0), channel_id=1, source_target_pairs={{0,4},{2,6},{1,5},{3,7},{8,12},{10,14},{9,13},{11,15},{16,20},{18,... | collective-permute-start | bytes 3145736 | tf_op jit(solution)/shard_map/ppermute | solution.py:358
  164.8 90.4 %collective-permute-start.3 = (bf16[512,1024]{1,0:T(8,128)(2,1)S(1)}, bf16[512,1024]{1,0:T(8,128)(2,1)}, u32[]{:S(2)}, u32[]{:S(2)}) collective-permute-start(bf16[512,1024]{1,0:T(8,128)(2,1)S(1)} %get-tuple-element.159.k0.v0), channel_id=1, source_target_pairs={{0,4},{2,6},{1,5},{3,7},{8,12},{10,14},{9,13},{11,15},{16,20},{18,... | collective-permute-start | bytes 3145736 | tf_op jit(solution)/shard_map/ppermute | solution.py:358
  167.5 92.5 %collective-permute-start.6 = (bf16[512,1024]{1,0:T(8,128)(2,1)S(1)}, bf16[512,1024]{1,0:T(8,128)(2,1)}, u32[]{:S(2)}, u32[]{:S(2)}) collective-permute-start(bf16[512,1024]{1,0:T(8,128)(2,1)S(1)} %get-tuple-element.160.k0.v0), channel_id=1, source_target_pairs={{0,2},{2,0},{4,6},{6,4},{1,3},{3,1},{5,7},{7,5},{8,10},{10,8},{12,... | collective-permute-start | bytes 3145736 | tf_op jit(solution)/shard_map/ppermute | solution.py:357
  210.7 49.4 %copy-start.11 = (bf16[512,1024]{1,0:T(8,128)(2,1)}, bf16[512,1024]{1,0:T(8,128)(2,1)S(1)}, u32[]{:S(2)}) copy-start(bf16[512,1024]{1,0:T(8,128)(2,1)S(1)} %collective-permute-done.7.k2.v2) | copy-start | bytes 3145732
  210.7 49.3 %collective-permute-start.8 = (bf16[512,1024]{1,0:T(8,128)(2,1)S(1)}, bf16[512,1024]{1,0:T(8,128)(2,1)}, u32[]{:S(2)}, u32[]{:S(2)}) collective-permute-start(bf16[512,1024]{1,0:T(8,128)(2,1)S(1)} %collective-permute-done.7.k2.v2), channel_id=1, source_target_pairs={{0,2},{2,0},{4,6},{6,4},{1,3},{3,1},{5,7},{7,5},{8,10},{10,8},{12,... | collective-permute-start | bytes 3145736 | tf_op jit(solution)/shard_map/ppermute | solution.py:359
  213.1 61.4 %collective-permute-start.2 = (bf16[512,1024]{1,0:T(8,128)(2,1)S(1)}, bf16[512,1024]{1,0:T(8,128)(2,1)}, u32[]{:S(2)}, u32[]{:S(2)}) collective-permute-start(bf16[512,1024]{1,0:T(8,128)(2,1)S(1)} %get-tuple-element.159.k0.v0), channel_id=1, source_target_pairs={{0,2},{2,0},{4,6},{6,4},{1,3},{3,1},{5,7},{7,5},{8,10},{10,8},{12,... | collective-permute-start | bytes 3145736 | tf_op jit(solution)/shard_map/ppermute | solution.py:357
  255.2 19.3 %collective-permute-start.4 = (bf16[512,1024]{1,0:T(8,128)(2,1)}, bf16[512,1024]{1,0:T(8,128)(2,1)}, u32[]{:S(2)}, u32[]{:S(2)}) collective-permute-start(bf16[512,1024]{1,0:T(8,128)(2,1)} %collective-permute-done.3.k2.v2), channel_id=1, source_target_pairs={{0,2},{2,0},{4,6},{6,4},{1,3},{3,1},{5,7},{7,5},{8,10},{10,8},{12,... | collective-permute-start | bytes 3145736 | tf_op jit(solution)/shard_map/ppermute | solution.py:359
  288.5 42.7 %collective-permute-start.5 = (bf16[512,2048]{1,0:T(8,128)(2,1)S(1)}, bf16[512,2048]{1,0:T(8,128)(2,1)S(1)}, u32[]{:S(2)}, u32[]{:S(2)}) collective-permute-start(bf16[512,2048]{1,0:T(8,128)(2,1)S(1)} %fusion.38), channel_id=1, source_target_pairs={{0,1},{1,0},{2,3},{3,2},{4,5},{5,4},{6,7},{7,6},{8,9},{9,8},{10,11... | collective-permute-start | bytes 6291464 | tf_op jit(solution)/shard_map/ppermute | solution.py:257
  290.0 86.2 %collective-permute-start.9 = (bf16[512,2048]{1,0:T(8,128)(2,1)S(1)}, bf16[512,2048]{1,0:T(8,128)(2,1)}, u32[]{:S(2)}, u32[]{:S(2)}) collective-permute-start(bf16[512,2048]{1,0:T(8,128)(2,1)S(1)} %copy-done.18), channel_id=1, source_target_pairs={{0,1},{1,0},{2,3},{3,2},{4,5},{5,4},{6,7},{7,6},{8,9},{9,8},{10,11... | collective-permute-start | bytes 6291464 | tf_op jit(solution)/shard_map/ppermute | solution.py:257
  455.6 377.9 %reduce-scatter.8.cloned.1.call-start = ((), (), s32[]{:S(2)}) async-start(), calls=%async_computation.8 | async-start | bytes 13369344 | tf_op jit(solution)/shard_map/reduce_scatter | solution.py:253
  455.6 27.4 %copy-start.15 = (bf16[1024,2048]{1,0:T(8,128)(2,1)S(1)}, bf16[1024,2048]{1,0:T(8,128)(2,1)}, u32[]{:S(2)}) copy-start(bf16[1024,2048]{1,0:T(8,128)(2,1)} %multiply_convert_fusion.3) | copy-start | bytes 12582916
  502.6 451.9 %reduce-scatter.12.cloned.1.call-start = ((), (), s32[]{:S(2)}) async-start(), calls=%async_computation.10 | async-start | bytes 4456448 | tf_op jit(solution)/shard_map/reduce_scatter | solution.py:253
  523.3 37.7 %slice-start.2 = ((s8[6291456]{0:T(1024)(128)(4,1)}), s8[4194304]{0:T(1024)(128)(4,1)S(1)}, s32[]{:S(2)}) async-start(s8[6291456]{0:T(1024)(128)(4,1)} %bitcast.189), calls=%async_computation.14 | async-start | bytes 8388608
  548.2 42.9 %collective-permute-start.11 = (bf16[512,2048]{1,0:T(8,128)(2,1)S(1)}, bf16[512,2048]{1,0:T(8,128)(2,1)}, u32[]{:S(2)}, u32[]{:S(2)}) collective-permute-start(bf16[512,2048]{1,0:T(8,128)(2,1)S(1)} %add_convert_fusion.1), channel_id=1, source_target_pairs={{0,1},{1,0},{2,3},{3,2},{4,5},{5,4},{6,7},{7,6},{8,9},{9,8},{10,11... | collective-permute-start | bytes 6291464 | tf_op jit(solution)/shard_map/ppermute | solution.py:257
  574.5 60.7 %collective-permute-start.10 = (bf16[512,2048]{1,0:T(8,128)(2,1)}, bf16[512,2048]{1,0:T(8,128)(2,1)}, u32[]{:S(2)}, u32[]{:S(2)}) collective-permute-start(bf16[512,2048]{1,0:T(8,128)(2,1)} %add_convert_fusion.2), channel_id=1, source_target_pairs={{0,1},{1,0},{2,3},{3,2},{4,5},{5,4},{6,7},{7,6},{8,9},{9,8},{10,11... | collective-permute-start | bytes 6291464 | tf_op jit(solution)/shard_map/ppermute | solution.py:257
  667.2 309.8 %reduce-scatter.14.cloned.1.call-start = ((), (), s32[]{:S(2)}) async-start(), calls=%async_computation.11 | async-start | bytes 13369344 | tf_op jit(solution)/shard_map/reduce_scatter | solution.py:253
  667.8 416.0 %reduce-scatter.10.cloned.1.call-start = ((), (), s32[]{:S(2)}) async-start(), calls=%async_computation.9 | async-start | bytes 8912896 | tf_op jit(solution)/shard_map/reduce_scatter | solution.py:253
  667.8 145.3 %collective-permute-start.12 = (bf16[1024,2048]{1,0:T(8,128)(2,1)}, bf16[1024,2048]{1,0:T(8,128)(2,1)}, u32[]{:S(2)}, u32[]{:S(2)}) collective-permute-start(bf16[1024,2048]{1,0:T(8,128)(2,1)} %fusion.27), channel_id=1, source_target_pairs={{0,1},{1,0},{2,3},{3,2},{4,5},{5,4},{6,7},{7,6},{8,9},{9,8},{10,11... | collective-permute-start | bytes 12582920 | tf_op jit(solution)/shard_map/ppermute | solution.py:257
  692.9 32.1 %collective-permute-start.17 = (bf16[2,512,512]{2,1,0:T(8,128)(2,1)}, bf16[2,512,512]{2,1,0:T(8,128)(2,1)S(1)}, u32[]{:S(2)}, u32[]{:S(2)}) collective-permute-start(bf16[2,512,512]{2,1,0:T(8,128)(2,1)} %get-tuple-element.85), channel_id=1, source_target_pairs={{0,2},{2,0},{4,6},{6,4},{1,3},{3,1},{5,7},{7,5},{8,10},{10,8},{12,... | collective-permute-start | bytes 3145736 | tf_op jit(solution)/shard_map/ppermute | solution.py:437
  718.7 8.7 collective-permute-start.14
  724.9 6.7 collective-permute-start.16
  725.3 54.5 %collective-permute-start.18 = (bf16[2,512,512]{2,1,0:T(8,128)(2,1)S(1)}, bf16[2,512,512]{2,1,0:T(8,128)(2,1)S(1)}, u32[]{:S(2)}, u32[]{:S(2)}) collective-permute-start(bf16[2,512,512]{2,1,0:T(8,128)(2,1)S(1)} %add_convert_fusion.3), channel_id=1, source_target_pairs={{4,0},{6,2},{5,1},{7,3},{12,8},{14,10},{13,9},{15,11},{20,16},{22,... | collective-permute-start | bytes 3145736 | tf_op jit(solution)/shard_map/ppermute | solution.py:438
  726.6 70.7 %collective-permute-start.13 = (bf16[2,512,512]{2,1,0:T(8,128)(2,1)}, bf16[2,512,512]{2,1,0:T(8,128)(2,1)S(1)}, u32[]{:S(2)}, u32[]{:S(2)}) collective-permute-start(bf16[2,512,512]{2,1,0:T(8,128)(2,1)} %get-tuple-element.76), channel_id=1, source_target_pairs={{0,2},{2,0},{4,6},{6,4},{1,3},{3,1},{5,7},{7,5},{8,10},{10,8},{12,... | collective-permute-start | bytes 3145736 | tf_op jit(solution)/shard_map/ppermute | solution.py:436
  730.3 82.8 %collective-permute-start.15 = (bf16[2,512,512]{2,1,0:T(8,128)(2,1)}, bf16[2,512,512]{2,1,0:T(8,128)(2,1)}, u32[]{:S(2)}, u32[]{:S(2)}) collective-permute-start(bf16[2,512,512]{2,1,0:T(8,128)(2,1)} %add_convert_fusion.4), channel_id=1, source_target_pairs={{4,0},{6,2},{5,1},{7,3},{12,8},{14,10},{13,9},{15,11},{20,16},{22,... | collective-permute-start | bytes 3145736 | tf_op jit(solution)/shard_map/ppermute | solution.py:438
  797.3 99.2 %copy-start.12 = (bf16[512,2048]{1,0:T(8,128)(2,1)}, bf16[512,2048]{1,0:T(8,128)(2,1)S(1)}, u32[]{:S(2)}) copy-start(bf16[512,2048]{1,0:T(8,128)(2,1)S(1)} %fusion.44) | copy-start | bytes 6291460
  847.8 51.1 %copy-start.42 = (f32[2,128]{1,0:T(2,128)S(1)}, f32[2,128]{1,0:T(2,128)}, u32[]{:S(2)}) copy-start(f32[2,128]{1,0:T(2,128)} %get-tuple-element.95) | copy-start | bytes 3076
  847.8 51.1 %copy-start.43 = (f32[2,128]{1,0:T(2,128)S(1)}, f32[2,128]{1,0:T(2,128)}, u32[]{:S(2)}) copy-start(f32[2,128]{1,0:T(2,128)} %get-tuple-element.96) | copy-start | bytes 3076
  847.8 48.7 %collective-permute-start.19 = (bf16[512,2048]{1,0:T(8,128)(2,1)S(1)}, bf16[512,2048]{1,0:T(8,128)(2,1)}, u32[]{:S(2)}, u32[]{:S(2)}) collective-permute-start(bf16[512,2048]{1,0:T(8,128)(2,1)S(1)} %fusion.44), channel_id=1, source_target_pairs={{0,1},{1,0},{2,3},{3,2},{4,5},{5,4},{6,7},{7,6},{8,9},{9,8},{10,11... | collective-permute-start | bytes 6291464 | tf_op jit(solution)/shard_map/ppermute | solution.py:257
  848.2 91.5 %collective-permute-start.20 = (bf16[512,2048]{1,0:T(8,128)(2,1)}, bf16[512,2048]{1,0:T(8,128)(2,1)}, u32[]{:S(2)}, u32[]{:S(2)}) collective-permute-start(bf16[512,2048]{1,0:T(8,128)(2,1)} %fusion.47), channel_id=1, source_target_pairs={{0,1},{1,0},{2,3},{3,2},{4,5},{5,4},{6,7},{7,6},{8,9},{9,8},{10,11... | collective-permute-start | bytes 6291464 | tf_op jit(solution)/shard_map/ppermute | solution.py:257
  851.1 88.7 %copy-start.13 = (bf16[512,2048]{1,0:T(8,128)(2,1)S(1)}, bf16[512,2048]{1,0:T(8,128)(2,1)}, u32[]{:S(2)}) copy-start(bf16[512,2048]{1,0:T(8,128)(2,1)} %fusion.47) | copy-start | bytes 6291460
  898.8 47.9 %copy-start.7 = (f32[512,2048]{1,0:T(8,128)}, f32[512,2048]{1,0:T(8,128)S(1)}, u32[]{:S(2)}) copy-start(f32[512,2048]{1,0:T(8,128)S(1)} %convert_add_fusion.1) | copy-start | bytes 12582916
  954.4 2.1 collective-permute-start.21
  956.6 9.2 collective-permute-start.22
  965.8 13.6 %collective-permute-start.23 = (f32[34,128]{1,0:T(8,128)S(1)}, f32[34,128]{1,0:T(8,128)S(1)}, u32[]{:S(2)}, u32[]{:S(2)}) collective-permute-start(f32[34,128]{1,0:T(8,128)S(1)} %fusion.86), channel_id=1, source_target_pairs={{0,8},{8,0},{16,24},{24,16},{1,9},{9,1},{17,25},{25,17},{2,10},{10... | collective-permute-start | bytes 52232 | tf_op jit(solution)/shard_map/ppermute | solution.py:268
  979.4 4.7 collective-permute-start.24
  984.2 13.6 %collective-permute-start.25 = (f32[34,128]{1,0:T(8,128)S(1)}, f32[34,128]{1,0:T(8,128)S(1)}, u32[]{:S(2)}, u32[]{:S(2)}) collective-permute-start(f32[34,128]{1,0:T(8,128)S(1)} %add.135), channel_id=1, source_target_pairs={{0,1},{1,0},{2,3},{3,2},{4,5},{5,4},{6,7},{7,6},{8,9},{9,8},{10,11... | collective-permute-start | bytes 52232 | tf_op jit(solution)/shard_map/ppermute | solution.py:268
  (36 other events, 305.5 us)
Sparse Core Ops, SparseCore 0:
  13.9 109.4 all-gather.2
  125.0 235.1 all-gather.4
  455.7 149.1 reduce-scatter.5
  608.8 144.5 reduce-scatter.7
  757.2 81.5 reduce-scatter.11
  842.7 134.2 reduce-scatter.13
  981.0 102.7 reduce-scatter.9

commit v4 on v3

--- a/solution.py
+++ b/solution.py
@@ -243,11 +243,38 @@
     )(raw, turn, gains, dq, d_own, d_near, d_far)
 
 
+def move_kernel(rank, source, out):
+    out[...] = source[...]
+
+
+def relative(values, rank, dp_size, seq_size):
+    total, width = values.shape
+    lanes = width // (dp_size * seq_size)
+
+    def pick(step, rank):
+        turn = step // dp_size
+        flip = (turn % 2) * 2 + turn // 2
+        return (0, (step % dp_size) * seq_size + jnp.bitwise_xor(rank[0], flip))
+
+    return pl.pallas_call(
+        move_kernel,
+        grid_spec=pltpu.PrefetchScalarGridSpec(
+            num_scalar_prefetch=1,
+            grid=(dp_size * seq_size,),
+            in_specs=[pl.BlockSpec((total, lanes), pick)],
+            out_specs=pl.BlockSpec((total, lanes), lambda step, rank: (0, step)),
+        ),
+        out_shape=jax.ShapeDtypeStruct(values.shape, values.dtype),
+        name="relative",
+    )(rank.reshape(1).astype(jnp.int32), values)
+
+
 def make_local(mp_size, seq_size, dp_size):
     data_axes = ("dp", "seq")
     pair = [(i, i ^ 1) for i in range(seq_size)]
     up_pairs = [(i, i + 2) for i in range(seq_size - 2)]
     down_pairs = [(i + 2, i) for i in range(seq_size - 2)]
+    cross = [(i, i ^ 2) for i in range(seq_size)]
 
     def scatter(grad):
         return lax.psum_scatter(grad, data_axes, scatter_dimension=0, tiled=True)
@@ -260,6 +287,27 @@
     def mp_part(part):
         part = lax.optimization_barrier(part.astype(BF16))
         return part, mp_other(part)
+
+    def pair_stage(left, right):
+        half = left.shape[1] // 2
+        theirs = tdot(left[:, half:], right).astype(BF16)
+        got = lax.ppermute(theirs, "seq", pair)
+        return (tdot(left[:, :half], right) + got.astype(F32)).astype(BF16)
+
+    def cross_stage(block):
+        half = block.shape[0] // 2
+        got = lax.ppermute(block[half:], "seq", cross)
+        return (block[:half].astype(F32) + got.astype(F32)).astype(BF16)
+
+    def line_stage(block):
+        place = lax.axis_index("dp")
+        blocks = block.reshape(dp_size, -1, block.shape[1])
+        owned = lax.dynamic_index_in_dim(blocks, place, 0, False).astype(F32)
+        for flip in range(1, dp_size):
+            sent = lax.dynamic_index_in_dim(blocks, jnp.bitwise_xor(place, flip), 0, False)
+            moves = [(i, i ^ flip) for i in range(dp_size)]
+            owned = owned + lax.ppermute(sent, "dp", moves).astype(F32)
+        return owned
 
     def butterfly(value, axis, size):
         flip = 1
@@ -396,13 +444,13 @@
             backs.append(
                 mp_part(rdot(grad_gate_in[cut], gate_full) + rdot(grad_up_in[cut], up_full))
             )
+        ffn_rel = relative(normed_ffn, rank, dp_size, seq_size)
+        up_block = pair_stage(ffn_rel, grad_up_in)
         gate_grad = tdot(normed_ffn, grad_gate_in).astype(BF16)
         gate_owned = scatter(gate_grad)
-        up_grad = tdot(normed_ffn, grad_up_in).astype(BF16)
-        up_owned = scatter(up_grad)
         down_mine = lax.optimization_barrier(rdot(act, down_t).astype(BF16))
-        backs, gate_grad, up_grad, down_mine = lax.optimization_barrier(
-            (backs, gate_grad, up_grad, down_mine)
+        backs, gate_grad, up_block, down_mine = lax.optimization_barrier(
+            (backs, gate_grad, up_block, down_mine)
         )
         down_other = mp_other(down_mine)
         gain_ffn_part = jnp.concatenate([mine for mine, _ in backs], axis=0).astype(F32)
@@ -413,6 +461,7 @@
         grad_middle_b = grad_middle.astype(BF16)
         grad_heads = dot(grad_middle_b, w_out_t).astype(BF16)
         out_owned = scatter(tdot(grad_middle_b, attn_heads).astype(BF16))
+        up_block = cross_stage(up_block)
 
         grads_in = []
         head_sums = []
@@ -438,24 +487,26 @@
             far = lax.ppermute(
                 (d_far + got_far.astype(F32)).astype(BF16), "seq", down_pairs
             )
+            if step == 0:
+                up_block, d_own = lax.optimization_barrier((up_block, d_own))
+                up_owned = line_stage(up_block)
             sides.append((grad_q, d_own, got, far))
         for step in range(MICRO):
-            if step == MICRO - 1:
-                down_other, down_owned, side = lax.optimization_barrier(
-                    (down_other, down_owned, sides[step])
-                )
+            side = sides[step]
+            if step == 0:
+                down_other, side = lax.optimization_barrier((down_other, side))
             else:
-                side = sides[step]
+                down_owned, side = lax.optimization_barrier((down_owned, side))
             grad_in, sums = rope_back(raw, turn, gain_heads, *side, step, q_cols, k_cols)
             grads_in.append(grad_in)
             head_sums.append(sums)
         layer_out = (middle + (down_mine.astype(F32) + down_other.astype(F32))).astype(BF16)
         backs = [mp_part(rdot(grad_in, w_qkv)) for grad_in in grads_in]
         grad_qkv_in = jnp.concatenate(grads_in, axis=0)
-        mines = [mine for mine, _ in backs]
-        grad_qkv_in, gate_owned, mines = lax.optimization_barrier(
-            (grad_qkv_in, gate_owned, mines)
-        )
+        grad_qkv_in, gate_owned, up_owned, backs[0], mine = lax.optimization_barrier(
+            (grad_qkv_in, gate_owned, up_owned, backs[0], backs[1][0])
+        )
+        backs[1] = (mine, backs[1][1])
         qkv_owned = scatter(tdot(normed_attn, grad_qkv_in).astype(BF16))
         gain_attn_part = jnp.concatenate([mine for mine, _ in backs], axis=0).astype(F32)
         gain_attn_part = jnp.sum(gain_attn_part * tokens * inv_attn, axis=0)

time: 1100 us -> 1020 us (0.927)
  waiting for transfers between devices: 561 us -> 437 us
  starting transfers between devices: 45.2 us -> 68.8 us
    reduce_scatter x5 -> x4, waiting for transfers between devices: 93 us -> 8.15 us  [scatter(): return lax.psum_scatter(grad, data_axes, scatter_dimension=0, tiled=True)]
    ppermute x7, waiting for transfers between devices: 210 us -> 146 us  [mp_other(): return lax.ppermute(part, 'mp', [(0, 1), (1, 0)])]
    ppermute x0 -> x5, waiting for transfers between devices: none -> 62.8 us  [the longest x3 53.1 us: line_stage(): owned = owned + lax.ppermute(sent, 'dp', moves).astype(F32)]
    ppermute x2, waiting for transfers between devices: 64 us -> 23 us  [local(): lax.ppermute((d_far + got_far.astype(F32)).astype(BF16), 'seq', down_pairs)]
    ppermute x5, starting transfers between devices: 3.46 us -> 27 us  [butterfly(): value = value + lax.ppermute(value, axis, moves)]
    dot_general x5 -> x6, matrix products: 79.4 us -> 85.9 us  [tdot(): lax.dot_general(left, right, (((0,), (0,)), ((), ())), preferred_element_...]
    unnamed x117 -> x121, local copies, waits for them, and re-layouts: 19.9 us -> 22.1 us
  transfers between devices with their start and end apart: 33 -> 37, of which waited for: 15 -> 14; matrix products, arithmetic and copies ran while one was open for 30% -> 32% of each run, Pallas kernels for 6% -> 8%
where the time goes in v4:
time: 1020 us; the launch traced here: 1010 us
  waiting for transfers between devices  437 us (43%)
  matrix products  273 us (27%)
  other arithmetic  91.5 us (9%)
  Pallas kernels  78.5 us (8%)
  starting transfers between devices  68.8 us (7%)
  local copies, waits for them, and re-layouts  42 us (4%)
  between operations  15.5 us (2%)
    ppermute x7, waiting for transfers between devices, mp_other(): return lax.ppermute(part, 'mp', [(0, 1), (1, 0)])  146 us
    all_gather x1, waiting for transfers between devices, local(): first = lax.all_gather(first, data_axes, axis=0, tiled=True)  105 us
    dot_general x5, matrix products, dot(): return jnp.dot(left, right, preferred_element_type=F32)  95.2 us
    dot_general x9, matrix products, rdot(): lax.dot_general(left, right, (((1,), (1,)), ((), ())), preferred_element_...  91.6 us
    dot_general x6, matrix products, tdot(): lax.dot_general(left, right, (((0,), (0,)), ((), ())), preferred_element_...  85.9 us
    ppermute x2, waiting for transfers between devices, local(): far = lax.ppermute(own, 'seq', up_pairs)  84 us
    ppermute x3, waiting for transfers between devices, line_stage(): owned = owned + lax.ppermute(sent, 'dp', moves).astype(F32)  53.1 us
    ppermute x5, starting transfers between devices, butterfly(): value = value + lax.ppermute(value, axis, moves)  27 us
  transfers between devices with their start and end apart: 37, of which 14 were waited for; matrix products, arithmetic and copies ran while one was open for 32% of the time, Pallas kernels for 8%

profile of v4, /device:TPU:0, one launch (start us, length us, event | category | flops | bytes accessed | tf_op | source)
XLA Modules:
  0.0 1005.9 jit_solution(15522072362840346172)
XLA Ops:
  18.6 104.9 %all-gather.3.cloned.1.call-done = bf16[2048,3200]{0,1:T(8,128)(2,1)} async-done(((bf16[128,3200]{0,1:T(8,128)(2,1)}), bf16[2048,3200]{0,1:T(8,128)(2,1)}) %all-gather.3.cloned.1.call-update) | async-done | bytes 13107216 | tf_op jit(solution)/shard_map/all_gather | solution.py:358
  138.2 11.0 %fusion.23.raw = f32[1024,2048]{1,0:T(8,128)} fusion(bf16[1024,2048]{1,0:T(8,128)(2,1)S(1)} %fusion.14, bf16[2048,3200]{0,1:T(8,128)(2,1)S(1)} %copy-done.50), kind=kOutput, calls=%fused_computation.48 | convolution fusion | flops 8589934592 | bytes 20971520 | tf_op jit(solution)/shard_map/dot_general | solution.py:25
  149.2 9.3 rope.1
  167.4 43.4 %collective-permute-done.7.k2.v2 = bf16[512,1024]{1,0:T(8,128)(2,1)S(1)} collective-permute-done((bf16[512,1024]{1,0:T(8,128)(2,1)S(1)}, bf16[512,1024]{1,0:T(8,128)(2,1)S(1)}, u32[]{:S(2)}, u32[]{:S(2)}) %collective-permute-start.7) | collective-permute-done | bytes 1048608 | tf_op jit(solution)/shard_map/ppermute | solution.py:406
  214.6 40.6 %collective-permute-done.3.k2.v2 = bf16[512,1024]{1,0:T(8,128)(2,1)} collective-permute-done((bf16[512,1024]{1,0:T(8,128)(2,1)S(1)}, bf16[512,1024]{1,0:T(8,128)(2,1)}, u32[]{:S(2)}, u32[]{:S(2)}) %collective-permute-start.3) | collective-permute-done | bytes 1048608 | tf_op jit(solution)/shard_map/ppermute | solution.py:406
  260.1 8.2 attend.3
  268.3 6.2 fusion.41
  276.0 9.1 attend.2
  285.1 5.1 fusion.38
  295.1 25.3 %collective-permute-done.9 = bf16[512,2048]{1,0:T(8,128)(2,1)} collective-permute-done((bf16[512,2048]{1,0:T(8,128)(2,1)}, bf16[512,2048]{1,0:T(8,128)(2,1)}, u32[]{:S(2)}, u32[]{:S(2)}) %collective-permute-start.9) | collective-permute-done | bytes 2097184 | tf_op jit(solution)/shard_map/ppermute | solution.py:284
  320.4 44.9 %collective-permute-done.5 = bf16[512,2048]{1,0:T(8,128)(2,1)} collective-permute-done((bf16[512,2048]{1,0:T(8,128)(2,1)S(1)}, bf16[512,2048]{1,0:T(8,128)(2,1)}, u32[]{:S(2)}, u32[]{:S(2)}) %collective-permute-start.5) | collective-permute-done | bytes 2097184 | tf_op jit(solution)/shard_map/ppermute | solution.py:284
  365.3 9.5 fusion.26
  382.2 19.1 %fusion.5 = f32[1024,3072]{1,0:T(8,128)} fusion(bf16[1024,2048]{1,0:T(8,128)(2,1)} %multiply_convert_fusion.3.source, bf16[3,2048,3072]{1,2,0:T(8,128)(2,1)} %all-gather.5.cloned.1.call-done), kind=kOutput, calls=%fused_computation.15 | convolution fusion | flops 12884901888 | bytes 29360128 | tf_op jit(solution)/shard_map/dot_general | solution.py:25
  401.3 23.8 %multiply_convert_fusion.2 = (bf16[1024,3072]{1,0:T(8,128)(2,1)}, f32[1024,3072]{1,0:T(8,128)}) fusion(f32[1024,3072]{1,0:T(8,128)} %fusion.5, bf16[1024,2048]{1,0:T(8,128)(2,1)} %multiply_convert_fusion.3.source, bf16[3,2048,3072]{1,2,0:T(8,128)(2,1)} %all-gather.5.cloned.1.call-done), kind=kOutput, calls=%fused_computation.7 | convolution fusion | flops 12903776256 | bytes 48234496 | tf_op jit(solution)/shard_map/dot_general | solution.py:25
  425.1 19.3 %convert_bitcast_fusion = bf16[2048,3072]{1,0:T(8,128)(2,1)} fusion(bf16[1024,3072]{1,0:T(8,128)(2,1)} %get-tuple-element.78, bf16[1024,2048]{1,0:T(8,128)(2,1)} %bitcast.172), kind=kOutput, calls=%fused_computation.6 | convolution fusion | flops 12891193344 | bytes 23068672 | tf_op jit(solution)/shard_map/dot_general | solution.py:29
  444.5 10.6 %relative.1 = bf16[1024,2048]{1,0:T(8,128)(2,1)} custom-call(s32[1]{0:T(128)} %bitcast.29.rank, bf16[1024,2048]{1,0:T(8,128)(2,1)} %multiply_convert_fusion.3.source), custom_call_target="tpu_custom_call" | custom-call | tf_op jit(solution)/shard_map/relative/pallas_call | solution.py:259
  455.1 30.8 %multiply_convert_fusion = (bf16[1024,3072]{1,0:T(8,128)(2,1)}, bf16[1024,3072]{1,0:T(8,128)(2,1)}) fusion(f32[1024,3072]{1,0:T(8,128)} %fusion.5, f32[1024,3072]{1,0:T(8,128)} %get-tuple-element.212, bf16[1024,2048]{1,0:T(8,128)(2,1)} %bitcast.173, bf16[3,2048,3072]{1,2,0:T(8,128)(2,1)} %all-gather.5.cloned.1.call-done), kind=kOutput, calls=%fused_computation.4 | convolution fusion | flops 12925796352 | bytes 54525952 | tf_op jit(solution)/shard_map/dot_general | solution.py:25
  485.9 18.6 %convolution_convert_fusion = bf16[2048,3072]{1,0:T(8,128)(2,1)} fusion(bf16[1024,2048]{1,0:T(8,128)(2,1)S(1)} %copy-done.14, bf16[1024,3072]{1,0:T(8,128)(2,1)} %get-tuple-element.176), kind=kOutput, calls=%fused_computation.10 | convolution fusion | flops 12891193344 | bytes 23068672 | tf_op jit(solution)/shard_map/dot_general | solution.py:29
  504.6 12.5 %convolution_convert_fusion.2 = bf16[1024,3072]{1,0:T(8,128)(2,1)} fusion(bf16[1024,3072]{1,0:T(8,128)(2,1)} %get-tuple-element.175, bf16[1024,2048]{1,0:T(8,128)(2,1)} %relative.1), kind=kOutput, calls=%fused_computation.51 | convolution fusion | flops 6445596672 | bytes 14680064 | tf_op jit(solution)/shard_map/dot_general | solution.py:29
  518.9 10.6 %fusion.3 = f32[512,2048]{1,0:T(8,128)S(1)} fusion(bf16[3,2048,3072]{1,2,0:T(8,128)(2,1)} %all-gather.5.cloned.1.call-done, bf16[1024,3072]{1,0:T(8,128)(2,1)} %get-tuple-element.176), kind=kOutput, calls=%fused_computation.13 | convolution fusion | flops 6442450944 | bytes 19922944 | tf_op jit(solution)/shard_map/dot_general | solution.py:33
  529.5 9.9 add_convert_fusion.3
  541.0 10.6 %fusion.4 = f32[512,2048]{1,0:T(8,128)S(1)} fusion(bf16[3,2048,3072]{1,2,0:T(8,128)(2,1)} %all-gather.5.cloned.1.call-done, bf16[1024,3072]{1,0:T(8,128)(2,1)} %get-tuple-element.176), kind=kOutput, calls=%fused_computation.14 | convolution fusion | flops 6442450944 | bytes 19922944 | tf_op jit(solution)/shard_map/dot_general | solution.py:33
  551.6 10.0 add_convert_fusion.4
  562.4 20.3 %fusion.27 = bf16[1024,2048]{1,0:T(8,128)(2,1)} fusion(bf16[1024,3072]{1,0:T(8,128)(2,1)} %get-tuple-element.78, bf16[3,2048,3072]{1,2,0:T(8,128)(2,1)} %all-gather.5.cloned.1.call-done), kind=kOutput, calls=%fused_computation.64 | convolution fusion | flops 12886999040 | bytes 23068672 | tf_op jit(solution)/shard_map/dot_general | solution.py:33
  582.7 11.3 %add_convert_fusion = bf16[1024,3072]{1,0:T(8,128)(2,1)S(1)} fusion(bf16[1024,3072]{1,0:T(8,128)(2,1)} %collective-permute-done.12, bf16[1024,3072]{1,0:T(8,128)(2,1)} %get-tuple-element.175, bf16[1024,2048]{1,0:T(8,128)(2,1)S(1)} %copy-done.22), kind=kOutput, calls=%fused_computation.3 | convolution fusion | flops 6451888128 | bytes 20971520 | tf_op jit(solution)/shard_map/dot_general | solution.py:29
  594.1 38.1 %collective-permute-done.10 = bf16[512,2048]{1,0:T(8,128)(2,1)S(1)} collective-permute-done((bf16[512,2048]{1,0:T(8,128)(2,1)S(1)}, bf16[512,2048]{1,0:T(8,128)(2,1)S(1)}, u32[]{:S(2)}, u32[]{:S(2)}) %collective-permute-start.10) | collective-permute-done | bytes 2097184 | tf_op jit(solution)/shard_map/ppermute | solution.py:284
  634.1 6.1 collective-permute-start.14
  651.0 7.8 subtract_add_fusion
  658.8 10.5 %fusion.64.g_out = bf16[1024,1024]{1,0:T(8,128)(2,1)} fusion(bf16[2048,3200]{0,1:T(8,128)(2,1)} %all-gather.3.cloned.1.call-done, f32[1024,2048]{1,0:T(8,128)} %subtract_add_fusion), kind=kOutput, calls=%fused_computation.91 | convolution fusion | flops 4298113024 | bytes 14680064 | tf_op jit(solution)/shard_map/dot_general | solution.py:25
  669.3 12.8 %attend_back.2 = (f32[512,1024]{1,0:T(8,128)}, f32[2,512,512]{2,1,0:T(8,128)}, bf16[2,512,512]{2,1,0:T(8,128)(2,1)}, f32[2,512,512]{2,1,0:T(8,128)}, bf16[2,512,512]{2,1,0:T(8,128)(2,1)}) custom-call(s32[4]{0:T(128)} %get-tuple-element.209.need, bf16[1024,1024]{1,0:T(8,128)(2,1)} %get-tuple-element.71.q, bf16[1024,1024]{1,0:T(8,128)(2,1)} %fusion.64.g_out, ...), custom_call_target="tpu_custom_call" | custom-call | tf_op jit(solution)/shard_map/attend_back/pallas_call | solution.py:137
  682.1 5.1 collective-permute-start.16
  687.4 12.9 %attend_back.3 = (f32[512,1024]{1,0:T(8,128)}, f32[2,512,512]{2,1,0:T(8,128)}, bf16[2,512,512]{2,1,0:T(8,128)(2,1)}, f32[2,512,512]{2,1,0:T(8,128)}, bf16[2,512,512]{2,1,0:T(8,128)(2,1)}) custom-call(s32[4]{0:T(128)} %get-tuple-element.210.need, bf16[1024,1024]{1,0:T(8,128)(2,1)} %get-tuple-element.71.q, bf16[1024,1024]{1,0:T(8,128)(2,1)} %fusion.64.g_out, ...), custom_call_target="tpu_custom_call" | custom-call | tf_op jit(solution)/shard_map/attend_back/pallas_call | solution.py:137
  700.3 6.6 collective-permute-start.19
  706.9 9.8 convolution_convert_fusion.3
  723.1 9.6 collective-permute-done.14
  739.6 23.0 %collective-permute-done.17.d_far = bf16[2,512,512]{2,1,0:T(8,128)(2,1)} collective-permute-done((bf16[2,512,512]{2,1,0:T(8,128)(2,1)S(1)}, bf16[2,512,512]{2,1,0:T(8,128)(2,1)}, u32[]{:S(2)}, u32[]{:S(2)}) %collective-permute-start.17) | collective-permute-done | bytes 1048608 | tf_op jit(solution)/shard_map/ppermute | solution.py:487
  762.6 7.9 rope_back.2
  770.4 10.4 %fusion.44 = bf16[512,2048]{1,0:T(8,128)(2,1)} fusion(bf16[512,2048]{1,0:T(8,128)(2,1)} %get-tuple-element.97, bf16[2048,3200]{0,1:T(8,128)(2,1)} %all-gather.3.cloned.1.call-done), kind=kOutput, calls=%fused_computation.78 | convolution fusion | flops 4296015872 | bytes 12582912 | tf_op jit(solution)/shard_map/dot_general | solution.py:33
  781.7 53.1 %collective-permute-done.22 = bf16[128,3072]{1,0:T(8,128)(2,1)} collective-permute-done((bf16[128,3072]{1,0:T(8,128)(2,1)}, bf16[128,3072]{1,0:T(8,128)(2,1)}, u32[]{:S(2)}, u32[]{:S(2)}) %collective-permute-start.22) | collective-permute-done | bytes 786464 | tf_op jit(solution)/shard_map/ppermute | solution.py:309
  838.1 7.7 rope_back.3
  845.8 8.7 fusion.47
  857.2 14.4 %convolution_convert_fusion.1 = bf16[2048,2048]{1,0:T(8,128)(2,1)} fusion(bf16[1024,2048]{1,0:T(8,128)(2,1)} %copy-done.21, bf16[1024,2048]{1,0:T(8,128)(2,1)} %pad_maximum_fusion.2), kind=kOutput, calls=%fused_computation.43 | convolution fusion | flops 8594128896 | bytes 16777216 | tf_op jit(solution)/shard_map/dot_general | solution.py:29
  877.0 38.1 %collective-permute-done.25 = bf16[512,2048]{1,0:T(8,128)(2,1)} collective-permute-done((bf16[512,2048]{1,0:T(8,128)(2,1)S(1)}, bf16[512,2048]{1,0:T(8,128)(2,1)}, u32[]{:S(2)}, u32[]{:S(2)}) %collective-permute-start.25) | collective-permute-done | bytes 2097184 | tf_op jit(solution)/shard_map/ppermute | solution.py:284
  923.7 6.3 fusion.10
  930.9 6.0 add_convert_fusion.1
  940.7 25.5 %collective-permute-start.28 = (f32[34,128]{1,0:T(8,128)S(1)}, f32[34,128]{1,0:T(8,128)S(1)}, u32[]{:S(2)}, u32[]{:S(2)}) collective-permute-start(f32[34,128]{1,0:T(8,128)S(1)} %fusion.93), channel_id=1, source_target_pairs={{0,8},{8,0},{16,24},{24,16},{1,9},{9,1},{17,25},{25,17},{2,10},{10... | collective-permute-start | bytes 52232 | tf_op jit(solution)/shard_map/ppermute | solution.py:316
  975.5 10.3 %fusion.18 = bf16[1024,2048]{1,0:T(8,128)(2,1)} fusion(f32[1024,2048]{1,0:T(8,128)} %subtract_add_fusion, bf16[2,1,512,2048]{3,2,1,0:T(8,128)(2,1)} %param.15, f32[1024]{0:T(1024)S(1)} %bitcast.191, f32[1024]{0:T(1024)S(1)} %bitcast.190, f32[2048]{0:T(1024)S(1)} %bitcast.182, f32[1024]{0:T(1024)S(1)} %bitcast.188, f32[512,2048]{1,0:T(8,128)} %copy-done.10, ...), kind=kLoop, calls=%fused_computation.36 | loop fusion | flops 18874368 | bytes 25186304 | tf_op jit(solution)/shard_map/convert_element_type | solution.py:528
  986.9 8.1 reduce-scatter.9.cloned.1.call-done
  (255 shorter events, 126.7 us)
Async XLA Ops:
  7.2 116.3 %all-gather.3.cloned.1.call-start = ((), (), s32[]{:S(2)}) async-start(), calls=%async_computation.4 | async-start | bytes 13926400 | tf_op jit(solution)/shard_map/all_gather | solution.py:358
  13.8 368.4 %all-gather.5.cloned.1.call-start = ((), (), s32[]{:S(2)}) async-start(), calls=%async_computation.5 | async-start | bytes 40108032 | tf_op jit(solution)/shard_map/all_gather | solution.py:361
  15.4 108.2 %copy-start.43 = (s32[2,1,512]{2,1,0:T(1,128)S(1)}, s32[2,1,512]{2,1,0:T(1,128)}, u32[]{:S(2)}) copy-start(s32[2,1,512]{2,1,0:T(1,128)} %param.27) | copy-start | bytes 12292
  15.4 108.5 %copy-start.45 = (s32[2,1,512]{2,1,0:T(1,128)S(1)}, s32[2,1,512]{2,1,0:T(1,128)}, u32[]{:S(2)}) copy-start(s32[2,1,512]{2,1,0:T(1,128)} %param.28) | copy-start | bytes 12292
  123.5 714.6 %reduce-scatter.5.cloned.1.call-start = ((), (), s32[]{:S(2)}) async-start(), calls=%async_computation.6 | async-start | bytes 13369344 | tf_op jit(solution)/shard_map/reduce_scatter | solution.py:280
  123.6 4.7 collective-permute-start
  128.3 5.2 collective-permute-start.1
  134.6 245.0 %copy-start.37 = (f32[2048,1]{0,1:T(1,128)}, f32[2048,1]{0,1:T(1,128)S(1)}, u32[]{:S(2)}) copy-start(f32[2048,1]{0,1:T(1,128)S(1)} %get-tuple-element.178) | copy-start | bytes 24580
  160.6 99.5 %copy-start.11 = (bf16[512,1024]{1,0:T(8,128)(2,1)}, bf16[512,1024]{1,0:T(8,128)(2,1)S(1)}, u32[]{:S(2)}) copy-start(bf16[512,1024]{1,0:T(8,128)(2,1)S(1)} %get-tuple-element.185.k0.v0) | copy-start | bytes 3145732
  160.6 107.7 %copy-start.12 = (bf16[512,1024]{1,0:T(8,128)(2,1)}, bf16[512,1024]{1,0:T(8,128)(2,1)S(1)}, u32[]{:S(2)}) copy-start(bf16[512,1024]{1,0:T(8,128)(2,1)S(1)} %get-tuple-element.184.k0.v0) | copy-start | bytes 3145732
  160.6 50.1 %collective-permute-start.7 = (bf16[512,1024]{1,0:T(8,128)(2,1)S(1)}, bf16[512,1024]{1,0:T(8,128)(2,1)S(1)}, u32[]{:S(2)}, u32[]{:S(2)}) collective-permute-start(bf16[512,1024]{1,0:T(8,128)(2,1)S(1)} %get-tuple-element.185.k0.v0), channel_id=1, source_target_pairs={{0,4},{2,6},{1,5},{3,7},{8,12},{10,14},{9,13},{11,15},{16,20},{18,... | collective-permute-start | bytes 3145736 | tf_op jit(solution)/shard_map/ppermute | solution.py:406
  164.8 90.4 %collective-permute-start.3 = (bf16[512,1024]{1,0:T(8,128)(2,1)S(1)}, bf16[512,1024]{1,0:T(8,128)(2,1)}, u32[]{:S(2)}, u32[]{:S(2)}) collective-permute-start(bf16[512,1024]{1,0:T(8,128)(2,1)S(1)} %get-tuple-element.184.k0.v0), channel_id=1, source_target_pairs={{0,4},{2,6},{1,5},{3,7},{8,12},{10,14},{9,13},{11,15},{16,20},{18,... | collective-permute-start | bytes 3145736 | tf_op jit(solution)/shard_map/ppermute | solution.py:406
  167.3 92.8 %collective-permute-start.6 = (bf16[512,1024]{1,0:T(8,128)(2,1)S(1)}, bf16[512,1024]{1,0:T(8,128)(2,1)}, u32[]{:S(2)}, u32[]{:S(2)}) collective-permute-start(bf16[512,1024]{1,0:T(8,128)(2,1)S(1)} %get-tuple-element.185.k0.v0), channel_id=1, source_target_pairs={{0,2},{2,0},{4,6},{6,4},{1,3},{3,1},{5,7},{7,5},{8,10},{10,8},{12,... | collective-permute-start | bytes 3145736 | tf_op jit(solution)/shard_map/ppermute | solution.py:405
  210.7 49.3 %copy-start.13 = (bf16[512,1024]{1,0:T(8,128)(2,1)}, bf16[512,1024]{1,0:T(8,128)(2,1)S(1)}, u32[]{:S(2)}) copy-start(bf16[512,1024]{1,0:T(8,128)(2,1)S(1)} %collective-permute-done.7.k2.v2) | copy-start | bytes 3145732
  210.7 49.3 %collective-permute-start.8 = (bf16[512,1024]{1,0:T(8,128)(2,1)S(1)}, bf16[512,1024]{1,0:T(8,128)(2,1)}, u32[]{:S(2)}, u32[]{:S(2)}) collective-permute-start(bf16[512,1024]{1,0:T(8,128)(2,1)S(1)} %collective-permute-done.7.k2.v2), channel_id=1, source_target_pairs={{0,2},{2,0},{4,6},{6,4},{1,3},{3,1},{5,7},{7,5},{8,10},{10,8},{12,... | collective-permute-start | bytes 3145736 | tf_op jit(solution)/shard_map/ppermute | solution.py:407
  213.1 62.9 %collective-permute-start.2 = (bf16[512,1024]{1,0:T(8,128)(2,1)S(1)}, bf16[512,1024]{1,0:T(8,128)(2,1)}, u32[]{:S(2)}, u32[]{:S(2)}) collective-permute-start(bf16[512,1024]{1,0:T(8,128)(2,1)S(1)} %get-tuple-element.184.k0.v0), channel_id=1, source_target_pairs={{0,2},{2,0},{4,6},{6,4},{1,3},{3,1},{5,7},{7,5},{8,10},{10,8},{12,... | collective-permute-start | bytes 3145736 | tf_op jit(solution)/shard_map/ppermute | solution.py:405
  255.2 20.8 %collective-permute-start.4 = (bf16[512,1024]{1,0:T(8,128)(2,1)}, bf16[512,1024]{1,0:T(8,128)(2,1)}, u32[]{:S(2)}, u32[]{:S(2)}) collective-permute-start(bf16[512,1024]{1,0:T(8,128)(2,1)} %collective-permute-done.3.k2.v2), channel_id=1, source_target_pairs={{0,2},{2,0},{4,6},{6,4},{1,3},{3,1},{5,7},{7,5},{8,10},{10,8},{12,... | collective-permute-start | bytes 3145736 | tf_op jit(solution)/shard_map/ppermute | solution.py:407
  274.5 45.9 %collective-permute-start.9 = (bf16[512,2048]{1,0:T(8,128)(2,1)}, bf16[512,2048]{1,0:T(8,128)(2,1)}, u32[]{:S(2)}, u32[]{:S(2)}) collective-permute-start(bf16[512,2048]{1,0:T(8,128)(2,1)} %fusion.41), channel_id=1, source_target_pairs={{0,1},{1,0},{2,3},{3,2},{4,5},{5,4},{6,7},{7,6},{8,9},{9,8},{10,11... | collective-permute-start | bytes 6291464 | tf_op jit(solution)/shard_map/ppermute | solution.py:284
  290.2 75.2 %collective-permute-start.5 = (bf16[512,2048]{1,0:T(8,128)(2,1)S(1)}, bf16[512,2048]{1,0:T(8,128)(2,1)}, u32[]{:S(2)}, u32[]{:S(2)}) collective-permute-start(bf16[512,2048]{1,0:T(8,128)(2,1)S(1)} %fusion.38), channel_id=1, source_target_pairs={{0,1},{1,0},{2,3},{3,2},{4,5},{5,4},{6,7},{7,6},{8,9},{9,8},{10,11... | collective-permute-start | bytes 6291464 | tf_op jit(solution)/shard_map/ppermute | solution.py:284
  444.4 412.8 %reduce-scatter.7.cloned.1.call-start = ((), (), s32[]{:S(2)}) async-start(), calls=%async_computation.7 | async-start | bytes 13369344 | tf_op jit(solution)/shard_map/reduce_scatter | solution.py:280
  504.6 432.4 %reduce-scatter.11.cloned.1.call-start = ((), (), s32[]{:S(2)}) async-start(), calls=%async_computation.9 | async-start | bytes 4456448 | tf_op jit(solution)/shard_map/reduce_scatter | solution.py:280
  517.1 65.6 %collective-permute-start.12 = (bf16[1024,3072]{1,0:T(8,128)(2,1)}, bf16[1024,3072]{1,0:T(8,128)(2,1)}, u32[]{:S(2)}, u32[]{:S(2)}) collective-permute-start(bf16[1024,3072]{1,0:T(8,128)(2,1)} %convolution_convert_fusion.2), channel_id=1, source_target_pairs={{0,2},{2,0},{4,6},{6,4},{1,3},{3,1},{5,7},{7,5},{8,10},{10,8},{12,... | collective-permute-start | bytes 18874376 | tf_op jit(solution)/shard_map/ppermute | solution.py:294
  539.4 54.7 %collective-permute-start.11 = (bf16[512,2048]{1,0:T(8,128)(2,1)S(1)}, bf16[512,2048]{1,0:T(8,128)(2,1)S(1)}, u32[]{:S(2)}, u32[]{:S(2)}) collective-permute-start(bf16[512,2048]{1,0:T(8,128)(2,1)S(1)} %add_convert_fusion.3), channel_id=1, source_target_pairs={{0,1},{1,0},{2,3},{3,2},{4,5},{5,4},{6,7},{7,6},{8,9},{9,8},{10,11... | collective-permute-start | bytes 6291464 | tf_op jit(solution)/shard_map/ppermute | solution.py:284
  561.6 80.2 %copy-start.19 = (bf16[512,2048]{1,0:T(8,128)(2,1)}, bf16[512,2048]{1,0:T(8,128)(2,1)S(1)}, u32[]{:S(2)}) copy-start(bf16[512,2048]{1,0:T(8,128)(2,1)S(1)} %add_convert_fusion.4) | copy-start | bytes 6291460
  561.6 70.6 %collective-permute-start.10 = (bf16[512,2048]{1,0:T(8,128)(2,1)S(1)}, bf16[512,2048]{1,0:T(8,128)(2,1)S(1)}, u32[]{:S(2)}, u32[]{:S(2)}) collective-permute-start(bf16[512,2048]{1,0:T(8,128)(2,1)S(1)} %add_convert_fusion.4), channel_id=1, source_target_pairs={{0,1},{1,0},{2,3},{3,2},{4,5},{5,4},{6,7},{7,6},{8,9},{9,8},{10,11... | collective-permute-start | bytes 6291464 | tf_op jit(solution)/shard_map/ppermute | solution.py:284
  594.0 48.5 %copy-start.20 = (bf16[1024,3072]{1,0:T(8,128)(2,1)}, bf16[1024,3072]{1,0:T(8,128)(2,1)S(1)}, u32[]{:S(2)}) copy-start(bf16[1024,3072]{1,0:T(8,128)(2,1)S(1)} %add_convert_fusion) | copy-start | bytes 18874372
  594.1 46.2 %copy-start.26 = (bf16[512,2048]{1,0:T(8,128)(2,1)}, bf16[512,2048]{1,0:T(8,128)(2,1)S(1)}, u32[]{:S(2)}) copy-start(bf16[512,2048]{1,0:T(8,128)(2,1)S(1)} %collective-permute-done.11) | copy-start | bytes 6291460
  634.1 98.5 %collective-permute-start.14 = (bf16[512,3072]{1,0:T(8,128)(2,1)}, bf16[512,3072]{1,0:T(8,128)(2,1)}, u32[]{:S(2)}, u32[]{:S(2)}) collective-permute-start(bf16[512,3072]{1,0:T(8,128)(2,1)} %slice.166), channel_id=1, source_target_pairs={{0,4},{2,6},{4,0},{6,2},{1,5},{3,7},{5,1},{7,3},{8,12},{10,14},{12... | collective-permute-start | bytes 9437192 | tf_op jit(solution)/shard_map/ppermute | solution.py:299
  640.3 122.3 %collective-permute-start.13 = (bf16[1024,2048]{1,0:T(8,128)(2,1)}, bf16[1024,2048]{1,0:T(8,128)(2,1)}, u32[]{:S(2)}, u32[]{:S(2)}) collective-permute-start(bf16[1024,2048]{1,0:T(8,128)(2,1)} %fusion.27), channel_id=1, source_target_pairs={{0,1},{1,0},{2,3},{3,2},{4,5},{5,4},{6,7},{7,6},{8,9},{9,8},{10,11... | collective-permute-start | bytes 12582920 | tf_op jit(solution)/shard_map/ppermute | solution.py:284
  682.1 34.7 %collective-permute-start.16 = (bf16[2,512,512]{2,1,0:T(8,128)(2,1)}, bf16[2,512,512]{2,1,0:T(8,128)(2,1)S(1)}, u32[]{:S(2)}, u32[]{:S(2)}) collective-permute-start(bf16[2,512,512]{2,1,0:T(8,128)(2,1)} %get-tuple-element.91), channel_id=1, source_target_pairs={{0,2},{2,0},{4,6},{6,4},{1,3},{3,1},{5,7},{7,5},{8,10},{10,8},{12,... | collective-permute-start | bytes 3145736 | tf_op jit(solution)/shard_map/ppermute | solution.py:486
  687.3 52.3 %collective-permute-start.15 = (bf16[2,512,512]{2,1,0:T(8,128)(2,1)}, bf16[2,512,512]{2,1,0:T(8,128)(2,1)}, u32[]{:S(2)}, u32[]{:S(2)}) collective-permute-start(bf16[2,512,512]{2,1,0:T(8,128)(2,1)} %get-tuple-element.89), channel_id=1, source_target_pairs={{0,2},{2,0},{4,6},{6,4},{1,3},{3,1},{5,7},{7,5},{8,10},{10,8},{12,... | collective-permute-start | bytes 3145736 | tf_op jit(solution)/shard_map/ppermute | solution.py:485
  700.3 18.9 %collective-permute-start.19 = (bf16[2,512,512]{2,1,0:T(8,128)(2,1)}, bf16[2,512,512]{2,1,0:T(8,128)(2,1)}, u32[]{:S(2)}, u32[]{:S(2)}) collective-permute-start(bf16[2,512,512]{2,1,0:T(8,128)(2,1)} %get-tuple-element.103), channel_id=1, source_target_pairs={{0,2},{2,0},{4,6},{6,4},{1,3},{3,1},{5,7},{7,5},{8,10},{10,8},{12,... | collective-permute-start | bytes 3145736 | tf_op jit(solution)/shard_map/ppermute | solution.py:486
  716.8 278.2 %reduce-scatter.9.cloned.1.call-start = ((), (), s32[]{:S(2)}) async-start(), calls=%async_computation.8 | async-start | bytes 8912896 | tf_op jit(solution)/shard_map/reduce_scatter | solution.py:280
  716.8 121.3 %collective-permute-start.18 = (bf16[2,512,512]{2,1,0:T(8,128)(2,1)}, bf16[2,512,512]{2,1,0:T(8,128)(2,1)}, u32[]{:S(2)}, u32[]{:S(2)}) collective-permute-start(bf16[2,512,512]{2,1,0:T(8,128)(2,1)} %get-tuple-element.101), channel_id=1, source_target_pairs={{0,2},{2,0},{4,6},{6,4},{1,3},{3,1},{5,7},{7,5},{8,10},{10,8},{12,... | collective-permute-start | bytes 3145736 | tf_op jit(solution)/shard_map/ppermute | solution.py:485
  719.2 43.4 %collective-permute-start.17 = (bf16[2,512,512]{2,1,0:T(8,128)(2,1)S(1)}, bf16[2,512,512]{2,1,0:T(8,128)(2,1)}, u32[]{:S(2)}, u32[]{:S(2)}) collective-permute-start(bf16[2,512,512]{2,1,0:T(8,128)(2,1)S(1)} %add_convert_fusion.6), channel_id=1, source_target_pairs={{4,0},{6,2},{5,1},{7,3},{12,8},{14,10},{13,9},{15,11},{20,16},{22,... | collective-permute-start | bytes 3145736 | tf_op jit(solution)/shard_map/ppermute | solution.py:487
  732.7 105.4 %collective-permute-start.20 = (bf16[2,512,512]{2,1,0:T(8,128)(2,1)}, bf16[2,512,512]{2,1,0:T(8,128)(2,1)}, u32[]{:S(2)}, u32[]{:S(2)}) collective-permute-start(bf16[2,512,512]{2,1,0:T(8,128)(2,1)} %add_convert_fusion.5), channel_id=1, source_target_pairs={{4,0},{6,2},{5,1},{7,3},{12,8},{14,10},{13,9},{15,11},{20,16},{22,... | collective-permute-start | bytes 3145736 | tf_op jit(solution)/shard_map/ppermute | solution.py:487
  739.6 41.2 %collective-permute-start.21 = (bf16[128,3072]{1,0:T(8,128)(2,1)}, bf16[128,3072]{1,0:T(8,128)(2,1)}, u32[]{:S(2)}, u32[]{:S(2)}) collective-permute-start(bf16[128,3072]{1,0:T(8,128)(2,1)} %get-tuple-element.181), channel_id=1, source_target_pairs={{0,8},{8,0},{16,24},{24,16},{1,9},{9,1},{17,25},{25,17},{2,10},{10... | collective-permute-start | bytes 2359304 | tf_op jit(solution)/shard_map/ppermute | solution.py:309
  762.6 72.3 %collective-permute-start.22 = (bf16[128,3072]{1,0:T(8,128)(2,1)}, bf16[128,3072]{1,0:T(8,128)(2,1)}, u32[]{:S(2)}, u32[]{:S(2)}) collective-permute-start(bf16[128,3072]{1,0:T(8,128)(2,1)} %get-tuple-element.183), channel_id=1, source_target_pairs={{0,16},{8,24},{16,0},{24,8},{1,17},{9,25},{17,1},{25,9},{2,18},{10... | collective-permute-start | bytes 2359304 | tf_op jit(solution)/shard_map/ppermute | solution.py:309
  762.6 72.3 %collective-permute-start.23 = (bf16[128,3072]{1,0:T(8,128)(2,1)}, bf16[128,3072]{1,0:T(8,128)(2,1)}, u32[]{:S(2)}, u32[]{:S(2)}) collective-permute-start(bf16[128,3072]{1,0:T(8,128)(2,1)} %get-tuple-element.182), channel_id=1, source_target_pairs={{0,24},{8,16},{16,8},{24,0},{1,25},{9,17},{17,9},{25,1},{2,26},{10... | collective-permute-start | bytes 2359304 | tf_op jit(solution)/shard_map/ppermute | solution.py:309
  780.8 76.4 %collective-permute-start.24 = (bf16[512,2048]{1,0:T(8,128)(2,1)}, bf16[512,2048]{1,0:T(8,128)(2,1)}, u32[]{:S(2)}, u32[]{:S(2)}) collective-permute-start(bf16[512,2048]{1,0:T(8,128)(2,1)} %fusion.44), channel_id=1, source_target_pairs={{0,1},{1,0},{2,3},{3,2},{4,5},{5,4},{6,7},{7,6},{8,9},{9,8},{10,11... | collective-permute-start | bytes 6291464 | tf_op jit(solution)/shard_map/ppermute | solution.py:284
  871.6 43.5 %collective-permute-start.25 = (bf16[512,2048]{1,0:T(8,128)(2,1)S(1)}, bf16[512,2048]{1,0:T(8,128)(2,1)}, u32[]{:S(2)}, u32[]{:S(2)}) collective-permute-start(bf16[512,2048]{1,0:T(8,128)(2,1)S(1)} %fusion.47), channel_id=1, source_target_pairs={{0,1},{1,0},{2,3},{3,2},{4,5},{5,4},{6,7},{7,6},{8,9},{9,8},{10,11... | collective-permute-start | bytes 6291464 | tf_op jit(solution)/shard_map/ppermute | solution.py:284
  873.8 41.3 %copy-start.16 = (bf16[512,2048]{1,0:T(8,128)(2,1)S(1)}, bf16[512,2048]{1,0:T(8,128)(2,1)}, u32[]{:S(2)}) copy-start(bf16[512,2048]{1,0:T(8,128)(2,1)} %copy-done.15) | copy-start | bytes 6291460
  877.0 40.5 %copy-start.9 = (f32[512,2048]{1,0:T(8,128)}, f32[512,2048]{1,0:T(8,128)S(1)}, u32[]{:S(2)}) copy-start(f32[512,2048]{1,0:T(8,128)S(1)} %convert_add_fusion.1) | copy-start | bytes 12582916
  930.0 6.8 collective-permute-start.26
  936.9 3.8 collective-permute-start.27
  940.7 28.6 %collective-permute-start.28 = (f32[34,128]{1,0:T(8,128)S(1)}, f32[34,128]{1,0:T(8,128)S(1)}, u32[]{:S(2)}, u32[]{:S(2)}) collective-permute-start(f32[34,128]{1,0:T(8,128)S(1)} %fusion.93), channel_id=1, source_target_pairs={{0,8},{8,0},{16,24},{24,16},{1,9},{9,1},{17,25},{25,17},{2,10},{10... | collective-permute-start | bytes 52232 | tf_op jit(solution)/shard_map/ppermute | solution.py:316
  969.3 5.0 collective-permute-start.29
  974.2 11.5 %collective-permute-start.30 = (f32[34,128]{1,0:T(8,128)S(1)}, f32[34,128]{1,0:T(8,128)S(1)}, u32[]{:S(2)}, u32[]{:S(2)}) collective-permute-start(f32[34,128]{1,0:T(8,128)S(1)} %add.170), channel_id=1, source_target_pairs={{0,1},{1,0},{2,3},{3,2},{4,5},{5,4},{6,7},{7,6},{8,9},{9,8},{10,11... | collective-permute-start | bytes 52232 | tf_op jit(solution)/shard_map/ppermute | solution.py:316
  (42 other events, 371.7 us)
Sparse Core Ops, SparseCore 0:
  13.9 109.4 all-gather.2
  125.0 235.1 all-gather.4
  444.5 140.1 reduce-scatter.4
  588.6 167.7 reduce-scatter.6
  760.1 89.1 reduce-scatter.10
  871.7 123.2 reduce-scatter.8

commit v5 on v4

--- a/solution.py
+++ b/solution.py
@@ -302,12 +302,11 @@
     def line_stage(block):
         place = lax.axis_index("dp")
         blocks = block.reshape(dp_size, -1, block.shape[1])
-        owned = lax.dynamic_index_in_dim(blocks, place, 0, False).astype(F32)
+        pieces = [lax.dynamic_index_in_dim(blocks, place, 0, False)]
         for flip in range(1, dp_size):
             sent = lax.dynamic_index_in_dim(blocks, jnp.bitwise_xor(place, flip), 0, False)
-            moves = [(i, i ^ flip) for i in range(dp_size)]
-            owned = owned + lax.ppermute(sent, "dp", moves).astype(F32)
-        return owned
+            pieces.append(lax.ppermute(sent, "dp", [(i, i ^ flip) for i in range(dp_size)]))
+        return pieces
 
     def butterfly(value, axis, size):
         flip = 1
@@ -396,6 +395,7 @@
         raw = dot(normed_attn, w_qkv)
         queries, pairs = rope(raw, turn, gain_heads, q_cols, k_cols)
 
+        cuts = [slice(step * rows, (step + 1) * rows) for step in range(MICRO)]
         kept = []
         middles = []
         heads_out = []
@@ -444,7 +444,9 @@
             backs.append(
                 mp_part(rdot(grad_gate_in[cut], gate_full) + rdot(grad_up_in[cut], up_full))
             )
-        ffn_rel = relative(normed_ffn, rank, dp_size, seq_size)
+        late, mine = lax.optimization_barrier((normed_ffn, backs[0][0]))
+        backs[0] = (mine, backs[0][1])
+        ffn_rel = relative(late, rank, dp_size, seq_size)
         up_block = pair_stage(ffn_rel, grad_up_in)
         gate_grad = tdot(normed_ffn, grad_gate_in).astype(BF16)
         gate_owned = scatter(gate_grad)
@@ -489,7 +491,7 @@
             )
             if step == 0:
                 up_block, d_own = lax.optimization_barrier((up_block, d_own))
-                up_owned = line_stage(up_block)
+                up_pieces = line_stage(up_block)
             sides.append((grad_q, d_own, got, far))
         for step in range(MICRO):
             side = sides[step]
@@ -503,29 +505,40 @@
         layer_out = (middle + (down_mine.astype(F32) + down_other.astype(F32))).astype(BF16)
         backs = [mp_part(rdot(grad_in, w_qkv)) for grad_in in grads_in]
         grad_qkv_in = jnp.concatenate(grads_in, axis=0)
-        grad_qkv_in, gate_owned, up_owned, backs[0], mine = lax.optimization_barrier(
-            (grad_qkv_in, gate_owned, up_owned, backs[0], backs[1][0])
+        unit = [(tokens[cut] * inv_attn[cut]) for cut in cuts]
+        gain_attn_part = sum(
+            jnp.sum(back[0].astype(F32) * part, axis=0) for back, part in zip(backs, unit)
+        )
+        grad_qkv_in, gate_owned, layer_out, gain_attn_part, backs[0], mine = (
+            lax.optimization_barrier(
+                (grad_qkv_in, gate_owned, layer_out, gain_attn_part, backs[0], backs[1][0])
+            )
         )
         backs[1] = (mine, backs[1][1])
         qkv_owned = scatter(tdot(normed_attn, grad_qkv_in).astype(BF16))
-        gain_attn_part = jnp.concatenate([mine for mine, _ in backs], axis=0).astype(F32)
-        gain_attn_part = jnp.sum(gain_attn_part * tokens * inv_attn, axis=0)
         head_sum = (head_sums[0] + head_sums[1]).reshape(-1)
         small = jnp.concatenate([gain_attn_part, gain_ffn_part, head_sum]).reshape(-1, HEAD)
         small = butterfly(small, "seq", seq_size)
         small = butterfly(small, "dp", dp_size)
-        small = butterfly(small, "mp", mp_size).reshape(-1)
+        small = butterfly(small, "mp", mp_size)
+
+        def finish(back, cut):
+            grads = back[0].astype(F32) + back[1].astype(F32)
+            return (
+                grad_middle[cut] + norm_back(grads, tokens[cut], inv_attn[cut], gain_attn)
+            ).astype(BF16)
+
+        early = finish(backs[0], cuts[0])
+        early, small, up_pieces, out_owned, backs[1] = lax.optimization_barrier(
+            (early, small, up_pieces, out_owned, backs[1])
+        )
+        up_owned = sum(piece.astype(F32) for piece in up_pieces)
+        grad_tokens = jnp.stack([early, finish(backs[1], cuts[1])])
+        small = small.reshape(-1)
         head_sum = small[2 * width :]
         owner = (lax.axis_index("dp") * seq_size + rank) * own_rows
         wide_sum = small[: 2 * width].reshape(2, width)
         wide_sum = lax.dynamic_slice_in_dim(wide_sum, owner, own_rows, 1)
-
-        grad_normed_attn = jnp.concatenate(
-            [mine.astype(F32) + other.astype(F32) for mine, other in backs], axis=0
-        )
-        grad_tokens = (
-            grad_middle + norm_back(grad_normed_attn, tokens, inv_attn, gain_attn)
-        ).astype(BF16)
 
         qkv_owned = qkv_owned.astype(F32)
         return (

time: 1020 us -> 1000 us (0.980)
  starting transfers between devices: 68.8 us -> 53.7 us
    ppermute x5, waiting for transfers between devices: 6.54 us -> 88.4 us  [butterfly(): value = value + lax.ppermute(value, axis, moves)]
    ppermute x3, waiting for transfers between devices: 53.1 us -> 0.01 us  [line_stage(): lax.ppermute(sent, 'dp', [(i, i ^ flip) for i in range(dp_size)])]
    ppermute x7, waiting for transfers between devices: 146 us -> 103 us  [mp_other(): return lax.ppermute(part, 'mp', [(0, 1), (1, 0)])]
    ppermute x5, starting transfers between devices: 27 us -> 1.48 us  [butterfly(): value = value + lax.ppermute(value, axis, moves)]
    ppermute x1, waiting for transfers between devices: 9.61 us -> 21.3 us  [cross_stage(): got = lax.ppermute(block[half:], 'seq', cross)]
    unnamed x121 -> x114, local copies, waits for them, and re-layouts: 22.1 us -> 19 us
  transfers between devices with their start and end apart: 37 -> 37, of which waited for: 14 -> 13; matrix products, arithmetic and copies ran while one was open for 32% -> 33% of each run, Pallas kernels for 8% -> 8%
where the time goes in v5:
time: 1000 us; the launch traced here: 991 us
  waiting for transfers between devices  433 us (43%)
  matrix products  272 us (27%)
  other arithmetic  97.9 us (10%)
  Pallas kernels  78.2 us (8%)
  starting transfers between devices  53.7 us (5%)
  local copies, waits for them, and re-layouts  40.4 us (4%)
  between operations  15.3 us (2%)
    all_gather x1, waiting for transfers between devices, local(): first = lax.all_gather(first, data_axes, axis=0, tiled=True)  105 us
    ppermute x7, waiting for transfers between devices, mp_other(): return lax.ppermute(part, 'mp', [(0, 1), (1, 0)])  103 us
    dot_general x5, matrix products, dot(): return jnp.dot(left, right, preferred_element_type=F32)  94.5 us
    dot_general x9, matrix products, rdot(): lax.dot_general(left, right, (((1,), (1,)), ((), ())), preferred_element_...  93.9 us
    ppermute x5, waiting for transfers between devices, butterfly(): value = value + lax.ppermute(value, axis, moves)  88.4 us
    ppermute x2, waiting for transfers between devices, local(): far = lax.ppermute(own, 'seq', up_pairs)  84 us
    dot_general x6, matrix products, tdot(): lax.dot_general(left, right, (((0,), (0,)), ((), ())), preferred_element_...  83.6 us
    pallas_call x2, Pallas kernels, attend_back(): pl.pallas_call(functools.partial(backward_kernel, tile, group), grid_spec...  26.2 us
  transfers between devices with their start and end apart: 37, of which 13 were waited for; matrix products, arithmetic and copies ran while one was open for 33% of the time, Pallas kernels for 8%

profile of v5, /device:TPU:0, one launch (start us, length us, event | category | flops | bytes accessed | tf_op | source)
XLA Modules:
  0.0 990.8 jit_solution(16703981822308803048)
XLA Ops:
  18.6 104.8 %all-gather.3.cloned.1.call-done = bf16[2048,3200]{0,1:T(8,128)(2,1)} async-done(((bf16[128,3200]{0,1:T(8,128)(2,1)}), bf16[2048,3200]{0,1:T(8,128)(2,1)}) %all-gather.3.cloned.1.call-update) | async-done | bytes 13107216 | tf_op jit(solution)/shard_map/all_gather | solution.py:357
  138.2 11.0 %fusion.15.raw = f32[1024,2048]{1,0:T(8,128)} fusion(bf16[1024,2048]{1,0:T(8,128)(2,1)S(1)} %fusion.10, bf16[2048,3200]{0,1:T(8,128)(2,1)S(1)} %copy-done.45), kind=kOutput, calls=%fused_computation.36 | convolution fusion | flops 8589934592 | bytes 20971520 | tf_op jit(solution)/shard_map/dot_general | solution.py:25
  149.2 9.3 rope.1
  160.6 5.1 collective-permute-start.3
  167.3 43.3 %collective-permute-done.3.k2.v2 = bf16[512,1024]{1,0:T(8,128)(2,1)} collective-permute-done((bf16[512,1024]{1,0:T(8,128)(2,1)S(1)}, bf16[512,1024]{1,0:T(8,128)(2,1)}, u32[]{:S(2)}, u32[]{:S(2)}) %collective-permute-start.3) | collective-permute-done | bytes 1048608 | tf_op jit(solution)/shard_map/ppermute | solution.py:406
  214.5 40.7 %collective-permute-done.7.k2.v2 = bf16[512,1024]{1,0:T(8,128)(2,1)S(1)} collective-permute-done((bf16[512,1024]{1,0:T(8,128)(2,1)S(1)}, bf16[512,1024]{1,0:T(8,128)(2,1)S(1)}, u32[]{:S(2)}, u32[]{:S(2)}) %collective-permute-start.7) | collective-permute-done | bytes 1048608 | tf_op jit(solution)/shard_map/ppermute | solution.py:406
  260.4 8.2 attend.2
  268.6 6.2 fusion.30
  276.3 8.8 attend.3
  295.4 25.7 %collective-permute-done.5 = bf16[512,2048]{1,0:T(8,128)(2,1)} collective-permute-done((bf16[512,2048]{1,0:T(8,128)(2,1)}, bf16[512,2048]{1,0:T(8,128)(2,1)}, u32[]{:S(2)}, u32[]{:S(2)}) %collective-permute-start.5) | collective-permute-done | bytes 2097184 | tf_op jit(solution)/shard_map/ppermute | solution.py:284
  321.1 44.9 %collective-permute-done.9 = bf16[512,2048]{1,0:T(8,128)(2,1)} collective-permute-done((bf16[512,2048]{1,0:T(8,128)(2,1)S(1)}, bf16[512,2048]{1,0:T(8,128)(2,1)}, u32[]{:S(2)}, u32[]{:S(2)}) %collective-permute-start.9) | collective-permute-done | bytes 2097184 | tf_op jit(solution)/shard_map/ppermute | solution.py:284
  366.0 9.5 add_add_fusion.1
  382.9 19.1 %fusion.5 = f32[1024,3072]{1,0:T(8,128)} fusion(bf16[1024,2048]{1,0:T(8,128)(2,1)} %multiply_convert_fusion.3.source, bf16[3,2048,3072]{1,2,0:T(8,128)(2,1)} %all-gather.5.cloned.1.call-done), kind=kOutput, calls=%fused_computation.15 | convolution fusion | flops 12884901888 | bytes 29360128 | tf_op jit(solution)/shard_map/dot_general | solution.py:25
  402.0 23.9 %multiply_convert_fusion.2 = (bf16[1024,3072]{1,0:T(8,128)(2,1)}, f32[1024,3072]{1,0:T(8,128)}) fusion(f32[1024,3072]{1,0:T(8,128)} %fusion.5, bf16[1024,2048]{1,0:T(8,128)(2,1)} %multiply_convert_fusion.3.source, bf16[3,2048,3072]{1,2,0:T(8,128)(2,1)} %all-gather.5.cloned.1.call-done), kind=kOutput, calls=%fused_computation.7 | convolution fusion | flops 12903776256 | bytes 48234496 | tf_op jit(solution)/shard_map/dot_general | solution.py:25
  425.9 19.4 %convert_bitcast_fusion = bf16[2048,3072]{1,0:T(8,128)(2,1)} fusion(bf16[1024,3072]{1,0:T(8,128)(2,1)} %get-tuple-element.92, bf16[1024,2048]{1,0:T(8,128)(2,1)} %bitcast.173), kind=kOutput, calls=%fused_computation.6 | convolution fusion | flops 12891193344 | bytes 23068672 | tf_op jit(solution)/shard_map/dot_general | solution.py:29
  445.4 30.1 %multiply_convert_fusion = (bf16[1024,3072]{1,0:T(8,128)(2,1)}, bf16[1024,3072]{1,0:T(8,128)(2,1)}) fusion(f32[1024,3072]{1,0:T(8,128)} %fusion.5, f32[1024,3072]{1,0:T(8,128)} %get-tuple-element.239, bf16[1024,2048]{1,0:T(8,128)(2,1)} %bitcast.174, bf16[3,2048,3072]{1,2,0:T(8,128)(2,1)} %all-gather.5.cloned.1.call-done), kind=kOutput, calls=%fused_computation.4 | convolution fusion | flops 12925796352 | bytes 54525952 | tf_op jit(solution)/shard_map/dot_general | solution.py:25
  475.5 19.3 %convolution_convert_fusion = bf16[2048,3072]{1,0:T(8,128)(2,1)} fusion(bf16[1024,2048]{1,0:T(8,128)(2,1)S(1)} %copy-done.11, bf16[1024,3072]{1,0:T(8,128)(2,1)} %get-tuple-element.200), kind=kOutput, calls=%fused_computation.10 | convolution fusion | flops 12891193344 | bytes 23068672 | tf_op jit(solution)/shard_map/dot_general | solution.py:29
  494.9 10.9 %fusion.4 = f32[512,2048]{1,0:T(8,128)S(1)} fusion(bf16[3,2048,3072]{1,2,0:T(8,128)(2,1)} %all-gather.5.cloned.1.call-done, bf16[1024,3072]{1,0:T(8,128)(2,1)} %get-tuple-element.200), kind=kOutput, calls=%fused_computation.14 | convolution fusion | flops 6442450944 | bytes 19922944 | tf_op jit(solution)/shard_map/dot_general | solution.py:33
  505.7 10.6 %add_convert_fusion.4 = bf16[512,2048]{1,0:T(8,128)(2,1)S(1)} fusion(f32[512,2048]{1,0:T(8,128)S(1)} %fusion.4, bf16[3,2048,3072]{1,2,0:T(8,128)(2,1)} %all-gather.5.cloned.1.call-done, bf16[1024,3072]{1,0:T(8,128)(2,1)} %get-tuple-element.199), kind=kOutput, calls=%fused_computation.57 | convolution fusion | flops 6444548096 | bytes 22020096 | tf_op jit(solution)/shard_map/dot_general | solution.py:33
  518.0 10.4 %relative.1 = bf16[1024,2048]{1,0:T(8,128)(2,1)} custom-call(s32[1]{0:T(128)} %bitcast.29.rank, bf16[1024,2048]{1,0:T(8,128)(2,1)} %multiply_convert_fusion.3.source), custom_call_target="tpu_custom_call" | custom-call | tf_op jit(solution)/shard_map/relative/pallas_call | solution.py:259
  528.4 10.1 %convolution_convert_fusion.2 = bf16[1024,3072]{1,0:T(8,128)(2,1)S(1)} fusion(bf16[1024,3072]{1,0:T(8,128)(2,1)} %get-tuple-element.199, bf16[1024,2048]{1,0:T(8,128)(2,1)} %relative.1), kind=kOutput, calls=%fused_computation.39 | convolution fusion | flops 6445596672 | bytes 14680064 | tf_op jit(solution)/shard_map/dot_general | solution.py:29
  540.3 10.6 %fusion.3 = f32[512,2048]{1,0:T(8,128)S(1)} fusion(bf16[3,2048,3072]{1,2,0:T(8,128)(2,1)} %all-gather.5.cloned.1.call-done, bf16[1024,3072]{1,0:T(8,128)(2,1)} %get-tuple-element.200), kind=kOutput, calls=%fused_computation.13 | convolution fusion | flops 6442450944 | bytes 19922944 | tf_op jit(solution)/shard_map/dot_general | solution.py:33
  550.9 11.2 %add_convert_fusion.3 = bf16[512,2048]{1,0:T(8,128)(2,1)S(1)} fusion(f32[512,2048]{1,0:T(8,128)S(1)} %fusion.3, bf16[3,2048,3072]{1,2,0:T(8,128)(2,1)} %all-gather.5.cloned.1.call-done, bf16[1024,3072]{1,0:T(8,128)(2,1)} %get-tuple-element.199), kind=kOutput, calls=%fused_computation.56 | convolution fusion | flops 6444548096 | bytes 22020096 | tf_op jit(solution)/shard_map/dot_general | solution.py:33
  563.2 20.1 %fusion.19 = bf16[1024,2048]{1,0:T(8,128)(2,1)} fusion(bf16[1024,3072]{1,0:T(8,128)(2,1)} %get-tuple-element.92, bf16[3,2048,3072]{1,2,0:T(8,128)(2,1)} %all-gather.5.cloned.1.call-done), kind=kOutput, calls=%fused_computation.60 | convolution fusion | flops 12886999040 | bytes 23068672 | tf_op jit(solution)/shard_map/dot_general | solution.py:33
  583.2 11.0 %add_convert_fusion = bf16[1024,3072]{1,0:T(8,128)(2,1)S(1)} fusion(bf16[1024,3072]{1,0:T(8,128)(2,1)} %collective-permute-done.12, bf16[1024,3072]{1,0:T(8,128)(2,1)} %get-tuple-element.199, bf16[1024,2048]{1,0:T(8,128)(2,1)S(1)} %copy-done.18), kind=kOutput, calls=%fused_computation.3 | convolution fusion | flops 6451888128 | bytes 20971520 | tf_op jit(solution)/shard_map/dot_general | solution.py:29
  594.3 15.6 %collective-permute-done.11 = bf16[512,2048]{1,0:T(8,128)(2,1)S(1)} collective-permute-done((bf16[512,2048]{1,0:T(8,128)(2,1)S(1)}, bf16[512,2048]{1,0:T(8,128)(2,1)S(1)}, u32[]{:S(2)}, u32[]{:S(2)}) %collective-permute-start.11) | collective-permute-done | bytes 2097184 | tf_op jit(solution)/shard_map/ppermute | solution.py:284
  613.3 10.6 %collective-permute-start.14 = (bf16[512,3072]{1,0:T(8,128)(2,1)}, bf16[512,3072]{1,0:T(8,128)(2,1)}, u32[]{:S(2)}, u32[]{:S(2)}) collective-permute-start(bf16[512,3072]{1,0:T(8,128)(2,1)} %slice.184), channel_id=1, source_target_pairs={{0,4},{2,6},{4,0},{6,2},{1,5},{3,7},{5,1},{7,3},{8,12},{10,14},{12... | collective-permute-start | bytes 9437192 | tf_op jit(solution)/shard_map/ppermute | solution.py:299
  634.7 7.7 subtract_add_fusion
  642.5 10.5 %fusion.57.g_out = bf16[1024,1024]{1,0:T(8,128)(2,1)} fusion(bf16[2048,3200]{0,1:T(8,128)(2,1)} %all-gather.3.cloned.1.call-done, f32[1024,2048]{1,0:T(8,128)} %subtract_add_fusion), kind=kOutput, calls=%fused_computation.88 | convolution fusion | flops 4298113024 | bytes 14680064 | tf_op jit(solution)/shard_map/dot_general | solution.py:25
  652.9 12.9 %attend_back.2 = (f32[512,1024]{1,0:T(8,128)}, f32[2,512,512]{2,1,0:T(8,128)}, bf16[2,512,512]{2,1,0:T(8,128)(2,1)}, f32[2,512,512]{2,1,0:T(8,128)}, bf16[2,512,512]{2,1,0:T(8,128)(2,1)}) custom-call(s32[4]{0:T(128)} %get-tuple-element.236.need, bf16[1024,1024]{1,0:T(8,128)(2,1)} %get-tuple-element.83.q, bf16[1024,1024]{1,0:T(8,128)(2,1)} %fusion.57.g_out, ...), custom_call_target="tpu_custom_call" | custom-call | tf_op jit(solution)/shard_map/attend_back/pallas_call | solution.py:137
  665.9 5.6 collective-permute-start.16
  671.5 13.2 %attend_back.3 = (f32[512,1024]{1,0:T(8,128)}, f32[2,512,512]{2,1,0:T(8,128)}, bf16[2,512,512]{2,1,0:T(8,128)(2,1)}, f32[2,512,512]{2,1,0:T(8,128)}, bf16[2,512,512]{2,1,0:T(8,128)(2,1)}) custom-call(s32[4]{0:T(128)} %get-tuple-element.237.need, bf16[1024,1024]{1,0:T(8,128)(2,1)} %get-tuple-element.83.q, bf16[1024,1024]{1,0:T(8,128)(2,1)} %fusion.57.g_out, ...), custom_call_target="tpu_custom_call" | custom-call | tf_op jit(solution)/shard_map/attend_back/pallas_call | solution.py:137
  684.7 6.2 collective-permute-start.18
  691.0 9.6 convolution_convert_fusion.3
  707.6 21.3 %collective-permute-done.14 = bf16[512,3072]{1,0:T(8,128)(2,1)} collective-permute-done((bf16[512,3072]{1,0:T(8,128)(2,1)}, bf16[512,3072]{1,0:T(8,128)(2,1)}, u32[]{:S(2)}, u32[]{:S(2)}) %collective-permute-start.14) | collective-permute-done | bytes 3145760 | tf_op jit(solution)/shard_map/ppermute | solution.py:299
  735.0 21.5 %collective-permute-done.17.d_far = bf16[2,512,512]{2,1,0:T(8,128)(2,1)} collective-permute-done((bf16[2,512,512]{2,1,0:T(8,128)(2,1)S(1)}, bf16[2,512,512]{2,1,0:T(8,128)(2,1)}, u32[]{:S(2)}, u32[]{:S(2)}) %collective-permute-start.17) | collective-permute-done | bytes 1048608 | tf_op jit(solution)/shard_map/ppermute | solution.py:489
  756.4 7.8 rope_back.2
  764.2 10.5 %fusion.36 = bf16[512,2048]{1,0:T(8,128)(2,1)} fusion(bf16[512,2048]{1,0:T(8,128)(2,1)} %get-tuple-element.110, bf16[2048,3200]{0,1:T(8,128)(2,1)} %all-gather.3.cloned.1.call-done), kind=kOutput, calls=%fused_computation.74 | convolution fusion | flops 4296015872 | bytes 12582912 | tf_op jit(solution)/shard_map/dot_general | solution.py:33
  775.9 6.2 add_convert_fusion.1
  783.1 7.6 rope_back.3
  790.7 8.7 fusion.39
  805.1 16.3 %collective-permute-done.21 = bf16[512,2048]{1,0:T(8,128)(2,1)} collective-permute-done((bf16[512,2048]{1,0:T(8,128)(2,1)}, bf16[512,2048]{1,0:T(8,128)(2,1)}, u32[]{:S(2)}, u32[]{:S(2)}) %collective-permute-start.21) | collective-permute-done | bytes 2097184 | tf_op jit(solution)/shard_map/ppermute | solution.py:284
  821.4 14.1 %convolution_convert_fusion.1 = bf16[2048,2048]{1,0:T(8,128)(2,1)} fusion(bf16[1024,2048]{1,0:T(8,128)(2,1)} %copy-done.17, bf16[1024,2048]{1,0:T(8,128)(2,1)} %pad_maximum_fusion.1), kind=kOutput, calls=%fused_computation.31 | convolution fusion | flops 8594128896 | bytes 16777216 | tf_op jit(solution)/shard_map/dot_general | solution.py:29
  845.5 5.2 multiply_reduce_fusion.5
  850.8 62.4 %collective-permute-done.24 = f32[34,128]{1,0:T(8,128)S(1)} collective-permute-done((f32[34,128]{1,0:T(8,128)S(1)}, f32[34,128]{1,0:T(8,128)S(1)}, u32[]{:S(2)}, u32[]{:S(2)}) %collective-permute-start.24) | collective-permute-done | bytes 17440 | tf_op jit(solution)/shard_map/ppermute | solution.py:315
  913.1 6.8 fusion.18
  919.9 26.0 %collective-permute-done.25 = f32[34,128]{1,0:T(8,128)S(1)} collective-permute-done((f32[34,128]{1,0:T(8,128)S(1)}, f32[34,128]{1,0:T(8,128)S(1)}, u32[]{:S(2)}, u32[]{:S(2)}) %collective-permute-start.25) | collective-permute-done | bytes 17440 | tf_op jit(solution)/shard_map/ppermute | solution.py:315
  970.4 9.7 reduce-scatter.11.cloned.1.call-done
  (250 shorter events, 135.2 us)
Async XLA Ops:
  7.2 116.3 %all-gather.3.cloned.1.call-start = ((), (), s32[]{:S(2)}) async-start(), calls=%async_computation.4 | async-start | bytes 13926400 | tf_op jit(solution)/shard_map/all_gather | solution.py:357
  13.8 369.1 %all-gather.5.cloned.1.call-start = ((), (), s32[]{:S(2)}) async-start(), calls=%async_computation.5 | async-start | bytes 40108032 | tf_op jit(solution)/shard_map/all_gather | solution.py:360
  15.4 108.2 %copy-start.38 = (s32[2,1,512]{2,1,0:T(1,128)S(1)}, s32[2,1,512]{2,1,0:T(1,128)}, u32[]{:S(2)}) copy-start(s32[2,1,512]{2,1,0:T(1,128)} %param.27) | copy-start | bytes 12292
  15.4 108.5 %copy-start.40 = (s32[2,1,512]{2,1,0:T(1,128)S(1)}, s32[2,1,512]{2,1,0:T(1,128)}, u32[]{:S(2)}) copy-start(s32[2,1,512]{2,1,0:T(1,128)} %param.28) | copy-start | bytes 12292
  123.5 658.7 %reduce-scatter.5.cloned.1.call-start = ((), (), s32[]{:S(2)}) async-start(), calls=%async_computation.6 | async-start | bytes 13369344 | tf_op jit(solution)/shard_map/reduce_scatter | solution.py:280
  123.6 4.7 collective-permute-start
  128.3 5.2 collective-permute-start.1
  134.6 245.6 %copy-start.32 = (f32[2048,1]{0,1:T(1,128)}, f32[2048,1]{0,1:T(1,128)S(1)}, u32[]{:S(2)}) copy-start(f32[2048,1]{0,1:T(1,128)S(1)} %get-tuple-element.201) | copy-start | bytes 24580
  160.5 99.8 %copy-start.9 = (bf16[512,1024]{1,0:T(8,128)(2,1)}, bf16[512,1024]{1,0:T(8,128)(2,1)S(1)}, u32[]{:S(2)}) copy-start(bf16[512,1024]{1,0:T(8,128)(2,1)S(1)} %get-tuple-element.209.k0.v0) | copy-start | bytes 3145732
  160.6 108.1 %copy-start.8 = (bf16[512,1024]{1,0:T(8,128)(2,1)}, bf16[512,1024]{1,0:T(8,128)(2,1)S(1)}, u32[]{:S(2)}) copy-start(bf16[512,1024]{1,0:T(8,128)(2,1)S(1)} %get-tuple-element.210.k0.v0) | copy-start | bytes 3145732
  160.6 50.1 %collective-permute-start.3 = (bf16[512,1024]{1,0:T(8,128)(2,1)S(1)}, bf16[512,1024]{1,0:T(8,128)(2,1)}, u32[]{:S(2)}, u32[]{:S(2)}) collective-permute-start(bf16[512,1024]{1,0:T(8,128)(2,1)S(1)} %get-tuple-element.209.k0.v0), channel_id=1, source_target_pairs={{0,4},{2,6},{1,5},{3,7},{8,12},{10,14},{9,13},{11,15},{16,20},{18,... | collective-permute-start | bytes 3145736 | tf_op jit(solution)/shard_map/ppermute | solution.py:406
  165.7 89.5 %collective-permute-start.7 = (bf16[512,1024]{1,0:T(8,128)(2,1)S(1)}, bf16[512,1024]{1,0:T(8,128)(2,1)S(1)}, u32[]{:S(2)}, u32[]{:S(2)}) collective-permute-start(bf16[512,1024]{1,0:T(8,128)(2,1)S(1)} %get-tuple-element.210.k0.v0), channel_id=1, source_target_pairs={{0,4},{2,6},{1,5},{3,7},{8,12},{10,14},{9,13},{11,15},{16,20},{18,... | collective-permute-start | bytes 3145736 | tf_op jit(solution)/shard_map/ppermute | solution.py:406
  167.2 93.1 %collective-permute-start.2 = (bf16[512,1024]{1,0:T(8,128)(2,1)S(1)}, bf16[512,1024]{1,0:T(8,128)(2,1)}, u32[]{:S(2)}, u32[]{:S(2)}) collective-permute-start(bf16[512,1024]{1,0:T(8,128)(2,1)S(1)} %get-tuple-element.209.k0.v0), channel_id=1, source_target_pairs={{0,2},{2,0},{4,6},{6,4},{1,3},{3,1},{5,7},{7,5},{8,10},{10,8},{12,... | collective-permute-start | bytes 3145736 | tf_op jit(solution)/shard_map/ppermute | solution.py:405
  210.7 49.7 %collective-permute-start.4 = (bf16[512,1024]{1,0:T(8,128)(2,1)}, bf16[512,1024]{1,0:T(8,128)(2,1)}, u32[]{:S(2)}, u32[]{:S(2)}) collective-permute-start(bf16[512,1024]{1,0:T(8,128)(2,1)} %collective-permute-done.3.k2.v2), channel_id=1, source_target_pairs={{0,2},{2,0},{4,6},{6,4},{1,3},{3,1},{5,7},{7,5},{8,10},{10,8},{12,... | collective-permute-start | bytes 3145736 | tf_op jit(solution)/shard_map/ppermute | solution.py:407
  213.0 63.3 %collective-permute-start.6 = (bf16[512,1024]{1,0:T(8,128)(2,1)S(1)}, bf16[512,1024]{1,0:T(8,128)(2,1)}, u32[]{:S(2)}, u32[]{:S(2)}) collective-permute-start(bf16[512,1024]{1,0:T(8,128)(2,1)S(1)} %get-tuple-element.210.k0.v0), channel_id=1, source_target_pairs={{0,2},{2,0},{4,6},{6,4},{1,3},{3,1},{5,7},{7,5},{8,10},{10,8},{12,... | collective-permute-start | bytes 3145736 | tf_op jit(solution)/shard_map/ppermute | solution.py:405
  255.2 21.1 %collective-permute-start.8 = (bf16[512,1024]{1,0:T(8,128)(2,1)S(1)}, bf16[512,1024]{1,0:T(8,128)(2,1)}, u32[]{:S(2)}, u32[]{:S(2)}) collective-permute-start(bf16[512,1024]{1,0:T(8,128)(2,1)S(1)} %collective-permute-done.7.k2.v2), channel_id=1, source_target_pairs={{0,2},{2,0},{4,6},{6,4},{1,3},{3,1},{5,7},{7,5},{8,10},{10,8},{12,... | collective-permute-start | bytes 3145736 | tf_op jit(solution)/shard_map/ppermute | solution.py:407
  274.8 46.3 %collective-permute-start.5 = (bf16[512,2048]{1,0:T(8,128)(2,1)}, bf16[512,2048]{1,0:T(8,128)(2,1)}, u32[]{:S(2)}, u32[]{:S(2)}) collective-permute-start(bf16[512,2048]{1,0:T(8,128)(2,1)} %fusion.30), channel_id=1, source_target_pairs={{0,1},{1,0},{2,3},{3,2},{4,5},{5,4},{6,7},{7,6},{8,9},{9,8},{10,11... | collective-permute-start | bytes 6291464 | tf_op jit(solution)/shard_map/ppermute | solution.py:284
  290.2 75.9 %collective-permute-start.9 = (bf16[512,2048]{1,0:T(8,128)(2,1)S(1)}, bf16[512,2048]{1,0:T(8,128)(2,1)}, u32[]{:S(2)}, u32[]{:S(2)}) collective-permute-start(bf16[512,2048]{1,0:T(8,128)(2,1)S(1)} %fusion.33), channel_id=1, source_target_pairs={{0,1},{1,0},{2,3},{3,2},{4,5},{5,4},{6,7},{7,6},{8,9},{9,8},{10,11... | collective-permute-start | bytes 6291464 | tf_op jit(solution)/shard_map/ppermute | solution.py:284
  445.3 376.1 %reduce-scatter.7.cloned.1.call-start = ((), (), s32[]{:S(2)}) async-start(), calls=%async_computation.7 | async-start | bytes 13369344 | tf_op jit(solution)/shard_map/reduce_scatter | solution.py:280
  445.4 30.1 %copy-start.11 = (bf16[1024,2048]{1,0:T(8,128)(2,1)S(1)}, bf16[1024,2048]{1,0:T(8,128)(2,1)}, u32[]{:S(2)}) copy-start(bf16[1024,2048]{1,0:T(8,128)(2,1)} %multiply_convert_fusion.3.source) | copy-start | bytes 12582916
  494.8 458.1 %reduce-scatter.9.cloned.1.call-start = ((), (), s32[]{:S(2)}) async-start(), calls=%async_computation.8 | async-start | bytes 4456448 | tf_op jit(solution)/shard_map/reduce_scatter | solution.py:280
  516.4 77.9 %collective-permute-start.10 = (bf16[512,2048]{1,0:T(8,128)(2,1)S(1)}, bf16[512,2048]{1,0:T(8,128)(2,1)}, u32[]{:S(2)}, u32[]{:S(2)}) collective-permute-start(bf16[512,2048]{1,0:T(8,128)(2,1)S(1)} %add_convert_fusion.4), channel_id=1, source_target_pairs={{0,1},{1,0},{2,3},{3,2},{4,5},{5,4},{6,7},{7,6},{8,9},{9,8},{10,11... | collective-permute-start | bytes 6291464 | tf_op jit(solution)/shard_map/ppermute | solution.py:284
  538.5 44.7 %collective-permute-start.12 = (bf16[1024,3072]{1,0:T(8,128)(2,1)S(1)}, bf16[1024,3072]{1,0:T(8,128)(2,1)}, u32[]{:S(2)}, u32[]{:S(2)}) collective-permute-start(bf16[1024,3072]{1,0:T(8,128)(2,1)S(1)} %convolution_convert_fusion.2), channel_id=1, source_target_pairs={{0,2},{2,0},{4,6},{6,4},{1,3},{3,1},{5,7},{7,5},{8,10},{10,8},{12,... | collective-permute-start | bytes 18874376 | tf_op jit(solution)/shard_map/ppermute | solution.py:294
  562.1 61.8 %copy-start.15 = (bf16[512,2048]{1,0:T(8,128)(2,1)}, bf16[512,2048]{1,0:T(8,128)(2,1)S(1)}, u32[]{:S(2)}) copy-start(bf16[512,2048]{1,0:T(8,128)(2,1)S(1)} %add_convert_fusion.3) | copy-start | bytes 6291460
  562.1 47.8 %collective-permute-start.11 = (bf16[512,2048]{1,0:T(8,128)(2,1)S(1)}, bf16[512,2048]{1,0:T(8,128)(2,1)S(1)}, u32[]{:S(2)}, u32[]{:S(2)}) collective-permute-start(bf16[512,2048]{1,0:T(8,128)(2,1)S(1)} %add_convert_fusion.3), channel_id=1, source_target_pairs={{0,1},{1,0},{2,3},{3,2},{4,5},{5,4},{6,7},{7,6},{8,9},{9,8},{10,11... | collective-permute-start | bytes 6291464 | tf_op jit(solution)/shard_map/ppermute | solution.py:284
  594.3 29.6 %copy-start.16 = (bf16[1024,3072]{1,0:T(8,128)(2,1)}, bf16[1024,3072]{1,0:T(8,128)(2,1)S(1)}, u32[]{:S(2)}) copy-start(bf16[1024,3072]{1,0:T(8,128)(2,1)S(1)} %add_convert_fusion) | copy-start | bytes 18874372
  609.9 146.5 %collective-permute-start.13 = (bf16[1024,2048]{1,0:T(8,128)(2,1)}, bf16[1024,2048]{1,0:T(8,128)(2,1)}, u32[]{:S(2)}, u32[]{:S(2)}) collective-permute-start(bf16[1024,2048]{1,0:T(8,128)(2,1)} %fusion.19), channel_id=1, source_target_pairs={{0,1},{1,0},{2,3},{3,2},{4,5},{5,4},{6,7},{7,6},{8,9},{9,8},{10,11... | collective-permute-start | bytes 12582920 | tf_op jit(solution)/shard_map/ppermute | solution.py:284
  613.3 115.7 %collective-permute-start.14 = (bf16[512,3072]{1,0:T(8,128)(2,1)}, bf16[512,3072]{1,0:T(8,128)(2,1)}, u32[]{:S(2)}, u32[]{:S(2)}) collective-permute-start(bf16[512,3072]{1,0:T(8,128)(2,1)} %slice.184), channel_id=1, source_target_pairs={{0,4},{2,6},{4,0},{6,2},{1,5},{3,7},{5,1},{7,3},{8,12},{10,14},{12... | collective-permute-start | bytes 9437192 | tf_op jit(solution)/shard_map/ppermute | solution.py:299
  665.9 34.8 %collective-permute-start.16 = (bf16[2,512,512]{2,1,0:T(8,128)(2,1)}, bf16[2,512,512]{2,1,0:T(8,128)(2,1)}, u32[]{:S(2)}, u32[]{:S(2)}) collective-permute-start(bf16[2,512,512]{2,1,0:T(8,128)(2,1)} %get-tuple-element.105), channel_id=1, source_target_pairs={{0,2},{2,0},{4,6},{6,4},{1,3},{3,1},{5,7},{7,5},{8,10},{10,8},{12,... | collective-permute-start | bytes 3145736 | tf_op jit(solution)/shard_map/ppermute | solution.py:488
  684.7 97.4 %collective-permute-start.18 = (bf16[2,512,512]{2,1,0:T(8,128)(2,1)}, bf16[2,512,512]{2,1,0:T(8,128)(2,1)S(1)}, u32[]{:S(2)}, u32[]{:S(2)}) collective-permute-start(bf16[2,512,512]{2,1,0:T(8,128)(2,1)} %get-tuple-element.114), channel_id=1, source_target_pairs={{0,2},{2,0},{4,6},{6,4},{1,3},{3,1},{5,7},{7,5},{8,10},{10,8},{12,... | collective-permute-start | bytes 3145736 | tf_op jit(solution)/shard_map/ppermute | solution.py:487
  690.9 12.7 %collective-permute-start.19 = (bf16[2,512,512]{2,1,0:T(8,128)(2,1)}, bf16[2,512,512]{2,1,0:T(8,128)(2,1)}, u32[]{:S(2)}, u32[]{:S(2)}) collective-permute-start(bf16[2,512,512]{2,1,0:T(8,128)(2,1)} %get-tuple-element.116), channel_id=1, source_target_pairs={{0,2},{2,0},{4,6},{6,4},{1,3},{3,1},{5,7},{7,5},{8,10},{10,8},{12,... | collective-permute-start | bytes 3145736 | tf_op jit(solution)/shard_map/ppermute | solution.py:488
  700.6 29.7 %slice-start.2 = ((s8[6291456]{0:T(1024)(128)(4,1)}), s8[2097152]{0:T(1024)(128)(4,1)S(1)}, s32[]{:S(2)}) async-start(s8[6291456]{0:T(1024)(128)(4,1)} %bitcast.171), calls=%async_computation.12 | async-start | bytes 4194304
  700.6 279.5 %reduce-scatter.11.cloned.1.call-start = ((), (), s32[]{:S(2)}) async-start(), calls=%async_computation.9 | async-start | bytes 8912896 | tf_op jit(solution)/shard_map/reduce_scatter | solution.py:280
  700.7 34.3 %collective-permute-start.15 = (bf16[2,512,512]{2,1,0:T(8,128)(2,1)}, bf16[2,512,512]{2,1,0:T(8,128)(2,1)}, u32[]{:S(2)}, u32[]{:S(2)}) collective-permute-start(bf16[2,512,512]{2,1,0:T(8,128)(2,1)} %get-tuple-element.103), channel_id=1, source_target_pairs={{0,2},{2,0},{4,6},{6,4},{1,3},{3,1},{5,7},{7,5},{8,10},{10,8},{12,... | collective-permute-start | bytes 3145736 | tf_op jit(solution)/shard_map/ppermute | solution.py:487
  703.6 52.8 %collective-permute-start.17 = (bf16[2,512,512]{2,1,0:T(8,128)(2,1)S(1)}, bf16[2,512,512]{2,1,0:T(8,128)(2,1)}, u32[]{:S(2)}, u32[]{:S(2)}) collective-permute-start(bf16[2,512,512]{2,1,0:T(8,128)(2,1)S(1)} %add_convert_fusion.6), channel_id=1, source_target_pairs={{4,0},{6,2},{5,1},{7,3},{12,8},{14,10},{13,9},{15,11},{20,16},{22,... | collective-permute-start | bytes 3145736 | tf_op jit(solution)/shard_map/ppermute | solution.py:489
  729.0 53.1 %collective-permute-start.20 = (bf16[2,512,512]{2,1,0:T(8,128)(2,1)}, bf16[2,512,512]{2,1,0:T(8,128)(2,1)}, u32[]{:S(2)}, u32[]{:S(2)}) collective-permute-start(bf16[2,512,512]{2,1,0:T(8,128)(2,1)} %add_convert_fusion.5), channel_id=1, source_target_pairs={{4,0},{6,2},{5,1},{7,3},{12,8},{14,10},{13,9},{15,11},{20,16},{22,... | collective-permute-start | bytes 3145736 | tf_op jit(solution)/shard_map/ppermute | solution.py:489
  774.7 46.7 %collective-permute-start.21 = (bf16[512,2048]{1,0:T(8,128)(2,1)}, bf16[512,2048]{1,0:T(8,128)(2,1)}, u32[]{:S(2)}, u32[]{:S(2)}) collective-permute-start(bf16[512,2048]{1,0:T(8,128)(2,1)} %fusion.36), channel_id=1, source_target_pairs={{0,1},{1,0},{2,3},{3,2},{4,5},{5,4},{6,7},{7,6},{8,9},{9,8},{10,11... | collective-permute-start | bytes 6291464 | tf_op jit(solution)/shard_map/ppermute | solution.py:284
  836.3 9.1 collective-permute-start.22
  839.7 113.1 %collective-permute-start.27 = (bf16[128,3072]{1,0:T(8,128)(2,1)}, bf16[128,3072]{1,0:T(8,128)(2,1)}, u32[]{:S(2)}, u32[]{:S(2)}) collective-permute-start(bf16[128,3072]{1,0:T(8,128)(2,1)} %get-tuple-element.207), channel_id=1, source_target_pairs={{0,8},{8,0},{16,24},{24,16},{1,9},{9,1},{17,25},{25,17},{2,10},{10... | collective-permute-start | bytes 2359304 | tf_op jit(solution)/shard_map/ppermute | solution.py:308
  839.7 113.2 %collective-permute-start.28 = (bf16[128,3072]{1,0:T(8,128)(2,1)}, bf16[128,3072]{1,0:T(8,128)(2,1)}, u32[]{:S(2)}, u32[]{:S(2)}) collective-permute-start(bf16[128,3072]{1,0:T(8,128)(2,1)} %get-tuple-element.206), channel_id=1, source_target_pairs={{0,16},{8,24},{16,0},{24,8},{1,17},{9,25},{17,1},{25,9},{2,18},{10... | collective-permute-start | bytes 2359304 | tf_op jit(solution)/shard_map/ppermute | solution.py:308
  839.7 113.2 %collective-permute-start.29 = (bf16[128,3072]{1,0:T(8,128)(2,1)}, bf16[128,3072]{1,0:T(8,128)(2,1)}, u32[]{:S(2)}, u32[]{:S(2)}) collective-permute-start(bf16[128,3072]{1,0:T(8,128)(2,1)} %get-tuple-element.205), channel_id=1, source_target_pairs={{0,24},{8,16},{16,8},{24,0},{1,25},{9,17},{17,9},{25,1},{2,26},{10... | collective-permute-start | bytes 2359304 | tf_op jit(solution)/shard_map/ppermute | solution.py:308
  844.1 108.8 %collective-permute-start.30 = (bf16[512,2048]{1,0:T(8,128)(2,1)S(1)}, bf16[512,2048]{1,0:T(8,128)(2,1)}, u32[]{:S(2)}, u32[]{:S(2)}) collective-permute-start(bf16[512,2048]{1,0:T(8,128)(2,1)S(1)} %fusion.39), channel_id=1, source_target_pairs={{0,1},{1,0},{2,3},{3,2},{4,5},{5,4},{6,7},{7,6},{8,9},{9,8},{10,11... | collective-permute-start | bytes 6291464 | tf_op jit(solution)/shard_map/ppermute | solution.py:284
  845.4 5.3 collective-permute-start.23
  850.7 62.5 %collective-permute-start.24 = (f32[34,128]{1,0:T(8,128)S(1)}, f32[34,128]{1,0:T(8,128)S(1)}, u32[]{:S(2)}, u32[]{:S(2)}) collective-permute-start(f32[34,128]{1,0:T(8,128)S(1)} %fusion.84), channel_id=1, source_target_pairs={{0,8},{8,0},{16,24},{24,16},{1,9},{9,1},{17,25},{25,17},{2,10},{10... | collective-permute-start | bytes 52232 | tf_op jit(solution)/shard_map/ppermute | solution.py:315
  913.1 32.8 %collective-permute-start.25 = (f32[34,128]{1,0:T(8,128)S(1)}, f32[34,128]{1,0:T(8,128)S(1)}, u32[]{:S(2)}, u32[]{:S(2)}) collective-permute-start(f32[34,128]{1,0:T(8,128)S(1)} %add.168), channel_id=1, source_target_pairs={{0,16},{8,24},{16,0},{24,8},{1,17},{9,25},{17,1},{25,9},{2,18},{10... | collective-permute-start | bytes 52232 | tf_op jit(solution)/shard_map/ppermute | solution.py:315
  913.1 34.1 %copy-start.28 = (bf16[128,3072]{1,0:T(8,128)(2,1)S(1)}, bf16[128,3072]{1,0:T(8,128)(2,1)}, u32[]{:S(2)}) copy-start(bf16[128,3072]{1,0:T(8,128)(2,1)} %reduce-scatter.5.cloned.1.call-done) | copy-start | bytes 2359300
  913.1 35.4 %copy-start.29 = (bf16[128,3072]{1,0:T(8,128)(2,1)S(1)}, bf16[128,3072]{1,0:T(8,128)(2,1)}, u32[]{:S(2)}) copy-start(bf16[128,3072]{1,0:T(8,128)(2,1)} %reduce-scatter.7.cloned.1.call-done) | copy-start | bytes 2359300
  946.0 6.9 collective-permute-start.26
  (39 other events, 302.7 us)
Sparse Core Ops, SparseCore 0:
  13.9 109.4 all-gather.2
  125.0 235.1 all-gather.4
  445.5 142.9 reduce-scatter.4
  592.3 163.2 reduce-scatter.6
  759.4 71.2 reduce-scatter.8
  835.7 144.3 reduce-scatter.10

commit v6 on v5

--- a/solution.py
+++ b/solution.py
@@ -496,9 +496,13 @@
         for step in range(MICRO):
             side = sides[step]
             if step == 0:
-                down_other, side = lax.optimization_barrier((down_other, side))
+                down_other, up_pieces[1], side = lax.optimization_barrier(
+                    (down_other, up_pieces[1], side)
+                )
             else:
-                down_owned, side = lax.optimization_barrier((down_owned, side))
+                down_owned, up_pieces[2], side = lax.optimization_barrier(
+                    (down_owned, up_pieces[2], side)
+                )
             grad_in, sums = rope_back(raw, turn, gain_heads, *side, step, q_cols, k_cols)
             grads_in.append(grad_in)
             head_sums.append(sums)
@@ -509,9 +513,17 @@
         gain_attn_part = sum(
             jnp.sum(back[0].astype(F32) * part, axis=0) for back, part in zip(backs, unit)
         )
-        grad_qkv_in, gate_owned, layer_out, gain_attn_part, backs[0], mine = (
+        grad_qkv_in, gate_owned, up_pieces[3:], layer_out, gain_attn_part, backs[0], mine = (
             lax.optimization_barrier(
-                (grad_qkv_in, gate_owned, layer_out, gain_attn_part, backs[0], backs[1][0])
+                (
+                    grad_qkv_in,
+                    gate_owned,
+                    up_pieces[3:],
+                    layer_out,
+                    gain_attn_part,
+                    backs[0],
+                    backs[1][0],
+                )
             )
         )
         backs[1] = (mine, backs[1][1])
@@ -529,8 +541,8 @@
             ).astype(BF16)
 
         early = finish(backs[0], cuts[0])
-        early, small, up_pieces, out_owned, backs[1] = lax.optimization_barrier(
-            (early, small, up_pieces, out_owned, backs[1])
+        early, small, out_owned, backs[1] = lax.optimization_barrier(
+            (early, small, out_owned, backs[1])
         )
         up_owned = sum(piece.astype(F32) for piece in up_pieces)
         grad_tokens = jnp.stack([early, finish(backs[1], cuts[1])])

time: 1000 us -> 990 us (0.990)
  waiting for transfers between devices: 433 us -> 411 us
  starting transfers between devices: 53.7 us -> 66.1 us
    ppermute x5, waiting for transfers between devices: 88.4 us -> 10.6 us  [butterfly(): value = value + lax.ppermute(value, axis, moves)]
    reduce_scatter x4, waiting for transfers between devices: 9.75 us -> 50.3 us  [scatter(): return lax.psum_scatter(grad, data_axes, scatter_dimension=0, tiled=True)]
    ppermute x3, waiting for transfers between devices: 0.01 us -> 31.8 us  [line_stage(): lax.ppermute(sent, 'dp', [(i, i ^ flip) for i in range(dp_size)])]
    ppermute x7, waiting for transfers between devices: 103 us -> 86 us  [mp_other(): return lax.ppermute(part, 'mp', [(0, 1), (1, 0)])]
    ppermute x2, waiting for transfers between devices: 21.5 us -> 9.75 us  [local(): lax.ppermute((d_far + got_far.astype(F32)).astype(BF16), 'seq', down_pairs)]
    ppermute x1, waiting for transfers between devices: 21.3 us -> 32.9 us  [cross_stage(): got = lax.ppermute(block[half:], 'seq', cross)]
    unnamed x114 -> x124, local copies, waits for them, and re-layouts: 19 us -> 20.6 us
  transfers between devices with their start and end apart: 37 -> 37, of which waited for: 13 -> 15; matrix products, arithmetic and copies ran while one was open for 33% -> 34% of each run, Pallas kernels for 8% -> 8%
where the time goes in v6:
time: 990 us; the launch traced here: 980 us
  waiting for transfers between devices  411 us (42%)
  matrix products  270 us (27%)
  other arithmetic  98.6 us (10%)
  Pallas kernels  78.5 us (8%)
  starting transfers between devices  66.1 us (7%)
  local copies, waits for them, and re-layouts  40.2 us (4%)
  between operations  15.5 us (2%)
    all_gather x1, waiting for transfers between devices, local(): first = lax.all_gather(first, data_axes, axis=0, tiled=True)  105 us
    dot_general x9, matrix products, rdot(): lax.dot_general(left, right, (((1,), (1,)), ((), ())), preferred_element_...  94.7 us
    dot_general x5, matrix products, dot(): return jnp.dot(left, right, preferred_element_type=F32)  94.5 us
    ppermute x7, waiting for transfers between devices, mp_other(): return lax.ppermute(part, 'mp', [(0, 1), (1, 0)])  86 us
    ppermute x2, waiting for transfers between devices, local(): far = lax.ppermute(own, 'seq', up_pairs)  84 us
    dot_general x6, matrix products, tdot(): lax.dot_general(left, right, (((0,), (0,)), ((), ())), preferred_element_...  80.7 us
    reduce_scatter x4, waiting for transfers between devices, scatter(): return lax.psum_scatter(grad, data_axes, scatter_dimension=0, tiled=True)  50.3 us
    ppermute x1, waiting for transfers between devices, cross_stage(): got = lax.ppermute(block[half:], 'seq', cross)  32.9 us
  transfers between devices with their start and end apart: 37, of which 15 were waited for; matrix products, arithmetic and copies ran while one was open for 34% of the time, Pallas kernels for 8%

profile of v6, /device:TPU:0, one launch (start us, length us, event | category | flops | bytes accessed | tf_op | source)
XLA Modules:
  0.0 980.0 jit_solution(12939190865123636798)
XLA Ops:
  18.6 104.8 %all-gather.3.cloned.1.call-done = bf16[2048,3200]{0,1:T(8,128)(2,1)} async-done(((bf16[128,3200]{0,1:T(8,128)(2,1)}), bf16[2048,3200]{0,1:T(8,128)(2,1)}) %all-gather.3.cloned.1.call-update) | async-done | bytes 13107216 | tf_op jit(solution)/shard_map/all_gather | solution.py:357
  138.2 11.2 %fusion.15.raw = f32[1024,2048]{1,0:T(8,128)} fusion(bf16[1024,2048]{1,0:T(8,128)(2,1)S(1)} %fusion.10, bf16[2048,3200]{0,1:T(8,128)(2,1)S(1)} %copy-done.49), kind=kOutput, calls=%fused_computation.36 | convolution fusion | flops 8589934592 | bytes 20971520 | tf_op jit(solution)/shard_map/dot_general | solution.py:25
  149.4 9.3 rope.1
  167.5 43.3 %collective-permute-done.3.k2.v2 = bf16[512,1024]{1,0:T(8,128)(2,1)} collective-permute-done((bf16[512,1024]{1,0:T(8,128)(2,1)S(1)}, bf16[512,1024]{1,0:T(8,128)(2,1)}, u32[]{:S(2)}, u32[]{:S(2)}) %collective-permute-start.3) | collective-permute-done | bytes 1048608 | tf_op jit(solution)/shard_map/ppermute | solution.py:406
  214.6 40.7 %collective-permute-done.7.k2.v2 = bf16[512,1024]{1,0:T(8,128)(2,1)S(1)} collective-permute-done((bf16[512,1024]{1,0:T(8,128)(2,1)S(1)}, bf16[512,1024]{1,0:T(8,128)(2,1)S(1)}, u32[]{:S(2)}, u32[]{:S(2)}) %collective-permute-start.7) | collective-permute-done | bytes 1048608 | tf_op jit(solution)/shard_map/ppermute | solution.py:406
  260.6 8.2 attend.2
  268.8 6.2 fusion.30
  276.5 8.7 attend.3
  295.8 25.5 %collective-permute-done.5 = bf16[512,2048]{1,0:T(8,128)(2,1)} collective-permute-done((bf16[512,2048]{1,0:T(8,128)(2,1)}, bf16[512,2048]{1,0:T(8,128)(2,1)}, u32[]{:S(2)}, u32[]{:S(2)}) %collective-permute-start.5) | collective-permute-done | bytes 2097184 | tf_op jit(solution)/shard_map/ppermute | solution.py:284
  321.3 44.9 %collective-permute-done.9 = bf16[512,2048]{1,0:T(8,128)(2,1)} collective-permute-done((bf16[512,2048]{1,0:T(8,128)(2,1)S(1)}, bf16[512,2048]{1,0:T(8,128)(2,1)}, u32[]{:S(2)}, u32[]{:S(2)}) %collective-permute-start.9) | collective-permute-done | bytes 2097184 | tf_op jit(solution)/shard_map/ppermute | solution.py:284
  366.2 9.5 add_add_fusion.1
  383.1 19.2 %fusion.5 = f32[1024,3072]{1,0:T(8,128)} fusion(bf16[1024,2048]{1,0:T(8,128)(2,1)} %multiply_convert_fusion.3.source, bf16[3,2048,3072]{1,2,0:T(8,128)(2,1)} %all-gather.5.cloned.1.call-done), kind=kOutput, calls=%fused_computation.15 | convolution fusion | flops 12884901888 | bytes 29360128 | tf_op jit(solution)/shard_map/dot_general | solution.py:25
  402.3 23.8 %multiply_convert_fusion.2 = (bf16[1024,3072]{1,0:T(8,128)(2,1)}, f32[1024,3072]{1,0:T(8,128)}) fusion(f32[1024,3072]{1,0:T(8,128)} %fusion.5, bf16[1024,2048]{1,0:T(8,128)(2,1)} %multiply_convert_fusion.3.source, bf16[3,2048,3072]{1,2,0:T(8,128)(2,1)} %all-gather.5.cloned.1.call-done), kind=kOutput, calls=%fused_computation.7 | convolution fusion | flops 12903776256 | bytes 48234496 | tf_op jit(solution)/shard_map/dot_general | solution.py:25
  426.0 19.4 %convert_bitcast_fusion = bf16[2048,3072]{1,0:T(8,128)(2,1)} fusion(bf16[1024,3072]{1,0:T(8,128)(2,1)} %get-tuple-element.91, bf16[1024,2048]{1,0:T(8,128)(2,1)} %bitcast.175), kind=kOutput, calls=%fused_computation.6 | convolution fusion | flops 12891193344 | bytes 23068672 | tf_op jit(solution)/shard_map/dot_general | solution.py:29
  445.5 29.9 %multiply_convert_fusion = (bf16[1024,3072]{1,0:T(8,128)(2,1)}, bf16[1024,3072]{1,0:T(8,128)(2,1)}) fusion(f32[1024,3072]{1,0:T(8,128)} %fusion.5, f32[1024,3072]{1,0:T(8,128)} %get-tuple-element.236, bf16[1024,2048]{1,0:T(8,128)(2,1)} %bitcast.176, bf16[3,2048,3072]{1,2,0:T(8,128)(2,1)} %all-gather.5.cloned.1.call-done), kind=kOutput, calls=%fused_computation.4 | convolution fusion | flops 12925796352 | bytes 54525952 | tf_op jit(solution)/shard_map/dot_general | solution.py:25
  475.4 11.5 %fusion.4 = f32[512,2048]{1,0:T(8,128)S(1)} fusion(bf16[3,2048,3072]{1,2,0:T(8,128)(2,1)} %all-gather.5.cloned.1.call-done, bf16[1024,3072]{1,0:T(8,128)(2,1)} %get-tuple-element.198), kind=kOutput, calls=%fused_computation.14 | convolution fusion | flops 6442450944 | bytes 19922944 | tf_op jit(solution)/shard_map/dot_general | solution.py:33
  486.9 10.9 %add_convert_fusion.4 = bf16[512,2048]{1,0:T(8,128)(2,1)S(1)} fusion(f32[512,2048]{1,0:T(8,128)S(1)} %fusion.4, bf16[3,2048,3072]{1,2,0:T(8,128)(2,1)} %all-gather.5.cloned.1.call-done, bf16[1024,3072]{1,0:T(8,128)(2,1)S(1)} %copy-done.50), kind=kOutput, calls=%fused_computation.57 | convolution fusion | flops 6444548096 | bytes 22020096 | tf_op jit(solution)/shard_map/dot_general | solution.py:33
  499.4 10.4 %relative.1 = bf16[1024,2048]{1,0:T(8,128)(2,1)} custom-call(s32[1]{0:T(128)} %bitcast.29.rank, bf16[1024,2048]{1,0:T(8,128)(2,1)} %multiply_convert_fusion.3.source), custom_call_target="tpu_custom_call" | custom-call | tf_op jit(solution)/shard_map/relative/pallas_call | solution.py:259
  509.8 19.8 %convolution_convert_fusion = bf16[2048,3072]{1,0:T(8,128)(2,1)} fusion(bf16[1024,2048]{1,0:T(8,128)(2,1)} %multiply_convert_fusion.3.source, bf16[1024,3072]{1,0:T(8,128)(2,1)} %get-tuple-element.198), kind=kOutput, calls=%fused_computation.10 | convolution fusion | flops 12891193344 | bytes 23068672 | tf_op jit(solution)/shard_map/dot_general | solution.py:29
  529.7 10.5 %convolution_convert_fusion.2 = bf16[1024,3072]{1,0:T(8,128)(2,1)S(1)} fusion(bf16[1024,3072]{1,0:T(8,128)(2,1)} %get-tuple-element.197, bf16[1024,2048]{1,0:T(8,128)(2,1)} %relative.1), kind=kOutput, calls=%fused_computation.39 | convolution fusion | flops 6445596672 | bytes 14680064 | tf_op jit(solution)/shard_map/dot_general | solution.py:29
  540.8 10.7 %fusion.3 = f32[512,2048]{1,0:T(8,128)S(1)} fusion(bf16[3,2048,3072]{1,2,0:T(8,128)(2,1)} %all-gather.5.cloned.1.call-done, bf16[1024,3072]{1,0:T(8,128)(2,1)} %get-tuple-element.198), kind=kOutput, calls=%fused_computation.13 | convolution fusion | flops 6442450944 | bytes 19922944 | tf_op jit(solution)/shard_map/dot_general | solution.py:33
  551.6 10.8 %add_convert_fusion.3 = bf16[512,2048]{1,0:T(8,128)(2,1)S(1)} fusion(f32[512,2048]{1,0:T(8,128)S(1)} %fusion.3, bf16[3,2048,3072]{1,2,0:T(8,128)(2,1)} %all-gather.5.cloned.1.call-done, bf16[1024,3072]{1,0:T(8,128)(2,1)} %get-tuple-element.197), kind=kOutput, calls=%fused_computation.56 | convolution fusion | flops 6444548096 | bytes 22020096 | tf_op jit(solution)/shard_map/dot_general | solution.py:33
  563.1 20.3 %fusion.19 = bf16[1024,2048]{1,0:T(8,128)(2,1)} fusion(bf16[1024,3072]{1,0:T(8,128)(2,1)} %get-tuple-element.91, bf16[3,2048,3072]{1,2,0:T(8,128)(2,1)} %all-gather.5.cloned.1.call-done), kind=kOutput, calls=%fused_computation.60 | convolution fusion | flops 12886999040 | bytes 23068672 | tf_op jit(solution)/shard_map/dot_general | solution.py:33
  583.5 10.8 %add_convert_fusion = bf16[1024,3072]{1,0:T(8,128)(2,1)S(1)} fusion(bf16[1024,3072]{1,0:T(8,128)(2,1)} %collective-permute-done.12, bf16[1024,3072]{1,0:T(8,128)(2,1)} %get-tuple-element.197, bf16[1024,2048]{1,0:T(8,128)(2,1)S(1)} %copy-done.18), kind=kOutput, calls=%fused_computation.3 | convolution fusion | flops 6451888128 | bytes 20971520 | tf_op jit(solution)/shard_map/dot_general | solution.py:29
  594.3 15.6 %collective-permute-done.11 = bf16[512,2048]{1,0:T(8,128)(2,1)S(1)} collective-permute-done((bf16[512,2048]{1,0:T(8,128)(2,1)S(1)}, bf16[512,2048]{1,0:T(8,128)(2,1)S(1)}, u32[]{:S(2)}, u32[]{:S(2)}) %collective-permute-start.11) | collective-permute-done | bytes 2097184 | tf_op jit(solution)/shard_map/ppermute | solution.py:284
  611.9 11.3 %collective-permute-start.14 = (bf16[512,3072]{1,0:T(8,128)(2,1)}, bf16[512,3072]{1,0:T(8,128)(2,1)}, u32[]{:S(2)}, u32[]{:S(2)}) collective-permute-start(bf16[512,3072]{1,0:T(8,128)(2,1)} %slice.183), channel_id=1, source_target_pairs={{0,4},{2,6},{4,0},{6,2},{1,5},{3,7},{5,1},{7,3},{8,12},{10,14},{12... | collective-permute-start | bytes 9437192 | tf_op jit(solution)/shard_map/ppermute | solution.py:299
  634.8 8.1 subtract_add_fusion
  643.0 10.4 %fusion.57.g_out = bf16[1024,1024]{1,0:T(8,128)(2,1)} fusion(bf16[2048,3200]{0,1:T(8,128)(2,1)} %all-gather.3.cloned.1.call-done, f32[1024,2048]{1,0:T(8,128)} %subtract_add_fusion), kind=kOutput, calls=%fused_computation.88 | convolution fusion | flops 4298113024 | bytes 14680064 | tf_op jit(solution)/shard_map/dot_general | solution.py:25
  653.4 13.1 %attend_back.2 = (f32[512,1024]{1,0:T(8,128)}, f32[2,512,512]{2,1,0:T(8,128)}, bf16[2,512,512]{2,1,0:T(8,128)(2,1)}, f32[2,512,512]{2,1,0:T(8,128)}, bf16[2,512,512]{2,1,0:T(8,128)(2,1)}) custom-call(s32[4]{0:T(128)} %get-tuple-element.233.need, bf16[1024,1024]{1,0:T(8,128)(2,1)} %get-tuple-element.82.q, bf16[1024,1024]{1,0:T(8,128)(2,1)} %fusion.57.g_out, ...), custom_call_target="tpu_custom_call" | custom-call | tf_op jit(solution)/shard_map/attend_back/pallas_call | solution.py:137
  666.5 5.4 collective-permute-start.17
  671.9 13.0 %attend_back.3 = (f32[512,1024]{1,0:T(8,128)}, f32[2,512,512]{2,1,0:T(8,128)}, bf16[2,512,512]{2,1,0:T(8,128)(2,1)}, f32[2,512,512]{2,1,0:T(8,128)}, bf16[2,512,512]{2,1,0:T(8,128)(2,1)}) custom-call(s32[4]{0:T(128)} %get-tuple-element.234.need, bf16[1024,1024]{1,0:T(8,128)(2,1)} %get-tuple-element.82.q, bf16[1024,1024]{1,0:T(8,128)(2,1)} %fusion.57.g_out, ...), custom_call_target="tpu_custom_call" | custom-call | tf_op jit(solution)/shard_map/attend_back/pallas_call | solution.py:137
  684.9 6.2 collective-permute-start.21
  695.5 32.9 %collective-permute-done.14 = bf16[512,3072]{1,0:T(8,128)(2,1)} collective-permute-done((bf16[512,3072]{1,0:T(8,128)(2,1)}, bf16[512,3072]{1,0:T(8,128)(2,1)}, u32[]{:S(2)}, u32[]{:S(2)}) %collective-permute-start.14) | collective-permute-done | bytes 3145760 | tf_op jit(solution)/shard_map/ppermute | solution.py:299
  735.6 6.2 convolution_convert_fusion.3
  747.3 9.7 collective-permute-done.18.d_far
  757.0 13.1 %collective-permute-done.15 = bf16[128,3072]{1,0:T(8,128)(2,1)} collective-permute-done((bf16[128,3072]{1,0:T(8,128)(2,1)}, bf16[128,3072]{1,0:T(8,128)(2,1)}, u32[]{:S(2)}, u32[]{:S(2)}) %collective-permute-start.15) | collective-permute-done | bytes 786464 | tf_op jit(solution)/shard_map/ppermute | solution.py:308
  770.2 7.4 collective-permute-start.23
  777.6 7.8 rope_back.2
  785.4 10.5 %fusion.36 = bf16[512,2048]{1,0:T(8,128)(2,1)} fusion(bf16[512,2048]{1,0:T(8,128)(2,1)} %get-tuple-element.110, bf16[2048,3200]{0,1:T(8,128)(2,1)} %all-gather.3.cloned.1.call-done), kind=kOutput, calls=%fused_computation.74 | convolution fusion | flops 4296015872 | bytes 12582912 | tf_op jit(solution)/shard_map/dot_general | solution.py:33
  798.0 6.0 add_convert_fusion.1
  804.1 18.7 %collective-permute-done.19 = bf16[128,3072]{1,0:T(8,128)(2,1)S(1)} collective-permute-done((bf16[128,3072]{1,0:T(8,128)(2,1)}, bf16[128,3072]{1,0:T(8,128)(2,1)S(1)}, u32[]{:S(2)}, u32[]{:S(2)}) %collective-permute-start.19) | collective-permute-done | bytes 786464 | tf_op jit(solution)/shard_map/ppermute | solution.py:308
  822.8 7.9 rope_back.3
  830.8 8.7 fusion.39
  845.2 14.1 %convolution_convert_fusion.1 = bf16[2048,2048]{1,0:T(8,128)(2,1)} fusion(bf16[1024,2048]{1,0:T(8,128)(2,1)} %copy-done.17, bf16[1024,2048]{1,0:T(8,128)(2,1)} %pad_maximum_fusion.1), kind=kOutput, calls=%fused_computation.31 | convolution fusion | flops 8594128896 | bytes 16777216 | tf_op jit(solution)/shard_map/dot_general | solution.py:29
  869.6 9.5 collective-permute-start.27
  879.1 8.1 fusion.18
  897.9 6.5 collective-permute-done.29
  918.7 50.3 %reduce-scatter.11.cloned.1.call-done = bf16[128,2048]{1,0:T(8,128)(2,1)} async-done(((bf16[2048,2048]{1,0:T(8,128)(2,1)}), bf16[128,2048]{1,0:T(8,128)(2,1)}) %reduce-scatter.11.cloned.1.call-update) | async-done | bytes 524304 | tf_op jit(solution)/shard_map/reduce_scatter | solution.py:280
  (260 shorter events, 143.5 us)
Async XLA Ops:
  7.2 116.3 %all-gather.3.cloned.1.call-start = ((), (), s32[]{:S(2)}) async-start(), calls=%async_computation.4 | async-start | bytes 13926400 | tf_op jit(solution)/shard_map/all_gather | solution.py:357
  13.8 369.3 %all-gather.5.cloned.1.call-start = ((), (), s32[]{:S(2)}) async-start(), calls=%async_computation.5 | async-start | bytes 40108032 | tf_op jit(solution)/shard_map/all_gather | solution.py:360
  15.4 108.2 %copy-start.42 = (s32[2,1,512]{2,1,0:T(1,128)S(1)}, s32[2,1,512]{2,1,0:T(1,128)}, u32[]{:S(2)}) copy-start(s32[2,1,512]{2,1,0:T(1,128)} %param.27) | copy-start | bytes 12292
  15.4 108.5 %copy-start.44 = (s32[2,1,512]{2,1,0:T(1,128)S(1)}, s32[2,1,512]{2,1,0:T(1,128)}, u32[]{:S(2)}) copy-start(s32[2,1,512]{2,1,0:T(1,128)} %param.28) | copy-start | bytes 12292
  123.5 699.3 %reduce-scatter.5.cloned.1.call-start = ((), (), s32[]{:S(2)}) async-start(), calls=%async_computation.6 | async-start | bytes 13369344 | tf_op jit(solution)/shard_map/reduce_scatter | solution.py:280
  123.6 4.7 collective-permute-start
  128.3 5.2 collective-permute-start.1
  134.6 245.8 %copy-start.36 = (f32[2048,1]{0,1:T(1,128)}, f32[2048,1]{0,1:T(1,128)S(1)}, u32[]{:S(2)}) copy-start(f32[2048,1]{0,1:T(1,128)S(1)} %get-tuple-element.199) | copy-start | bytes 24580
  160.6 99.9 %copy-start.9 = (bf16[512,1024]{1,0:T(8,128)(2,1)}, bf16[512,1024]{1,0:T(8,128)(2,1)S(1)}, u32[]{:S(2)}) copy-start(bf16[512,1024]{1,0:T(8,128)(2,1)S(1)} %get-tuple-element.206.k0.v0) | copy-start | bytes 3145732
  160.7 108.2 %copy-start.8 = (bf16[512,1024]{1,0:T(8,128)(2,1)}, bf16[512,1024]{1,0:T(8,128)(2,1)S(1)}, u32[]{:S(2)}) copy-start(bf16[512,1024]{1,0:T(8,128)(2,1)S(1)} %get-tuple-element.207.k0.v0) | copy-start | bytes 3145732
  160.7 50.2 %collective-permute-start.3 = (bf16[512,1024]{1,0:T(8,128)(2,1)S(1)}, bf16[512,1024]{1,0:T(8,128)(2,1)}, u32[]{:S(2)}, u32[]{:S(2)}) collective-permute-start(bf16[512,1024]{1,0:T(8,128)(2,1)S(1)} %get-tuple-element.206.k0.v0), channel_id=1, source_target_pairs={{0,4},{2,6},{1,5},{3,7},{8,12},{10,14},{9,13},{11,15},{16,20},{18,... | collective-permute-start | bytes 3145736 | tf_op jit(solution)/shard_map/ppermute | solution.py:406
  165.9 89.5 %collective-permute-start.7 = (bf16[512,1024]{1,0:T(8,128)(2,1)S(1)}, bf16[512,1024]{1,0:T(8,128)(2,1)S(1)}, u32[]{:S(2)}, u32[]{:S(2)}) collective-permute-start(bf16[512,1024]{1,0:T(8,128)(2,1)S(1)} %get-tuple-element.207.k0.v0), channel_id=1, source_target_pairs={{0,4},{2,6},{1,5},{3,7},{8,12},{10,14},{9,13},{11,15},{16,20},{18,... | collective-permute-start | bytes 3145736 | tf_op jit(solution)/shard_map/ppermute | solution.py:406
  167.5 93.1 %collective-permute-start.2 = (bf16[512,1024]{1,0:T(8,128)(2,1)S(1)}, bf16[512,1024]{1,0:T(8,128)(2,1)}, u32[]{:S(2)}, u32[]{:S(2)}) collective-permute-start(bf16[512,1024]{1,0:T(8,128)(2,1)S(1)} %get-tuple-element.206.k0.v0), channel_id=1, source_target_pairs={{0,2},{2,0},{4,6},{6,4},{1,3},{3,1},{5,7},{7,5},{8,10},{10,8},{12,... | collective-permute-start | bytes 3145736 | tf_op jit(solution)/shard_map/ppermute | solution.py:405
  210.9 49.7 %collective-permute-start.4 = (bf16[512,1024]{1,0:T(8,128)(2,1)}, bf16[512,1024]{1,0:T(8,128)(2,1)}, u32[]{:S(2)}, u32[]{:S(2)}) collective-permute-start(bf16[512,1024]{1,0:T(8,128)(2,1)} %collective-permute-done.3.k2.v2), channel_id=1, source_target_pairs={{0,2},{2,0},{4,6},{6,4},{1,3},{3,1},{5,7},{7,5},{8,10},{10,8},{12,... | collective-permute-start | bytes 3145736 | tf_op jit(solution)/shard_map/ppermute | solution.py:407
  213.1 63.4 %collective-permute-start.6 = (bf16[512,1024]{1,0:T(8,128)(2,1)S(1)}, bf16[512,1024]{1,0:T(8,128)(2,1)}, u32[]{:S(2)}, u32[]{:S(2)}) collective-permute-start(bf16[512,1024]{1,0:T(8,128)(2,1)S(1)} %get-tuple-element.207.k0.v0), channel_id=1, source_target_pairs={{0,2},{2,0},{4,6},{6,4},{1,3},{3,1},{5,7},{7,5},{8,10},{10,8},{12,... | collective-permute-start | bytes 3145736 | tf_op jit(solution)/shard_map/ppermute | solution.py:405
  255.4 21.1 %collective-permute-start.8 = (bf16[512,1024]{1,0:T(8,128)(2,1)S(1)}, bf16[512,1024]{1,0:T(8,128)(2,1)}, u32[]{:S(2)}, u32[]{:S(2)}) collective-permute-start(bf16[512,1024]{1,0:T(8,128)(2,1)S(1)} %collective-permute-done.7.k2.v2), channel_id=1, source_target_pairs={{0,2},{2,0},{4,6},{6,4},{1,3},{3,1},{5,7},{7,5},{8,10},{10,8},{12,... | collective-permute-start | bytes 3145736 | tf_op jit(solution)/shard_map/ppermute | solution.py:407
  275.0 46.3 %collective-permute-start.5 = (bf16[512,2048]{1,0:T(8,128)(2,1)}, bf16[512,2048]{1,0:T(8,128)(2,1)}, u32[]{:S(2)}, u32[]{:S(2)}) collective-permute-start(bf16[512,2048]{1,0:T(8,128)(2,1)} %fusion.30), channel_id=1, source_target_pairs={{0,1},{1,0},{2,3},{3,2},{4,5},{5,4},{6,7},{7,6},{8,9},{9,8},{10,11... | collective-permute-start | bytes 6291464 | tf_op jit(solution)/shard_map/ppermute | solution.py:284
  290.4 75.9 %collective-permute-start.9 = (bf16[512,2048]{1,0:T(8,128)(2,1)S(1)}, bf16[512,2048]{1,0:T(8,128)(2,1)}, u32[]{:S(2)}, u32[]{:S(2)}) collective-permute-start(bf16[512,2048]{1,0:T(8,128)(2,1)S(1)} %fusion.33), channel_id=1, source_target_pairs={{0,1},{1,0},{2,3},{3,2},{4,5},{5,4},{6,7},{7,6},{8,9},{9,8},{10,11... | collective-permute-start | bytes 6291464 | tf_op jit(solution)/shard_map/ppermute | solution.py:284
  445.4 399.8 %reduce-scatter.7.cloned.1.call-start = ((), (), s32[]{:S(2)}) async-start(), calls=%async_computation.7 | async-start | bytes 13369344 | tf_op jit(solution)/shard_map/reduce_scatter | solution.py:280
  497.8 96.5 %collective-permute-start.10 = (bf16[512,2048]{1,0:T(8,128)(2,1)S(1)}, bf16[512,2048]{1,0:T(8,128)(2,1)}, u32[]{:S(2)}, u32[]{:S(2)}) collective-permute-start(bf16[512,2048]{1,0:T(8,128)(2,1)S(1)} %add_convert_fusion.4), channel_id=1, source_target_pairs={{0,1},{1,0},{2,3},{3,2},{4,5},{5,4},{6,7},{7,6},{8,9},{9,8},{10,11... | collective-permute-start | bytes 6291464 | tf_op jit(solution)/shard_map/ppermute | solution.py:284
  529.6 374.7 %reduce-scatter.9.cloned.1.call-start = ((), (), s32[]{:S(2)}) async-start(), calls=%async_computation.8 | async-start | bytes 4456448 | tf_op jit(solution)/shard_map/reduce_scatter | solution.py:280
  540.2 43.3 %collective-permute-start.12 = (bf16[1024,3072]{1,0:T(8,128)(2,1)S(1)}, bf16[1024,3072]{1,0:T(8,128)(2,1)}, u32[]{:S(2)}, u32[]{:S(2)}) collective-permute-start(bf16[1024,3072]{1,0:T(8,128)(2,1)S(1)} %convolution_convert_fusion.2), channel_id=1, source_target_pairs={{0,2},{2,0},{4,6},{6,4},{1,3},{3,1},{5,7},{7,5},{8,10},{10,8},{12,... | collective-permute-start | bytes 18874376 | tf_op jit(solution)/shard_map/ppermute | solution.py:294
  562.3 61.6 %copy-start.15 = (bf16[512,2048]{1,0:T(8,128)(2,1)}, bf16[512,2048]{1,0:T(8,128)(2,1)S(1)}, u32[]{:S(2)}) copy-start(bf16[512,2048]{1,0:T(8,128)(2,1)S(1)} %add_convert_fusion.3) | copy-start | bytes 6291460
  562.3 21.1 %copy-start.18 = (bf16[1024,2048]{1,0:T(8,128)(2,1)S(1)}, bf16[1024,2048]{1,0:T(8,128)(2,1)}, u32[]{:S(2)}) copy-start(bf16[1024,2048]{1,0:T(8,128)(2,1)} %relative.1) | copy-start | bytes 12582916
  562.3 47.5 %collective-permute-start.11 = (bf16[512,2048]{1,0:T(8,128)(2,1)S(1)}, bf16[512,2048]{1,0:T(8,128)(2,1)S(1)}, u32[]{:S(2)}, u32[]{:S(2)}) collective-permute-start(bf16[512,2048]{1,0:T(8,128)(2,1)S(1)} %add_convert_fusion.3), channel_id=1, source_target_pairs={{0,1},{1,0},{2,3},{3,2},{4,5},{5,4},{6,7},{7,6},{8,9},{9,8},{10,11... | collective-permute-start | bytes 6291464 | tf_op jit(solution)/shard_map/ppermute | solution.py:284
  594.3 29.6 %copy-start.16 = (bf16[1024,3072]{1,0:T(8,128)(2,1)}, bf16[1024,3072]{1,0:T(8,128)(2,1)S(1)}, u32[]{:S(2)}) copy-start(bf16[1024,3072]{1,0:T(8,128)(2,1)S(1)} %add_convert_fusion) | copy-start | bytes 18874372
  611.9 116.5 %collective-permute-start.14 = (bf16[512,3072]{1,0:T(8,128)(2,1)}, bf16[512,3072]{1,0:T(8,128)(2,1)}, u32[]{:S(2)}, u32[]{:S(2)}) collective-permute-start(bf16[512,3072]{1,0:T(8,128)(2,1)} %slice.183), channel_id=1, source_target_pairs={{0,4},{2,6},{4,0},{6,2},{1,5},{3,7},{5,1},{7,3},{8,12},{10,14},{12... | collective-permute-start | bytes 9437192 | tf_op jit(solution)/shard_map/ppermute | solution.py:299
  623.2 154.5 %collective-permute-start.13 = (bf16[1024,2048]{1,0:T(8,128)(2,1)}, bf16[1024,2048]{1,0:T(8,128)(2,1)}, u32[]{:S(2)}, u32[]{:S(2)}) collective-permute-start(bf16[1024,2048]{1,0:T(8,128)(2,1)} %fusion.19), channel_id=1, source_target_pairs={{0,1},{1,0},{2,3},{3,2},{4,5},{5,4},{6,7},{7,6},{8,9},{9,8},{10,11... | collective-permute-start | bytes 12582920 | tf_op jit(solution)/shard_map/ppermute | solution.py:284
  666.5 24.7 %collective-permute-start.17 = (bf16[2,512,512]{2,1,0:T(8,128)(2,1)}, bf16[2,512,512]{2,1,0:T(8,128)(2,1)}, u32[]{:S(2)}, u32[]{:S(2)}) collective-permute-start(bf16[2,512,512]{2,1,0:T(8,128)(2,1)} %get-tuple-element.105), channel_id=1, source_target_pairs={{0,2},{2,0},{4,6},{6,4},{1,3},{3,1},{5,7},{7,5},{8,10},{10,8},{12,... | collective-permute-start | bytes 3145736 | tf_op jit(solution)/shard_map/ppermute | solution.py:488
  684.9 57.0 %collective-permute-start.21 = (bf16[2,512,512]{2,1,0:T(8,128)(2,1)}, bf16[2,512,512]{2,1,0:T(8,128)(2,1)}, u32[]{:S(2)}, u32[]{:S(2)}) collective-permute-start(bf16[2,512,512]{2,1,0:T(8,128)(2,1)} %get-tuple-element.116), channel_id=1, source_target_pairs={{0,2},{2,0},{4,6},{6,4},{1,3},{3,1},{5,7},{7,5},{8,10},{10,8},{12,... | collective-permute-start | bytes 3145736 | tf_op jit(solution)/shard_map/ppermute | solution.py:488
  691.1 54.9 %collective-permute-start.16 = (bf16[2,512,512]{2,1,0:T(8,128)(2,1)}, bf16[2,512,512]{2,1,0:T(8,128)(2,1)S(1)}, u32[]{:S(2)}, u32[]{:S(2)}) collective-permute-start(bf16[2,512,512]{2,1,0:T(8,128)(2,1)} %get-tuple-element.103), channel_id=1, source_target_pairs={{0,2},{2,0},{4,6},{6,4},{1,3},{3,1},{5,7},{7,5},{8,10},{10,8},{12,... | collective-permute-start | bytes 3145736 | tf_op jit(solution)/shard_map/ppermute | solution.py:487
  691.2 44.4 %slice-start.2 = ((s8[8388608]{0:T(1024)(128)(4,1)}), s8[4194304]{0:T(1024)(128)(4,1)S(1)}, s32[]{:S(2)}) async-start(s8[8388608]{0:T(1024)(128)(4,1)} %bitcast.170), calls=%async_computation.12 | async-start | bytes 8388608
  693.9 41.6 %slice-start.3 = ((s8[8388608]{0:T(1024)(128)(4,1)}), s8[4194304]{0:T(1024)(128)(4,1)S(1)}, s32[]{:S(2)}) async-start(s8[8388608]{0:T(1024)(128)(4,1)} %bitcast.170), calls=%async_computation.13 | async-start | bytes 8388608
  693.9 63.1 %collective-permute-start.18 = (bf16[2,512,512]{2,1,0:T(8,128)(2,1)}, bf16[2,512,512]{2,1,0:T(8,128)(2,1)}, u32[]{:S(2)}, u32[]{:S(2)}) collective-permute-start(bf16[2,512,512]{2,1,0:T(8,128)(2,1)} %add_convert_fusion.6), channel_id=1, source_target_pairs={{4,0},{6,2},{5,1},{7,3},{12,8},{14,10},{13,9},{15,11},{20,16},{22,... | collective-permute-start | bytes 3145736 | tf_op jit(solution)/shard_map/ppermute | solution.py:489
  735.6 34.6 %collective-permute-start.15 = (bf16[128,3072]{1,0:T(8,128)(2,1)}, bf16[128,3072]{1,0:T(8,128)(2,1)}, u32[]{:S(2)}, u32[]{:S(2)}) collective-permute-start(bf16[128,3072]{1,0:T(8,128)(2,1)} %get-tuple-element.205), channel_id=1, source_target_pairs={{0,8},{8,0},{16,24},{24,16},{1,9},{9,1},{17,25},{25,17},{2,10},{10... | collective-permute-start | bytes 2359304 | tf_op jit(solution)/shard_map/ppermute | solution.py:308
  741.8 227.3 %reduce-scatter.11.cloned.1.call-start = ((), (), s32[]{:S(2)}) async-start(), calls=%async_computation.9 | async-start | bytes 8912896 | tf_op jit(solution)/shard_map/reduce_scatter | solution.py:280
  741.9 62.2 %collective-permute-start.20 = (bf16[2,512,512]{2,1,0:T(8,128)(2,1)}, bf16[2,512,512]{2,1,0:T(8,128)(2,1)}, u32[]{:S(2)}, u32[]{:S(2)}) collective-permute-start(bf16[2,512,512]{2,1,0:T(8,128)(2,1)} %get-tuple-element.114), channel_id=1, source_target_pairs={{0,2},{2,0},{4,6},{6,4},{1,3},{3,1},{5,7},{7,5},{8,10},{10,8},{12,... | collective-permute-start | bytes 3145736 | tf_op jit(solution)/shard_map/ppermute | solution.py:487
  746.0 31.6 %copy-start.27 = (bf16[2,512,512]{2,1,0:T(8,128)(2,1)}, bf16[2,512,512]{2,1,0:T(8,128)(2,1)S(1)}, u32[]{:S(2)}) copy-start(bf16[2,512,512]{2,1,0:T(8,128)(2,1)S(1)} %collective-permute-done.16.d_near) | copy-start | bytes 3145732
  746.0 58.1 %collective-permute-start.22 = (bf16[2,512,512]{2,1,0:T(8,128)(2,1)}, bf16[2,512,512]{2,1,0:T(8,128)(2,1)S(1)}, u32[]{:S(2)}, u32[]{:S(2)}) collective-permute-start(bf16[2,512,512]{2,1,0:T(8,128)(2,1)} %add_convert_fusion.5), channel_id=1, source_target_pairs={{4,0},{6,2},{5,1},{7,3},{12,8},{14,10},{13,9},{15,11},{20,16},{22,... | collective-permute-start | bytes 3145736 | tf_op jit(solution)/shard_map/ppermute | solution.py:489
  757.0 65.7 %collective-permute-start.19 = (bf16[128,3072]{1,0:T(8,128)(2,1)}, bf16[128,3072]{1,0:T(8,128)(2,1)S(1)}, u32[]{:S(2)}, u32[]{:S(2)}) collective-permute-start(bf16[128,3072]{1,0:T(8,128)(2,1)} %get-tuple-element.204), channel_id=1, source_target_pairs={{0,16},{8,24},{16,0},{24,8},{1,17},{9,25},{17,1},{25,9},{2,18},{10... | collective-permute-start | bytes 2359304 | tf_op jit(solution)/shard_map/ppermute | solution.py:308
  770.2 75.0 %collective-permute-start.23 = (bf16[128,3072]{1,0:T(8,128)(2,1)}, bf16[128,3072]{1,0:T(8,128)(2,1)}, u32[]{:S(2)}, u32[]{:S(2)}) collective-permute-start(bf16[128,3072]{1,0:T(8,128)(2,1)} %get-tuple-element.203), channel_id=1, source_target_pairs={{0,24},{8,16},{16,8},{24,0},{1,25},{9,17},{17,9},{25,1},{2,26},{10... | collective-permute-start | bytes 2359304 | tf_op jit(solution)/shard_map/ppermute | solution.py:308
  795.9 49.3 %collective-permute-start.24 = (bf16[512,2048]{1,0:T(8,128)(2,1)}, bf16[512,2048]{1,0:T(8,128)(2,1)}, u32[]{:S(2)}, u32[]{:S(2)}) collective-permute-start(bf16[512,2048]{1,0:T(8,128)(2,1)} %fusion.36), channel_id=1, source_target_pairs={{0,1},{1,0},{2,3},{3,2},{4,5},{5,4},{6,7},{7,6},{8,9},{9,8},{10,11... | collective-permute-start | bytes 6291464 | tf_op jit(solution)/shard_map/ppermute | solution.py:284
  859.3 45.0 %collective-permute-start.30 = (bf16[512,2048]{1,0:T(8,128)(2,1)S(1)}, bf16[512,2048]{1,0:T(8,128)(2,1)}, u32[]{:S(2)}, u32[]{:S(2)}) collective-permute-start(bf16[512,2048]{1,0:T(8,128)(2,1)S(1)} %fusion.39), channel_id=1, source_target_pairs={{0,1},{1,0},{2,3},{3,2},{4,5},{5,4},{6,7},{7,6},{8,9},{9,8},{10,11... | collective-permute-start | bytes 6291464 | tf_op jit(solution)/shard_map/ppermute | solution.py:284
  861.3 4.4 collective-permute-start.25
  865.7 3.8 collective-permute-start.26
  869.6 17.6 %collective-permute-start.27 = (f32[34,128]{1,0:T(8,128)S(1)}, f32[34,128]{1,0:T(8,128)S(1)}, u32[]{:S(2)}, u32[]{:S(2)}) collective-permute-start(f32[34,128]{1,0:T(8,128)S(1)} %fusion.86), channel_id=1, source_target_pairs={{0,8},{8,0},{16,24},{24,16},{1,9},{9,1},{17,25},{25,17},{2,10},{10... | collective-permute-start | bytes 52232 | tf_op jit(solution)/shard_map/ppermute | solution.py:315
  887.2 4.7 collective-permute-start.28
  891.9 12.4 %collective-permute-start.29 = (f32[34,128]{1,0:T(8,128)S(1)}, f32[34,128]{1,0:T(8,128)S(1)}, u32[]{:S(2)}, u32[]{:S(2)}) collective-permute-start(f32[34,128]{1,0:T(8,128)S(1)} %add.172), channel_id=1, source_target_pairs={{0,1},{1,0},{2,3},{3,2},{4,5},{5,4},{6,7},{7,6},{8,9},{9,8},{10,11... | collective-permute-start | bytes 52232 | tf_op jit(solution)/shard_map/ppermute | solution.py:315
  (44 other events, 303.4 us)
Sparse Core Ops, SparseCore 0:
  13.9 109.4 all-gather.2
  125.0 235.1 all-gather.4
  445.5 142.9 reduce-scatter.4
  592.5 171.9 reduce-scatter.6
  768.2 88.5 reduce-scatter.8
  860.7 108.3 reduce-scatter.10

commit v7 on v6

--- a/solution.py
+++ b/solution.py
@@ -451,7 +451,7 @@
         gate_grad = tdot(normed_ffn, grad_gate_in).astype(BF16)
         gate_owned = scatter(gate_grad)
         down_mine = lax.optimization_barrier(rdot(act, down_t).astype(BF16))
-        backs, gate_grad, up_block, down_mine = lax.optimization_barrier(
+        backs, gate_grad, _, down_mine = lax.optimization_barrier(
             (backs, gate_grad, up_block, down_mine)
         )
         down_other = mp_other(down_mine)

time: 990 us -> 986 us (level)
    reduce_scatter x4, waiting for transfers between devices: 50.3 us -> 70.1 us  [scatter(): return lax.psum_scatter(grad, data_axes, scatter_dimension=0, tiled=True)]
    ppermute x7, waiting for transfers between devices: 86 us -> 72.7 us  [mp_other(): return lax.ppermute(part, 'mp', [(0, 1), (1, 0)])]
  transfers between devices with their start and end apart: 37 -> 37, of which waited for: 15 -> 14; matrix products, arithmetic and copies ran while one was open for 34% -> 33% of each run, Pallas kernels for 8% -> 8%
where the time goes in v7:
time: 986 us; the launch traced here: 979 us
  waiting for transfers between devices  418 us (42%)
  matrix products  270 us (27%)
  other arithmetic  97.4 us (10%)
  Pallas kernels  78.6 us (8%)
  starting transfers between devices  58.2 us (6%)
  local copies, waits for them, and re-layouts  41.8 us (4%)
  between operations  15.5 us (2%)
    all_gather x1, waiting for transfers between devices, local(): first = lax.all_gather(first, data_axes, axis=0, tiled=True)  105 us
    dot_general x5, matrix products, dot(): return jnp.dot(left, right, preferred_element_type=F32)  94.5 us
    dot_general x9, matrix products, rdot(): lax.dot_general(left, right, (((1,), (1,)), ((), ())), preferred_element_...  94.3 us
    ppermute x2, waiting for transfers between devices, local(): far = lax.ppermute(own, 'seq', up_pairs)  84 us
    dot_general x6, matrix products, tdot(): lax.dot_general(left, right, (((0,), (0,)), ((), ())), preferred_element_...  80.7 us
    ppermute x7, waiting for transfers between devices, mp_other(): return lax.ppermute(part, 'mp', [(0, 1), (1, 0)])  72.7 us
    reduce_scatter x4, waiting for transfers between devices, scatter(): return lax.psum_scatter(grad, data_axes, scatter_dimension=0, tiled=True)  70.1 us
    ppermute x3, waiting for transfers between devices, line_stage(): lax.ppermute(sent, 'dp', [(i, i ^ flip) for i in range(dp_size)])  31.7 us
  transfers between devices with their start and end apart: 37, of which 14 were waited for; matrix products, arithmetic and copies ran while one was open for 33% of the time, Pallas kernels for 8%

profile of v7, /device:TPU:0, one launch (start us, length us, event | category | flops | bytes accessed | tf_op | source)
XLA Modules:
  0.0 978.6 jit_solution(498852003400474124)
XLA Ops:
  18.6 104.8 %all-gather.3.cloned.1.call-done = bf16[2048,3200]{0,1:T(8,128)(2,1)} async-done(((bf16[128,3200]{0,1:T(8,128)(2,1)}), bf16[2048,3200]{0,1:T(8,128)(2,1)}) %all-gather.3.cloned.1.call-update) | async-done | bytes 13107216 | tf_op jit(solution)/shard_map/all_gather | solution.py:357
  138.2 11.2 %fusion.15.raw = f32[1024,2048]{1,0:T(8,128)} fusion(bf16[1024,2048]{1,0:T(8,128)(2,1)S(1)} %fusion.10, bf16[2048,3200]{0,1:T(8,128)(2,1)S(1)} %copy-done.49), kind=kOutput, calls=%fused_computation.36 | convolution fusion | flops 8589934592 | bytes 20971520 | tf_op jit(solution)/shard_map/dot_general | solution.py:25
  149.4 9.3 rope.1
  160.7 5.2 collective-permute-start.3
  167.5 43.3 %collective-permute-done.3.k2.v2 = bf16[512,1024]{1,0:T(8,128)(2,1)} collective-permute-done((bf16[512,1024]{1,0:T(8,128)(2,1)S(1)}, bf16[512,1024]{1,0:T(8,128)(2,1)}, u32[]{:S(2)}, u32[]{:S(2)}) %collective-permute-start.3) | collective-permute-done | bytes 1048608 | tf_op jit(solution)/shard_map/ppermute | solution.py:406
  214.6 40.7 %collective-permute-done.7.k2.v2 = bf16[512,1024]{1,0:T(8,128)(2,1)S(1)} collective-permute-done((bf16[512,1024]{1,0:T(8,128)(2,1)S(1)}, bf16[512,1024]{1,0:T(8,128)(2,1)S(1)}, u32[]{:S(2)}, u32[]{:S(2)}) %collective-permute-start.7) | collective-permute-done | bytes 1048608 | tf_op jit(solution)/shard_map/ppermute | solution.py:406
  260.6 8.2 attend.2
  268.8 6.2 fusion.30
  276.5 8.7 attend.3
  285.3 5.1 fusion.33
  295.8 25.5 %collective-permute-done.5 = bf16[512,2048]{1,0:T(8,128)(2,1)} collective-permute-done((bf16[512,2048]{1,0:T(8,128)(2,1)}, bf16[512,2048]{1,0:T(8,128)(2,1)}, u32[]{:S(2)}, u32[]{:S(2)}) %collective-permute-start.5) | collective-permute-done | bytes 2097184 | tf_op jit(solution)/shard_map/ppermute | solution.py:284
  321.3 44.9 %collective-permute-done.9 = bf16[512,2048]{1,0:T(8,128)(2,1)} collective-permute-done((bf16[512,2048]{1,0:T(8,128)(2,1)S(1)}, bf16[512,2048]{1,0:T(8,128)(2,1)}, u32[]{:S(2)}, u32[]{:S(2)}) %collective-permute-start.9) | collective-permute-done | bytes 2097184 | tf_op jit(solution)/shard_map/ppermute | solution.py:284
  366.2 9.5 add_add_fusion.1
  383.1 19.2 %fusion.5 = f32[1024,3072]{1,0:T(8,128)} fusion(bf16[1024,2048]{1,0:T(8,128)(2,1)} %multiply_convert_fusion.3.source, bf16[3,2048,3072]{1,2,0:T(8,128)(2,1)} %all-gather.5.cloned.1.call-done), kind=kOutput, calls=%fused_computation.15 | convolution fusion | flops 12884901888 | bytes 29360128 | tf_op jit(solution)/shard_map/dot_general | solution.py:25
  402.3 23.8 %multiply_convert_fusion.2 = (bf16[1024,3072]{1,0:T(8,128)(2,1)}, f32[1024,3072]{1,0:T(8,128)}) fusion(f32[1024,3072]{1,0:T(8,128)} %fusion.5, bf16[1024,2048]{1,0:T(8,128)(2,1)} %multiply_convert_fusion.3.source, bf16[3,2048,3072]{1,2,0:T(8,128)(2,1)} %all-gather.5.cloned.1.call-done), kind=kOutput, calls=%fused_computation.7 | convolution fusion | flops 12903776256 | bytes 48234496 | tf_op jit(solution)/shard_map/dot_general | solution.py:25
  426.0 19.4 %convert_bitcast_fusion = bf16[2048,3072]{1,0:T(8,128)(2,1)} fusion(bf16[1024,3072]{1,0:T(8,128)(2,1)} %get-tuple-element.90, bf16[1024,2048]{1,0:T(8,128)(2,1)} %bitcast.175), kind=kOutput, calls=%fused_computation.6 | convolution fusion | flops 12891193344 | bytes 23068672 | tf_op jit(solution)/shard_map/dot_general | solution.py:29
  445.5 30.0 %multiply_convert_fusion.1 = (bf16[1024,3072]{1,0:T(8,128)(2,1)}, bf16[1024,3072]{1,0:T(8,128)(2,1)}) fusion(f32[1024,3072]{1,0:T(8,128)} %fusion.5, f32[1024,3072]{1,0:T(8,128)} %get-tuple-element.234, bf16[1024,2048]{1,0:T(8,128)(2,1)} %bitcast.176, bf16[3,2048,3072]{1,2,0:T(8,128)(2,1)} %all-gather.5.cloned.1.call-done), kind=kOutput, calls=%fused_computation.5 | convolution fusion | flops 12925796352 | bytes 54525952 | tf_op jit(solution)/shard_map/dot_general | solution.py:25
  475.5 11.5 %fusion.4 = f32[512,2048]{1,0:T(8,128)S(1)} fusion(bf16[3,2048,3072]{1,2,0:T(8,128)(2,1)} %all-gather.5.cloned.1.call-done, bf16[1024,3072]{1,0:T(8,128)(2,1)} %get-tuple-element.195), kind=kOutput, calls=%fused_computation.14 | convolution fusion | flops 6442450944 | bytes 19922944 | tf_op jit(solution)/shard_map/dot_general | solution.py:33
  487.0 10.9 %add_convert_fusion.4 = bf16[512,2048]{1,0:T(8,128)(2,1)S(1)} fusion(f32[512,2048]{1,0:T(8,128)S(1)} %fusion.4, bf16[3,2048,3072]{1,2,0:T(8,128)(2,1)} %all-gather.5.cloned.1.call-done, bf16[1024,3072]{1,0:T(8,128)(2,1)S(1)} %copy-done.50), kind=kOutput, calls=%fused_computation.57 | convolution fusion | flops 6444548096 | bytes 22020096 | tf_op jit(solution)/shard_map/dot_general | solution.py:33
  499.6 10.4 %relative.1 = bf16[1024,2048]{1,0:T(8,128)(2,1)} custom-call(s32[1]{0:T(128)} %bitcast.29.rank, bf16[1024,2048]{1,0:T(8,128)(2,1)} %multiply_convert_fusion.3.source), custom_call_target="tpu_custom_call" | custom-call | tf_op jit(solution)/shard_map/relative/pallas_call | solution.py:259
  509.9 19.8 %convolution_convert_fusion = bf16[2048,3072]{1,0:T(8,128)(2,1)} fusion(bf16[1024,2048]{1,0:T(8,128)(2,1)} %multiply_convert_fusion.3.source, bf16[1024,3072]{1,0:T(8,128)(2,1)} %get-tuple-element.195), kind=kOutput, calls=%fused_computation.10 | convolution fusion | flops 12891193344 | bytes 23068672 | tf_op jit(solution)/shard_map/dot_general | solution.py:29
  529.8 10.5 %convolution_convert_fusion.2 = bf16[1024,3072]{1,0:T(8,128)(2,1)S(1)} fusion(bf16[1024,3072]{1,0:T(8,128)(2,1)} %get-tuple-element.196, bf16[1024,2048]{1,0:T(8,128)(2,1)} %relative.1), kind=kOutput, calls=%fused_computation.39 | convolution fusion | flops 6445596672 | bytes 14680064 | tf_op jit(solution)/shard_map/dot_general | solution.py:29
  540.8 10.7 %fusion.3 = f32[512,2048]{1,0:T(8,128)S(1)} fusion(bf16[3,2048,3072]{1,2,0:T(8,128)(2,1)} %all-gather.5.cloned.1.call-done, bf16[1024,3072]{1,0:T(8,128)(2,1)} %get-tuple-element.195), kind=kOutput, calls=%fused_computation.13 | convolution fusion | flops 6442450944 | bytes 19922944 | tf_op jit(solution)/shard_map/dot_general | solution.py:33
  551.6 10.7 %add_convert_fusion.3 = bf16[512,2048]{1,0:T(8,128)(2,1)S(1)} fusion(f32[512,2048]{1,0:T(8,128)S(1)} %fusion.3, bf16[3,2048,3072]{1,2,0:T(8,128)(2,1)} %all-gather.5.cloned.1.call-done, bf16[1024,3072]{1,0:T(8,128)(2,1)} %get-tuple-element.196), kind=kOutput, calls=%fused_computation.56 | convolution fusion | flops 6444548096 | bytes 22020096 | tf_op jit(solution)/shard_map/dot_general | solution.py:33
  563.2 20.3 %fusion.19 = bf16[1024,2048]{1,0:T(8,128)(2,1)} fusion(bf16[1024,3072]{1,0:T(8,128)(2,1)} %get-tuple-element.90, bf16[3,2048,3072]{1,2,0:T(8,128)(2,1)} %all-gather.5.cloned.1.call-done), kind=kOutput, calls=%fused_computation.60 | convolution fusion | flops 12886999040 | bytes 23068672 | tf_op jit(solution)/shard_map/dot_general | solution.py:33
  583.5 10.8 %add_convert_fusion = bf16[1024,3072]{1,0:T(8,128)(2,1)S(1)} fusion(bf16[1024,3072]{1,0:T(8,128)(2,1)} %collective-permute-done.12, bf16[1024,3072]{1,0:T(8,128)(2,1)} %get-tuple-element.196, bf16[1024,2048]{1,0:T(8,128)(2,1)S(1)} %copy-done.18), kind=kOutput, calls=%fused_computation.3 | convolution fusion | flops 6451888128 | bytes 20971520 | tf_op jit(solution)/shard_map/dot_general | solution.py:29
  596.3 11.4 %collective-permute-start.14 = (bf16[512,3072]{1,0:T(8,128)(2,1)}, bf16[512,3072]{1,0:T(8,128)(2,1)}, u32[]{:S(2)}, u32[]{:S(2)}) collective-permute-start(bf16[512,3072]{1,0:T(8,128)(2,1)} %slice.216), channel_id=1, source_target_pairs={{0,4},{2,6},{4,0},{6,2},{1,5},{3,7},{5,1},{7,3},{8,12},{10,14},{12... | collective-permute-start | bytes 9437192 | tf_op jit(solution)/shard_map/ppermute | solution.py:299
  623.3 8.1 subtract_add_fusion
  631.5 10.4 %fusion.57.g_out = bf16[1024,1024]{1,0:T(8,128)(2,1)} fusion(bf16[2048,3200]{0,1:T(8,128)(2,1)} %all-gather.3.cloned.1.call-done, f32[1024,2048]{1,0:T(8,128)} %subtract_add_fusion), kind=kOutput, calls=%fused_computation.88 | convolution fusion | flops 4298113024 | bytes 14680064 | tf_op jit(solution)/shard_map/dot_general | solution.py:25
  641.9 13.0 %attend_back.2 = (f32[512,1024]{1,0:T(8,128)}, f32[2,512,512]{2,1,0:T(8,128)}, bf16[2,512,512]{2,1,0:T(8,128)(2,1)}, f32[2,512,512]{2,1,0:T(8,128)}, bf16[2,512,512]{2,1,0:T(8,128)(2,1)}) custom-call(s32[4]{0:T(128)} %get-tuple-element.231.need, bf16[1024,1024]{1,0:T(8,128)(2,1)} %get-tuple-element.81.q, bf16[1024,1024]{1,0:T(8,128)(2,1)} %fusion.57.g_out, ...), custom_call_target="tpu_custom_call" | custom-call | tf_op jit(solution)/shard_map/attend_back/pallas_call | solution.py:137
  654.9 5.5 collective-permute-start.17
  660.5 12.9 %attend_back.3 = (f32[512,1024]{1,0:T(8,128)}, f32[2,512,512]{2,1,0:T(8,128)}, bf16[2,512,512]{2,1,0:T(8,128)(2,1)}, f32[2,512,512]{2,1,0:T(8,128)}, bf16[2,512,512]{2,1,0:T(8,128)(2,1)}) custom-call(s32[4]{0:T(128)} %get-tuple-element.232.need, bf16[1024,1024]{1,0:T(8,128)(2,1)} %get-tuple-element.81.q, bf16[1024,1024]{1,0:T(8,128)(2,1)} %fusion.57.g_out, ...), custom_call_target="tpu_custom_call" | custom-call | tf_op jit(solution)/shard_map/attend_back/pallas_call | solution.py:137
  673.4 6.3 collective-permute-start.21
  684.0 26.4 %collective-permute-done.14 = bf16[512,3072]{1,0:T(8,128)(2,1)} collective-permute-done((bf16[512,3072]{1,0:T(8,128)(2,1)}, bf16[512,3072]{1,0:T(8,128)(2,1)}, u32[]{:S(2)}, u32[]{:S(2)}) %collective-permute-start.14) | collective-permute-done | bytes 3145760 | tf_op jit(solution)/shard_map/ppermute | solution.py:299
  717.8 6.2 convolution_convert_fusion.3
  729.4 11.9 %collective-permute-done.18.d_far = bf16[2,512,512]{2,1,0:T(8,128)(2,1)} collective-permute-done((bf16[2,512,512]{2,1,0:T(8,128)(2,1)}, bf16[2,512,512]{2,1,0:T(8,128)(2,1)}, u32[]{:S(2)}, u32[]{:S(2)}) %collective-permute-start.18) | collective-permute-done | bytes 1048608 | tf_op jit(solution)/shard_map/ppermute | solution.py:489
  741.3 17.8 %collective-permute-done.15 = bf16[128,3072]{1,0:T(8,128)(2,1)} collective-permute-done((bf16[128,3072]{1,0:T(8,128)(2,1)}, bf16[128,3072]{1,0:T(8,128)(2,1)}, u32[]{:S(2)}, u32[]{:S(2)}) %collective-permute-start.15) | collective-permute-done | bytes 786464 | tf_op jit(solution)/shard_map/ppermute | solution.py:308
  759.1 7.8 rope_back.2
  766.9 10.0 %fusion.36 = bf16[512,2048]{1,0:T(8,128)(2,1)} fusion(bf16[512,2048]{1,0:T(8,128)(2,1)} %get-tuple-element.108, bf16[2048,3200]{0,1:T(8,128)(2,1)} %all-gather.3.cloned.1.call-done), kind=kOutput, calls=%fused_computation.74 | convolution fusion | flops 4296015872 | bytes 12582912 | tf_op jit(solution)/shard_map/dot_general | solution.py:33
  778.7 6.0 add_convert_fusion.1
  784.7 13.9 %collective-permute-done.19 = bf16[128,3072]{1,0:T(8,128)(2,1)S(1)} collective-permute-done((bf16[128,3072]{1,0:T(8,128)(2,1)}, bf16[128,3072]{1,0:T(8,128)(2,1)S(1)}, u32[]{:S(2)}, u32[]{:S(2)}) %collective-permute-start.19) | collective-permute-done | bytes 786464 | tf_op jit(solution)/shard_map/ppermute | solution.py:308
  798.6 8.1 rope_back.3
  806.8 8.8 fusion.39
  821.6 14.1 %convolution_convert_fusion.1 = bf16[2048,2048]{1,0:T(8,128)(2,1)} fusion(bf16[1024,2048]{1,0:T(8,128)(2,1)} %copy-done.17, bf16[1024,2048]{1,0:T(8,128)(2,1)} %pad_maximum_fusion.1), kind=kOutput, calls=%fused_computation.31 | convolution fusion | flops 8594128896 | bytes 16777216 | tf_op jit(solution)/shard_map/dot_general | solution.py:29
  841.3 5.9 collective-permute-start.26
  849.5 6.7 fusion.18
  870.2 13.0 %collective-permute-done.29 = f32[34,128]{1,0:T(8,128)S(1)} collective-permute-done((f32[34,128]{1,0:T(8,128)S(1)}, f32[34,128]{1,0:T(8,128)S(1)}, u32[]{:S(2)}, u32[]{:S(2)}) %collective-permute-start.29) | collective-permute-done | bytes 17440 | tf_op jit(solution)/shard_map/ppermute | solution.py:315
  897.7 70.0 %reduce-scatter.11.cloned.1.call-done = bf16[128,2048]{1,0:T(8,128)(2,1)} async-done(((bf16[2048,2048]{1,0:T(8,128)(2,1)}), bf16[128,2048]{1,0:T(8,128)(2,1)}) %reduce-scatter.11.cloned.1.call-update) | async-done | bytes 524304 | tf_op jit(solution)/shard_map/reduce_scatter | solution.py:280
  (260 shorter events, 138.2 us)
Async XLA Ops:
  7.2 116.3 %all-gather.3.cloned.1.call-start = ((), (), s32[]{:S(2)}) async-start(), calls=%async_computation.4 | async-start | bytes 13926400 | tf_op jit(solution)/shard_map/all_gather | solution.py:357
  13.8 369.3 %all-gather.5.cloned.1.call-start = ((), (), s32[]{:S(2)}) async-start(), calls=%async_computation.5 | async-start | bytes 40108032 | tf_op jit(solution)/shard_map/all_gather | solution.py:360
  15.4 108.2 %copy-start.42 = (s32[2,1,512]{2,1,0:T(1,128)S(1)}, s32[2,1,512]{2,1,0:T(1,128)}, u32[]{:S(2)}) copy-start(s32[2,1,512]{2,1,0:T(1,128)} %param.27) | copy-start | bytes 12292
  15.4 108.5 %copy-start.44 = (s32[2,1,512]{2,1,0:T(1,128)S(1)}, s32[2,1,512]{2,1,0:T(1,128)}, u32[]{:S(2)}) copy-start(s32[2,1,512]{2,1,0:T(1,128)} %param.28) | copy-start | bytes 12292
  123.5 675.1 %reduce-scatter.5.cloned.1.call-start = ((), (), s32[]{:S(2)}) async-start(), calls=%async_computation.6 | async-start | bytes 13369344 | tf_op jit(solution)/shard_map/reduce_scatter | solution.py:280
  123.6 4.7 collective-permute-start
  128.3 5.2 collective-permute-start.1
  134.6 245.8 %copy-start.36 = (f32[2048,1]{0,1:T(1,128)}, f32[2048,1]{0,1:T(1,128)S(1)}, u32[]{:S(2)}) copy-start(f32[2048,1]{0,1:T(1,128)S(1)} %get-tuple-element.197) | copy-start | bytes 24580
  160.6 99.9 %copy-start.9 = (bf16[512,1024]{1,0:T(8,128)(2,1)}, bf16[512,1024]{1,0:T(8,128)(2,1)S(1)}, u32[]{:S(2)}) copy-start(bf16[512,1024]{1,0:T(8,128)(2,1)S(1)} %get-tuple-element.204.k0.v0) | copy-start | bytes 3145732
  160.7 108.2 %copy-start.8 = (bf16[512,1024]{1,0:T(8,128)(2,1)}, bf16[512,1024]{1,0:T(8,128)(2,1)S(1)}, u32[]{:S(2)}) copy-start(bf16[512,1024]{1,0:T(8,128)(2,1)S(1)} %get-tuple-element.205.k0.v0) | copy-start | bytes 3145732
  160.7 50.2 %collective-permute-start.3 = (bf16[512,1024]{1,0:T(8,128)(2,1)S(1)}, bf16[512,1024]{1,0:T(8,128)(2,1)}, u32[]{:S(2)}, u32[]{:S(2)}) collective-permute-start(bf16[512,1024]{1,0:T(8,128)(2,1)S(1)} %get-tuple-element.204.k0.v0), channel_id=1, source_target_pairs={{0,4},{2,6},{1,5},{3,7},{8,12},{10,14},{9,13},{11,15},{16,20},{18,... | collective-permute-start | bytes 3145736 | tf_op jit(solution)/shard_map/ppermute | solution.py:406
  165.9 89.5 %collective-permute-start.7 = (bf16[512,1024]{1,0:T(8,128)(2,1)S(1)}, bf16[512,1024]{1,0:T(8,128)(2,1)S(1)}, u32[]{:S(2)}, u32[]{:S(2)}) collective-permute-start(bf16[512,1024]{1,0:T(8,128)(2,1)S(1)} %get-tuple-element.205.k0.v0), channel_id=1, source_target_pairs={{0,4},{2,6},{1,5},{3,7},{8,12},{10,14},{9,13},{11,15},{16,20},{18,... | collective-permute-start | bytes 3145736 | tf_op jit(solution)/shard_map/ppermute | solution.py:406
  167.5 93.1 %collective-permute-start.2 = (bf16[512,1024]{1,0:T(8,128)(2,1)S(1)}, bf16[512,1024]{1,0:T(8,128)(2,1)}, u32[]{:S(2)}, u32[]{:S(2)}) collective-permute-start(bf16[512,1024]{1,0:T(8,128)(2,1)S(1)} %get-tuple-element.204.k0.v0), channel_id=1, source_target_pairs={{0,2},{2,0},{4,6},{6,4},{1,3},{3,1},{5,7},{7,5},{8,10},{10,8},{12,... | collective-permute-start | bytes 3145736 | tf_op jit(solution)/shard_map/ppermute | solution.py:405
  210.9 49.7 %collective-permute-start.4 = (bf16[512,1024]{1,0:T(8,128)(2,1)}, bf16[512,1024]{1,0:T(8,128)(2,1)}, u32[]{:S(2)}, u32[]{:S(2)}) collective-permute-start(bf16[512,1024]{1,0:T(8,128)(2,1)} %collective-permute-done.3.k2.v2), channel_id=1, source_target_pairs={{0,2},{2,0},{4,6},{6,4},{1,3},{3,1},{5,7},{7,5},{8,10},{10,8},{12,... | collective-permute-start | bytes 3145736 | tf_op jit(solution)/shard_map/ppermute | solution.py:407
  213.1 63.4 %collective-permute-start.6 = (bf16[512,1024]{1,0:T(8,128)(2,1)S(1)}, bf16[512,1024]{1,0:T(8,128)(2,1)}, u32[]{:S(2)}, u32[]{:S(2)}) collective-permute-start(bf16[512,1024]{1,0:T(8,128)(2,1)S(1)} %get-tuple-element.205.k0.v0), channel_id=1, source_target_pairs={{0,2},{2,0},{4,6},{6,4},{1,3},{3,1},{5,7},{7,5},{8,10},{10,8},{12,... | collective-permute-start | bytes 3145736 | tf_op jit(solution)/shard_map/ppermute | solution.py:405
  255.4 21.1 %collective-permute-start.8 = (bf16[512,1024]{1,0:T(8,128)(2,1)S(1)}, bf16[512,1024]{1,0:T(8,128)(2,1)}, u32[]{:S(2)}, u32[]{:S(2)}) collective-permute-start(bf16[512,1024]{1,0:T(8,128)(2,1)S(1)} %collective-permute-done.7.k2.v2), channel_id=1, source_target_pairs={{0,2},{2,0},{4,6},{6,4},{1,3},{3,1},{5,7},{7,5},{8,10},{10,8},{12,... | collective-permute-start | bytes 3145736 | tf_op jit(solution)/shard_map/ppermute | solution.py:407
  275.0 46.3 %collective-permute-start.5 = (bf16[512,2048]{1,0:T(8,128)(2,1)}, bf16[512,2048]{1,0:T(8,128)(2,1)}, u32[]{:S(2)}, u32[]{:S(2)}) collective-permute-start(bf16[512,2048]{1,0:T(8,128)(2,1)} %fusion.30), channel_id=1, source_target_pairs={{0,1},{1,0},{2,3},{3,2},{4,5},{5,4},{6,7},{7,6},{8,9},{9,8},{10,11... | collective-permute-start | bytes 6291464 | tf_op jit(solution)/shard_map/ppermute | solution.py:284
  290.4 75.9 %collective-permute-start.9 = (bf16[512,2048]{1,0:T(8,128)(2,1)S(1)}, bf16[512,2048]{1,0:T(8,128)(2,1)}, u32[]{:S(2)}, u32[]{:S(2)}) collective-permute-start(bf16[512,2048]{1,0:T(8,128)(2,1)S(1)} %fusion.33), channel_id=1, source_target_pairs={{0,1},{1,0},{2,3},{3,2},{4,5},{5,4},{6,7},{7,6},{8,9},{9,8},{10,11... | collective-permute-start | bytes 6291464 | tf_op jit(solution)/shard_map/ppermute | solution.py:284
  445.4 376.2 %reduce-scatter.7.cloned.1.call-start = ((), (), s32[]{:S(2)}) async-start(), calls=%async_computation.7 | async-start | bytes 13369344 | tf_op jit(solution)/shard_map/reduce_scatter | solution.py:280
  497.9 109.8 %collective-permute-start.10 = (bf16[512,2048]{1,0:T(8,128)(2,1)S(1)}, bf16[512,2048]{1,0:T(8,128)(2,1)}, u32[]{:S(2)}, u32[]{:S(2)}) collective-permute-start(bf16[512,2048]{1,0:T(8,128)(2,1)S(1)} %add_convert_fusion.4), channel_id=1, source_target_pairs={{0,1},{1,0},{2,3},{3,2},{4,5},{5,4},{6,7},{7,6},{8,9},{9,8},{10,11... | collective-permute-start | bytes 6291464 | tf_op jit(solution)/shard_map/ppermute | solution.py:284
  529.8 353.5 %reduce-scatter.9.cloned.1.call-start = ((), (), s32[]{:S(2)}) async-start(), calls=%async_computation.8 | async-start | bytes 4456448 | tf_op jit(solution)/shard_map/reduce_scatter | solution.py:280
  540.3 43.2 %collective-permute-start.12 = (bf16[1024,3072]{1,0:T(8,128)(2,1)S(1)}, bf16[1024,3072]{1,0:T(8,128)(2,1)}, u32[]{:S(2)}, u32[]{:S(2)}) collective-permute-start(bf16[1024,3072]{1,0:T(8,128)(2,1)S(1)} %convolution_convert_fusion.2), channel_id=1, source_target_pairs={{0,2},{2,0},{4,6},{6,4},{1,3},{3,1},{5,7},{7,5},{8,10},{10,8},{12,... | collective-permute-start | bytes 18874376 | tf_op jit(solution)/shard_map/ppermute | solution.py:294
  562.3 49.6 %copy-start.15 = (bf16[512,2048]{1,0:T(8,128)(2,1)}, bf16[512,2048]{1,0:T(8,128)(2,1)S(1)}, u32[]{:S(2)}) copy-start(bf16[512,2048]{1,0:T(8,128)(2,1)S(1)} %add_convert_fusion.3) | copy-start | bytes 6291460
  562.3 21.1 %copy-start.18 = (bf16[1024,2048]{1,0:T(8,128)(2,1)S(1)}, bf16[1024,2048]{1,0:T(8,128)(2,1)}, u32[]{:S(2)}) copy-start(bf16[1024,2048]{1,0:T(8,128)(2,1)} %relative.1) | copy-start | bytes 12582916
  562.4 47.6 %collective-permute-start.11 = (bf16[512,2048]{1,0:T(8,128)(2,1)S(1)}, bf16[512,2048]{1,0:T(8,128)(2,1)S(1)}, u32[]{:S(2)}, u32[]{:S(2)}) collective-permute-start(bf16[512,2048]{1,0:T(8,128)(2,1)S(1)} %add_convert_fusion.3), channel_id=1, source_target_pairs={{0,1},{1,0},{2,3},{3,2},{4,5},{5,4},{6,7},{7,6},{8,9},{9,8},{10,11... | collective-permute-start | bytes 6291464 | tf_op jit(solution)/shard_map/ppermute | solution.py:284
  596.3 114.1 %collective-permute-start.14 = (bf16[512,3072]{1,0:T(8,128)(2,1)}, bf16[512,3072]{1,0:T(8,128)(2,1)}, u32[]{:S(2)}, u32[]{:S(2)}) collective-permute-start(bf16[512,3072]{1,0:T(8,128)(2,1)} %slice.216), channel_id=1, source_target_pairs={{0,4},{2,6},{4,0},{6,2},{1,5},{3,7},{5,1},{7,3},{8,12},{10,14},{12... | collective-permute-start | bytes 9437192 | tf_op jit(solution)/shard_map/ppermute | solution.py:299
  611.2 147.8 %collective-permute-start.13 = (bf16[1024,2048]{1,0:T(8,128)(2,1)}, bf16[1024,2048]{1,0:T(8,128)(2,1)}, u32[]{:S(2)}, u32[]{:S(2)}) collective-permute-start(bf16[1024,2048]{1,0:T(8,128)(2,1)} %fusion.19), channel_id=1, source_target_pairs={{0,1},{1,0},{2,3},{3,2},{4,5},{5,4},{6,7},{7,6},{8,9},{9,8},{10,11... | collective-permute-start | bytes 12582920 | tf_op jit(solution)/shard_map/ppermute | solution.py:284
  654.9 24.8 %collective-permute-start.17 = (bf16[2,512,512]{2,1,0:T(8,128)(2,1)}, bf16[2,512,512]{2,1,0:T(8,128)(2,1)}, u32[]{:S(2)}, u32[]{:S(2)}) collective-permute-start(bf16[2,512,512]{2,1,0:T(8,128)(2,1)} %get-tuple-element.103), channel_id=1, source_target_pairs={{0,2},{2,0},{4,6},{6,4},{1,3},{3,1},{5,7},{7,5},{8,10},{10,8},{12,... | collective-permute-start | bytes 3145736 | tf_op jit(solution)/shard_map/ppermute | solution.py:488
  660.4 19.3 %copy-start.19 = (f32[2,512,512]{2,1,0:T(8,128)S(1)}, f32[2,512,512]{2,1,0:T(8,128)}, u32[]{:S(2)}) copy-start(f32[2,512,512]{2,1,0:T(8,128)} %get-tuple-element.102) | copy-start | bytes 6291460
  673.4 50.6 %collective-permute-start.21 = (bf16[2,512,512]{2,1,0:T(8,128)(2,1)}, bf16[2,512,512]{2,1,0:T(8,128)(2,1)}, u32[]{:S(2)}, u32[]{:S(2)}) collective-permute-start(bf16[2,512,512]{2,1,0:T(8,128)(2,1)} %get-tuple-element.114), channel_id=1, source_target_pairs={{0,2},{2,0},{4,6},{6,4},{1,3},{3,1},{5,7},{7,5},{8,10},{10,8},{12,... | collective-permute-start | bytes 3145736 | tf_op jit(solution)/shard_map/ppermute | solution.py:488
  679.7 48.4 %collective-permute-start.16 = (bf16[2,512,512]{2,1,0:T(8,128)(2,1)}, bf16[2,512,512]{2,1,0:T(8,128)(2,1)S(1)}, u32[]{:S(2)}, u32[]{:S(2)}) collective-permute-start(bf16[2,512,512]{2,1,0:T(8,128)(2,1)} %get-tuple-element.101), channel_id=1, source_target_pairs={{0,2},{2,0},{4,6},{6,4},{1,3},{3,1},{5,7},{7,5},{8,10},{10,8},{12,... | collective-permute-start | bytes 3145736 | tf_op jit(solution)/shard_map/ppermute | solution.py:487
  679.7 38.0 %slice-start.2 = ((s8[8388608]{0:T(1024)(128)(4,1)}), s8[4194304]{0:T(1024)(128)(4,1)S(1)}, s32[]{:S(2)}) async-start(s8[8388608]{0:T(1024)(128)(4,1)} %bitcast.170), calls=%async_computation.12 | async-start | bytes 8388608
  682.5 35.3 %slice-start.3 = ((s8[8388608]{0:T(1024)(128)(4,1)}), s8[4194304]{0:T(1024)(128)(4,1)S(1)}, s32[]{:S(2)}) async-start(s8[8388608]{0:T(1024)(128)(4,1)} %bitcast.170), calls=%async_computation.13 | async-start | bytes 8388608
  682.5 58.8 %collective-permute-start.18 = (bf16[2,512,512]{2,1,0:T(8,128)(2,1)}, bf16[2,512,512]{2,1,0:T(8,128)(2,1)}, u32[]{:S(2)}, u32[]{:S(2)}) collective-permute-start(bf16[2,512,512]{2,1,0:T(8,128)(2,1)} %add_convert_fusion.6), channel_id=1, source_target_pairs={{4,0},{6,2},{5,1},{7,3},{12,8},{14,10},{13,9},{15,11},{20,16},{22,... | collective-permute-start | bytes 3145736 | tf_op jit(solution)/shard_map/ppermute | solution.py:489
  717.7 41.3 %collective-permute-start.15 = (bf16[128,3072]{1,0:T(8,128)(2,1)}, bf16[128,3072]{1,0:T(8,128)(2,1)}, u32[]{:S(2)}, u32[]{:S(2)}) collective-permute-start(bf16[128,3072]{1,0:T(8,128)(2,1)} %get-tuple-element.203), channel_id=1, source_target_pairs={{0,8},{8,0},{16,24},{24,16},{1,9},{9,1},{17,25},{25,17},{2,10},{10... | collective-permute-start | bytes 2359304 | tf_op jit(solution)/shard_map/ppermute | solution.py:308
  724.0 243.8 %reduce-scatter.11.cloned.1.call-start = ((), (), s32[]{:S(2)}) async-start(), calls=%async_computation.9 | async-start | bytes 8912896 | tf_op jit(solution)/shard_map/reduce_scatter | solution.py:280
  724.0 60.7 %collective-permute-start.20 = (bf16[2,512,512]{2,1,0:T(8,128)(2,1)}, bf16[2,512,512]{2,1,0:T(8,128)(2,1)}, u32[]{:S(2)}, u32[]{:S(2)}) collective-permute-start(bf16[2,512,512]{2,1,0:T(8,128)(2,1)} %get-tuple-element.112), channel_id=1, source_target_pairs={{0,2},{2,0},{4,6},{6,4},{1,3},{3,1},{5,7},{7,5},{8,10},{10,8},{12,... | collective-permute-start | bytes 3145736 | tf_op jit(solution)/shard_map/ppermute | solution.py:487
  728.1 31.0 %copy-start.27 = (bf16[2,512,512]{2,1,0:T(8,128)(2,1)}, bf16[2,512,512]{2,1,0:T(8,128)(2,1)S(1)}, u32[]{:S(2)}) copy-start(bf16[2,512,512]{2,1,0:T(8,128)(2,1)S(1)} %collective-permute-done.16.d_near) | copy-start | bytes 3145732
  728.1 56.6 %collective-permute-start.22 = (bf16[2,512,512]{2,1,0:T(8,128)(2,1)}, bf16[2,512,512]{2,1,0:T(8,128)(2,1)S(1)}, u32[]{:S(2)}, u32[]{:S(2)}) collective-permute-start(bf16[2,512,512]{2,1,0:T(8,128)(2,1)} %add_convert_fusion.5), channel_id=1, source_target_pairs={{4,0},{6,2},{5,1},{7,3},{12,8},{14,10},{13,9},{15,11},{20,16},{22,... | collective-permute-start | bytes 3145736 | tf_op jit(solution)/shard_map/ppermute | solution.py:489
  741.3 57.3 %collective-permute-start.19 = (bf16[128,3072]{1,0:T(8,128)(2,1)}, bf16[128,3072]{1,0:T(8,128)(2,1)S(1)}, u32[]{:S(2)}, u32[]{:S(2)}) collective-permute-start(bf16[128,3072]{1,0:T(8,128)(2,1)} %get-tuple-element.202), channel_id=1, source_target_pairs={{0,16},{8,24},{16,0},{24,8},{1,17},{9,25},{17,1},{25,9},{2,18},{10... | collective-permute-start | bytes 2359304 | tf_op jit(solution)/shard_map/ppermute | solution.py:308
  759.1 62.5 %collective-permute-start.23 = (bf16[128,3072]{1,0:T(8,128)(2,1)}, bf16[128,3072]{1,0:T(8,128)(2,1)}, u32[]{:S(2)}, u32[]{:S(2)}) collective-permute-start(bf16[128,3072]{1,0:T(8,128)(2,1)} %get-tuple-element.201), channel_id=1, source_target_pairs={{0,24},{8,16},{16,8},{24,0},{1,25},{9,17},{17,9},{25,1},{2,26},{10... | collective-permute-start | bytes 2359304 | tf_op jit(solution)/shard_map/ppermute | solution.py:308
  776.9 44.7 %collective-permute-start.24 = (bf16[512,2048]{1,0:T(8,128)(2,1)}, bf16[512,2048]{1,0:T(8,128)(2,1)}, u32[]{:S(2)}, u32[]{:S(2)}) collective-permute-start(bf16[512,2048]{1,0:T(8,128)(2,1)} %fusion.36), channel_id=1, source_target_pairs={{0,1},{1,0},{2,3},{3,2},{4,5},{5,4},{6,7},{7,6},{8,9},{9,8},{10,11... | collective-permute-start | bytes 6291464 | tf_op jit(solution)/shard_map/ppermute | solution.py:284
  835.7 47.6 %collective-permute-start.30 = (bf16[512,2048]{1,0:T(8,128)(2,1)S(1)}, bf16[512,2048]{1,0:T(8,128)(2,1)}, u32[]{:S(2)}, u32[]{:S(2)}) collective-permute-start(bf16[512,2048]{1,0:T(8,128)(2,1)S(1)} %fusion.39), channel_id=1, source_target_pairs={{0,1},{1,0},{2,3},{3,2},{4,5},{5,4},{6,7},{7,6},{8,9},{9,8},{10,11... | collective-permute-start | bytes 6291464 | tf_op jit(solution)/shard_map/ppermute | solution.py:284
  836.8 4.5 collective-permute-start.25
  841.3 8.0 collective-permute-start.26
  849.4 6.8 collective-permute-start.27
  856.1 7.3 collective-permute-start.28
  863.4 19.8 %collective-permute-start.29 = (f32[34,128]{1,0:T(8,128)S(1)}, f32[34,128]{1,0:T(8,128)S(1)}, u32[]{:S(2)}, u32[]{:S(2)}) collective-permute-start(f32[34,128]{1,0:T(8,128)S(1)} %add.172), channel_id=1, source_target_pairs={{0,1},{1,0},{2,3},{3,2},{4,5},{5,4},{6,7},{7,6},{8,9},{9,8},{10,11... | collective-permute-start | bytes 52232 | tf_op jit(solution)/shard_map/ppermute | solution.py:315
  (44 other events, 295.7 us)
Sparse Core Ops, SparseCore 0:
  13.9 109.4 all-gather.2
  125.0 235.1 all-gather.4
  445.5 142.9 reduce-scatter.4
  592.4 195.1 reduce-scatter.6
  791.3 70.1 reduce-scatter.8
  865.5 102.2 reduce-scatter.10

commit v8 on v7

--- a/solution.py
+++ b/solution.py
@@ -355,7 +355,7 @@
         )
         first = jnp.concatenate([w_query, w_key, w_value, w_out.T, gains], axis=1)
         first = lax.all_gather(first, data_axes, axis=0, tiled=True)
-        second = jnp.stack([w_gate, w_up, w_down.T])
+        second = jnp.stack([w_gate, w_up])
         second, first = lax.optimization_barrier((second, first))
         second = lax.all_gather(second, data_axes, axis=1, tiled=True)
         tokens = hidden.reshape(total, width).astype(F32)
@@ -386,13 +386,15 @@
         w_out_t = first[:, qkv_cols : qkv_cols + q_cols]
         gain_attn = first[:, qkv_cols + q_cols].astype(F32)
         gain_ffn = first[:, qkv_cols + q_cols + 64].astype(F32)
-        gate_full, up_full, down_t = second[0], second[1], second[2]
+        gate_full, up_full = second[0], second[1]
         gain_heads = jnp.stack([norm_query, norm_key]).astype(F32)
 
         cot = lax.optimization_barrier(cotangent.reshape(total, width))
 
         normed_attn = (tokens * inv_attn * gain_attn).astype(BF16)
         raw = dot(normed_attn, w_qkv)
+        down_own, raw = lax.optimization_barrier((w_down.T, raw))
+        down_t = lax.all_gather(down_own, data_axes, axis=0, tiled=True)
         queries, pairs = rope(raw, turn, gain_heads, q_cols, k_cols)
 
         cuts = [slice(step * rows, (step + 1) * rows) for step in range(MICRO)]

time: 986 us -> 1000 us (1.014)
  waiting for transfers between devices: 418 us -> 438 us
    unnamed x124 -> x116, local copies, waits for them, and re-layouts: 22.2 us -> 16.6 us
  transfers between devices with their start and end apart: 37 -> 38, of which waited for: 14 -> 14; matrix products, arithmetic and copies ran while one was open for 33% -> 40% of each run, Pallas kernels for 8% -> 8%
where the time goes in v8:
time: 1000 us; the launch traced here: 999 us
  waiting for transfers between devices  438 us (44%)
  matrix products  276 us (28%)
  other arithmetic  101 us (10%)
  Pallas kernels  78.4 us (8%)
  starting transfers between devices  53.3 us (5%)
  local copies, waits for them, and re-layouts  36.2 us (4%)
  between operations  15.5 us (2%)
    all_gather x1, waiting for transfers between devices, local(): first = lax.all_gather(first, data_axes, axis=0, tiled=True)  107 us
    dot_general x5, matrix products, dot(): return jnp.dot(left, right, preferred_element_type=F32)  98.5 us
    dot_general x9, matrix products, rdot(): lax.dot_general(left, right, (((1,), (1,)), ((), ())), preferred_element_...  97.1 us
    ppermute x2, waiting for transfers between devices, local(): far = lax.ppermute(own, 'seq', up_pairs)  84 us
    dot_general x6, matrix products, tdot(): lax.dot_general(left, right, (((0,), (0,)), ((), ())), preferred_element_...  80.6 us
    reduce_scatter x4, waiting for transfers between devices, scatter(): return lax.psum_scatter(grad, data_axes, scatter_dimension=0, tiled=True)  79 us
    ppermute x7, waiting for transfers between devices, mp_other(): return lax.ppermute(part, 'mp', [(0, 1), (1, 0)])  72.9 us
    ppermute x3, waiting for transfers between devices, line_stage(): lax.ppermute(sent, 'dp', [(i, i ^ flip) for i in range(dp_size)])  33.5 us
  transfers between devices with their start and end apart: 38, of which 14 were waited for; matrix products, arithmetic and copies ran while one was open for 40% of the time, Pallas kernels for 8%

profile of v8, /device:TPU:0, one launch (start us, length us, event | category | flops | bytes accessed | tf_op | source)
XLA Modules:
  0.0 998.8 jit_solution(4926964303470143953)
XLA Ops:
  16.5 107.0 %all-gather.4.cloned.1.call-done = bf16[2048,3200]{0,1:T(8,128)(2,1)} async-done(((bf16[128,3200]{0,1:T(8,128)(2,1)}), bf16[2048,3200]{0,1:T(8,128)(2,1)}) %all-gather.4.cloned.1.call-update) | async-done | bytes 13107216 | tf_op jit(solution)/shard_map/all_gather | solution.py:357
  138.0 14.9 %fusion.13.raw = f32[1024,2048]{1,0:T(8,128)} fusion(bf16[1024,2048]{1,0:T(8,128)(2,1)S(1)} %fusion.8, bf16[2048,3200]{0,1:T(8,128)(2,1)} %all-gather.4.cloned.1.call-done), kind=kOutput, calls=%fused_computation.33 | convolution fusion | flops 8589934592 | bytes 20971520 | tf_op jit(solution)/shard_map/dot_general | solution.py:25
  153.6 9.5 rope.1
  164.9 5.5 collective-permute-start.3
  172.0 43.4 %collective-permute-done.3.k2.v2 = bf16[512,1024]{1,0:T(8,128)(2,1)} collective-permute-done((bf16[512,1024]{1,0:T(8,128)(2,1)S(1)}, bf16[512,1024]{1,0:T(8,128)(2,1)}, u32[]{:S(2)}, u32[]{:S(2)}) %collective-permute-start.3) | collective-permute-done | bytes 1048608 | tf_op jit(solution)/shard_map/ppermute | solution.py:408
  219.2 40.7 %collective-permute-done.7.k2.v2 = bf16[512,1024]{1,0:T(8,128)(2,1)S(1)} collective-permute-done((bf16[512,1024]{1,0:T(8,128)(2,1)S(1)}, bf16[512,1024]{1,0:T(8,128)(2,1)S(1)}, u32[]{:S(2)}, u32[]{:S(2)}) %collective-permute-start.7) | collective-permute-done | bytes 1048608 | tf_op jit(solution)/shard_map/ppermute | solution.py:408
  265.1 8.3 attend.2
  273.3 6.2 fusion.27
  281.0 8.7 attend.3
  289.6 5.0 fusion.30
  299.7 26.0 %collective-permute-done.5 = bf16[512,2048]{1,0:T(8,128)(2,1)} collective-permute-done((bf16[512,2048]{1,0:T(8,128)(2,1)}, bf16[512,2048]{1,0:T(8,128)(2,1)}, u32[]{:S(2)}, u32[]{:S(2)}) %collective-permute-start.5) | collective-permute-done | bytes 2097184 | tf_op jit(solution)/shard_map/ppermute | solution.py:284
  325.7 44.9 %collective-permute-done.9 = bf16[512,2048]{1,0:T(8,128)(2,1)} collective-permute-done((bf16[512,2048]{1,0:T(8,128)(2,1)S(1)}, bf16[512,2048]{1,0:T(8,128)(2,1)}, u32[]{:S(2)}, u32[]{:S(2)}) %collective-permute-start.9) | collective-permute-done | bytes 2097184 | tf_op jit(solution)/shard_map/ppermute | solution.py:284
  370.6 9.5 add_add_fusion.1
  387.6 19.1 %fusion.3 = f32[1024,3072]{1,0:T(8,128)} fusion(bf16[1024,2048]{1,0:T(8,128)(2,1)} %multiply_convert_fusion.3.source, bf16[2,2048,3072]{2,1,0:T(8,128)(2,1)} %all-gather.6.cloned.1.call-done), kind=kOutput, calls=%fused_computation.12 | convolution fusion | flops 12884901888 | bytes 29360128 | tf_op jit(solution)/shard_map/dot_general | solution.py:25
  406.7 23.6 %multiply_convert_fusion.2 = (bf16[1024,3072]{1,0:T(8,128)(2,1)}, f32[1024,3072]{1,0:T(8,128)}) fusion(f32[1024,3072]{1,0:T(8,128)} %fusion.3, bf16[1024,2048]{1,0:T(8,128)(2,1)} %multiply_convert_fusion.3.source, bf16[2,2048,3072]{2,1,0:T(8,128)(2,1)} %all-gather.6.cloned.1.call-done), kind=kOutput, calls=%fused_computation.6 | convolution fusion | flops 12903776256 | bytes 48234496 | tf_op jit(solution)/shard_map/dot_general | solution.py:25
  430.3 19.3 %convert_bitcast_fusion = bf16[2048,3072]{1,0:T(8,128)(2,1)} fusion(bf16[1024,3072]{1,0:T(8,128)(2,1)} %get-tuple-element.94, bf16[1024,2048]{1,0:T(8,128)(2,1)} %bitcast.167), kind=kOutput, calls=%fused_computation.5 | convolution fusion | flops 12891193344 | bytes 23068672 | tf_op jit(solution)/shard_map/dot_general | solution.py:29
  449.7 30.2 %multiply_convert_fusion.1 = (bf16[1024,3072]{1,0:T(8,128)(2,1)}, bf16[1024,3072]{1,0:T(8,128)(2,1)}) fusion(f32[1024,3072]{1,0:T(8,128)} %fusion.3, f32[1024,3072]{1,0:T(8,128)} %get-tuple-element.238, bf16[1024,2048]{1,0:T(8,128)(2,1)} %bitcast.168, bf16[2048,3072]{0,1:T(8,128)(2,1)} %all-gather.8.cloned.1.call-done), kind=kOutput, calls=%fused_computation.4 | convolution fusion | flops 12925796352 | bytes 54525952 | tf_op jit(solution)/shard_map/dot_general | solution.py:25
  480.0 11.7 %fusion.2 = f32[512,2048]{1,0:T(8,128)S(1)} fusion(bf16[2,2048,3072]{2,1,0:T(8,128)(2,1)} %all-gather.6.cloned.1.call-done, bf16[1024,3072]{1,0:T(8,128)(2,1)} %get-tuple-element.199), kind=kOutput, calls=%fused_computation.11 | convolution fusion | flops 6442450944 | bytes 19922944 | tf_op jit(solution)/shard_map/dot_general | solution.py:33
  491.7 11.2 %add_convert_fusion.4 = bf16[512,2048]{1,0:T(8,128)(2,1)S(1)} fusion(f32[512,2048]{1,0:T(8,128)S(1)} %fusion.2, bf16[2,2048,3072]{2,1,0:T(8,128)(2,1)} %all-gather.6.cloned.1.call-done, bf16[1024,3072]{1,0:T(8,128)(2,1)S(1)} %copy-done.47), kind=kOutput, calls=%fused_computation.54 | convolution fusion | flops 6444548096 | bytes 22020096 | tf_op jit(solution)/shard_map/dot_general | solution.py:33
  503.7 10.4 %relative.1 = bf16[1024,2048]{1,0:T(8,128)(2,1)} custom-call(s32[1]{0:T(128)} %bitcast.27.rank, bf16[1024,2048]{1,0:T(8,128)(2,1)} %multiply_convert_fusion.3.source), custom_call_target="tpu_custom_call" | custom-call | tf_op jit(solution)/shard_map/relative/pallas_call | solution.py:259
  514.1 19.9 %convolution_convert_fusion = bf16[2048,3072]{1,0:T(8,128)(2,1)} fusion(bf16[1024,2048]{1,0:T(8,128)(2,1)} %multiply_convert_fusion.3.source, bf16[1024,3072]{1,0:T(8,128)(2,1)} %get-tuple-element.199), kind=kOutput, calls=%fused_computation.9 | convolution fusion | flops 12891193344 | bytes 23068672 | tf_op jit(solution)/shard_map/dot_general | solution.py:29
  534.0 10.4 %convolution_convert_fusion.2 = bf16[1024,3072]{1,0:T(8,128)(2,1)S(1)} fusion(bf16[1024,3072]{1,0:T(8,128)(2,1)} %get-tuple-element.200, bf16[1024,2048]{1,0:T(8,128)(2,1)} %relative.1), kind=kOutput, calls=%fused_computation.36 | convolution fusion | flops 6445596672 | bytes 14680064 | tf_op jit(solution)/shard_map/dot_general | solution.py:29
  546.3 12.1 %fusion.1 = f32[512,2048]{1,0:T(8,128)} fusion(bf16[2,2048,3072]{2,1,0:T(8,128)(2,1)} %all-gather.6.cloned.1.call-done, bf16[1024,3072]{1,0:T(8,128)(2,1)} %get-tuple-element.199), kind=kOutput, calls=%fused_computation.10 | convolution fusion | flops 6442450944 | bytes 19922944 | tf_op jit(solution)/shard_map/dot_general | solution.py:33
  558.4 11.2 %add_convert_fusion.3 = bf16[512,2048]{1,0:T(8,128)(2,1)S(1)} fusion(f32[512,2048]{1,0:T(8,128)} %fusion.1, bf16[2,2048,3072]{2,1,0:T(8,128)(2,1)} %all-gather.6.cloned.1.call-done, bf16[1024,3072]{1,0:T(8,128)(2,1)} %get-tuple-element.200), kind=kOutput, calls=%fused_computation.53 | convolution fusion | flops 6444548096 | bytes 22020096 | tf_op jit(solution)/shard_map/dot_general | solution.py:33
  570.4 20.4 %convolution_convert_fusion.3 = bf16[1024,2048]{1,0:T(8,128)(2,1)} fusion(bf16[1024,3072]{1,0:T(8,128)(2,1)} %get-tuple-element.94, bf16[2048,3072]{0,1:T(8,128)(2,1)} %all-gather.8.cloned.1.call-done), kind=kOutput, calls=%fused_computation.57 | convolution fusion | flops 12886999040 | bytes 23068672 | tf_op jit(solution)/shard_map/dot_general | solution.py:33
  590.8 10.8 %add_convert_fusion = bf16[1024,3072]{1,0:T(8,128)(2,1)S(1)} fusion(bf16[1024,3072]{1,0:T(8,128)(2,1)} %collective-permute-done.12, bf16[1024,3072]{1,0:T(8,128)(2,1)} %get-tuple-element.200, bf16[1024,2048]{1,0:T(8,128)(2,1)S(1)} %copy-done.18), kind=kOutput, calls=%fused_computation.2 | convolution fusion | flops 6451888128 | bytes 20971520 | tf_op jit(solution)/shard_map/dot_general | solution.py:29
  603.7 11.7 %collective-permute-start.14 = (bf16[512,3072]{1,0:T(8,128)(2,1)}, bf16[512,3072]{1,0:T(8,128)(2,1)}, u32[]{:S(2)}, u32[]{:S(2)}) collective-permute-start(bf16[512,3072]{1,0:T(8,128)(2,1)} %slice.211), channel_id=1, source_target_pairs={{0,4},{2,6},{4,0},{6,2},{1,5},{3,7},{5,1},{7,3},{8,12},{10,14},{12... | collective-permute-start | bytes 9437192 | tf_op jit(solution)/shard_map/ppermute | solution.py:299
  628.7 8.6 subtract_add_fusion
  637.3 10.7 %fusion.54.g_out = bf16[1024,1024]{1,0:T(8,128)(2,1)} fusion(bf16[2048,3200]{0,1:T(8,128)(2,1)} %all-gather.4.cloned.1.call-done, f32[1024,2048]{1,0:T(8,128)} %subtract_add_fusion), kind=kOutput, calls=%fused_computation.84 | convolution fusion | flops 4298113024 | bytes 14680064 | tf_op jit(solution)/shard_map/dot_general | solution.py:25
  647.9 12.9 %attend_back.2 = (f32[512,1024]{1,0:T(8,128)}, f32[2,512,512]{2,1,0:T(8,128)}, bf16[2,512,512]{2,1,0:T(8,128)(2,1)}, f32[2,512,512]{2,1,0:T(8,128)}, bf16[2,512,512]{2,1,0:T(8,128)(2,1)}) custom-call(s32[4]{0:T(128)} %get-tuple-element.235.need, bf16[1024,1024]{1,0:T(8,128)(2,1)} %get-tuple-element.84.q, bf16[1024,1024]{1,0:T(8,128)(2,1)} %fusion.54.g_out, ...), custom_call_target="tpu_custom_call" | custom-call | tf_op jit(solution)/shard_map/attend_back/pallas_call | solution.py:137
  660.8 5.1 collective-permute-start.17
  666.0 13.0 %attend_back.3 = (f32[512,1024]{1,0:T(8,128)}, f32[2,512,512]{2,1,0:T(8,128)}, bf16[2,512,512]{2,1,0:T(8,128)(2,1)}, f32[2,512,512]{2,1,0:T(8,128)}, bf16[2,512,512]{2,1,0:T(8,128)(2,1)}) custom-call(s32[4]{0:T(128)} %get-tuple-element.236.need, bf16[1024,1024]{1,0:T(8,128)(2,1)} %get-tuple-element.84.q, bf16[1024,1024]{1,0:T(8,128)(2,1)} %fusion.54.g_out, ...), custom_call_target="tpu_custom_call" | custom-call | tf_op jit(solution)/shard_map/attend_back/pallas_call | solution.py:137
  679.0 6.2 collective-permute-start.21
  689.5 28.1 %collective-permute-done.14 = bf16[512,3072]{1,0:T(8,128)(2,1)} collective-permute-done((bf16[512,3072]{1,0:T(8,128)(2,1)}, bf16[512,3072]{1,0:T(8,128)(2,1)}, u32[]{:S(2)}, u32[]{:S(2)}) %collective-permute-start.14) | collective-permute-done | bytes 3145760 | tf_op jit(solution)/shard_map/ppermute | solution.py:299
  725.0 6.1 convolution_convert_fusion.4
  736.6 14.1 %collective-permute-done.18.d_far = bf16[2,512,512]{2,1,0:T(8,128)(2,1)} collective-permute-done((bf16[2,512,512]{2,1,0:T(8,128)(2,1)}, bf16[2,512,512]{2,1,0:T(8,128)(2,1)}, u32[]{:S(2)}, u32[]{:S(2)}) %collective-permute-start.18) | collective-permute-done | bytes 1048608 | tf_op jit(solution)/shard_map/ppermute | solution.py:491
  750.7 15.6 %collective-permute-done.15 = bf16[128,3072]{1,0:T(8,128)(2,1)} collective-permute-done((bf16[128,3072]{1,0:T(8,128)(2,1)}, bf16[128,3072]{1,0:T(8,128)(2,1)}, u32[]{:S(2)}, u32[]{:S(2)}) %collective-permute-start.15) | collective-permute-done | bytes 786464 | tf_op jit(solution)/shard_map/ppermute | solution.py:308
  766.2 7.8 rope_back.2
  774.0 10.1 %fusion.33 = bf16[512,2048]{1,0:T(8,128)(2,1)} fusion(bf16[512,2048]{1,0:T(8,128)(2,1)} %get-tuple-element.112, bf16[2048,3200]{0,1:T(8,128)(2,1)} %all-gather.4.cloned.1.call-done), kind=kOutput, calls=%fused_computation.71 | convolution fusion | flops 4296015872 | bytes 12582912 | tf_op jit(solution)/shard_map/dot_general | solution.py:33
  784.1 6.0 add_convert_fusion.1
  790.1 17.9 %collective-permute-done.19 = bf16[128,3072]{1,0:T(8,128)(2,1)S(1)} collective-permute-done((bf16[128,3072]{1,0:T(8,128)(2,1)}, bf16[128,3072]{1,0:T(8,128)(2,1)S(1)}, u32[]{:S(2)}, u32[]{:S(2)}) %collective-permute-start.19) | collective-permute-done | bytes 786464 | tf_op jit(solution)/shard_map/ppermute | solution.py:308
  808.1 7.9 rope_back.3
  816.0 9.2 fusion.36
  831.0 14.1 %convolution_convert_fusion.1 = bf16[2048,2048]{1,0:T(8,128)(2,1)} fusion(bf16[1024,2048]{1,0:T(8,128)(2,1)} %copy-done.17, bf16[1024,2048]{1,0:T(8,128)(2,1)} %pad_maximum_fusion.1), kind=kOutput, calls=%fused_computation.28 | convolution fusion | flops 8594128896 | bytes 16777216 | tf_op jit(solution)/shard_map/dot_general | solution.py:29
  856.5 6.7 fusion.16
  876.9 16.1 %collective-permute-done.29 = f32[34,128]{1,0:T(8,128)S(1)} collective-permute-done((f32[34,128]{1,0:T(8,128)S(1)}, f32[34,128]{1,0:T(8,128)S(1)}, u32[]{:S(2)}, u32[]{:S(2)}) %collective-permute-start.29) | collective-permute-done | bytes 17440 | tf_op jit(solution)/shard_map/ppermute | solution.py:315
  900.4 6.1 fusion.53
  908.9 79.0 %reduce-scatter.11.cloned.1.call-done = bf16[128,2048]{1,0:T(8,128)(2,1)} async-done(((bf16[2048,2048]{1,0:T(8,128)(2,1)}), bf16[128,2048]{1,0:T(8,128)(2,1)}) %reduce-scatter.11.cloned.1.call-update) | async-done | bytes 524304 | tf_op jit(solution)/shard_map/reduce_scatter | solution.py:280
  (255 shorter events, 130.7 us)
Async XLA Ops:
  7.2 116.3 %copy-start.40 = (s32[2,1,512]{2,1,0:T(1,128)S(1)}, s32[2,1,512]{2,1,0:T(1,128)}, u32[]{:S(2)}) copy-start(s32[2,1,512]{2,1,0:T(1,128)} %param.27) | copy-start | bytes 12292
  7.2 116.6 %copy-start.42 = (s32[2,1,512]{2,1,0:T(1,128)S(1)}, s32[2,1,512]{2,1,0:T(1,128)}, u32[]{:S(2)}) copy-start(s32[2,1,512]{2,1,0:T(1,128)} %param.28) | copy-start | bytes 12292
  7.2 116.2 %all-gather.4.cloned.1.call-start = ((), (), s32[]{:S(2)}) async-start(), calls=%async_computation.4 | async-start | bytes 13926400 | tf_op jit(solution)/shard_map/all_gather | solution.py:357
  13.7 373.8 %all-gather.6.cloned.1.call-start = ((), (), s32[]{:S(2)}) async-start(), calls=%async_computation.5 | async-start | bytes 26738688 | tf_op jit(solution)/shard_map/all_gather | solution.py:360
  123.4 326.3 %all-gather.8.cloned.1.call-start = ((), (), s32[]{:S(2)}) async-start(), calls=%async_computation.6 | async-start | bytes 13369344 | tf_op jit(solution)/shard_map/all_gather | solution.py:397
  123.5 4.7 collective-permute-start
  128.2 4.8 collective-permute-start.1
  134.1 250.8 %copy-start.34 = (f32[2048,1]{0,1:T(1,128)}, f32[2048,1]{0,1:T(1,128)S(1)}, u32[]{:S(2)}) copy-start(f32[2048,1]{0,1:T(1,128)S(1)} %get-tuple-element.201) | copy-start | bytes 24580
  152.9 655.1 %reduce-scatter.5.cloned.1.call-start = ((), (), s32[]{:S(2)}) async-start(), calls=%async_computation.7 | async-start | bytes 13369344 | tf_op jit(solution)/shard_map/reduce_scatter | solution.py:280
  164.8 100.2 %copy-start.9 = (bf16[512,1024]{1,0:T(8,128)(2,1)}, bf16[512,1024]{1,0:T(8,128)(2,1)S(1)}, u32[]{:S(2)}) copy-start(bf16[512,1024]{1,0:T(8,128)(2,1)S(1)} %get-tuple-element.208.k0.v0) | copy-start | bytes 3145732
  164.9 108.5 %copy-start.8 = (bf16[512,1024]{1,0:T(8,128)(2,1)}, bf16[512,1024]{1,0:T(8,128)(2,1)S(1)}, u32[]{:S(2)}) copy-start(bf16[512,1024]{1,0:T(8,128)(2,1)S(1)} %get-tuple-element.209.k0.v0) | copy-start | bytes 3145732
  164.9 50.5 %collective-permute-start.3 = (bf16[512,1024]{1,0:T(8,128)(2,1)S(1)}, bf16[512,1024]{1,0:T(8,128)(2,1)}, u32[]{:S(2)}, u32[]{:S(2)}) collective-permute-start(bf16[512,1024]{1,0:T(8,128)(2,1)S(1)} %get-tuple-element.208.k0.v0), channel_id=1, source_target_pairs={{0,4},{2,6},{1,5},{3,7},{8,12},{10,14},{9,13},{11,15},{16,20},{18,... | collective-permute-start | bytes 3145736 | tf_op jit(solution)/shard_map/ppermute | solution.py:408
  170.3 89.5 %collective-permute-start.7 = (bf16[512,1024]{1,0:T(8,128)(2,1)S(1)}, bf16[512,1024]{1,0:T(8,128)(2,1)S(1)}, u32[]{:S(2)}, u32[]{:S(2)}) collective-permute-start(bf16[512,1024]{1,0:T(8,128)(2,1)S(1)} %get-tuple-element.209.k0.v0), channel_id=1, source_target_pairs={{0,4},{2,6},{1,5},{3,7},{8,12},{10,14},{9,13},{11,15},{16,20},{18,... | collective-permute-start | bytes 3145736 | tf_op jit(solution)/shard_map/ppermute | solution.py:408
  171.9 93.2 %collective-permute-start.2 = (bf16[512,1024]{1,0:T(8,128)(2,1)S(1)}, bf16[512,1024]{1,0:T(8,128)(2,1)}, u32[]{:S(2)}, u32[]{:S(2)}) collective-permute-start(bf16[512,1024]{1,0:T(8,128)(2,1)S(1)} %get-tuple-element.208.k0.v0), channel_id=1, source_target_pairs={{0,2},{2,0},{4,6},{6,4},{1,3},{3,1},{5,7},{7,5},{8,10},{10,8},{12,... | collective-permute-start | bytes 3145736 | tf_op jit(solution)/shard_map/ppermute | solution.py:407
  215.3 49.7 %collective-permute-start.4 = (bf16[512,1024]{1,0:T(8,128)(2,1)}, bf16[512,1024]{1,0:T(8,128)(2,1)}, u32[]{:S(2)}, u32[]{:S(2)}) collective-permute-start(bf16[512,1024]{1,0:T(8,128)(2,1)} %collective-permute-done.3.k2.v2), channel_id=1, source_target_pairs={{0,2},{2,0},{4,6},{6,4},{1,3},{3,1},{5,7},{7,5},{8,10},{10,8},{12,... | collective-permute-start | bytes 3145736 | tf_op jit(solution)/shard_map/ppermute | solution.py:409
  217.6 63.3 %collective-permute-start.6 = (bf16[512,1024]{1,0:T(8,128)(2,1)S(1)}, bf16[512,1024]{1,0:T(8,128)(2,1)}, u32[]{:S(2)}, u32[]{:S(2)}) collective-permute-start(bf16[512,1024]{1,0:T(8,128)(2,1)S(1)} %get-tuple-element.209.k0.v0), channel_id=1, source_target_pairs={{0,2},{2,0},{4,6},{6,4},{1,3},{3,1},{5,7},{7,5},{8,10},{10,8},{12,... | collective-permute-start | bytes 3145736 | tf_op jit(solution)/shard_map/ppermute | solution.py:407
  259.8 21.1 %collective-permute-start.8 = (bf16[512,1024]{1,0:T(8,128)(2,1)S(1)}, bf16[512,1024]{1,0:T(8,128)(2,1)}, u32[]{:S(2)}, u32[]{:S(2)}) collective-permute-start(bf16[512,1024]{1,0:T(8,128)(2,1)S(1)} %collective-permute-done.7.k2.v2), channel_id=1, source_target_pairs={{0,2},{2,0},{4,6},{6,4},{1,3},{3,1},{5,7},{7,5},{8,10},{10,8},{12,... | collective-permute-start | bytes 3145736 | tf_op jit(solution)/shard_map/ppermute | solution.py:409
  279.5 46.2 %collective-permute-start.5 = (bf16[512,2048]{1,0:T(8,128)(2,1)}, bf16[512,2048]{1,0:T(8,128)(2,1)}, u32[]{:S(2)}, u32[]{:S(2)}) collective-permute-start(bf16[512,2048]{1,0:T(8,128)(2,1)} %fusion.27), channel_id=1, source_target_pairs={{0,1},{1,0},{2,3},{3,2},{4,5},{5,4},{6,7},{7,6},{8,9},{9,8},{10,11... | collective-permute-start | bytes 6291464 | tf_op jit(solution)/shard_map/ppermute | solution.py:284
  294.6 76.0 %collective-permute-start.9 = (bf16[512,2048]{1,0:T(8,128)(2,1)S(1)}, bf16[512,2048]{1,0:T(8,128)(2,1)}, u32[]{:S(2)}, u32[]{:S(2)}) collective-permute-start(bf16[512,2048]{1,0:T(8,128)(2,1)S(1)} %fusion.30), channel_id=1, source_target_pairs={{0,1},{1,0},{2,3},{3,2},{4,5},{5,4},{6,7},{7,6},{8,9},{9,8},{10,11... | collective-permute-start | bytes 6291464 | tf_op jit(solution)/shard_map/ppermute | solution.py:284
  449.6 381.4 %reduce-scatter.7.cloned.1.call-start = ((), (), s32[]{:S(2)}) async-start(), calls=%async_computation.8 | async-start | bytes 13369344 | tf_op jit(solution)/shard_map/reduce_scatter | solution.py:280
  502.9 112.5 %collective-permute-start.10 = (bf16[512,2048]{1,0:T(8,128)(2,1)S(1)}, bf16[512,2048]{1,0:T(8,128)(2,1)}, u32[]{:S(2)}, u32[]{:S(2)}) collective-permute-start(bf16[512,2048]{1,0:T(8,128)(2,1)S(1)} %add_convert_fusion.4), channel_id=1, source_target_pairs={{0,1},{1,0},{2,3},{3,2},{4,5},{5,4},{6,7},{7,6},{8,9},{9,8},{10,11... | collective-permute-start | bytes 6291464 | tf_op jit(solution)/shard_map/ppermute | solution.py:284
  534.0 359.0 %reduce-scatter.9.cloned.1.call-start = ((), (), s32[]{:S(2)}) async-start(), calls=%async_computation.9 | async-start | bytes 4456448 | tf_op jit(solution)/shard_map/reduce_scatter | solution.py:280
  544.5 46.4 %collective-permute-start.12 = (bf16[1024,3072]{1,0:T(8,128)(2,1)S(1)}, bf16[1024,3072]{1,0:T(8,128)(2,1)}, u32[]{:S(2)}, u32[]{:S(2)}) collective-permute-start(bf16[1024,3072]{1,0:T(8,128)(2,1)S(1)} %convolution_convert_fusion.2), channel_id=1, source_target_pairs={{0,2},{2,0},{4,6},{6,4},{1,3},{3,1},{5,7},{7,5},{8,10},{10,8},{12,... | collective-permute-start | bytes 18874376 | tf_op jit(solution)/shard_map/ppermute | solution.py:294
  569.7 48.3 %copy-start.15 = (bf16[512,2048]{1,0:T(8,128)(2,1)}, bf16[512,2048]{1,0:T(8,128)(2,1)S(1)}, u32[]{:S(2)}) copy-start(bf16[512,2048]{1,0:T(8,128)(2,1)S(1)} %add_convert_fusion.3) | copy-start | bytes 6291460
  569.7 21.1 %copy-start.18 = (bf16[1024,2048]{1,0:T(8,128)(2,1)S(1)}, bf16[1024,2048]{1,0:T(8,128)(2,1)}, u32[]{:S(2)}) copy-start(bf16[1024,2048]{1,0:T(8,128)(2,1)} %relative.1) | copy-start | bytes 12582916
  569.7 47.7 %collective-permute-start.11 = (bf16[512,2048]{1,0:T(8,128)(2,1)S(1)}, bf16[512,2048]{1,0:T(8,128)(2,1)S(1)}, u32[]{:S(2)}, u32[]{:S(2)}) collective-permute-start(bf16[512,2048]{1,0:T(8,128)(2,1)S(1)} %add_convert_fusion.3), channel_id=1, source_target_pairs={{0,1},{1,0},{2,3},{3,2},{4,5},{5,4},{6,7},{7,6},{8,9},{9,8},{10,11... | collective-permute-start | bytes 6291464 | tf_op jit(solution)/shard_map/ppermute | solution.py:284
  603.7 113.9 %collective-permute-start.14 = (bf16[512,3072]{1,0:T(8,128)(2,1)}, bf16[512,3072]{1,0:T(8,128)(2,1)}, u32[]{:S(2)}, u32[]{:S(2)}) collective-permute-start(bf16[512,3072]{1,0:T(8,128)(2,1)} %slice.211), channel_id=1, source_target_pairs={{0,4},{2,6},{4,0},{6,2},{1,5},{3,7},{5,1},{7,3},{8,12},{10,14},{12... | collective-permute-start | bytes 9437192 | tf_op jit(solution)/shard_map/ppermute | solution.py:299
  617.4 148.9 %collective-permute-start.13 = (bf16[1024,2048]{1,0:T(8,128)(2,1)}, bf16[1024,2048]{1,0:T(8,128)(2,1)}, u32[]{:S(2)}, u32[]{:S(2)}) collective-permute-start(bf16[1024,2048]{1,0:T(8,128)(2,1)} %convolution_convert_fusion.3), channel_id=1, source_target_pairs={{0,1},{1,0},{2,3},{3,2},{4,5},{5,4},{6,7},{7,6},{8,9},{9,8},{10,11... | collective-permute-start | bytes 12582920 | tf_op jit(solution)/shard_map/ppermute | solution.py:284
  660.8 24.4 %collective-permute-start.17 = (bf16[2,512,512]{2,1,0:T(8,128)(2,1)}, bf16[2,512,512]{2,1,0:T(8,128)(2,1)}, u32[]{:S(2)}, u32[]{:S(2)}) collective-permute-start(bf16[2,512,512]{2,1,0:T(8,128)(2,1)} %get-tuple-element.107), channel_id=1, source_target_pairs={{0,2},{2,0},{4,6},{6,4},{1,3},{3,1},{5,7},{7,5},{8,10},{10,8},{12,... | collective-permute-start | bytes 3145736 | tf_op jit(solution)/shard_map/ppermute | solution.py:490
  679.0 52.2 %collective-permute-start.21 = (bf16[2,512,512]{2,1,0:T(8,128)(2,1)}, bf16[2,512,512]{2,1,0:T(8,128)(2,1)}, u32[]{:S(2)}, u32[]{:S(2)}) collective-permute-start(bf16[2,512,512]{2,1,0:T(8,128)(2,1)} %get-tuple-element.118), channel_id=1, source_target_pairs={{0,2},{2,0},{4,6},{6,4},{1,3},{3,1},{5,7},{7,5},{8,10},{10,8},{12,... | collective-permute-start | bytes 3145736 | tf_op jit(solution)/shard_map/ppermute | solution.py:490
  685.2 50.1 %collective-permute-start.16 = (bf16[2,512,512]{2,1,0:T(8,128)(2,1)}, bf16[2,512,512]{2,1,0:T(8,128)(2,1)S(1)}, u32[]{:S(2)}, u32[]{:S(2)}) collective-permute-start(bf16[2,512,512]{2,1,0:T(8,128)(2,1)} %get-tuple-element.105), channel_id=1, source_target_pairs={{0,2},{2,0},{4,6},{6,4},{1,3},{3,1},{5,7},{7,5},{8,10},{10,8},{12,... | collective-permute-start | bytes 3145736 | tf_op jit(solution)/shard_map/ppermute | solution.py:489
  685.3 39.7 %slice-start.2 = ((s8[8388608]{0:T(1024)(128)(4,1)}), s8[4194304]{0:T(1024)(128)(4,1)S(1)}, s32[]{:S(2)}) async-start(s8[8388608]{0:T(1024)(128)(4,1)} %bitcast.162), calls=%async_computation.13 | async-start | bytes 8388608
  688.0 37.0 %slice-start.3 = ((s8[8388608]{0:T(1024)(128)(4,1)}), s8[4194304]{0:T(1024)(128)(4,1)S(1)}, s32[]{:S(2)}) async-start(s8[8388608]{0:T(1024)(128)(4,1)} %bitcast.162), calls=%async_computation.14 | async-start | bytes 8388608
  688.0 62.7 %collective-permute-start.18 = (bf16[2,512,512]{2,1,0:T(8,128)(2,1)}, bf16[2,512,512]{2,1,0:T(8,128)(2,1)}, u32[]{:S(2)}, u32[]{:S(2)}) collective-permute-start(bf16[2,512,512]{2,1,0:T(8,128)(2,1)} %add_convert_fusion.6), channel_id=1, source_target_pairs={{4,0},{6,2},{5,1},{7,3},{12,8},{14,10},{13,9},{15,11},{20,16},{22,... | collective-permute-start | bytes 3145736 | tf_op jit(solution)/shard_map/ppermute | solution.py:491
  725.0 41.2 %collective-permute-start.15 = (bf16[128,3072]{1,0:T(8,128)(2,1)}, bf16[128,3072]{1,0:T(8,128)(2,1)}, u32[]{:S(2)}, u32[]{:S(2)}) collective-permute-start(bf16[128,3072]{1,0:T(8,128)(2,1)} %get-tuple-element.207), channel_id=1, source_target_pairs={{0,8},{8,0},{16,24},{24,16},{1,9},{9,1},{17,25},{25,17},{2,10},{10... | collective-permute-start | bytes 2359304 | tf_op jit(solution)/shard_map/ppermute | solution.py:308
  731.2 256.7 %reduce-scatter.11.cloned.1.call-start = ((), (), s32[]{:S(2)}) async-start(), calls=%async_computation.10 | async-start | bytes 8912896 | tf_op jit(solution)/shard_map/reduce_scatter | solution.py:280
  731.2 58.9 %collective-permute-start.20 = (bf16[2,512,512]{2,1,0:T(8,128)(2,1)}, bf16[2,512,512]{2,1,0:T(8,128)(2,1)}, u32[]{:S(2)}, u32[]{:S(2)}) collective-permute-start(bf16[2,512,512]{2,1,0:T(8,128)(2,1)} %get-tuple-element.116), channel_id=1, source_target_pairs={{0,2},{2,0},{4,6},{6,4},{1,3},{3,1},{5,7},{7,5},{8,10},{10,8},{12,... | collective-permute-start | bytes 3145736 | tf_op jit(solution)/shard_map/ppermute | solution.py:489
  735.3 30.9 %copy-start.26 = (bf16[2,512,512]{2,1,0:T(8,128)(2,1)}, bf16[2,512,512]{2,1,0:T(8,128)(2,1)S(1)}, u32[]{:S(2)}) copy-start(bf16[2,512,512]{2,1,0:T(8,128)(2,1)S(1)} %collective-permute-done.16.d_near) | copy-start | bytes 3145732
  735.3 54.8 %collective-permute-start.22 = (bf16[2,512,512]{2,1,0:T(8,128)(2,1)}, bf16[2,512,512]{2,1,0:T(8,128)(2,1)S(1)}, u32[]{:S(2)}, u32[]{:S(2)}) collective-permute-start(bf16[2,512,512]{2,1,0:T(8,128)(2,1)} %add_convert_fusion.5), channel_id=1, source_target_pairs={{4,0},{6,2},{5,1},{7,3},{12,8},{14,10},{13,9},{15,11},{20,16},{22,... | collective-permute-start | bytes 3145736 | tf_op jit(solution)/shard_map/ppermute | solution.py:491
  750.7 57.4 %collective-permute-start.19 = (bf16[128,3072]{1,0:T(8,128)(2,1)}, bf16[128,3072]{1,0:T(8,128)(2,1)S(1)}, u32[]{:S(2)}, u32[]{:S(2)}) collective-permute-start(bf16[128,3072]{1,0:T(8,128)(2,1)} %get-tuple-element.206), channel_id=1, source_target_pairs={{0,16},{8,24},{16,0},{24,8},{1,17},{9,25},{17,1},{25,9},{2,18},{10... | collective-permute-start | bytes 2359304 | tf_op jit(solution)/shard_map/ppermute | solution.py:308
  766.2 64.8 %collective-permute-start.23 = (bf16[128,3072]{1,0:T(8,128)(2,1)}, bf16[128,3072]{1,0:T(8,128)(2,1)}, u32[]{:S(2)}, u32[]{:S(2)}) collective-permute-start(bf16[128,3072]{1,0:T(8,128)(2,1)} %get-tuple-element.205), channel_id=1, source_target_pairs={{0,24},{8,16},{16,8},{24,0},{1,25},{9,17},{17,9},{25,1},{2,26},{10... | collective-permute-start | bytes 2359304 | tf_op jit(solution)/shard_map/ppermute | solution.py:308
  784.1 46.9 %collective-permute-start.24 = (bf16[512,2048]{1,0:T(8,128)(2,1)}, bf16[512,2048]{1,0:T(8,128)(2,1)}, u32[]{:S(2)}, u32[]{:S(2)}) collective-permute-start(bf16[512,2048]{1,0:T(8,128)(2,1)} %fusion.33), channel_id=1, source_target_pairs={{0,1},{1,0},{2,3},{3,2},{4,5},{5,4},{6,7},{7,6},{8,9},{9,8},{10,11... | collective-permute-start | bytes 6291464 | tf_op jit(solution)/shard_map/ppermute | solution.py:284
  845.1 47.9 %collective-permute-start.30 = (bf16[512,2048]{1,0:T(8,128)(2,1)S(1)}, bf16[512,2048]{1,0:T(8,128)(2,1)}, u32[]{:S(2)}, u32[]{:S(2)}) collective-permute-start(bf16[512,2048]{1,0:T(8,128)(2,1)S(1)} %fusion.36), channel_id=1, source_target_pairs={{0,1},{1,0},{2,3},{3,2},{4,5},{5,4},{6,7},{7,6},{8,9},{9,8},{10,11... | collective-permute-start | bytes 6291464 | tf_op jit(solution)/shard_map/ppermute | solution.py:284
  846.8 4.5 collective-permute-start.25
  851.2 5.2 collective-permute-start.26
  856.4 6.8 collective-permute-start.27
  863.2 7.4 collective-permute-start.28
  870.7 22.3 %collective-permute-start.29 = (f32[34,128]{1,0:T(8,128)S(1)}, f32[34,128]{1,0:T(8,128)S(1)}, u32[]{:S(2)}, u32[]{:S(2)}) collective-permute-start(f32[34,128]{1,0:T(8,128)S(1)} %add.172), channel_id=1, source_target_pairs={{0,1},{1,0},{2,3},{3,2},{4,5},{5,4},{6,7},{7,6},{8,9},{9,8},{10,11... | collective-permute-start | bytes 52232 | tf_op jit(solution)/shard_map/ppermute | solution.py:315
  (42 other events, 321.0 us)
Sparse Core Ops, SparseCore 0:
  13.9 109.4 all-gather.3
  125.5 167.7 all-gather.5
  295.5 107.1 all-gather.7
  449.8 148.4 reduce-scatter.4
  602.1 194.9 reduce-scatter.6
  800.9 80.4 reduce-scatter.8
  885.5 102.4 reduce-scatter.10
